TPU v7x, 32 devices: a whole 2x2x4 slice. The times are simulated.
32 devices in a mesh: views: 8 (over y, x, core), heads: 4 (over z).
Axes of the slice: x: 2, y: 2, z: 4, core: 2. Of those that a mesh axis runs over, the one named last changes fastest.
Arguments:
- latents: bfloat16 [32, 256, 1024], P('views'), may hold values from -6 to 6
- norm_gain: float32 [1024], replicated, may hold values from 0.25 to 1.75
- w_qkv: bfloat16 [3, 1024, 1024], P(None, None, 'heads'), may hold values from -0.1875 to 0.1875
- w_out: bfloat16 [1024, 1024], P('heads'), may hold values from -0.1875 to 0.1875
- intersection: int32 [32, 2], replicated, may hold values 0 or 1
- match_block: int32 [8192, 1], P('views'), may hold values from 0 to 7; in each aligned block of 1024 rows (0 to 1023, 1024 to 2047, ...) at most 256 rows name the same one
- match_row: int32 [8192], P('views'), may hold values from 0 to 1023
- confidence: float32 [8192], P('views'), may hold values from 0.2 to 1
Outputs:
- refined: float32 [32, 256, 1024], P('views', None, 'heads')
Inputs may be any that keep to these rules, and one draw needn't show every extreme that they name: `match_block`: among the rows of one device (1024 aligned rows), at most 256 name the same block, and some block is named by exactly 256 of them.
All inputs are finite; a program needn't handle non-finite values.
Results may differ from a plain program's by a relative error of at most 0.012.
The roundings to bfloat16 on the way count: a program that leaves them out, or rounds other values in their place, can miss the bound.
Values may be sent and summed in bfloat16 or wider, within the bound.
No kernel may reach another device: no remote copies, remote signals or barrier semaphores. Data moves between devices by JAX's collectives and lax.ppermute only.
A program may use at most 128 MiB of HBM per device.

v0:
```python
import jax
import jax.numpy as jnp
from jax import lax
from jax.experimental import pallas as pl
from jax.experimental.pallas import tpu as pltpu
from jax.sharding import PartitionSpec as P


HEAD_DIM = 64
LANES = 128

coupling = 0.5
epsilon = 1e-06

bf16 = jnp.bfloat16
f32 = jnp.float32


def cost(flops, bytes_accessed, transcendentals=0):
    return pl.CostEstimate(
        flops=int(flops), bytes_accessed=int(bytes_accessed), transcendentals=int(transcendentals)
    )


def dot(a, b):
    return jnp.dot(a, b, preferred_element_type=f32)


VMEM_SPEC = pl.BlockSpec(memory_space=pltpu.VMEM)
SMEM_SPEC = pl.BlockSpec(memory_space=pltpu.SMEM)
ANY_SPEC = pl.BlockSpec(memory_space=pl.ANY)


def grant(mib):
    return pltpu.CompilerParams(vmem_limit_bytes=mib << 20)


def many(spec, count):
    return [spec] * count


def project_views(meta, latents, gain, w_qkv, which, w_out=None):
    _, tokens, width = latents.shape
    sub = w_qkv.shape[2]
    count = len(which)
    scale = HEAD_DIM ** (-0.5)
    order = (2, 0, 1)

    extra = 0 if w_out is None else 1
    strip = sub // 2

    def body(meta_ref, lat_hbm, gain_hbm, w_hbm, *refs):
        outs, (buffer, gains, ws, sems) = refs[extra : 2 * count + extra], refs[-4:]
        splits = []
        if extra:
            own, pair, other = refs[2 * count + 1 : 2 * count + 4]
            side = meta_ref[1] // 2
            near = pl.ds(pl.multiple_of(side * 2 * sub, 2 * sub), 2 * sub)
            away = pl.ds(pl.multiple_of((1 - side) * 2 * sub, 2 * sub), 2 * sub)
            mine = pl.ds(pl.multiple_of((meta_ref[0] % 2) * strip, strip), strip)
            for i, (source, target) in enumerate(
                (
                    (refs[0].at[:, near], own),
                    (refs[0].at[mine, near], pair.at[0]),
                    (refs[0].at[mine, away], pair.at[1]),
                    (refs[0].at[mine, away], other),
                )
            ):
                splits.append(pltpu.make_async_copy(source, target, sems.at[count + 4 + i]))
        copies = [
            pltpu.make_async_copy(lat_hbm.at[v], buffer.at[i], sems.at[i])
            for i, v in enumerate(which)
        ]
        copies.insert(1, pltpu.make_async_copy(gain_hbm, gains, sems.at[count]))
        w_copies = {
            part: pltpu.make_async_copy(w_hbm.at[part], ws.at[part], sems.at[count + 1 + part])
            for part in order
        }
        copies[0].start()
        copies[1].start()
        for part in order:
            w_copies[part].start()
        for copy in copies[2:] + splits:
            copy.start()
        for i in range(count):
            copies[i if i == 0 else i + 1].wait()
            if i == 0:
                copies[1].wait()
            wide = buffer[i].astype(f32)
            mean_square = jnp.mean(wide * wide, axis=-1, keepdims=True)
            normed = (wide * lax.rsqrt(mean_square + epsilon) * gains[...]).astype(bf16)
            if i == 0:
                w_copies[2].wait()
            values = dot(normed, ws[2])
            if i == 0:
                w_copies[0].wait()
            queries = dot(normed, ws[0])
            if i == 0:
                w_copies[1].wait()
            outs[2 * i + 1][0] = dot(normed, ws[1]).astype(bf16)
            outs[2 * i + 1][1] = jnp.transpose(values).astype(bf16)
            outs[2 * i][...] = jnp.transpose(queries).astype(bf16) * jnp.asarray(scale, bf16)
        for copy in splits:
            copy.wait()

    out_shape = []
    for _ in which:
        out_shape += [
            jax.ShapeDtypeStruct((sub, tokens), bf16),
            jax.ShapeDtypeStruct((2, tokens, sub), bf16),
        ]
    if extra:
        out_shape += [
            jax.ShapeDtypeStruct((sub, 2 * sub), bf16),
            jax.ShapeDtypeStruct((2, strip, 2 * sub), bf16),
            jax.ShapeDtypeStruct((strip, 2 * sub), bf16),
        ]
    outs = pl.pallas_call(
        body,
        in_specs=[SMEM_SPEC] + many(ANY_SPEC, 3 + extra),
        out_specs=many(VMEM_SPEC, len(out_shape)),
        out_shape=out_shape,
        scratch_shapes=[
            pltpu.VMEM((count, tokens, width), bf16),
            pltpu.VMEM((1, width), f32),
            pltpu.VMEM((3, width, sub), bf16),
            pltpu.SemaphoreType.DMA((count + 8,)),
        ],
        name="project_views",
        compiler_params=grant(52),
        cost_estimate=cost(
            count * 6 * tokens * width * sub, count * tokens * (width + 3 * sub) * 2 + 6 * width * sub
        ),
    )(meta, latents, gain, w_qkv, *([w_out] if extra else []))
    return {v: (outs[2 * i], outs[2 * i + 1]) for i, v in enumerate(which)}, outs[2 * count :]


ONES = 16
SAFE_TOTAL = 1e30
FAR = 1e30


def head_scores(q_ref, kv_ref, h):
    per = LANES // HEAD_DIM
    j, slot = h // per, h % per
    own = q_ref[h * HEAD_DIM : (h + 1) * HEAD_DIM, :]
    zero = jnp.zeros_like(own)
    padded = jnp.concatenate([own if s == slot else zero for s in range(per)], axis=0)
    return dot(kv_ref[0, :, j * LANES : (j + 1) * LANES], padded)


def head_values(kv_ref, h):
    rows = kv_ref[1, h * HEAD_DIM : (h + 1) * HEAD_DIM, :]
    return jnp.concatenate([rows, jnp.ones((ONES, rows.shape[1]), bf16)], axis=0)


def attention_cost(tokens, sub, pairs):
    heads = sub // HEAD_DIM
    return cost(
        pairs * heads * tokens * tokens * 4 * LANES,
        pairs * tokens * sub * 8,
        pairs * heads * tokens * tokens,
    )


def far_if_absent(inter_ref, at, offset):
    return jnp.where(inter_ref[offset, at] > 0, 0.0, FAR).astype(f32)


def sources_of(view, local_views, window):
    found = []
    for o in range(window):
        if view + o + 1 < local_views:
            found.append((view + o + 1, view, o))
        if view - o - 1 >= 0:
            found.append((view - o - 1, view - o - 1, o))
    return found


def attend(
    meta, inter, queries, blocks, remote, plan, window, earlier=None, last=True, merged=False
):
    local_views = len(blocks)
    sub, tokens = queries[0].shape
    heads = sub // HEAD_DIM
    tall = HEAD_DIM + ONES
    views_total = inter.shape[1]
    names = sorted(remote)
    count = len(plan)
    held = 0 if earlier is None else 2

    def body(meta_ref, inter_ref, *refs):
        before, refs = refs[:held], refs[held:]
        qs, refs = refs[:count], refs[count:]
        kvs, refs = refs[:local_views], refs[local_views:]
        far_kvs, refs = dict(zip(names, refs[: len(names)])), refs[len(names) :]
        first = meta_ref[0] * local_views

        def global_view(source):
            at = first + source
            return jnp.where(at < 0, at + views_total, at) if source < 0 else at

        def keys_of(i):
            view, sources = plan[i]
            keys = [] if held else [(kvs[view], None, None)]
            if not held:
                keys += [(kvs[t], source, o) for t, source, o in sources_of(view, local_views, window)]
            return keys + [(far_kvs[name], source, o) for name, source, o in sources]

        if last:
            outs = [refs[0].at[i] for i in range(count)] if merged else refs[:count]
        units = [(i, h, k) for i in range(count) for h in range(heads) for k in keys_of(i)]
        far = {}
        for _, _, (_, source, o) in units:
            if source is not None and (source, o) not in far:
                far[source, o] = far_if_absent(inter_ref, global_view(source), o)
        upcoming = head_scores(qs[units[0][0]], units[0][2][0], units[0][1])
        worst = jnp.zeros((1, tokens), f32)
        n = 0
        for i, (view, _) in enumerate(plan):
            parts = []
            for h in range(heads):
                keys = keys_of(i)
                weights = []
                top = before[1][i, h : h + 1, :] if held else None
                for _, source, o in keys:
                    scores = upcoming
                    n += 1
                    if n < len(units):
                        ni, nh, (nk, _, _) = units[n]
                        upcoming = head_scores(qs[ni], nk, nh)
                    if source is None:
                        top = jnp.max(scores, axis=0, keepdims=True)
                        shift = top
                    else:
                        shift = top + far[source, o]
                    weights.append(jnp.exp(scores - shift).astype(bf16))
                values = jnp.concatenate([head_values(k[0], h) for k in keys], axis=1)
                sums = dot(values, jnp.concatenate(weights, axis=0))
                if held:
                    sums = sums + before[0][i, h * tall : (h + 1) * tall, :]
                if not last:
                    refs[0][i, h * tall : (h + 1) * tall, :] = sums
                    refs[1][i, h : h + 1, :] = top
                    continue
                total = sums[HEAD_DIM : HEAD_DIM + 1, :]
                worst = jnp.maximum(worst, jnp.where(total < SAFE_TOTAL, 0.0, 1.0))
                parts.append(sums[:HEAD_DIM, :] * (1.0 / total))
            if last:
                outs[i][...] = jnp.transpose(jnp.concatenate(parts, axis=0)).astype(bf16)
        if not last:
            return
        work, work_stat = refs[-2:]

        @pl.when(jnp.max(worst) > 0.0)
        def _():
            for i, (view, sources) in enumerate(plan):
                exact_add(qs[i], kvs[view], work, work_stat, heads, True)
                every = [(kvs[t], s, o) for t, s, o in sources_of(view, local_views, window)]
                every += [(far_kvs[name], s, o) for name, s, o in sources]
                for kv, source, o in every:

                    @pl.when(inter_ref[o, global_view(source)] > 0)
                    def _(i=i, kv=kv):
                        exact_add(qs[i], kv, work, work_stat, heads, False)

                parts = []
                for h in range(heads):
                    total = work_stat[h, 1:2, :]
                    parts.append(work[h * HEAD_DIM : (h + 1) * HEAD_DIM, :] * (1.0 / total))
                outs[i][...] = jnp.transpose(jnp.concatenate(parts, axis=0)).astype(bf16)

    if last:
        out_shape = [jax.ShapeDtypeStruct((tokens, sub), bf16)] * count
        if merged:
            out_shape = [jax.ShapeDtypeStruct((count, tokens, sub), bf16)]
        scratch = [pltpu.VMEM((sub, tokens), f32), pltpu.VMEM((heads, 8, tokens), f32)]
    else:
        out_shape = [
            jax.ShapeDtypeStruct((count, heads * tall, tokens), f32),
            jax.ShapeDtypeStruct((count, heads, tokens), f32),
        ]
        scratch = []
    pairs = sum(len(s) for _, s in plan)
    if not held:
        pairs += sum(1 + len(sources_of(v, local_views, window)) for v, _ in plan)
    return pl.pallas_call(
        body,
        in_specs=[SMEM_SPEC, SMEM_SPEC]
        + many(VMEM_SPEC, held + count + local_views + len(names)),
        out_specs=many(VMEM_SPEC, len(out_shape)),
        out_shape=out_shape,
        scratch_shapes=scratch,
        name="attend" if last else "attend_local",
        compiler_params=grant(12),
        cost_estimate=attention_cost(tokens, sub, pairs),
    )(
        meta,
        inter,
        *(earlier or ()),
        *queries,
        *[blocks[v] for v in range(local_views)],
        *[remote[name] for name in names],
    )


def exact_add(q_ref, kv_ref, work, work_stat, heads, start):
    per = LANES // HEAD_DIM

    def one_head(h, _):
        base = pl.multiple_of((h // per) * LANES, LANES)
        queries = q_ref[pl.ds(base, LANES), :]
        owner = lax.broadcasted_iota(jnp.int32, queries.shape, 0) // HEAD_DIM
        queries = jnp.where(owner == h % per, queries.astype(f32), 0.0).astype(bf16)
        scores = dot(kv_ref[0, :, pl.ds(base, LANES)], queries)
        top = jnp.max(scores, axis=0, keepdims=True)
        rows = pl.ds(pl.multiple_of(h * HEAD_DIM, HEAD_DIM), HEAD_DIM)
        values = kv_ref[1, rows, :]
        if not start:
            old = work_stat[h, 0:1, :]
            top = jnp.maximum(old, top)
        weights = jnp.exp(scores - top)
        total = jnp.sum(weights, axis=0, keepdims=True)
        sums = dot(values, weights.astype(bf16))
        if not start:
            fade = jnp.exp(old - top)
            total = total + work_stat[h, 1:2, :] * fade
            sums = sums + work[rows, :] * fade
        work_stat[h, 0:1, :] = top
        work_stat[h, 1:2, :] = total
        work[rows, :] = sums
        return 0

    lax.fori_loop(0, heads, one_head, 0)


def project_out(meta, attended, weights, latents, views):
    count = len(attended)
    groups = len(attended[0])
    arrays = []
    for row in attended:
        for array, _ in row:
            if not any(array is a for a in arrays):
                arrays.append(array)
    spots = [
        [([a is array for a in arrays].index(True), index) for array, index in row] for row in attended
    ]
    tokens, sub = arrays[0].shape[-2:]

    def pick(refs, spot):
        ref, index = refs[spot[0]], spot[1]
        return ref[...] if index is None else ref[index]

    def body(meta_ref, *refs):
        att, refs = refs[: len(arrays)], refs[len(arrays) :]
        ws, refs = refs[: len(weights)], refs[len(weights) :]
        lat_hbm, refs = refs[0], refs[1:]
        owns, others = refs[:count], refs[count : 2 * count]
        buffer, sems = refs[2 * count :]
        columns = pl.ds(pl.multiple_of((meta_ref[1] // 2) * 2 * sub, 2 * sub), 2 * sub)
        copies = [
            pltpu.make_async_copy(lat_hbm.at[v, :, columns], buffer.at[i], sems.at[i])
            for i, v in enumerate(views)
        ]
        for copy in copies:
            copy.start()
        odd = meta_ref[1] % 2 == 1
        second = meta_ref[0] % 2 == 1
        rows = [ws[0][...]]
        for mine, theirs in zip(ws[1 : 1 + groups - 1], ws[groups:]):
            mine, theirs = mine[...], theirs[...]
            if len(mine.shape) == 3:
                mine, theirs = mine[0], theirs[0]
            rows.append(jnp.where(second, theirs, mine))
            rows.append(jnp.where(second, mine, theirs))
        matrix = jnp.concatenate(rows, axis=0)
        for i in range(count):
            total = dot(jnp.concatenate([pick(att, spot) for spot in spots[i]], axis=1), matrix)
            copies[i].wait()
            layer = (buffer[i].astype(f32) + total).astype(bf16)
            low, high = layer[:, :sub], layer[:, sub:]
            owns[i][...] = jnp.where(odd, high, low)
            others[i][...] = jnp.where(odd, low, high)

    outs = pl.pallas_call(
        body,
        in_specs=[SMEM_SPEC]
        + many(VMEM_SPEC, len(arrays) + len(weights))
        + [ANY_SPEC],
        out_specs=many(VMEM_SPEC, 2 * count),
        out_shape=[jax.ShapeDtypeStruct((tokens, sub), bf16)] * (2 * count),
        scratch_shapes=[
            pltpu.VMEM((count, tokens, 2 * sub), bf16),
            pltpu.SemaphoreType.DMA((count,)),
        ],
        name="project_out",
        compiler_params=grant(12),
        cost_estimate=cost(
            groups * count * tokens * sub * 4 * sub,
            groups * (count * tokens * sub + 2 * sub * sub) * 2 + count * tokens * sub * 8,
        ),
    )(meta, *arrays, *weights, latents)
    return outs[:count], outs[count:]


def prepare_requests(block_rows, token_rows, peers, capacity):
    strips, lanes = block_rows.shape

    def body(block_ref, token_ref, wanted_ref, code_ref):
        before = (
            lax.broadcasted_iota(jnp.int32, (lanes, lanes), 0)
            < lax.broadcasted_iota(jnp.int32, (lanes, lanes), 1)
        ).astype(bf16)
        peer_ids = lax.broadcasted_iota(jnp.int32, (peers, lanes), 0)
        carry = jnp.zeros((peers, 1), f32)
        slots, lefts = [], []
        for i in range(strips):
            block = block_ref[i : i + 1, :]
            hit = (peer_ids == block).astype(f32)
            rank = dot(hit.astype(bf16), before) + carry
            carry = carry + jnp.sum(hit, axis=1, keepdims=True)
            slot = jnp.sum(rank * hit, axis=0, keepdims=True)
            slots.append(slot)
            code_ref[i : i + 1, :] = block * capacity + slot.astype(jnp.int32)
            token = token_ref[i : i + 1, :]
            coarse = (token // 32).astype(f32)
            fine = (token % 32).astype(f32)
            lefts.append(jnp.concatenate([hit * coarse, hit * fine], axis=0).astype(bf16))
        columns = jnp.transpose(jnp.concatenate(slots, axis=0))
        place = lax.broadcasted_iota(jnp.int32, (lanes, capacity), 1).astype(f32)
        total = jnp.zeros((2 * peers, capacity), f32)
        for i in range(strips):
            spot = (columns[:, i : i + 1] == place).astype(bf16)
            total = total + dot(lefts[i], spot)
        wanted_ref[...] = (total[:peers] * 32.0 + total[peers:]).astype(jnp.int32)

    return pl.pallas_call(
        body,
        in_specs=[VMEM_SPEC, VMEM_SPEC],
        out_specs=[VMEM_SPEC, VMEM_SPEC],
        out_shape=[
            jax.ShapeDtypeStruct((peers, capacity), jnp.int32),
            jax.ShapeDtypeStruct((strips, lanes), jnp.int32),
        ],
        name="prepare_requests",
        compiler_params=grant(8),
        cost_estimate=cost(2 * strips * lanes * lanes * capacity, 3 * strips * lanes * 4),
    )(block_rows, token_rows)


def picks(offsets, width):
    clamped = jnp.minimum(jnp.maximum(offsets, -1.0), float(width)).astype(bf16)
    place = lax.broadcasted_iota(jnp.int32, (offsets.shape[0], width), 1).astype(f32).astype(bf16)
    spread = jnp.broadcast_to(clamped, place.shape)
    return jnp.where(spread == place, jnp.ones_like(place), jnp.zeros_like(place))


def gather_rows(meta, wanted, pieces):
    peers, capacity = wanted.shape
    tokens, sub = pieces[0][0].shape
    local_views = len(pieces)
    rows = local_views * tokens
    flat = [p for pair in pieces for p in pair]

    def body(meta_ref, wanted_ref, *refs):
        ins = refs[: len(flat)]
        layer, outs = refs[len(flat)], refs[len(flat) + 1 :]
        end = jnp.logical_or(meta_ref[1] == 0, meta_ref[1] == meta_ref[2] - 1)
        for v in range(local_views):
            layer[v * tokens : (v + 1) * tokens, :] = jnp.where(
                end, ins[2 * v + 1][...], ins[2 * v][...]
            )
        lines = [wanted_ref[pl.ds(lax.bitwise_xor(meta_ref[0], m), 1), :] for m in range(peers)]
        columns = jnp.transpose(jnp.concatenate(lines, axis=0).astype(f32))
        for mask in range(peers):
            column = columns[:, mask : mask + 1]
            pick = jnp.concatenate(
                [picks(column - float(v * tokens), tokens) for v in range(local_views)], axis=1
            )
            outs[mask][...] = dot(pick, layer[...]).astype(bf16)

    return pl.pallas_call(
        body,
        in_specs=[SMEM_SPEC] + many(VMEM_SPEC, 1 + len(flat)),
        out_specs=many(VMEM_SPEC, 1 + peers),
        out_shape=[jax.ShapeDtypeStruct((rows, sub), bf16)]
        + [jax.ShapeDtypeStruct((capacity, sub), bf16)] * peers,
        name="gather_rows",
        compiler_params=grant(12),
        cost_estimate=cost(2 * peers * capacity * rows * sub, 2 * (rows + peers * capacity) * sub * 2),
    )(meta, wanted, *flat)


def finish_rows(meta, code, confidence, layer, replies, tokens):
    rows, sub = layer.shape
    peers = len(replies)
    capacity = replies[0].shape[0]
    _, lanes = code.shape
    blocks = rows // tokens
    per = tokens // lanes

    def body(meta_ref, code_ref, conf_ref, layer_ref, *refs):
        reps, (out_hbm, buffer, sems) = refs[:peers], refs[peers:]
        codes = jnp.transpose(code_ref[...].astype(f32))
        confs = jnp.transpose(conf_ref[...]) * coupling
        copies = []
        for g in range(blocks):

            def column(turned):
                return jnp.concatenate(
                    [turned[:, g * per + j : g * per + j + 1] for j in range(per)], axis=0
                )

            code_column = column(codes)
            pick = jnp.concatenate(
                [
                    picks(
                        code_column
                        - (lax.bitwise_xor(meta_ref[0], mask) * capacity).astype(f32),
                        capacity,
                    )
                    for mask in range(peers)
                ],
                axis=1,
            )
            fetched = dot(pick, jnp.concatenate([r[...] for r in reps], axis=0))
            wide = layer_ref[g * tokens : (g + 1) * tokens, :].astype(f32)
            buffer[g] = wide + column(confs) * (fetched - wide)
            copies.append(
                pltpu.make_async_copy(
                    buffer.at[g], out_hbm.at[pl.ds(g * tokens, tokens), :], sems.at[g]
                )
            )
            copies[-1].start()
        for copy in copies:
            copy.wait()

    return pl.pallas_call(
        body,
        in_specs=[SMEM_SPEC] + many(VMEM_SPEC, 3 + peers),
        out_specs=ANY_SPEC,
        out_shape=jax.ShapeDtypeStruct((rows, sub), f32),
        scratch_shapes=[
            pltpu.VMEM((blocks, tokens, sub), f32),
            pltpu.SemaphoreType.DMA((blocks,)),
        ],
        name="finish_rows",
        compiler_params=grant(12),
        cost_estimate=cost(2 * peers * capacity * rows * sub, rows * sub * 6 + peers * capacity * sub * 2),
    )(meta, code, confidence, layer, *replies)


def per_device(latents, norm_gain, w_qkv, w_out, intersection, match_block, match_row, confidence):
    local_views, tokens, width = latents.shape
    window = intersection.shape[1]
    sub = w_qkv.shape[2]
    peers = lax.axis_size("views")
    ends = lax.axis_size("heads")
    rows = local_views * tokens
    capacity = 2 * rows // peers
    assert local_views == 4 and window == 2 and ends == 4 and tokens == sub
    view_at, head_at = lax.axis_index("views"), lax.axis_index("heads")
    spot = jnp.arange(4, dtype=jnp.int32)
    meta = jnp.where(spot == 0, view_at, jnp.where(spot == 1, head_at, ends)).astype(jnp.int32)

    def along(x, by):
        return lax.ppermute(x, "views", [(i, (i + by) % peers) for i in range(peers)])

    def partner(x, mask):
        return lax.ppermute(x, "views", [(i, i ^ mask) for i in range(peers)])

    def across(x, pairs):
        return lax.ppermute(x, "heads", pairs)

    def after(x, done):
        return lax.optimization_barrier((x, done))[0]

    beside, middle, back = [(0, 1), (3, 2)], [(1, 2), (2, 1)], [(1, 0), (2, 3)]
    gain = norm_gain.reshape(1, width)
    inter = intersection.T
    projected, _ = project_views(meta, latents, gain, w_qkv, (0, local_views - 1))
    next_first = along(projected[0][1], -1)
    prev_last = along(projected[3][1], 1)
    more, (own_half, w_pair, w_other) = project_views(
        meta, latents, gain, w_qkv, (1, 2), after(w_out, projected[0][0])
    )
    projected.update(more)
    queries = {v: projected[v][0] for v in range(local_views)}
    blocks = {v: projected[v][1] for v in range(local_views)}
    w_beside = across(w_pair, beside)
    w_middle = across(w_other, middle)

    inner_plan = [(1, [("prev_last", -1, 1)]), (2, [("next_first", 2, 1)])]
    inner_queries = [queries[1], queries[2]]
    local = attend(
        meta, inter, inner_queries, blocks, {}, [(v, []) for v, _ in inner_plan], window, last=False
    )
    next_second = along(after(blocks[1], local[0]), -1)
    prev_second = along(after(blocks[2], local[0]), 1)
    remote = dict(prev_last=prev_last, next_first=next_first)
    (inner,) = attend(
        meta,
        inter,
        inner_queries,
        blocks,
        remote,
        inner_plan,
        window,
        earlier=tuple(local),
        merged=True,
    )
    inner_beside = across(inner, beside)
    inner_middle = across(inner, middle)
    w_far = across(after(w_beside[1], inner), middle)

    remote.update(prev_second=prev_second, next_second=next_second)
    outer_plan = [
        (0, [("prev_last", -1, 0), ("prev_second", -2, 1)]),
        (3, [("next_first", 3, 0), ("next_second", 3, 1)]),
    ]
    outer_queries = [after(queries[0], inner), queries[3]]
    outer = attend(meta, inter, outer_queries, blocks, remote, outer_plan, window)
    strips = rows // LANES
    wanted, code = prepare_requests(
        after(match_block.reshape(strips, LANES), outer[0]),
        match_row.reshape(strips, LANES),
        peers,
        capacity,
    )
    wanted = lax.all_to_all(wanted, "views", split_axis=0, concat_axis=0, tiled=True)

    outer_beside, outer_middle, outer_far = [None] * 2, [None] * 2, [None] * 2
    for i in range(2):
        outer_beside[i] = across(outer[i], beside)
        outer_middle[i] = across(outer[i], middle)
    inner_far = across(inner_beside, middle)
    for i in range(2):
        outer_far[i] = across(outer_beside[i], middle)
    w_mine = [w_beside, w_middle, w_far]
    w_theirs = [partner(w, 1) for w in w_mine]
    weights = [own_half, *w_mine, *w_theirs]
    formed = {}
    for views, attended in (
        ((1, 2), [[(x, i) for x in (inner, inner_beside, inner_middle, inner_far)] for i in (0, 1)]),
        ((0,), [[(x[0], None) for x in (outer, outer_beside, outer_middle, outer_far)]]),
        ((3,), [[(x[1], None) for x in (outer, outer_beside, outer_middle, outer_far)]]),
    ):
        if not formed:
            weights[0] = after(weights[0], wanted)
        owns, others = project_out(meta, attended, weights, latents, views)
        returned = [across(x, back) for x in others]
        for v, own, got in zip(views, owns, returned):
            formed[v] = (own, got)

    pieces = [formed[v] for v in range(local_views)]
    layer, *outgoing = gather_rows(meta, wanted, pieces)
    replies = [outgoing[0]]
    for mask in range(1, peers):
        replies.append(partner(outgoing[mask], mask))
    refined = finish_rows(
        meta, code, confidence.reshape(strips, LANES), layer, replies, tokens
    )
    return refined.reshape(local_views, tokens, sub)


def solution(mesh):
    in_specs = (
        P("views", None, None),
        P(),
        P(None, None, "heads"),
        P("heads", None),
        P(),
        P("views", None),
        P("views"),
        P("views"),
    )
    out_specs = P("views", None, "heads")
    return jax.shard_map(
        per_device, mesh=mesh, in_specs=in_specs, out_specs=out_specs, check_vma=False
    )
```

profile of v0, /device:TPU:0, one launch (start us, length us, event | category | flops | bytes accessed | tf_op | source)
XLA Modules:
  0.0 128.1 jit_solution(16559602548418614000)
XLA Ops:
  0.0 0.7 copy-done.2
  0.8 4.0 %project_views.2 = (bf16[256,256]{1,0:T(8,128)(2,1)S(1)}, bf16[2,256,256]{2,1,0:T(8,128)(2,1)S(1)}, bf16[256,256]{1,0:T(8,128)(2,1)S(1)}, bf16[2,256,256]{2,1,0:T(8,128)(2,1)S(1)}) custom-call(s32[4]{0:T(128)S(1)} %compare_select_fusion.1.meta_ref, bf16[4,256,1024]{2,1,0:T(8,128)(2,1)} %refs_11_.5, f32[1,1024]{1,0:T(1,128)S(1)} %bitcast.12, ...), custom_call_target="tpu_custom_call" | custom-call | flops 805306368 | bytes 3407872 | tf_op jit(solution)/shard_map/project_views/pallas_call | solution.py:118
  4.7 3.4 %collective-permute-start = (bf16[2,256,256]{2,1,0:T(8,128)(2,1)S(1)}, bf16[2,256,256]{2,1,0:T(8,128)(2,1)S(1)}, u32[]{:S(2)}, u32[]{:S(2)}) collective-permute-start(bf16[2,256,256]{2,1,0:T(8,128)(2,1)S(1)} %get-tuple-element.50.refs_2_.refs_4_), channel_id=1, source_target_pairs={{0,28},{4,0},{8,4},{12,8},{16,12},{20,16},{24,20},{28,24},{1,29},{... | collective-permute-start | bytes 786440 | tf_op jit(solution)/shard_map/ppermute | solution.py:567
  8.1 4.0 %project_views.3 = (bf16[256,256]{1,0:T(8,128)(2,1)S(1)}, bf16[2,256,256]{2,1,0:T(8,128)(2,1)S(1)}, bf16[256,256]{1,0:T(8,128)(2,1)S(1)}, bf16[2,256,256]{2,1,0:...) custom-call(s32[4]{0:T(128)S(1)} %compare_select_fusion.1.meta_ref, ...), custom_call_target="tpu_custom_call" | custom-call | flops 805306368 | bytes 3407872 | tf_op jit(solution)/shard_map/project_views/pallas_call | solution.py:118
  12.1 0.7 collective-permute-start.8
  12.8 2.9 %attend_local.1 = (f32[2,320,256]{2,1,0:T(8,128)S(1)}, f32[2,4,256]{2,1,0:T(4,128)S(1)}) custom-call(s32[4]{0:T(128)S(1)} %compare_select_fusion.1.meta_ref, s32[2,32]{1,0:T(2,128)S(1)} %bitcast.16, bf16[256,256]{1,0:T(8,128)(2,1)S(1)} %get-tuple-element.48.refs_0_.refs_2_, bf16[256,256]{1,0:T(8,128)(2,1)S(1)} %get-tuple-element.49.refs_1_.refs_3_, ...), custom_call_target="tpu_custom_call" | custom-call | flops 1073741824 | bytes 4194304 | tf_op jit(solution)/shard_map/attend_local/pallas_call | solution.py:287
  15.8 2.7 %collective-permute-start.2 = (bf16[2,256,256]{2,1,0:T(8,128)(2,1)S(1)}, bf16[2,256,256]{2,1,0:T(8,128)(2,1)S(1)}, u32[]{:S(2)}, u32[]{:S(2)}) collective-permute-start(bf16[2,256,256]{2,1,0:T(8,128)(2,1)S(1)} %get-tuple-element.58.refs_3_.refs_5_), channel_id=1, source_target_pairs={{0,28},{4,0},{8,4},{12,8},{16,12},{20,16},{24,20},{28,24},{1,29},{... | collective-permute-start | bytes 786440 | tf_op jit(solution)/shard_map/ppermute | solution.py:567
  18.5 6.0 %collective-permute-start.7 = (bf16[2,128,512]{2,1,0:T(8,128)(2,1)S(1)}, bf16[2,128,512]{2,1,0:T(8,128)(2,1)S(1)}, u32[]{:S(2)}, u32[]{:S(2)}) collective-permute-start(bf16[2,128,512]{2,1,0:T(8,128)(2,1)S(1)} %get-tuple-element.66), channel_id=1, source_target_pairs={{0,1},{3,2},{4,5},{7,6},{8,9},{11,10},{12,13},{15,14},{16,17},{19,... | collective-permute-start | bytes 786440 | tf_op jit(solution)/shard_map/ppermute | solution.py:573
  24.5 0.1 collective-permute-start.11
  24.6 1.7 %attend.2.refs_0_ = bf16[2,256,256]{2,1,0:T(8,128)(2,1)S(1)} custom-call(s32[4]{0:T(128)S(1)} %compare_select_fusion.1.meta_ref, s32[2,32]{1,0:T(2,128)S(1)} %bitcast.17, f32[2,320,256]{2,1,0:T(8,128)S(1)} %get-tuple-element.54.refs_0_, f32[2,4,256]{2,1,0:T(4,128)S(1)} %get-tuple-element.55.refs_1_, bf16[256,256]{1,0:T(8,128)(2,1)S(1)} %get-tuple-element.48.refs_0_.refs_2_, ...), custom_call_target="tpu_custom_call" | custom-call | flops 268435456 | bytes 1048576 | tf_op jit(solution)/shard_map/attend/pallas_call | solution.py:287
  26.4 3.5 %attend.3 = (bf16[256,256]{1,0:T(8,128)(2,1)S(1)}, bf16[256,256]{1,0:T(8,128)(2,1)S(1)}) custom-call(s32[4]{0:T(128)S(1)} %compare_select_fusion.1.meta_ref, s32[2,32]{1,0:T(2,128)S(1)} %bitcast.18, bf16[256,256]{1,0:T(8,128)(2,1)S(1)} %get-tuple-element.56.refs_0_, bf16[256,256]{1,0:T(8,128)(2,1)S(1)} %get-tuple-element.57.refs_1_, ...), custom_call_target="tpu_custom_call" | custom-call | flops 1342177280 | bytes 5242880 | tf_op jit(solution)/shard_map/attend/pallas_call | solution.py:287
  29.9 5.0 %collective-permute-start.4 = (bf16[256,256]{1,0:T(8,128)(2,1)S(1)}, bf16[256,256]{1,0:T(8,128)(2,1)S(1)}, u32[]{:S(2)}, u32[]{:S(2)}) collective-permute-start(bf16[256,256]{1,0:T(8,128)(2,1)S(1)} %get-tuple-element.60.refs_0_), channel_id=1, source_target_pairs={{0,1},{3,2},{4,5},{7,6},{8,9},{11,10},{12,13},{15,14},{16,17},{19,... | collective-permute-start | bytes 393224 | tf_op jit(solution)/shard_map/ppermute | solution.py:573
  34.9 0.7 collective-permute-start.5
  35.5 3.0 %collective-permute-start.14 = (bf16[2,256,256]{2,1,0:T(8,128)(2,1)S(1)}, bf16[2,256,256]{2,1,0:T(8,128)(2,1)S(1)}, u32[]{:S(2)}, u32[]{:S(2)}) collective-permute-start(bf16[2,256,256]{2,1,0:T(8,128)(2,1)S(1)} %attend.2.refs_0_), channel_id=1, source_target_pairs={{0,1},{3,2},{4,5},{7,6},{8,9},{11,10},{12,13},{15,14},{16,17},{19,... | collective-permute-start | bytes 786440 | tf_op jit(solution)/shard_map/ppermute | solution.py:573
  38.6 17.4 %collective-permute-start.10 = (bf16[2,128,512]{2,1,0:T(8,128)(2,1)S(1)}, bf16[2,128,512]{2,1,0:T(8,128)(2,1)S(1)}, u32[]{:S(2)}, u32[]{:S(2)}) collective-permute-start(bf16[2,128,512]{2,1,0:T(8,128)(2,1)S(1)} %collective-permute-done.7.refs_5_), channel_id=1, source_target_pairs={{0,4},{4,0},{8,12},{12,8},{16,20},{20,16},{24,28},{28,24},{1,5},{5... | collective-permute-start | bytes 786440 | tf_op jit(solution)/shard_map/ppermute | solution.py:570
  55.9 0.7 collective-permute-start.9
  56.6 4.4 %collective-permute-start.19 = (bf16[256,256]{1,0:T(8,128)(2,1)S(1)}, bf16[256,256]{1,0:T(8,128)(2,1)S(1)}, u32[]{:S(2)}, u32[]{:S(2)}) collective-permute-start(bf16[256,256]{1,0:T(8,128)(2,1)S(1)} %get-tuple-element.75.refs_0_), channel_id=1, source_target_pairs={{0,1},{3,2},{4,5},{7,6},{8,9},{11,10},{12,13},{15,14},{16,17},{19,... | collective-permute-start | bytes 393224 | tf_op jit(solution)/shard_map/ppermute | solution.py:573
  61.0 0.7 collective-permute-start.6
  61.7 0.7 collective-permute-start.15
  62.4 0.7 collective-permute-start.16
  63.1 0.6 collective-permute-done.19.refs_1_
  63.7 0.7 collective-permute-start.20
  64.3 0.7 collective-permute-start.21
  65.0 0.7 prepare_requests.1
  65.7 17.8 %all_to_all.11 = s32[8,1,256]{2,1,0:T(1,128)S(1)} all-to-all(s32[8,1,256]{2,1,0:T(1,128)S(1)} %copy.9), channel_id=1, replica_groups=mesh['views'=8,'heads'=4] {'views'}, dimensions={0} | all-to-all | bytes 16384 | tf_op jit(solution)/shard_map/all_to_all | solution.py:630
  83.6 1.1 project_out.3
  84.7 1.3 %collective-permute-start.13 = (bf16[256,256]{1,0:T(8,128)(2,1)S(1)}, bf16[256,256]{1,0:T(8,128)(2,1)S(1)}, u32[]{:S(2)}, u32[]{:S(2)}) collective-permute-start(bf16[256,256]{1,0:T(8,128)(2,1)S(1)} %get-tuple-element.70), channel_id=1, source_target_pairs={{1,0},{2,3},{5,4},{6,7},{9,8},{10,11},{13,12},{14,15},{17,16},{18,... | collective-permute-start | bytes 393224 | tf_op jit(solution)/shard_map/ppermute | solution.py:573
  86.0 1.1 project_out.5
  87.1 1.3 %collective-permute-start.22 = (bf16[256,256]{1,0:T(8,128)(2,1)S(1)}, bf16[256,256]{1,0:T(8,128)(2,1)S(1)}, u32[]{:S(2)}, u32[]{:S(2)}) collective-permute-start(bf16[256,256]{1,0:T(8,128)(2,1)S(1)} %get-tuple-element.77), channel_id=1, source_target_pairs={{1,0},{2,3},{5,4},{6,7},{9,8},{10,11},{13,12},{14,15},{17,16},{18,... | collective-permute-start | bytes 393224 | tf_op jit(solution)/shard_map/ppermute | solution.py:573
  88.4 1.6 %project_out.4 = (bf16[256,256]{1,0:T(8,128)(2,1)S(1)}, bf16[256,256]{1,0:T(8,128)(2,1)S(1)}, bf16[256,256]{1,0:T(8,128)(2,1)S(1)}, bf16[256,256]{1,0:T(8,128)(2,1)S(1)}) custom-call(s32[4]{0:T(128)S(1)} %compare_select_fusion.1.meta_ref, bf16[2,256,256]{2,1,0:T(8,128)(2,1)S(1)} %attend.2.refs_0_, bf16[2,256,256]{2,1,0:T(8,128)(2,1)S(1)} %collective-permute-done.14.refs_1_, ...), custom_call_target="tpu_custom_call" | custom-call | flops 536870912 | bytes 3145728 | tf_op jit(solution)/shard_map/project_out/pallas_call | solution.py:385
  90.1 1.3 %collective-permute-start.17 = (bf16[256,256]{1,0:T(8,128)(2,1)S(1)}, bf16[256,256]{1,0:T(8,128)(2,1)S(1)}, u32[]{:S(2)}, u32[]{:S(2)}) collective-permute-start(bf16[256,256]{1,0:T(8,128)(2,1)S(1)} %get-tuple-element.72), channel_id=1, source_target_pairs={{1,0},{2,3},{5,4},{6,7},{9,8},{10,11},{13,12},{14,15},{17,16},{18,... | collective-permute-start | bytes 393224 | tf_op jit(solution)/shard_map/ppermute | solution.py:573
  91.4 1.3 %collective-permute-start.18 = (bf16[256,256]{1,0:T(8,128)(2,1)S(1)}, bf16[256,256]{1,0:T(8,128)(2,1)S(1)}, u32[]{:S(2)}, u32[]{:S(2)}) collective-permute-start(bf16[256,256]{1,0:T(8,128)(2,1)S(1)} %get-tuple-element.74), channel_id=1, source_target_pairs={{1,0},{2,3},{5,4},{6,7},{9,8},{10,11},{13,12},{14,15},{17,16},{18,... | collective-permute-start | bytes 393224 | tf_op jit(solution)/shard_map/ppermute | solution.py:573
  92.7 6.7 %collective-permute-done.13.refs_1_ = bf16[256,256]{1,0:T(8,128)(2,1)S(1)} collective-permute-done((bf16[256,256]{1,0:T(8,128)(2,1)S(1)}, bf16[256,256]{1,0:T(8,128)(2,1)S(1)}, u32[]{:S(2)}, u32[]{:S(2)}) %collective-permute-start.13) | collective-permute-done | bytes 131104 | tf_op jit(solution)/shard_map/ppermute | solution.py:573
  99.4 2.7 %collective-permute-done.22.refs_7_ = bf16[256,256]{1,0:T(8,128)(2,1)S(1)} collective-permute-done((bf16[256,256]{1,0:T(8,128)(2,1)S(1)}, bf16[256,256]{1,0:T(8,128)(2,1)S(1)}, u32[]{:S(2)}, u32[]{:S(2)}) %collective-permute-start.22) | collective-permute-done | bytes 131104 | tf_op jit(solution)/shard_map/ppermute | solution.py:573
  102.1 3.3 %collective-permute-done.17.refs_3_ = bf16[256,256]{1,0:T(8,128)(2,1)S(1)} collective-permute-done((bf16[256,256]{1,0:T(8,128)(2,1)S(1)}, bf16[256,256]{1,0:T(8,128)(2,1)S(1)}, u32[]{:S(2)}, u32[]{:S(2)}) %collective-permute-start.17) | collective-permute-done | bytes 131104 | tf_op jit(solution)/shard_map/ppermute | solution.py:573
  105.3 2.1 %collective-permute-done.18.refs_5_ = bf16[256,256]{1,0:T(8,128)(2,1)S(1)} collective-permute-done((bf16[256,256]{1,0:T(8,128)(2,1)S(1)}, bf16[256,256]{1,0:T(8,128)(2,1)S(1)}, u32[]{:S(2)}, u32[]{:S(2)}) %collective-permute-start.18) | collective-permute-done | bytes 131104 | tf_op jit(solution)/shard_map/ppermute | solution.py:573
  107.5 2.1 %gather_rows.1 = (bf16[1024,256]{1,0:T(8,128)(2,1)S(1)}, bf16[256,256]{1,0:T(8,128)(2,1)S(1)}, bf16[256,256]{1,0:T(8,128)(2,1)S(1)}, bf16[256,256]{1,0:T(8,128)(...) custom-call(s32[4]{0:T(128)S(1)} %compare_select_fusion.1.meta_ref, ...), custom_call_target="tpu_custom_call" | custom-call | flops 1073741824 | bytes 3145728 | tf_op jit(solution)/shard_map/gather_rows/pallas_call | solution.py:482
  109.5 0.1 collective-permute-start.23
  109.6 0.9 collective-permute-start.24
  110.5 0.9 collective-permute-start.25
  111.5 0.8 collective-permute-start.26
  112.3 0.9 collective-permute-start.27
  113.2 0.9 collective-permute-start.28
  114.0 2.0 %collective-permute-done.24.refs_2_ = bf16[256,256]{1,0:T(8,128)(2,1)S(1)} collective-permute-done((bf16[256,256]{1,0:T(8,128)(2,1)S(1)}, bf16[256,256]{1,0:T(8,128)(2,1)S(1)}, u32[]{:S(2)}, u32[]{:S(2)}) %collective-permute-start.24) | collective-permute-done | bytes 131104 | tf_op jit(solution)/shard_map/ppermute | solution.py:570
  116.0 1.7 %collective-permute-done.25.refs_3_ = bf16[256,256]{1,0:T(8,128)(2,1)S(1)} collective-permute-done((bf16[256,256]{1,0:T(8,128)(2,1)S(1)}, bf16[256,256]{1,0:T(8,128)(2,1)S(1)}, u32[]{:S(2)}, u32[]{:S(2)}) %collective-permute-start.25) | collective-permute-done | bytes 131104 | tf_op jit(solution)/shard_map/ppermute | solution.py:570
  117.8 0.1 collective-permute-done.26.refs_4_
  117.8 7.2 %collective-permute-done.27.refs_5_ = bf16[256,256]{1,0:T(8,128)(2,1)S(1)} collective-permute-done((bf16[256,256]{1,0:T(8,128)(2,1)S(1)}, bf16[256,256]{1,0:T(8,128)(2,1)S(1)}, u32[]{:S(2)}, u32[]{:S(2)}) %collective-permute-start.27) | collective-permute-done | bytes 131104 | tf_op jit(solution)/shard_map/ppermute | solution.py:570
  125.0 2.9 %finish_rows.1 = f32[1024,256]{1,0:T(8,128)} custom-call(s32[4]{0:T(128)S(1)} %compare_select_fusion.1.meta_ref, s32[8,128]{1,0:T(8,128)S(1)} %get-tuple-element.62.code_ref, f32[8,128]{1,0:T(8,128)S(1)} %bitcast.21, bf16[1024,256]{1,0:T(8,128)(2,1)S(1)} %get-tuple-element.78.layer_ref, bf16[256,256]{1,0:T(8,128)(2,1)S(1)} %get-tuple-element.79.refs_0_, ...), custom_call_target="tpu_custom_call" | custom-call | flops 1073741824 | bytes 2621440 | tf_op jit(solution)/shard_map/finish_rows/pallas_call | solution.py:538
  (42 shorter events, 0.1 us)
Async XLA Ops:
  0.0 8.1 %copy-start.1 = (bf16[256,1024]{1,0:T(8,128)(2,1)S(1)}, bf16[256,1024]{1,0:T(8,128)(2,1)}, u32[]{:S(2)}) copy-start(bf16[256,1024]{1,0:T(8,128)(2,1)} %refs_0_) | copy-start | bytes 1572868
  0.0 0.7 copy-start.2
  4.7 19.8 %collective-permute-start = (bf16[2,256,256]{2,1,0:T(8,128)(2,1)S(1)}, bf16[2,256,256]{2,1,0:T(8,128)(2,1)S(1)}, u32[]{:S(2)}, u32[]{:S(2)}) collective-permute-start(bf16[2,256,256]{2,1,0:T(8,128)(2,1)S(1)} %get-tuple-element.50.refs_2_.refs_4_), channel_id=1, source_target_pairs={{0,28},{4,0},{8,4},{12,8},{16,12},{20,16},{24,20},{28,24},{1,29},{... | collective-permute-start | bytes 786440 | tf_op jit(solution)/shard_map/ppermute | solution.py:567
  8.1 16.4 %collective-permute-start.1 = (bf16[2,256,256]{2,1,0:T(8,128)(2,1)S(1)}, bf16[2,256,256]{2,1,0:T(8,128)(2,1)S(1)}, u32[]{:S(2)}, u32[]{:S(2)}) collective-permute-start(bf16[2,256,256]{2,1,0:T(8,128)(2,1)S(1)} %get-tuple-element.53.refs_5_.refs_7_), channel_id=1, source_target_pairs={{0,4},{4,8},{8,12},{12,16},{16,20},{20,24},{24,28},{28,0},{1,5},{5... | collective-permute-start | bytes 786440 | tf_op jit(solution)/shard_map/ppermute | solution.py:567
  8.1 4.7 %copy-start.3 = (s32[32,2]{0,1:T(2,128)S(1)}, s32[32,2]{0,1:T(2,128)}, u32[]{:S(2)}) copy-start(s32[32,2]{0,1:T(2,128)} %param.12) | copy-start | bytes 772
  12.1 6.4 %collective-permute-start.8 = (bf16[128,512]{1,0:T(8,128)(2,1)S(1)}, bf16[128,512]{1,0:T(8,128)(2,1)S(1)}, u32[]{:S(2)}, u32[]{:S(2)}) collective-permute-start(bf16[128,512]{1,0:T(8,128)(2,1)S(1)} %get-tuple-element.67), channel_id=1, source_target_pairs={{1,2},{2,1},{5,6},{6,5},{9,10},{10,9},{13,14},{14,13},{17,18},{18,... | collective-permute-start | bytes 393224 | tf_op jit(solution)/shard_map/ppermute | solution.py:573
  15.8 10.5 %collective-permute-start.2 = (bf16[2,256,256]{2,1,0:T(8,128)(2,1)S(1)}, bf16[2,256,256]{2,1,0:T(8,128)(2,1)S(1)}, u32[]{:S(2)}, u32[]{:S(2)}) collective-permute-start(bf16[2,256,256]{2,1,0:T(8,128)(2,1)S(1)} %get-tuple-element.58.refs_3_.refs_5_), channel_id=1, source_target_pairs={{0,28},{4,0},{8,4},{12,8},{16,12},{20,16},{24,20},{28,24},{1,29},{... | collective-permute-start | bytes 786440 | tf_op jit(solution)/shard_map/ppermute | solution.py:567
  18.5 7.9 %collective-permute-start.3 = (bf16[2,256,256]{2,1,0:T(8,128)(2,1)S(1)}, bf16[2,256,256]{2,1,0:T(8,128)(2,1)S(1)}, u32[]{:S(2)}, u32[]{:S(2)}) collective-permute-start(bf16[2,256,256]{2,1,0:T(8,128)(2,1)S(1)} %get-tuple-element.59.refs_4_.refs_6_), channel_id=1, source_target_pairs={{0,4},{4,8},{8,12},{12,16},{16,20},{20,24},{24,28},{28,0},{1,5},{5... | collective-permute-start | bytes 786440 | tf_op jit(solution)/shard_map/ppermute | solution.py:567
  18.5 20.1 %collective-permute-start.7 = (bf16[2,128,512]{2,1,0:T(8,128)(2,1)S(1)}, bf16[2,128,512]{2,1,0:T(8,128)(2,1)S(1)}, u32[]{:S(2)}, u32[]{:S(2)}) collective-permute-start(bf16[2,128,512]{2,1,0:T(8,128)(2,1)S(1)} %get-tuple-element.66), channel_id=1, source_target_pairs={{0,1},{3,2},{4,5},{7,6},{8,9},{11,10},{12,13},{15,14},{16,17},{19,... | collective-permute-start | bytes 786440 | tf_op jit(solution)/shard_map/ppermute | solution.py:573
  24.5 31.4 %collective-permute-start.11 = (bf16[128,512]{1,0:T(8,128)(2,1)S(1)}, bf16[128,512]{1,0:T(8,128)(2,1)S(1)}, u32[]{:S(2)}, u32[]{:S(2)}) collective-permute-start(bf16[128,512]{1,0:T(8,128)(2,1)S(1)} %collective-permute-done.8.refs_6_), channel_id=1, source_target_pairs={{0,4},{4,0},{8,12},{12,8},{16,20},{20,16},{24,28},{28,24},{1,5},{5... | collective-permute-start | bytes 393224 | tf_op jit(solution)/shard_map/ppermute | solution.py:570
  26.3 38.7 %copy-start.4 = (s32[1024,1]{0,1:T(1,128)S(1)}, s32[1024,1]{0,1:T(1,128)}, u32[]{:S(2)}) copy-start(s32[1024,1]{0,1:T(1,128)} %param.13) | copy-start | bytes 12292
  26.3 38.7 %copy-start.5 = (s32[1024]{0:T(1024)S(1)}, s32[1024]{0:T(1024)}, u32[]{:S(2)}) copy-start(s32[1024]{0:T(1024)} %param.14) | copy-start | bytes 12292
  26.3 57.2 %copy-start = (bf16[4,256,1024]{2,1,0:T(8,128)(2,1)S(1)}, bf16[4,256,1024]{2,1,0:T(8,128)(2,1)}, u32[]{:S(2)}) copy-start(bf16[4,256,1024]{2,1,0:T(8,128)(2,1)} %refs_11_.5) | copy-start | bytes 6291460
  29.9 26.8 %collective-permute-start.4 = (bf16[256,256]{1,0:T(8,128)(2,1)S(1)}, bf16[256,256]{1,0:T(8,128)(2,1)S(1)}, u32[]{:S(2)}, u32[]{:S(2)}) collective-permute-start(bf16[256,256]{1,0:T(8,128)(2,1)S(1)} %get-tuple-element.60.refs_0_), channel_id=1, source_target_pairs={{0,1},{3,2},{4,5},{7,6},{8,9},{11,10},{12,13},{15,14},{16,17},{19,... | collective-permute-start | bytes 393224 | tf_op jit(solution)/shard_map/ppermute | solution.py:573
  34.9 26.1 %collective-permute-start.5 = (bf16[256,256]{1,0:T(8,128)(2,1)S(1)}, bf16[256,256]{1,0:T(8,128)(2,1)S(1)}, u32[]{:S(2)}, u32[]{:S(2)}) collective-permute-start(bf16[256,256]{1,0:T(8,128)(2,1)S(1)} %get-tuple-element.60.refs_0_), channel_id=1, source_target_pairs={{1,2},{2,1},{5,6},{6,5},{9,10},{10,9},{13,14},{14,13},{17,18},{18,... | collective-permute-start | bytes 393224 | tf_op jit(solution)/shard_map/ppermute | solution.py:573
  35.5 26.9 %collective-permute-start.14 = (bf16[2,256,256]{2,1,0:T(8,128)(2,1)S(1)}, bf16[2,256,256]{2,1,0:T(8,128)(2,1)S(1)}, u32[]{:S(2)}, u32[]{:S(2)}) collective-permute-start(bf16[2,256,256]{2,1,0:T(8,128)(2,1)S(1)} %attend.2.refs_0_), channel_id=1, source_target_pairs={{0,1},{3,2},{4,5},{7,6},{8,9},{11,10},{12,13},{15,14},{16,17},{19,... | collective-permute-start | bytes 786440 | tf_op jit(solution)/shard_map/ppermute | solution.py:573
  38.6 25.8 %collective-permute-start.10 = (bf16[2,128,512]{2,1,0:T(8,128)(2,1)S(1)}, bf16[2,128,512]{2,1,0:T(8,128)(2,1)S(1)}, u32[]{:S(2)}, u32[]{:S(2)}) collective-permute-start(bf16[2,128,512]{2,1,0:T(8,128)(2,1)S(1)} %collective-permute-done.7.refs_5_), channel_id=1, source_target_pairs={{0,4},{4,0},{8,12},{12,8},{16,20},{20,16},{24,28},{28,24},{1,5},{5... | collective-permute-start | bytes 786440 | tf_op jit(solution)/shard_map/ppermute | solution.py:570
  55.9 5.8 %collective-permute-start.9 = (bf16[128,512]{1,0:T(8,128)(2,1)S(1)}, bf16[128,512]{1,0:T(8,128)(2,1)S(1)}, u32[]{:S(2)}, u32[]{:S(2)}) collective-permute-start(bf16[128,512]{1,0:T(8,128)(2,1)S(1)} %slice_bitcast_fusion), channel_id=1, source_target_pairs={{1,2},{2,1},{5,6},{6,5},{9,10},{10,9},{13,14},{14,13},{17,18},{18,... | collective-permute-start | bytes 393224 | tf_op jit(solution)/shard_map/ppermute | solution.py:573
  56.6 7.0 %collective-permute-start.19 = (bf16[256,256]{1,0:T(8,128)(2,1)S(1)}, bf16[256,256]{1,0:T(8,128)(2,1)S(1)}, u32[]{:S(2)}, u32[]{:S(2)}) collective-permute-start(bf16[256,256]{1,0:T(8,128)(2,1)S(1)} %get-tuple-element.75.refs_0_), channel_id=1, source_target_pairs={{0,1},{3,2},{4,5},{7,6},{8,9},{11,10},{12,13},{15,14},{16,17},{19,... | collective-permute-start | bytes 393224 | tf_op jit(solution)/shard_map/ppermute | solution.py:573
  61.0 2.6 %collective-permute-start.6 = (bf16[256,256]{1,0:T(8,128)(2,1)S(1)}, bf16[256,256]{1,0:T(8,128)(2,1)S(1)}, u32[]{:S(2)}, u32[]{:S(2)}) collective-permute-start(bf16[256,256]{1,0:T(8,128)(2,1)S(1)} %collective-permute-done.4.refs_1_), channel_id=1, source_target_pairs={{1,2},{2,1},{5,6},{6,5},{9,10},{10,9},{13,14},{14,13},{17,18},{18,... | collective-permute-start | bytes 393224 | tf_op jit(solution)/shard_map/ppermute | solution.py:573
  61.7 26.7 %collective-permute-start.15 = (bf16[2,256,256]{2,1,0:T(8,128)(2,1)S(1)}, bf16[2,256,256]{2,1,0:T(8,128)(2,1)S(1)}, u32[]{:S(2)}, u32[]{:S(2)}) collective-permute-start(bf16[2,256,256]{2,1,0:T(8,128)(2,1)S(1)} %attend.2.refs_0_), channel_id=1, source_target_pairs={{1,2},{2,1},{5,6},{6,5},{9,10},{10,9},{13,14},{14,13},{17,18},{18,... | collective-permute-start | bytes 786440 | tf_op jit(solution)/shard_map/ppermute | solution.py:573
  62.4 26.0 %collective-permute-start.16 = (bf16[2,256,256]{2,1,0:T(8,128)(2,1)S(1)}, bf16[2,256,256]{2,1,0:T(8,128)(2,1)S(1)}, u32[]{:S(2)}, u32[]{:S(2)}) collective-permute-start(bf16[2,256,256]{2,1,0:T(8,128)(2,1)S(1)} %collective-permute-done.14.refs_1_), channel_id=1, source_target_pairs={{1,2},{2,1},{5,6},{6,5},{9,10},{10,9},{13,14},{14,13},{17,18},{18,... | collective-permute-start | bytes 786440 | tf_op jit(solution)/shard_map/ppermute | solution.py:573
  63.6 19.9 %collective-permute-start.12 = (bf16[128,512]{1,0:T(8,128)(2,1)S(1)}, bf16[128,512]{1,0:T(8,128)(2,1)S(1)}, u32[]{:S(2)}, u32[]{:S(2)}) collective-permute-start(bf16[128,512]{1,0:T(8,128)(2,1)S(1)} %collective-permute-done.9.refs_7_), channel_id=1, source_target_pairs={{0,4},{4,0},{8,12},{12,8},{16,20},{20,16},{24,28},{28,24},{1,5},{5... | collective-permute-start | bytes 393224 | tf_op jit(solution)/shard_map/ppermute | solution.py:570
  63.7 22.3 %collective-permute-start.20 = (bf16[256,256]{1,0:T(8,128)(2,1)S(1)}, bf16[256,256]{1,0:T(8,128)(2,1)S(1)}, u32[]{:S(2)}, u32[]{:S(2)}) collective-permute-start(bf16[256,256]{1,0:T(8,128)(2,1)S(1)} %get-tuple-element.75.refs_0_), channel_id=1, source_target_pairs={{1,2},{2,1},{5,6},{6,5},{9,10},{10,9},{13,14},{14,13},{17,18},{18,... | collective-permute-start | bytes 393224 | tf_op jit(solution)/shard_map/ppermute | solution.py:573
  64.3 21.7 %collective-permute-start.21 = (bf16[256,256]{1,0:T(8,128)(2,1)S(1)}, bf16[256,256]{1,0:T(8,128)(2,1)S(1)}, u32[]{:S(2)}, u32[]{:S(2)}) collective-permute-start(bf16[256,256]{1,0:T(8,128)(2,1)S(1)} %collective-permute-done.19.refs_1_), channel_id=1, source_target_pairs={{1,2},{2,1},{5,6},{6,5},{9,10},{10,9},{13,14},{14,13},{17,18},{18,... | collective-permute-start | bytes 393224 | tf_op jit(solution)/shard_map/ppermute | solution.py:573
  84.7 14.7 %collective-permute-start.13 = (bf16[256,256]{1,0:T(8,128)(2,1)S(1)}, bf16[256,256]{1,0:T(8,128)(2,1)S(1)}, u32[]{:S(2)}, u32[]{:S(2)}) collective-permute-start(bf16[256,256]{1,0:T(8,128)(2,1)S(1)} %get-tuple-element.70), channel_id=1, source_target_pairs={{1,0},{2,3},{5,4},{6,7},{9,8},{10,11},{13,12},{14,15},{17,16},{18,... | collective-permute-start | bytes 393224 | tf_op jit(solution)/shard_map/ppermute | solution.py:573
  87.1 15.0 %collective-permute-start.22 = (bf16[256,256]{1,0:T(8,128)(2,1)S(1)}, bf16[256,256]{1,0:T(8,128)(2,1)S(1)}, u32[]{:S(2)}, u32[]{:S(2)}) collective-permute-start(bf16[256,256]{1,0:T(8,128)(2,1)S(1)} %get-tuple-element.77), channel_id=1, source_target_pairs={{1,0},{2,3},{5,4},{6,7},{9,8},{10,11},{13,12},{14,15},{17,16},{18,... | collective-permute-start | bytes 393224 | tf_op jit(solution)/shard_map/ppermute | solution.py:573
  90.1 35.0 %copy-start.6 = (f32[1024]{0:T(1024)S(1)}, f32[1024]{0:T(1024)}, u32[]{:S(2)}) copy-start(f32[1024]{0:T(1024)} %param.15) | copy-start | bytes 12292
  90.1 15.2 %collective-permute-start.17 = (bf16[256,256]{1,0:T(8,128)(2,1)S(1)}, bf16[256,256]{1,0:T(8,128)(2,1)S(1)}, u32[]{:S(2)}, u32[]{:S(2)}) collective-permute-start(bf16[256,256]{1,0:T(8,128)(2,1)S(1)} %get-tuple-element.72), channel_id=1, source_target_pairs={{1,0},{2,3},{5,4},{6,7},{9,8},{10,11},{13,12},{14,15},{17,16},{18,... | collective-permute-start | bytes 393224 | tf_op jit(solution)/shard_map/ppermute | solution.py:573
  91.4 16.1 %collective-permute-start.18 = (bf16[256,256]{1,0:T(8,128)(2,1)S(1)}, bf16[256,256]{1,0:T(8,128)(2,1)S(1)}, u32[]{:S(2)}, u32[]{:S(2)}) collective-permute-start(bf16[256,256]{1,0:T(8,128)(2,1)S(1)} %get-tuple-element.74), channel_id=1, source_target_pairs={{1,0},{2,3},{5,4},{6,7},{9,8},{10,11},{13,12},{14,15},{17,16},{18,... | collective-permute-start | bytes 393224 | tf_op jit(solution)/shard_map/ppermute | solution.py:573
  109.5 3.6 %collective-permute-start.23 = (bf16[256,256]{1,0:T(8,128)(2,1)S(1)}, bf16[256,256]{1,0:T(8,128)(2,1)S(1)}, u32[]{:S(2)}, u32[]{:S(2)}) collective-permute-start(bf16[256,256]{1,0:T(8,128)(2,1)S(1)} %get-tuple-element.80), channel_id=1, source_target_pairs={{0,4},{4,0},{8,12},{12,8},{16,20},{20,16},{24,28},{28,24},{1,5},{5... | collective-permute-start | bytes 393224 | tf_op jit(solution)/shard_map/ppermute | solution.py:570
  109.6 6.4 %collective-permute-start.24 = (bf16[256,256]{1,0:T(8,128)(2,1)S(1)}, bf16[256,256]{1,0:T(8,128)(2,1)S(1)}, u32[]{:S(2)}, u32[]{:S(2)}) collective-permute-start(bf16[256,256]{1,0:T(8,128)(2,1)S(1)} %get-tuple-element.81), channel_id=1, source_target_pairs={{0,8},{4,12},{8,0},{12,4},{16,24},{20,28},{24,16},{28,20},{1,9},{5... | collective-permute-start | bytes 393224 | tf_op jit(solution)/shard_map/ppermute | solution.py:570
  110.5 7.2 %collective-permute-start.25 = (bf16[256,256]{1,0:T(8,128)(2,1)S(1)}, bf16[256,256]{1,0:T(8,128)(2,1)S(1)}, u32[]{:S(2)}, u32[]{:S(2)}) collective-permute-start(bf16[256,256]{1,0:T(8,128)(2,1)S(1)} %get-tuple-element.82), channel_id=1, source_target_pairs={{0,12},{4,8},{8,4},{12,0},{16,28},{20,24},{24,20},{28,16},{1,13},{... | collective-permute-start | bytes 393224 | tf_op jit(solution)/shard_map/ppermute | solution.py:570
  111.5 6.4 %collective-permute-start.26 = (bf16[256,256]{1,0:T(8,128)(2,1)S(1)}, bf16[256,256]{1,0:T(8,128)(2,1)S(1)}, u32[]{:S(2)}, u32[]{:S(2)}) collective-permute-start(bf16[256,256]{1,0:T(8,128)(2,1)S(1)} %get-tuple-element.83), channel_id=1, source_target_pairs={{0,16},{4,20},{8,24},{12,28},{16,0},{20,4},{24,8},{28,12},{1,17},{... | collective-permute-start | bytes 393224 | tf_op jit(solution)/shard_map/ppermute | solution.py:570
  112.3 12.7 %collective-permute-start.27 = (bf16[256,256]{1,0:T(8,128)(2,1)S(1)}, bf16[256,256]{1,0:T(8,128)(2,1)S(1)}, u32[]{:S(2)}, u32[]{:S(2)}) collective-permute-start(bf16[256,256]{1,0:T(8,128)(2,1)S(1)} %get-tuple-element.84), channel_id=1, source_target_pairs={{0,20},{4,16},{8,28},{12,24},{16,4},{20,0},{24,12},{28,8},{1,21},{... | collective-permute-start | bytes 393224 | tf_op jit(solution)/shard_map/ppermute | solution.py:570
  113.2 11.9 %collective-permute-start.28 = (bf16[256,256]{1,0:T(8,128)(2,1)S(1)}, bf16[256,256]{1,0:T(8,128)(2,1)S(1)}, u32[]{:S(2)}, u32[]{:S(2)}) collective-permute-start(bf16[256,256]{1,0:T(8,128)(2,1)S(1)} %get-tuple-element.85), channel_id=1, source_target_pairs={{0,24},{4,28},{8,16},{12,20},{16,8},{20,12},{24,0},{28,4},{1,25},{... | collective-permute-start | bytes 393224 | tf_op jit(solution)/shard_map/ppermute | solution.py:570
  116.0 9.0 %collective-permute-start.29 = (bf16[256,256]{1,0:T(8,128)(2,1)S(1)}, bf16[256,256]{1,0:T(8,128)(2,1)S(1)}, u32[]{:S(2)}, u32[]{:S(2)}) collective-permute-start(bf16[256,256]{1,0:T(8,128)(2,1)S(1)} %get-tuple-element.86), channel_id=1, source_target_pairs={{0,28},{4,24},{8,20},{12,16},{16,12},{20,8},{24,4},{28,0},{1,29},{... | collective-permute-start | bytes 393224 | tf_op jit(solution)/shard_map/ppermute | solution.py:570
where the time goes:
time: 129 us; the launch traced here: 128 us
  starting transfers between devices  56.9 us (44%)
  waiting for transfers between devices  26.4 us (20%)
  Pallas kernels  25.5 us (20%)
  blocking collectives  17.8 us (14%)
    ppermute x16, starting transfers between devices, across(): return lax.ppermute(x, 'heads', pairs)  28.9 us
    ppermute x10, starting transfers between devices, partner(): return lax.ppermute(x, 'views', [(i, i ^ mask) for i in range(peers)])  21.9 us
    all_to_all x1, blocking collectives, per_device(): lax.all_to_all(wanted, 'views', split_axis=0, concat_axis=0, tiled=True)  17.8 us
    ppermute x16, waiting for transfers between devices, across(): return lax.ppermute(x, 'heads', pairs)  15.4 us
    ppermute x10, waiting for transfers between devices, partner(): return lax.ppermute(x, 'views', [(i, i ^ mask) for i in range(peers)])  11 us
    pallas_call x3, Pallas kernels, attend(): pl.pallas_call(body, in_specs=[SMEM_SPEC, SMEM_SPEC] + many(VMEM_SPEC, he...  8.16 us
    pallas_call x2, Pallas kernels, project_views(): pl.pallas_call(body, in_specs=[SMEM_SPEC] + many(ANY_SPEC, 3 + extra), ou...  7.92 us
    ppermute x4, starting transfers between devices, along(): lax.ppermute(x, 'views', [(i, (i + by) % peers) for i in range(peers)])  6.13 us
  transfers between devices with their start and end apart: 30, of which 9 were waited for; matrix products, arithmetic and copies ran while one was open for 0% of the time, Pallas kernels for 13%

commit v1 on v0

--- a/solution.py
+++ b/solution.py
@@ -8,6 +8,7 @@
 
 HEAD_DIM = 64
 LANES = 128
+VIEW_ORDER = (1, 2, 0, 3)
 
 coupling = 0.5
 epsilon = 1e-06
@@ -39,53 +40,36 @@
     return [spec] * count
 
 
-def project_views(meta, latents, gain, w_qkv, which, w_out=None):
+def project_views(meta, latents, gain, w_qkv, which):
     _, tokens, width = latents.shape
     sub = w_qkv.shape[2]
     count = len(which)
     scale = HEAD_DIM ** (-0.5)
     order = (2, 0, 1)
 
-    extra = 0 if w_out is None else 1
-    strip = sub // 2
-
     def body(meta_ref, lat_hbm, gain_hbm, w_hbm, *refs):
-        outs, (buffer, gains, ws, sems) = refs[extra : 2 * count + extra], refs[-4:]
-        splits = []
-        if extra:
-            own, pair, other = refs[2 * count + 1 : 2 * count + 4]
-            side = meta_ref[1] // 2
-            near = pl.ds(pl.multiple_of(side * 2 * sub, 2 * sub), 2 * sub)
-            away = pl.ds(pl.multiple_of((1 - side) * 2 * sub, 2 * sub), 2 * sub)
-            mine = pl.ds(pl.multiple_of((meta_ref[0] % 2) * strip, strip), strip)
-            for i, (source, target) in enumerate(
-                (
-                    (refs[0].at[:, near], own),
-                    (refs[0].at[mine, near], pair.at[0]),
-                    (refs[0].at[mine, away], pair.at[1]),
-                    (refs[0].at[mine, away], other),
-                )
-            ):
-                splits.append(pltpu.make_async_copy(source, target, sems.at[count + 4 + i]))
+        outs, (halves, buffer, gains, ws, sems) = refs[: 2 * count], refs[2 * count :]
+        here = pl.ds(pl.multiple_of((meta_ref[1] // 2) * (width // 2), width // 2), width // 2)
+        kept = [
+            pltpu.make_async_copy(buffer.at[i, :, here], halves.at[i], sems.at[count + 4 + i])
+            for i in range(count)
+        ]
         copies = [
             pltpu.make_async_copy(lat_hbm.at[v], buffer.at[i], sems.at[i])
             for i, v in enumerate(which)
         ]
-        copies.insert(1, pltpu.make_async_copy(gain_hbm, gains, sems.at[count]))
+        gain_copy = pltpu.make_async_copy(gain_hbm, gains, sems.at[count])
         w_copies = {
             part: pltpu.make_async_copy(w_hbm.at[part], ws.at[part], sems.at[count + 1 + part])
             for part in order
         }
-        copies[0].start()
-        copies[1].start()
-        for part in order:
-            w_copies[part].start()
-        for copy in copies[2:] + splits:
+        for copy in [copies[0], gain_copy] + [w_copies[p] for p in order] + copies[1:]:
             copy.start()
         for i in range(count):
-            copies[i if i == 0 else i + 1].wait()
+            copies[i].wait()
+            kept[i].start()
             if i == 0:
-                copies[1].wait()
+                gain_copy.wait()
             wide = buffer[i].astype(f32)
             mean_square = jnp.mean(wide * wide, axis=-1, keepdims=True)
             normed = (wide * lax.rsqrt(mean_square + epsilon) * gains[...]).astype(bf16)
@@ -100,7 +84,7 @@
             outs[2 * i + 1][0] = dot(normed, ws[1]).astype(bf16)
             outs[2 * i + 1][1] = jnp.transpose(values).astype(bf16)
             outs[2 * i][...] = jnp.transpose(queries).astype(bf16) * jnp.asarray(scale, bf16)
-        for copy in splits:
+        for copy in kept:
             copy.wait()
 
     out_shape = []
@@ -109,30 +93,25 @@
             jax.ShapeDtypeStruct((sub, tokens), bf16),
             jax.ShapeDtypeStruct((2, tokens, sub), bf16),
         ]
-    if extra:
-        out_shape += [
-            jax.ShapeDtypeStruct((sub, 2 * sub), bf16),
-            jax.ShapeDtypeStruct((2, strip, 2 * sub), bf16),
-            jax.ShapeDtypeStruct((strip, 2 * sub), bf16),
-        ]
+    out_shape.append(jax.ShapeDtypeStruct((count, tokens, width // 2), bf16))
     outs = pl.pallas_call(
         body,
-        in_specs=[SMEM_SPEC] + many(ANY_SPEC, 3 + extra),
+        in_specs=[SMEM_SPEC] + many(ANY_SPEC, 3),
         out_specs=many(VMEM_SPEC, len(out_shape)),
         out_shape=out_shape,
         scratch_shapes=[
             pltpu.VMEM((count, tokens, width), bf16),
             pltpu.VMEM((1, width), f32),
             pltpu.VMEM((3, width, sub), bf16),
-            pltpu.SemaphoreType.DMA((count + 8,)),
+            pltpu.SemaphoreType.DMA((2 * count + 4,)),
         ],
         name="project_views",
-        compiler_params=grant(52),
+        compiler_params=grant(50),
         cost_estimate=cost(
             count * 6 * tokens * width * sub, count * tokens * (width + 3 * sub) * 2 + 6 * width * sub
         ),
-    )(meta, latents, gain, w_qkv, *([w_out] if extra else []))
-    return {v: (outs[2 * i], outs[2 * i + 1]) for i, v in enumerate(which)}, outs[2 * count :]
+    )(meta, latents, gain, w_qkv)
+    return {v: (outs[2 * i], outs[2 * i + 1]) for i, v in enumerate(which)}, outs[-1]
 
 
 ONES = 16
@@ -334,73 +313,56 @@
     lax.fori_loop(0, heads, one_head, 0)
 
 
-def project_out(meta, attended, weights, latents, views):
-    count = len(attended)
-    groups = len(attended[0])
-    arrays = []
-    for row in attended:
-        for array, _ in row:
-            if not any(array is a for a in arrays):
-                arrays.append(array)
-    spots = [
-        [([a is array for a in arrays].index(True), index) for array, index in row] for row in attended
-    ]
-    tokens, sub = arrays[0].shape[-2:]
-
-    def pick(refs, spot):
-        ref, index = refs[spot[0]], spot[1]
-        return ref[...] if index is None else ref[index]
-
-    def body(meta_ref, *refs):
-        att, refs = refs[: len(arrays)], refs[len(arrays) :]
-        ws, refs = refs[: len(weights)], refs[len(weights) :]
-        lat_hbm, refs = refs[0], refs[1:]
-        owns, others = refs[:count], refs[count : 2 * count]
-        buffer, sems = refs[2 * count :]
-        columns = pl.ds(pl.multiple_of((meta_ref[1] // 2) * 2 * sub, 2 * sub), 2 * sub)
-        copies = [
-            pltpu.make_async_copy(lat_hbm.at[v, :, columns], buffer.at[i], sems.at[i])
-            for i, v in enumerate(views)
-        ]
-        for copy in copies:
-            copy.start()
+def partial_out(meta, attended, near, w_own, w_near, halves, place):
+    tokens, sub = attended.shape
+    width = w_own.shape[1]
+    half = width // 2
+
+    def body(meta_ref, att, near_ref, own_ref, near_w_ref, halves_ref, keep, send):
+        side = meta_ref[1] // 2
+        here = pl.ds(pl.multiple_of(side * half, half), half)
+        away = pl.ds(pl.multiple_of((1 - side) * half, half), half)
+        rows = jnp.concatenate([att[...], near_ref[...]], axis=1)
+        send[...] = dot(
+            rows, jnp.concatenate([own_ref[:, away], near_w_ref[:, away]], axis=0)
+        ).astype(bf16)
+        total = dot(rows, jnp.concatenate([own_ref[:, here], near_w_ref[:, here]], axis=0))
+        keep[...] = halves_ref[place].astype(f32) + total
+
+    return pl.pallas_call(
+        body,
+        in_specs=[SMEM_SPEC] + many(VMEM_SPEC, 5),
+        out_specs=many(VMEM_SPEC, 2),
+        out_shape=[
+            jax.ShapeDtypeStruct((tokens, half), f32),
+            jax.ShapeDtypeStruct((tokens, half), bf16),
+        ],
+        name="partial_out",
+        compiler_params=grant(12),
+        cost_estimate=cost(4 * tokens * sub * width, 4 * sub * width + tokens * width * 6),
+    )(meta, attended, near, w_own, w_near, halves)
+
+
+def merge_out(meta, keep, got):
+    tokens, half = keep.shape
+    sub = half // 2
+
+    def body(meta_ref, keep_ref, got_ref, own, other):
+        layer = (keep_ref[...] + got_ref[...].astype(f32)).astype(bf16)
+        low, high = layer[:, :sub], layer[:, sub:]
         odd = meta_ref[1] % 2 == 1
-        second = meta_ref[0] % 2 == 1
-        rows = [ws[0][...]]
-        for mine, theirs in zip(ws[1 : 1 + groups - 1], ws[groups:]):
-            mine, theirs = mine[...], theirs[...]
-            if len(mine.shape) == 3:
-                mine, theirs = mine[0], theirs[0]
-            rows.append(jnp.where(second, theirs, mine))
-            rows.append(jnp.where(second, mine, theirs))
-        matrix = jnp.concatenate(rows, axis=0)
-        for i in range(count):
-            total = dot(jnp.concatenate([pick(att, spot) for spot in spots[i]], axis=1), matrix)
-            copies[i].wait()
-            layer = (buffer[i].astype(f32) + total).astype(bf16)
-            low, high = layer[:, :sub], layer[:, sub:]
-            owns[i][...] = jnp.where(odd, high, low)
-            others[i][...] = jnp.where(odd, low, high)
-
-    outs = pl.pallas_call(
+        own[...] = jnp.where(odd, high, low)
+        other[...] = jnp.where(odd, low, high)
+
+    return pl.pallas_call(
         body,
-        in_specs=[SMEM_SPEC]
-        + many(VMEM_SPEC, len(arrays) + len(weights))
-        + [ANY_SPEC],
-        out_specs=many(VMEM_SPEC, 2 * count),
-        out_shape=[jax.ShapeDtypeStruct((tokens, sub), bf16)] * (2 * count),
-        scratch_shapes=[
-            pltpu.VMEM((count, tokens, 2 * sub), bf16),
-            pltpu.SemaphoreType.DMA((count,)),
-        ],
-        name="project_out",
-        compiler_params=grant(12),
-        cost_estimate=cost(
-            groups * count * tokens * sub * 4 * sub,
-            groups * (count * tokens * sub + 2 * sub * sub) * 2 + count * tokens * sub * 8,
-        ),
-    )(meta, *arrays, *weights, latents)
-    return outs[:count], outs[count:]
+        in_specs=[SMEM_SPEC] + many(VMEM_SPEC, 2),
+        out_specs=many(VMEM_SPEC, 2),
+        out_shape=[jax.ShapeDtypeStruct((tokens, sub), bf16)] * 2,
+        name="merge_out",
+        compiler_params=grant(8),
+        cost_estimate=cost(tokens * half * 2, tokens * half * 8),
+    )(meta, keep, got)
 
 
 def prepare_requests(block_rows, token_rows, peers, capacity):
@@ -578,17 +540,13 @@
     beside, middle, back = [(0, 1), (3, 2)], [(1, 2), (2, 1)], [(1, 0), (2, 3)]
     gain = norm_gain.reshape(1, width)
     inter = intersection.T
-    projected, _ = project_views(meta, latents, gain, w_qkv, (0, local_views - 1))
-    next_first = along(projected[0][1], -1)
-    prev_last = along(projected[3][1], 1)
-    more, (own_half, w_pair, w_other) = project_views(
-        meta, latents, gain, w_qkv, (1, 2), after(w_out, projected[0][0])
-    )
-    projected.update(more)
+    loaded = (0, local_views - 1, 1, 2)
+    projected, halves = project_views(meta, latents, gain, w_qkv, loaded)
     queries = {v: projected[v][0] for v in range(local_views)}
     blocks = {v: projected[v][1] for v in range(local_views)}
-    w_beside = across(w_pair, beside)
-    w_middle = across(w_other, middle)
+    next_first = along(blocks[0], -1)
+    prev_last = along(blocks[3], 1)
+    w_near = across(after(w_out, queries[1]), beside)
 
     inner_plan = [(1, [("prev_last", -1, 1)]), (2, [("next_first", 2, 1)])]
     inner_queries = [queries[1], queries[2]]
@@ -598,28 +556,17 @@
     next_second = along(after(blocks[1], local[0]), -1)
     prev_second = along(after(blocks[2], local[0]), 1)
     remote = dict(prev_last=prev_last, next_first=next_first)
-    (inner,) = attend(
-        meta,
-        inter,
-        inner_queries,
-        blocks,
-        remote,
-        inner_plan,
-        window,
-        earlier=tuple(local),
-        merged=True,
-    )
-    inner_beside = across(inner, beside)
-    inner_middle = across(inner, middle)
-    w_far = across(after(w_beside[1], inner), middle)
-
+    inner = attend(
+        meta, inter, inner_queries, blocks, remote, inner_plan, window, earlier=tuple(local)
+    )
     remote.update(prev_second=prev_second, next_second=next_second)
     outer_plan = [
         (0, [("prev_last", -1, 0), ("prev_second", -2, 1)]),
         (3, [("next_first", 3, 0), ("next_second", 3, 1)]),
     ]
-    outer_queries = [after(queries[0], inner), queries[3]]
+    outer_queries = [after(queries[0], inner[0]), queries[3]]
     outer = attend(meta, inter, outer_queries, blocks, remote, outer_plan, window)
+    attended = {1: inner[0], 2: inner[1], 0: outer[0], 3: outer[1]}
     strips = rows // LANES
     wanted, code = prepare_requests(
         after(match_block.reshape(strips, LANES), outer[0]),
@@ -627,30 +574,19 @@
         peers,
         capacity,
     )
-    wanted = lax.all_to_all(wanted, "views", split_axis=0, concat_axis=0, tiled=True)
-
-    outer_beside, outer_middle, outer_far = [None] * 2, [None] * 2, [None] * 2
-    for i in range(2):
-        outer_beside[i] = across(outer[i], beside)
-        outer_middle[i] = across(outer[i], middle)
-    inner_far = across(inner_beside, middle)
-    for i in range(2):
-        outer_far[i] = across(outer_beside[i], middle)
-    w_mine = [w_beside, w_middle, w_far]
-    w_theirs = [partner(w, 1) for w in w_mine]
-    weights = [own_half, *w_mine, *w_theirs]
-    formed = {}
-    for views, attended in (
-        ((1, 2), [[(x, i) for x in (inner, inner_beside, inner_middle, inner_far)] for i in (0, 1)]),
-        ((0,), [[(x[0], None) for x in (outer, outer_beside, outer_middle, outer_far)]]),
-        ((3,), [[(x[1], None) for x in (outer, outer_beside, outer_middle, outer_far)]]),
-    ):
-        if not formed:
-            weights[0] = after(weights[0], wanted)
-        owns, others = project_out(meta, attended, weights, latents, views)
-        returned = [across(x, back) for x in others]
-        for v, own, got in zip(views, owns, returned):
-            formed[v] = (own, got)
+    keep, got, formed = {}, {}, {}
+    for n, v in enumerate(VIEW_ORDER):
+        near = across(attended[v], beside)
+        if n == 2:
+            wanted = lax.all_to_all(
+                after(wanted, send), "views", split_axis=0, concat_axis=0, tiled=True
+            )
+            near = after(near, wanted)
+        keep[v], send = partial_out(meta, attended[v], near, w_out, w_near, halves, loaded.index(v))
+        got[v] = across(send, middle)
+    for v in VIEW_ORDER:
+        own, other = merge_out(meta, keep[v], got[v])
+        formed[v] = (own, across(other, back))
 
     pieces = [formed[v] for v in range(local_views)]
     layer, *outgoing = gather_rows(meta, wanted, pieces)

time: 129 us -> 121 us (0.938)
  blocking collectives: 17.8 us -> 0 us
  starting transfers between devices: 56.9 us -> 64.6 us
  waiting for transfers between devices: 26.4 us -> 21.4 us
  local copies, waits for them, and re-layouts: 0.8 us -> 4.58 us
  Pallas kernels: 25.5 us -> 28.8 us
    all_to_all x0 -> x1, starting transfers between devices: none -> 31.6 us  [per_device(): lax.all_to_all(after(wanted, send), 'views', split_axis=0, concat_axis=0,...]
    all_to_all x1 -> x0, blocking collectives: 17.8 us -> none  [per_device(): lax.all_to_all(wanted, 'views', split_axis=0, concat_axis=0, tiled=True)]
    ppermute x10 -> x7, starting transfers between devices: 21.9 us -> 7.38 us  [partner(): return lax.ppermute(x, 'views', [(i, i ^ mask) for i in range(peers)])]
    ppermute x16 -> x13, starting transfers between devices: 28.9 us -> 19.8 us  [across(): return lax.ppermute(x, 'heads', pairs)]
    ppermute x16 -> x13, waiting for transfers between devices: 15.4 us -> 11.9 us  [across(): return lax.ppermute(x, 'heads', pairs)]
    pallas_call x5 -> x9, Pallas kernels: 11.7 us -> 15 us  [the longest x4 6.11 us: partial_out(): pl.pallas_call(body, in_specs=[SMEM_SPEC] + many(VMEM_SPEC, 5), out_specs...]
    unnamed x15 -> x25, local copies, waits for them, and re-layouts: 0.78 us -> 3.98 us
    ppermute x10 -> x7, waiting for transfers between devices: 11 us -> 7.9 us  [partner(): return lax.ppermute(x, 'views', [(i, i ^ mask) for i in range(peers)])]
  transfers between devices with their start and end apart: 30 -> 25, of which waited for: 9 -> 8; matrix products, arithmetic and copies ran while one was open for 0% -> 1% of each run, Pallas kernels for 13% -> 15%
where the time goes in v1:
time: 121 us; the launch traced here: 120 us
  starting transfers between devices  64.6 us (53%)
  Pallas kernels  28.8 us (24%)
  waiting for transfers between devices  21.4 us (18%)
  local copies, waits for them, and re-layouts  4.58 us (4%)
    all_to_all x1, starting transfers between devices, per_device(): lax.all_to_all(after(wanted, send), 'views', split_axis=0, concat_axis=0,...  31.6 us
    ppermute x13, starting transfers between devices, across(): return lax.ppermute(x, 'heads', pairs)  19.8 us
    ppermute x13, waiting for transfers between devices, across(): return lax.ppermute(x, 'heads', pairs)  11.9 us
    pallas_call x3, Pallas kernels, attend(): pl.pallas_call(body, in_specs=[SMEM_SPEC, SMEM_SPEC] + many(VMEM_SPEC, he...  8.15 us
    ppermute x7, waiting for transfers between devices, partner(): return lax.ppermute(x, 'views', [(i, i ^ mask) for i in range(peers)])  7.9 us
    ppermute x7, starting transfers between devices, partner(): return lax.ppermute(x, 'views', [(i, i ^ mask) for i in range(peers)])  7.38 us
    pallas_call x4, Pallas kernels, partial_out(): pl.pallas_call(body, in_specs=[SMEM_SPEC] + many(VMEM_SPEC, 5), out_specs...  6.11 us
    ppermute x4, starting transfers between devices, along(): lax.ppermute(x, 'views', [(i, (i + by) % peers) for i in range(peers)])  5.84 us
  transfers between devices with their start and end apart: 25, of which 8 were waited for; matrix products, arithmetic and copies ran while one was open for 1% of the time, Pallas kernels for 15%

profile of v1, /device:TPU:0, one launch (start us, length us, event | category | flops | bytes accessed | tf_op | source)
XLA Modules:
  0.0 119.8 jit_solution(16154763814742747906)
XLA Ops:
  0.0 0.7 copy-done.8
  0.7 5.7 %project_views.1 = (bf16[256,256]{1,0:T(8,128)(2,1)S(1)}, bf16[2,256,256]{2,1,0:T(8,128)(2,1)S(1)}, bf16[256,256]{1,0:T(8,128)(2,1)S(1)}, bf16[2,256,256]{2,1,0:...) custom-call(s32[4]{0:T(128)S(1)} %compare_select_fusion.1.meta_ref, ...), custom_call_target="tpu_custom_call" | custom-call | flops 1610612736 | bytes 5242880 | tf_op jit(solution)/shard_map/project_views/pallas_call | solution.py:97
  6.4 3.4 %collective-permute-start = (bf16[2,256,256]{2,1,0:T(8,128)(2,1)S(1)}, bf16[2,256,256]{2,1,0:T(8,128)(2,1)S(1)}, u32[]{:S(2)}, u32[]{:S(2)}) collective-permute-start(bf16[2,256,256]{2,1,0:T(8,128)(2,1)S(1)} %get-tuple-element.57.refs_2_.refs_4_), channel_id=1, source_target_pairs={{0,28},{4,0},{8,4},{12,8},{16,12},{20,16},{24,20},{28,24},{1,29},{... | collective-permute-start | bytes 786440 | tf_op jit(solution)/shard_map/ppermute | solution.py:529
  9.8 3.5 %collective-permute-start.5 = (bf16[256,1024]{1,0:T(8,128)(2,1)S(1)}, bf16[256,1024]{1,0:T(8,128)(2,1)S(1)}, u32[]{:S(2)}, u32[]{:S(2)}) collective-permute-start(bf16[256,1024]{1,0:T(8,128)(2,1)S(1)} %copy-done), channel_id=1, source_target_pairs={{0,1},{3,2},{4,5},{7,6},{8,9},{11,10},{12,13},{15,14},{16,17},{19,... | collective-permute-start | bytes 1572872 | tf_op jit(solution)/shard_map/ppermute | solution.py:535
  13.3 2.9 %attend_local.1 = (f32[2,320,256]{2,1,0:T(8,128)S(1)}, f32[2,4,256]{2,1,0:T(4,128)S(1)}) custom-call(s32[4]{0:T(128)S(1)} %compare_select_fusion.1.meta_ref, s32[2,32]{1,0:T(2,128)S(1)} %bitcast.12, bf16[256,256]{1,0:T(8,128)(2,1)S(1)} %get-tuple-element.55.refs_0_.refs_2_, bf16[256,256]{1,0:T(8,128)(2,1)S(1)} %get-tuple-element.56.refs_1_.refs_3_, ...), custom_call_target="tpu_custom_call" | custom-call | flops 1073741824 | bytes 4194304 | tf_op jit(solution)/shard_map/attend_local/pallas_call | solution.py:266
  16.3 2.4 %collective-permute-start.2 = (bf16[2,256,256]{2,1,0:T(8,128)(2,1)S(1)}, bf16[2,256,256]{2,1,0:T(8,128)(2,1)S(1)}, u32[]{:S(2)}, u32[]{:S(2)}) collective-permute-start(bf16[2,256,256]{2,1,0:T(8,128)(2,1)S(1)} %get-tuple-element.66.refs_3_.refs_5_), channel_id=1, source_target_pairs={{0,28},{4,0},{8,4},{12,8},{16,12},{20,16},{24,20},{28,24},{1,29},{... | collective-permute-start | bytes 786440 | tf_op jit(solution)/shard_map/ppermute | solution.py:529
  18.7 1.7 %attend.2 = (bf16[256,256]{1,0:T(8,128)(2,1)S(1)}, bf16[256,256]{1,0:T(8,128)(2,1)S(1)}) custom-call(s32[4]{0:T(128)S(1)} %compare_select_fusion.1.meta_ref, s32[2,32]{1,0:T(2,128)S(1)} %bitcast.13, f32[2,320,256]{2,1,0:T(8,128)S(1)} %get-tuple-element.61.refs_0_, f32[2,4,256]{2,1,0:T(4,128)S(1)} %get-tuple-element.62.refs_1_, ...), custom_call_target="tpu_custom_call" | custom-call | flops 268435456 | bytes 1048576 | tf_op jit(solution)/shard_map/attend/pallas_call | solution.py:266
  20.4 2.3 %collective-permute-start.9 = (bf16[256,256]{1,0:T(8,128)(2,1)S(1)}, bf16[256,256]{1,0:T(8,128)(2,1)S(1)}, u32[]{:S(2)}, u32[]{:S(2)}) collective-permute-start(bf16[256,256]{1,0:T(8,128)(2,1)S(1)} %get-tuple-element.63.att), channel_id=1, source_target_pairs={{0,1},{3,2},{4,5},{7,6},{8,9},{11,10},{12,13},{15,14},{16,17},{19,... | collective-permute-start | bytes 393224 | tf_op jit(solution)/shard_map/ppermute | solution.py:535
  22.7 1.3 %collective-permute-start.4 = (bf16[256,256]{1,0:T(8,128)(2,1)S(1)}, bf16[256,256]{1,0:T(8,128)(2,1)S(1)}, u32[]{:S(2)}, u32[]{:S(2)}) collective-permute-start(bf16[256,256]{1,0:T(8,128)(2,1)S(1)} %get-tuple-element.72.att), channel_id=1, source_target_pairs={{0,1},{3,2},{4,5},{7,6},{8,9},{11,10},{12,13},{15,14},{16,17},{19,... | collective-permute-start | bytes 393224 | tf_op jit(solution)/shard_map/ppermute | solution.py:535
  24.0 1.5 %collective-permute-done.3.refs_9_ = bf16[2,256,256]{2,1,0:T(8,128)(2,1)S(1)} collective-permute-done((bf16[2,256,256]{2,1,0:T(8,128)(2,1)S(1)}, bf16[2,256,256]{2,1,0:T(8,128)(2,1)S(1)}, u32[]{:S(2)}, u32[]{:S(2)}) %collective-permute-start.3) | collective-permute-done | bytes 262176 | tf_op jit(solution)/shard_map/ppermute | solution.py:529
  25.6 3.5 %attend.3 = (bf16[256,256]{1,0:T(8,128)(2,1)S(1)}, bf16[256,256]{1,0:T(8,128)(2,1)S(1)}) custom-call(s32[4]{0:T(128)S(1)} %compare_select_fusion.1.meta_ref, s32[2,32]{1,0:T(2,128)S(1)} %bitcast.14, bf16[256,256]{1,0:T(8,128)(2,1)S(1)} %get-tuple-element.64.refs_0_, bf16[256,256]{1,0:T(8,128)(2,1)S(1)} %get-tuple-element.65.refs_1_, ...), custom_call_target="tpu_custom_call" | custom-call | flops 1342177280 | bytes 5242880 | tf_op jit(solution)/shard_map/attend/pallas_call | solution.py:266
  29.1 1.6 %collective-permute-start.14 = (bf16[256,256]{1,0:T(8,128)(2,1)S(1)}, bf16[256,256]{1,0:T(8,128)(2,1)S(1)}, u32[]{:S(2)}, u32[]{:S(2)}) collective-permute-start(bf16[256,256]{1,0:T(8,128)(2,1)S(1)} %get-tuple-element.89.att), channel_id=1, source_target_pairs={{0,1},{3,2},{4,5},{7,6},{8,9},{11,10},{12,13},{15,14},{16,17},{19,... | collective-permute-start | bytes 393224 | tf_op jit(solution)/shard_map/ppermute | solution.py:535
  30.6 1.9 %collective-permute-start.6 = (bf16[256,256]{1,0:T(8,128)(2,1)S(1)}, bf16[256,256]{1,0:T(8,128)(2,1)}, u32[]{:S(2)}, u32[]{:S(2)}) collective-permute-start(bf16[256,256]{1,0:T(8,128)(2,1)S(1)} %get-tuple-element.68.att), channel_id=1, source_target_pairs={{0,1},{3,2},{4,5},{7,6},{8,9},{11,10},{12,13},{15,14},{16,17},{19,... | collective-permute-start | bytes 393224 | tf_op jit(solution)/shard_map/ppermute | solution.py:535
  32.6 0.7 prepare_requests.1
  33.3 1.6 %partial_out.4 = (f32[256,512]{1,0:T(8,128)S(1)}, bf16[256,512]{1,0:T(8,128)(2,1)}) custom-call(s32[4]{0:T(128)S(1)} %compare_select_fusion.1.meta_ref, bf16[256,256]{1,0:T(8,128)(2,1)S(1)} %get-tuple-element.72.att, bf16[256,256]{1,0:T(8,128)(2,1)S(1)} %collective-permute-done.4.near_ref, bf16[256,1024]{1,0:T(8,128)(2,1)S(1)} %copy-done, ...), custom_call_target="tpu_custom_call" | custom-call | flops 268435456 | bytes 2621440 | tf_op jit(solution)/shard_map/partial_out/pallas_call | solution.py:332
  34.9 0.7 collective-permute-start.12
  35.5 0.6 copy.9
  36.1 31.6 %all-to-all-start = ((s32[8,1,256]{2,1,0:T(1,128)}), s32[8,1,256]{2,1,0:T(1,128)S(1)}, u32[]{:S(2)}, u32[]{:S(2)}) async-start(s32[8,1,256]{2,1,0:T(1,128)} %copy.9), calls=%async_computation | async-start | bytes 16384 | tf_op jit(solution)/shard_map/all_to_all | solution.py:581
  67.7 1.6 %partial_out.6 = (f32[256,512]{1,0:T(8,128)S(1)}, bf16[256,512]{1,0:T(8,128)(2,1)}) custom-call(s32[4]{0:T(128)S(1)} %compare_select_fusion.1.meta_ref, bf16[256,256]{1,0:T(8,128)(2,1)S(1)} %get-tuple-element.63.att, bf16[256,256]{1,0:T(8,128)(2,1)S(1)} %collective-permute-done.9.near_ref, bf16[256,1024]{1,0:T(8,128)(2,1)S(1)} %copy-done, ...), custom_call_target="tpu_custom_call" | custom-call | flops 268435456 | bytes 2621440 | tf_op jit(solution)/shard_map/partial_out/pallas_call | solution.py:332
  69.3 0.8 copy-done.1
  70.1 1.4 %collective-permute-start.10 = (bf16[256,512]{1,0:T(8,128)(2,1)}, bf16[256,512]{1,0:T(8,128)(2,1)}, u32[]{:S(2)}, u32[]{:S(2)}) collective-permute-start(bf16[256,512]{1,0:T(8,128)(2,1)} %get-tuple-element.83), channel_id=1, source_target_pairs={{1,2},{2,1},{5,6},{6,5},{9,10},{10,9},{13,14},{14,13},{17,18},{18,... | collective-permute-start | bytes 786440 | tf_op jit(solution)/shard_map/ppermute | solution.py:535
  71.5 0.7 copy-done.5
  72.1 0.9 copy-done.4
  73.0 0.9 copy-done.6
  73.9 1.6 %partial_out.7 = (f32[256,512]{1,0:T(8,128)S(1)}, bf16[256,512]{1,0:T(8,128)(2,1)}) custom-call(s32[4]{0:T(128)S(1)} %compare_select_fusion.1.meta_ref, bf16[256,256]{1,0:T(8,128)(2,1)S(1)} %copy-done.4, bf16[256,256]{1,0:T(8,128)(2,1)S(1)} %copy-done.6, bf16[256,1024]{1,0:T(8,128)(2,1)S(1)} %copy-done, ...), custom_call_target="tpu_custom_call" | custom-call | flops 268435456 | bytes 2621440 | tf_op jit(solution)/shard_map/partial_out/pallas_call | solution.py:332
  75.5 1.4 %collective-permute-start.15 = (bf16[256,512]{1,0:T(8,128)(2,1)}, bf16[256,512]{1,0:T(8,128)(2,1)}, u32[]{:S(2)}, u32[]{:S(2)}) collective-permute-start(bf16[256,512]{1,0:T(8,128)(2,1)} %get-tuple-element.91), channel_id=1, source_target_pairs={{1,2},{2,1},{5,6},{6,5},{9,10},{10,9},{13,14},{14,13},{17,18},{18,... | collective-permute-start | bytes 786440 | tf_op jit(solution)/shard_map/ppermute | solution.py:535
  76.9 1.4 %partial_out.5 = (f32[256,512]{1,0:T(8,128)S(1)}, bf16[256,512]{1,0:T(8,128)(2,1)S(1)}) custom-call(s32[4]{0:T(128)S(1)} %compare_select_fusion.1.meta_ref, bf16[256,256]{1,0:T(8,128)(2,1)S(1)} %get-tuple-element.68.att, bf16[256,256]{1,0:T(8,128)(2,1)} %collective-permute-done.6.near_ref, bf16[256,1024]{1,0:T(8,128)(2,1)S(1)} %copy-done, ...), custom_call_target="tpu_custom_call" | custom-call | flops 268435456 | bytes 2621440 | tf_op jit(solution)/shard_map/partial_out/pallas_call | solution.py:332
  78.3 0.7 collective-permute-start.7
  79.0 1.0 merge_out.5
  80.0 1.3 %collective-permute-start.11 = (bf16[256,256]{1,0:T(8,128)(2,1)S(1)}, bf16[256,256]{1,0:T(8,128)(2,1)S(1)}, u32[]{:S(2)}, u32[]{:S(2)}) collective-permute-start(bf16[256,256]{1,0:T(8,128)(2,1)S(1)} %get-tuple-element.85), channel_id=1, source_target_pairs={{1,0},{2,3},{5,4},{6,7},{9,8},{10,11},{13,12},{14,15},{17,16},{18,... | collective-permute-start | bytes 393224 | tf_op jit(solution)/shard_map/ppermute | solution.py:535
  81.3 0.6 merge_out.6
  82.0 1.3 %collective-permute-start.13 = (bf16[256,256]{1,0:T(8,128)(2,1)S(1)}, bf16[256,256]{1,0:T(8,128)(2,1)S(1)}, u32[]{:S(2)}, u32[]{:S(2)}) collective-permute-start(bf16[256,256]{1,0:T(8,128)(2,1)S(1)} %get-tuple-element.88), channel_id=1, source_target_pairs={{1,0},{2,3},{5,4},{6,7},{9,8},{10,11},{13,12},{14,15},{17,16},{18,... | collective-permute-start | bytes 393224 | tf_op jit(solution)/shard_map/ppermute | solution.py:535
  83.3 1.0 merge_out.7
  84.3 1.3 %collective-permute-start.16 = (bf16[256,256]{1,0:T(8,128)(2,1)S(1)}, bf16[256,256]{1,0:T(8,128)(2,1)S(1)}, u32[]{:S(2)}, u32[]{:S(2)}) collective-permute-start(bf16[256,256]{1,0:T(8,128)(2,1)S(1)} %get-tuple-element.93), channel_id=1, source_target_pairs={{1,0},{2,3},{5,4},{6,7},{9,8},{10,11},{13,12},{14,15},{17,16},{18,... | collective-permute-start | bytes 393224 | tf_op jit(solution)/shard_map/ppermute | solution.py:535
  85.6 0.6 merge_out.4
  86.2 1.3 %collective-permute-start.8 = (bf16[256,256]{1,0:T(8,128)(2,1)S(1)}, bf16[256,256]{1,0:T(8,128)(2,1)S(1)}, u32[]{:S(2)}, u32[]{:S(2)}) collective-permute-start(bf16[256,256]{1,0:T(8,128)(2,1)S(1)} %get-tuple-element.81), channel_id=1, source_target_pairs={{1,0},{2,3},{5,4},{6,7},{9,8},{10,11},{13,12},{14,15},{17,16},{18,... | collective-permute-start | bytes 393224 | tf_op jit(solution)/shard_map/ppermute | solution.py:535
  87.5 4.3 %collective-permute-done.11.refs_3_ = bf16[256,256]{1,0:T(8,128)(2,1)S(1)} collective-permute-done((bf16[256,256]{1,0:T(8,128)(2,1)S(1)}, bf16[256,256]{1,0:T(8,128)(2,1)S(1)}, u32[]{:S(2)}, u32[]{:S(2)}) %collective-permute-start.11) | collective-permute-done | bytes 131104 | tf_op jit(solution)/shard_map/ppermute | solution.py:535
  91.9 2.8 %collective-permute-done.13.refs_5_ = bf16[256,256]{1,0:T(8,128)(2,1)S(1)} collective-permute-done((bf16[256,256]{1,0:T(8,128)(2,1)S(1)}, bf16[256,256]{1,0:T(8,128)(2,1)S(1)}, u32[]{:S(2)}, u32[]{:S(2)}) %collective-permute-start.13) | collective-permute-done | bytes 131104 | tf_op jit(solution)/shard_map/ppermute | solution.py:535
  94.7 2.3 %collective-permute-done.16.refs_7_ = bf16[256,256]{1,0:T(8,128)(2,1)S(1)} collective-permute-done((bf16[256,256]{1,0:T(8,128)(2,1)S(1)}, bf16[256,256]{1,0:T(8,128)(2,1)S(1)}, u32[]{:S(2)}, u32[]{:S(2)}) %collective-permute-start.16) | collective-permute-done | bytes 131104 | tf_op jit(solution)/shard_map/ppermute | solution.py:535
  97.0 2.5 %collective-permute-done.8.refs_1_ = bf16[256,256]{1,0:T(8,128)(2,1)S(1)} collective-permute-done((bf16[256,256]{1,0:T(8,128)(2,1)S(1)}, bf16[256,256]{1,0:T(8,128)(2,1)S(1)}, u32[]{:S(2)}, u32[]{:S(2)}) %collective-permute-start.8) | collective-permute-done | bytes 131104 | tf_op jit(solution)/shard_map/ppermute | solution.py:535
  99.4 2.1 %gather_rows.1 = (bf16[1024,256]{1,0:T(8,128)(2,1)S(1)}, bf16[256,256]{1,0:T(8,128)(2,1)S(1)}, bf16[256,256]{1,0:T(8,128)(2,1)S(1)}, bf16[256,256]{1,0:T(8,128)(...) custom-call(s32[4]{0:T(128)S(1)} %compare_select_fusion.1.meta_ref, ...), custom_call_target="tpu_custom_call" | custom-call | flops 1073741824 | bytes 3145728 | tf_op jit(solution)/shard_map/gather_rows/pallas_call | solution.py:444
  101.6 1.7 %collective-permute-start.18 = (bf16[256,256]{1,0:T(8,128)(2,1)S(1)}, bf16[256,256]{1,0:T(8,128)(2,1)S(1)}, u32[]{:S(2)}, u32[]{:S(2)}) collective-permute-start(bf16[256,256]{1,0:T(8,128)(2,1)S(1)} %get-tuple-element.97), channel_id=1, source_target_pairs={{0,8},{4,12},{8,0},{12,4},{16,24},{20,28},{24,16},{28,20},{1,9},{5... | collective-permute-start | bytes 393224 | tf_op jit(solution)/shard_map/ppermute | solution.py:532
  103.4 1.7 %collective-permute-start.20 = (bf16[256,256]{1,0:T(8,128)(2,1)S(1)}, bf16[256,256]{1,0:T(8,128)(2,1)S(1)}, u32[]{:S(2)}, u32[]{:S(2)}) collective-permute-start(bf16[256,256]{1,0:T(8,128)(2,1)S(1)} %get-tuple-element.99), channel_id=1, source_target_pairs={{0,16},{4,20},{8,24},{12,28},{16,0},{20,4},{24,8},{28,12},{1,17},{... | collective-permute-start | bytes 393224 | tf_op jit(solution)/shard_map/ppermute | solution.py:532
  105.1 2.6 %collective-permute-start.22 = (bf16[256,256]{1,0:T(8,128)(2,1)S(1)}, bf16[256,256]{1,0:T(8,128)(2,1)S(1)}, u32[]{:S(2)}, u32[]{:S(2)}) collective-permute-start(bf16[256,256]{1,0:T(8,128)(2,1)S(1)} %get-tuple-element.101), channel_id=1, source_target_pairs={{0,24},{4,28},{8,16},{12,20},{16,8},{20,12},{24,0},{28,4},{1,25},{... | collective-permute-start | bytes 393224 | tf_op jit(solution)/shard_map/ppermute | solution.py:532
  108.0 1.2 collective-permute-start.23
  109.2 0.8 collective-permute-done.19.refs_3_
  110.0 6.8 %collective-permute-done.21.refs_5_ = bf16[256,256]{1,0:T(8,128)(2,1)S(1)} collective-permute-done((bf16[256,256]{1,0:T(8,128)(2,1)S(1)}, bf16[256,256]{1,0:T(8,128)(2,1)S(1)}, u32[]{:S(2)}, u32[]{:S(2)}) %collective-permute-start.21) | collective-permute-done | bytes 131104 | tf_op jit(solution)/shard_map/ppermute | solution.py:532
  116.8 2.9 %finish_rows.1 = f32[1024,256]{1,0:T(8,128)} custom-call(s32[4]{0:T(128)S(1)} %compare_select_fusion.1.meta_ref, s32[8,128]{1,0:T(8,128)S(1)} %get-tuple-element.70.code_ref, f32[8,128]{1,0:T(8,128)S(1)} %bitcast.18, bf16[1024,256]{1,0:T(8,128)(2,1)S(1)} %get-tuple-element.94.layer_ref, bf16[256,256]{1,0:T(8,128)(2,1)S(1)} %get-tuple-element.95.refs_0_, ...), custom_call_target="tpu_custom_call" | custom-call | flops 1073741824 | bytes 2621440 | tf_op jit(solution)/shard_map/finish_rows/pallas_call | solution.py:500
  (44 shorter events, 0.7 us)
Async XLA Ops:
  0.0 0.7 copy-start.8
  0.7 9.1 %copy-start = (bf16[256,1024]{1,0:T(8,128)(2,1)S(1)}, bf16[256,1024]{1,0:T(8,128)(2,1)}, u32[]{:S(2)}) copy-start(bf16[256,1024]{1,0:T(8,128)(2,1)} %own_ref.7) | copy-start | bytes 1572868
  0.7 12.6 %copy-start.7 = (s32[32,2]{0,1:T(2,128)S(1)}, s32[32,2]{0,1:T(2,128)}, u32[]{:S(2)}) copy-start(s32[32,2]{0,1:T(2,128)} %param.12) | copy-start | bytes 772
  6.4 12.3 %collective-permute-start = (bf16[2,256,256]{2,1,0:T(8,128)(2,1)S(1)}, bf16[2,256,256]{2,1,0:T(8,128)(2,1)S(1)}, u32[]{:S(2)}, u32[]{:S(2)}) collective-permute-start(bf16[2,256,256]{2,1,0:T(8,128)(2,1)S(1)} %get-tuple-element.57.refs_2_.refs_4_), channel_id=1, source_target_pairs={{0,28},{4,0},{8,4},{12,8},{16,12},{20,16},{24,20},{28,24},{1,29},{... | collective-permute-start | bytes 786440 | tf_op jit(solution)/shard_map/ppermute | solution.py:529
  9.8 8.9 %collective-permute-start.1 = (bf16[2,256,256]{2,1,0:T(8,128)(2,1)S(1)}, bf16[2,256,256]{2,1,0:T(8,128)(2,1)S(1)}, u32[]{:S(2)}, u32[]{:S(2)}) collective-permute-start(bf16[2,256,256]{2,1,0:T(8,128)(2,1)S(1)} %get-tuple-element.60.refs_5_.refs_7_), channel_id=1, source_target_pairs={{0,4},{4,8},{8,12},{12,16},{16,20},{20,24},{24,28},{28,0},{1,5},{5... | collective-permute-start | bytes 786440 | tf_op jit(solution)/shard_map/ppermute | solution.py:529
  9.8 23.5 %collective-permute-start.5 = (bf16[256,1024]{1,0:T(8,128)(2,1)S(1)}, bf16[256,1024]{1,0:T(8,128)(2,1)S(1)}, u32[]{:S(2)}, u32[]{:S(2)}) collective-permute-start(bf16[256,1024]{1,0:T(8,128)(2,1)S(1)} %copy-done), channel_id=1, source_target_pairs={{0,1},{3,2},{4,5},{7,6},{8,9},{11,10},{12,13},{15,14},{16,17},{19,... | collective-permute-start | bytes 1572872 | tf_op jit(solution)/shard_map/ppermute | solution.py:535
  16.3 7.8 %collective-permute-start.2 = (bf16[2,256,256]{2,1,0:T(8,128)(2,1)S(1)}, bf16[2,256,256]{2,1,0:T(8,128)(2,1)S(1)}, u32[]{:S(2)}, u32[]{:S(2)}) collective-permute-start(bf16[2,256,256]{2,1,0:T(8,128)(2,1)S(1)} %get-tuple-element.66.refs_3_.refs_5_), channel_id=1, source_target_pairs={{0,28},{4,0},{8,4},{12,8},{16,12},{20,16},{24,20},{28,24},{1,29},{... | collective-permute-start | bytes 786440 | tf_op jit(solution)/shard_map/ppermute | solution.py:529
  18.7 6.9 %collective-permute-start.3 = (bf16[2,256,256]{2,1,0:T(8,128)(2,1)S(1)}, bf16[2,256,256]{2,1,0:T(8,128)(2,1)S(1)}, u32[]{:S(2)}, u32[]{:S(2)}) collective-permute-start(bf16[2,256,256]{2,1,0:T(8,128)(2,1)S(1)} %get-tuple-element.67.refs_4_.refs_6_), channel_id=1, source_target_pairs={{0,4},{4,8},{8,12},{12,16},{16,20},{20,24},{24,28},{28,0},{1,5},{5... | collective-permute-start | bytes 786440 | tf_op jit(solution)/shard_map/ppermute | solution.py:529
  20.4 47.3 %collective-permute-start.9 = (bf16[256,256]{1,0:T(8,128)(2,1)S(1)}, bf16[256,256]{1,0:T(8,128)(2,1)S(1)}, u32[]{:S(2)}, u32[]{:S(2)}) collective-permute-start(bf16[256,256]{1,0:T(8,128)(2,1)S(1)} %get-tuple-element.63.att), channel_id=1, source_target_pairs={{0,1},{3,2},{4,5},{7,6},{8,9},{11,10},{12,13},{15,14},{16,17},{19,... | collective-permute-start | bytes 393224 | tf_op jit(solution)/shard_map/ppermute | solution.py:535
  22.7 10.6 %collective-permute-start.4 = (bf16[256,256]{1,0:T(8,128)(2,1)S(1)}, bf16[256,256]{1,0:T(8,128)(2,1)S(1)}, u32[]{:S(2)}, u32[]{:S(2)}) collective-permute-start(bf16[256,256]{1,0:T(8,128)(2,1)S(1)} %get-tuple-element.72.att), channel_id=1, source_target_pairs={{0,1},{3,2},{4,5},{7,6},{8,9},{11,10},{12,13},{15,14},{16,17},{19,... | collective-permute-start | bytes 393224 | tf_op jit(solution)/shard_map/ppermute | solution.py:535
  25.6 7.0 %copy-start.9 = (s32[1024,1]{0,1:T(1,128)S(1)}, s32[1024,1]{0,1:T(1,128)}, u32[]{:S(2)}) copy-start(s32[1024,1]{0,1:T(1,128)} %param.13) | copy-start | bytes 12292
  25.6 7.0 %copy-start.10 = (s32[1024]{0:T(1024)S(1)}, s32[1024]{0:T(1024)}, u32[]{:S(2)}) copy-start(s32[1024]{0:T(1024)} %param.14) | copy-start | bytes 12292
  29.1 40.2 %copy-start.3 = (bf16[256,256]{1,0:T(8,128)(2,1)}, bf16[256,256]{1,0:T(8,128)(2,1)S(1)}, u32[]{:S(2)}) copy-start(bf16[256,256]{1,0:T(8,128)(2,1)S(1)} %get-tuple-element.89.att) | copy-start | bytes 393220
  29.1 42.4 %collective-permute-start.14 = (bf16[256,256]{1,0:T(8,128)(2,1)S(1)}, bf16[256,256]{1,0:T(8,128)(2,1)S(1)}, u32[]{:S(2)}, u32[]{:S(2)}) collective-permute-start(bf16[256,256]{1,0:T(8,128)(2,1)S(1)} %get-tuple-element.89.att), channel_id=1, source_target_pairs={{0,1},{3,2},{4,5},{7,6},{8,9},{11,10},{12,13},{15,14},{16,17},{19,... | collective-permute-start | bytes 393224 | tf_op jit(solution)/shard_map/ppermute | solution.py:535
  30.6 46.2 %collective-permute-start.6 = (bf16[256,256]{1,0:T(8,128)(2,1)S(1)}, bf16[256,256]{1,0:T(8,128)(2,1)}, u32[]{:S(2)}, u32[]{:S(2)}) collective-permute-start(bf16[256,256]{1,0:T(8,128)(2,1)S(1)} %get-tuple-element.68.att), channel_id=1, source_target_pairs={{0,1},{3,2},{4,5},{7,6},{8,9},{11,10},{12,13},{15,14},{16,17},{19,... | collective-permute-start | bytes 393224 | tf_op jit(solution)/shard_map/ppermute | solution.py:535
  34.9 46.5 %collective-permute-start.12 = (bf16[256,512]{1,0:T(8,128)(2,1)}, bf16[256,512]{1,0:T(8,128)(2,1)S(1)}, u32[]{:S(2)}, u32[]{:S(2)}) collective-permute-start(bf16[256,512]{1,0:T(8,128)(2,1)} %get-tuple-element.75), channel_id=1, source_target_pairs={{1,2},{2,1},{5,6},{6,5},{9,10},{10,9},{13,14},{14,13},{17,18},{18,... | collective-permute-start | bytes 786440 | tf_op jit(solution)/shard_map/ppermute | solution.py:535
  36.1 40.7 %all-to-all-start = ((s32[8,1,256]{2,1,0:T(1,128)}), s32[8,1,256]{2,1,0:T(1,128)S(1)}, u32[]{:S(2)}, u32[]{:S(2)}) async-start(s32[8,1,256]{2,1,0:T(1,128)} %copy.9), calls=%async_computation | async-start | bytes 16384 | tf_op jit(solution)/shard_map/all_to_all | solution.py:581
  69.3 0.8 copy-start.1
  70.1 8.9 %collective-permute-start.10 = (bf16[256,512]{1,0:T(8,128)(2,1)}, bf16[256,512]{1,0:T(8,128)(2,1)}, u32[]{:S(2)}, u32[]{:S(2)}) collective-permute-start(bf16[256,512]{1,0:T(8,128)(2,1)} %get-tuple-element.83), channel_id=1, source_target_pairs={{1,2},{2,1},{5,6},{6,5},{9,10},{10,9},{13,14},{14,13},{17,18},{18,... | collective-permute-start | bytes 786440 | tf_op jit(solution)/shard_map/ppermute | solution.py:535
  71.5 0.7 copy-start.5
  72.1 0.9 copy-start.4
  73.0 0.9 copy-start.6
  75.5 7.8 %collective-permute-start.15 = (bf16[256,512]{1,0:T(8,128)(2,1)}, bf16[256,512]{1,0:T(8,128)(2,1)}, u32[]{:S(2)}, u32[]{:S(2)}) collective-permute-start(bf16[256,512]{1,0:T(8,128)(2,1)} %get-tuple-element.91), channel_id=1, source_target_pairs={{1,2},{2,1},{5,6},{6,5},{9,10},{10,9},{13,14},{14,13},{17,18},{18,... | collective-permute-start | bytes 786440 | tf_op jit(solution)/shard_map/ppermute | solution.py:535
  76.9 2.1 %copy-start.2 = (f32[256,512]{1,0:T(8,128)S(1)}, f32[256,512]{1,0:T(8,128)}, u32[]{:S(2)}) copy-start(f32[256,512]{1,0:T(8,128)} %copy-done.1) | copy-start | bytes 1572868
  78.3 7.3 %collective-permute-start.7 = (bf16[256,512]{1,0:T(8,128)(2,1)S(1)}, bf16[256,512]{1,0:T(8,128)(2,1)S(1)}, u32[]{:S(2)}, u32[]{:S(2)}) collective-permute-start(bf16[256,512]{1,0:T(8,128)(2,1)S(1)} %get-tuple-element.79), channel_id=1, source_target_pairs={{1,2},{2,1},{5,6},{6,5},{9,10},{10,9},{13,14},{14,13},{17,18},{18,... | collective-permute-start | bytes 786440 | tf_op jit(solution)/shard_map/ppermute | solution.py:535
  80.0 11.8 %collective-permute-start.11 = (bf16[256,256]{1,0:T(8,128)(2,1)S(1)}, bf16[256,256]{1,0:T(8,128)(2,1)S(1)}, u32[]{:S(2)}, u32[]{:S(2)}) collective-permute-start(bf16[256,256]{1,0:T(8,128)(2,1)S(1)} %get-tuple-element.85), channel_id=1, source_target_pairs={{1,0},{2,3},{5,4},{6,7},{9,8},{10,11},{13,12},{14,15},{17,16},{18,... | collective-permute-start | bytes 393224 | tf_op jit(solution)/shard_map/ppermute | solution.py:535
  82.0 12.7 %collective-permute-start.13 = (bf16[256,256]{1,0:T(8,128)(2,1)S(1)}, bf16[256,256]{1,0:T(8,128)(2,1)S(1)}, u32[]{:S(2)}, u32[]{:S(2)}) collective-permute-start(bf16[256,256]{1,0:T(8,128)(2,1)S(1)} %get-tuple-element.88), channel_id=1, source_target_pairs={{1,0},{2,3},{5,4},{6,7},{9,8},{10,11},{13,12},{14,15},{17,16},{18,... | collective-permute-start | bytes 393224 | tf_op jit(solution)/shard_map/ppermute | solution.py:535
  84.3 12.7 %collective-permute-start.16 = (bf16[256,256]{1,0:T(8,128)(2,1)S(1)}, bf16[256,256]{1,0:T(8,128)(2,1)S(1)}, u32[]{:S(2)}, u32[]{:S(2)}) collective-permute-start(bf16[256,256]{1,0:T(8,128)(2,1)S(1)} %get-tuple-element.93), channel_id=1, source_target_pairs={{1,0},{2,3},{5,4},{6,7},{9,8},{10,11},{13,12},{14,15},{17,16},{18,... | collective-permute-start | bytes 393224 | tf_op jit(solution)/shard_map/ppermute | solution.py:535
  86.2 30.6 %copy-start.11 = (f32[1024]{0:T(1024)S(1)}, f32[1024]{0:T(1024)}, u32[]{:S(2)}) copy-start(f32[1024]{0:T(1024)} %param.15) | copy-start | bytes 12292
  86.2 13.2 %collective-permute-start.8 = (bf16[256,256]{1,0:T(8,128)(2,1)S(1)}, bf16[256,256]{1,0:T(8,128)(2,1)S(1)}, u32[]{:S(2)}, u32[]{:S(2)}) collective-permute-start(bf16[256,256]{1,0:T(8,128)(2,1)S(1)} %get-tuple-element.81), channel_id=1, source_target_pairs={{1,0},{2,3},{5,4},{6,7},{9,8},{10,11},{13,12},{14,15},{17,16},{18,... | collective-permute-start | bytes 393224 | tf_op jit(solution)/shard_map/ppermute | solution.py:535
  101.5 3.6 %collective-permute-start.17 = (bf16[256,256]{1,0:T(8,128)(2,1)S(1)}, bf16[256,256]{1,0:T(8,128)(2,1)S(1)}, u32[]{:S(2)}, u32[]{:S(2)}) collective-permute-start(bf16[256,256]{1,0:T(8,128)(2,1)S(1)} %get-tuple-element.96), channel_id=1, source_target_pairs={{0,4},{4,0},{8,12},{12,8},{16,20},{20,16},{24,28},{28,24},{1,5},{5... | collective-permute-start | bytes 393224 | tf_op jit(solution)/shard_map/ppermute | solution.py:532
  101.6 6.4 %collective-permute-start.18 = (bf16[256,256]{1,0:T(8,128)(2,1)S(1)}, bf16[256,256]{1,0:T(8,128)(2,1)S(1)}, u32[]{:S(2)}, u32[]{:S(2)}) collective-permute-start(bf16[256,256]{1,0:T(8,128)(2,1)S(1)} %get-tuple-element.97), channel_id=1, source_target_pairs={{0,8},{4,12},{8,0},{12,4},{16,24},{20,28},{24,16},{28,20},{1,9},{5... | collective-permute-start | bytes 393224 | tf_op jit(solution)/shard_map/ppermute | solution.py:532
  103.3 6.7 %collective-permute-start.19 = (bf16[256,256]{1,0:T(8,128)(2,1)S(1)}, bf16[256,256]{1,0:T(8,128)(2,1)S(1)}, u32[]{:S(2)}, u32[]{:S(2)}) collective-permute-start(bf16[256,256]{1,0:T(8,128)(2,1)S(1)} %get-tuple-element.98), channel_id=1, source_target_pairs={{0,12},{4,8},{8,4},{12,0},{16,28},{20,24},{24,20},{28,16},{1,13},{... | collective-permute-start | bytes 393224 | tf_op jit(solution)/shard_map/ppermute | solution.py:532
  103.4 6.6 %collective-permute-start.20 = (bf16[256,256]{1,0:T(8,128)(2,1)S(1)}, bf16[256,256]{1,0:T(8,128)(2,1)S(1)}, u32[]{:S(2)}, u32[]{:S(2)}) collective-permute-start(bf16[256,256]{1,0:T(8,128)(2,1)S(1)} %get-tuple-element.99), channel_id=1, source_target_pairs={{0,16},{4,20},{8,24},{12,28},{16,0},{20,4},{24,8},{28,12},{1,17},{... | collective-permute-start | bytes 393224 | tf_op jit(solution)/shard_map/ppermute | solution.py:532
  105.1 11.7 %collective-permute-start.21 = (bf16[256,256]{1,0:T(8,128)(2,1)S(1)}, bf16[256,256]{1,0:T(8,128)(2,1)S(1)}, u32[]{:S(2)}, u32[]{:S(2)}) collective-permute-start(bf16[256,256]{1,0:T(8,128)(2,1)S(1)} %get-tuple-element.100), channel_id=1, source_target_pairs={{0,20},{4,16},{8,28},{12,24},{16,4},{20,0},{24,12},{28,8},{1,21},{... | collective-permute-start | bytes 393224 | tf_op jit(solution)/shard_map/ppermute | solution.py:532
  105.1 11.7 %collective-permute-start.22 = (bf16[256,256]{1,0:T(8,128)(2,1)S(1)}, bf16[256,256]{1,0:T(8,128)(2,1)S(1)}, u32[]{:S(2)}, u32[]{:S(2)}) collective-permute-start(bf16[256,256]{1,0:T(8,128)(2,1)S(1)} %get-tuple-element.101), channel_id=1, source_target_pairs={{0,24},{4,28},{8,16},{12,20},{16,8},{20,12},{24,0},{28,4},{1,25},{... | collective-permute-start | bytes 393224 | tf_op jit(solution)/shard_map/ppermute | solution.py:532
  108.0 8.8 %collective-permute-start.23 = (bf16[256,256]{1,0:T(8,128)(2,1)S(1)}, bf16[256,256]{1,0:T(8,128)(2,1)S(1)}, u32[]{:S(2)}, u32[]{:S(2)}) collective-permute-start(bf16[256,256]{1,0:T(8,128)(2,1)S(1)} %get-tuple-element.102), channel_id=1, source_target_pairs={{0,28},{4,24},{8,20},{12,16},{16,12},{20,8},{24,4},{28,0},{1,29},{... | collective-permute-start | bytes 393224 | tf_op jit(solution)/shard_map/ppermute | solution.py:532

commit v2 on v1

--- a/solution.py
+++ b/solution.py
@@ -40,15 +40,19 @@
     return [spec] * count
 
 
-def project_views(meta, latents, gain, w_qkv, which):
+def project_views(meta, latents, gain, w_qkv, w_out, which):
     _, tokens, width = latents.shape
     sub = w_qkv.shape[2]
     count = len(which)
     scale = HEAD_DIM ** (-0.5)
     order = (2, 0, 1)
 
-    def body(meta_ref, lat_hbm, gain_hbm, w_hbm, *refs):
-        outs, (halves, buffer, gains, ws, sems) = refs[: 2 * count], refs[2 * count :]
+    strip = sub // 2
+
+    def body(meta_ref, lat_hbm, gain_hbm, w_hbm, w_out_hbm, *refs):
+        outs, (halves, w_half, buffer, gains, ws, sems) = refs[: 2 * count], refs[2 * count :]
+        mine = pl.ds(pl.multiple_of((meta_ref[0] % 2) * strip, strip), strip)
+        w_copy = pltpu.make_async_copy(w_out_hbm.at[mine], w_half, sems.at[2 * count + 4])
         here = pl.ds(pl.multiple_of((meta_ref[1] // 2) * (width // 2), width // 2), width // 2)
         kept = [
             pltpu.make_async_copy(buffer.at[i, :, here], halves.at[i], sems.at[count + 4 + i])
@@ -63,16 +67,19 @@
             part: pltpu.make_async_copy(w_hbm.at[part], ws.at[part], sems.at[count + 1 + part])
             for part in order
         }
-        for copy in [copies[0], gain_copy] + [w_copies[p] for p in order] + copies[1:]:
+        for copy in copies[:2] + [gain_copy] + [w_copies[p] for p in order] + copies[2:] + [w_copy]:
             copy.start()
-        for i in range(count):
-            copies[i].wait()
-            kept[i].start()
-            if i == 0:
-                gain_copy.wait()
-            wide = buffer[i].astype(f32)
-            mean_square = jnp.mean(wide * wide, axis=-1, keepdims=True)
-            normed = (wide * lax.rsqrt(mean_square + epsilon) * gains[...]).astype(bf16)
+        for i in range(0, count, 2):
+            normed = []
+            for j in (i, i + 1):
+                copies[j].wait()
+                kept[j].start()
+                if j == 0:
+                    gain_copy.wait()
+                wide = buffer[j].astype(f32)
+                mean_square = jnp.mean(wide * wide, axis=-1, keepdims=True)
+                normed.append((wide * lax.rsqrt(mean_square + epsilon) * gains[...]).astype(bf16))
+            normed = jnp.concatenate(normed, axis=0)
             if i == 0:
                 w_copies[2].wait()
             values = dot(normed, ws[2])
@@ -81,9 +88,13 @@
             queries = dot(normed, ws[0])
             if i == 0:
                 w_copies[1].wait()
-            outs[2 * i + 1][0] = dot(normed, ws[1]).astype(bf16)
-            outs[2 * i + 1][1] = jnp.transpose(values).astype(bf16)
-            outs[2 * i][...] = jnp.transpose(queries).astype(bf16) * jnp.asarray(scale, bf16)
+            keys = dot(normed, ws[1]).astype(bf16)
+            for j in (i, i + 1):
+                at = slice((j - i) * tokens, (j - i + 1) * tokens)
+                outs[2 * j + 1][1] = jnp.transpose(values[at]).astype(bf16)
+                outs[2 * j][...] = jnp.transpose(queries[at]).astype(bf16) * jnp.asarray(scale, bf16)
+                outs[2 * j + 1][0] = keys[at]
+        w_copy.wait()
         for copy in kept:
             copy.wait()
 
@@ -94,24 +105,25 @@
             jax.ShapeDtypeStruct((2, tokens, sub), bf16),
         ]
     out_shape.append(jax.ShapeDtypeStruct((count, tokens, width // 2), bf16))
+    out_shape.append(jax.ShapeDtypeStruct((strip, w_out.shape[1]), bf16))
     outs = pl.pallas_call(
         body,
-        in_specs=[SMEM_SPEC] + many(ANY_SPEC, 3),
+        in_specs=[SMEM_SPEC] + many(ANY_SPEC, 4),
         out_specs=many(VMEM_SPEC, len(out_shape)),
         out_shape=out_shape,
         scratch_shapes=[
             pltpu.VMEM((count, tokens, width), bf16),
             pltpu.VMEM((1, width), f32),
             pltpu.VMEM((3, width, sub), bf16),
-            pltpu.SemaphoreType.DMA((2 * count + 4,)),
+            pltpu.SemaphoreType.DMA((2 * count + 5,)),
         ],
         name="project_views",
-        compiler_params=grant(50),
+        compiler_params=grant(52),
         cost_estimate=cost(
             count * 6 * tokens * width * sub, count * tokens * (width + 3 * sub) * 2 + 6 * width * sub
         ),
-    )(meta, latents, gain, w_qkv)
-    return {v: (outs[2 * i], outs[2 * i + 1]) for i, v in enumerate(which)}, outs[-1]
+    )(meta, latents, gain, w_qkv, w_out)
+    return {v: (outs[2 * i], outs[2 * i + 1]) for i, v in enumerate(which)}, outs[-2], outs[-1]
 
 
 ONES = 16
@@ -313,25 +325,31 @@
     lax.fori_loop(0, heads, one_head, 0)
 
 
-def partial_out(meta, attended, near, w_own, w_near, halves, place):
+def partial_out(meta, attended, near, w_own, w_mine, w_theirs, halves, place):
     tokens, sub = attended.shape
     width = w_own.shape[1]
     half = width // 2
 
-    def body(meta_ref, att, near_ref, own_ref, near_w_ref, halves_ref, keep, send):
+    def body(meta_ref, att, near_ref, own_ref, mine_ref, theirs_ref, halves_ref, keep, send):
         side = meta_ref[1] // 2
         here = pl.ds(pl.multiple_of(side * half, half), half)
         away = pl.ds(pl.multiple_of((1 - side) * half, half), half)
-        rows = jnp.concatenate([att[...], near_ref[...]], axis=1)
-        send[...] = dot(
-            rows, jnp.concatenate([own_ref[:, away], near_w_ref[:, away]], axis=0)
-        ).astype(bf16)
-        total = dot(rows, jnp.concatenate([own_ref[:, here], near_w_ref[:, here]], axis=0))
+        second = meta_ref[0] % 2
+        strip = sub // 2
+        mine = near_ref[:, pl.ds(pl.multiple_of(second * strip, strip), strip)]
+        theirs = near_ref[:, pl.ds(pl.multiple_of((1 - second) * strip, strip), strip)]
+        rows = jnp.concatenate([att[...], mine, theirs], axis=1)
+
+        def columns(at):
+            return jnp.concatenate([own_ref[:, at], mine_ref[:, at], theirs_ref[:, at]], axis=0)
+
+        send[...] = dot(rows, columns(away)).astype(bf16)
+        total = dot(rows, columns(here))
         keep[...] = halves_ref[place].astype(f32) + total
 
     return pl.pallas_call(
         body,
-        in_specs=[SMEM_SPEC] + many(VMEM_SPEC, 5),
+        in_specs=[SMEM_SPEC] + many(VMEM_SPEC, 6),
         out_specs=many(VMEM_SPEC, 2),
         out_shape=[
             jax.ShapeDtypeStruct((tokens, half), f32),
@@ -340,7 +358,7 @@
         name="partial_out",
         compiler_params=grant(12),
         cost_estimate=cost(4 * tokens * sub * width, 4 * sub * width + tokens * width * 6),
-    )(meta, attended, near, w_own, w_near, halves)
+    )(meta, attended, near, w_own, w_mine, w_theirs, halves)
 
 
 def merge_out(meta, keep, got):
@@ -418,7 +436,7 @@
 
 
 def gather_rows(meta, wanted, pieces):
-    peers, capacity = wanted.shape
+    peers, capacity = int(round(wanted.shape[0] ** 0.5)), wanted.shape[1]
     tokens, sub = pieces[0][0].shape
     local_views = len(pieces)
     rows = local_views * tokens
@@ -432,7 +450,7 @@
             layer[v * tokens : (v + 1) * tokens, :] = jnp.where(
                 end, ins[2 * v + 1][...], ins[2 * v][...]
             )
-        lines = [wanted_ref[pl.ds(lax.bitwise_xor(meta_ref[0], m), 1), :] for m in range(peers)]
+        lines = [wanted_ref[pl.ds(m * peers + meta_ref[0], 1), :] for m in range(peers)]
         columns = jnp.transpose(jnp.concatenate(lines, axis=0).astype(f32))
         for mask in range(peers):
             column = columns[:, mask : mask + 1]
@@ -541,12 +559,12 @@
     gain = norm_gain.reshape(1, width)
     inter = intersection.T
     loaded = (0, local_views - 1, 1, 2)
-    projected, halves = project_views(meta, latents, gain, w_qkv, loaded)
+    projected, halves, w_half = project_views(meta, latents, gain, w_qkv, w_out, loaded)
     queries = {v: projected[v][0] for v in range(local_views)}
     blocks = {v: projected[v][1] for v in range(local_views)}
     next_first = along(blocks[0], -1)
     prev_last = along(blocks[3], 1)
-    w_near = across(after(w_out, queries[1]), beside)
+    w_mine = across(w_half, beside)
 
     inner_plan = [(1, [("prev_last", -1, 1)]), (2, [("next_first", 2, 1)])]
     inner_queries = [queries[1], queries[2]]
@@ -567,23 +585,25 @@
     outer_queries = [after(queries[0], inner[0]), queries[3]]
     outer = attend(meta, inter, outer_queries, blocks, remote, outer_plan, window)
     attended = {1: inner[0], 2: inner[1], 0: outer[0], 3: outer[1]}
+    w_theirs = partner(after(w_mine, inner[0]), 1)
+    keep, got, formed = {}, {}, {}
+    for v in VIEW_ORDER:
+        near = across(attended[v], beside)
+        keep[v], send = partial_out(
+            meta, attended[v], near, w_out, w_mine, w_theirs, halves, loaded.index(v)
+        )
+        got[v] = across(send, middle)
     strips = rows // LANES
     wanted, code = prepare_requests(
-        after(match_block.reshape(strips, LANES), outer[0]),
+        after(match_block.reshape(strips, LANES), send),
         match_row.reshape(strips, LANES),
         peers,
         capacity,
     )
-    keep, got, formed = {}, {}, {}
-    for n, v in enumerate(VIEW_ORDER):
-        near = across(attended[v], beside)
-        if n == 2:
-            wanted = lax.all_to_all(
-                after(wanted, send), "views", split_axis=0, concat_axis=0, tiled=True
-            )
-            near = after(near, wanted)
-        keep[v], send = partial_out(meta, attended[v], near, w_out, w_near, halves, loaded.index(v))
-        got[v] = across(send, middle)
+    mask = 1
+    while mask < peers:
+        wanted = jnp.concatenate([wanted, partner(wanted, mask)], axis=0)
+        mask *= 2
     for v in VIEW_ORDER:
         own, other = merge_out(meta, keep[v], got[v])
         formed[v] = (own, across(other, back))

time: 121 us -> 120 us (level)
  waiting for transfers between devices: 21.4 us -> 30.3 us
  local copies, waits for them, and re-layouts: 4.58 us -> 0.72 us
  starting transfers between devices: 64.6 us -> 61.1 us
  Pallas kernels: 28.8 us -> 26.9 us
    all_to_all x1 -> x0, starting transfers between devices: 31.6 us -> none  [per_device(): lax.all_to_all(after(wanted, send), 'views', split_axis=0, concat_axis=0,...]
    ppermute x7 -> x11, starting transfers between devices: 7.38 us -> 34.8 us  [partner(): return lax.ppermute(x, 'views', [(i, i ^ mask) for i in range(peers)])]
    ppermute x4, waiting for transfers between devices: 1.53 us -> 5.05 us  [along(): lax.ppermute(x, 'views', [(i, (i + by) % peers) for i in range(peers)])]
    unnamed x25 -> x14, local copies, waits for them, and re-layouts: 3.98 us -> 0.72 us
    ppermute x13, waiting for transfers between devices: 11.9 us -> 14.9 us  [across(): return lax.ppermute(x, 'heads', pairs)]
    ppermute x7 -> x11, waiting for transfers between devices: 7.9 us -> 10.3 us  [partner(): return lax.ppermute(x, 'views', [(i, i ^ mask) for i in range(peers)])]
  transfers between devices with their start and end apart: 25 -> 28, of which waited for: 8 -> 10; matrix products, arithmetic and copies ran while one was open for 1% -> 0% of each run, Pallas kernels for 15% -> 13%
where the time goes in v2:
time: 120 us
  starting transfers between devices  61.1 us (51%)
  waiting for transfers between devices  30.3 us (25%)
  Pallas kernels  26.9 us (22%)
    ppermute x11, starting transfers between devices, partner(): return lax.ppermute(x, 'views', [(i, i ^ mask) for i in range(peers)])  34.8 us
    ppermute x13, starting transfers between devices, across(): return lax.ppermute(x, 'heads', pairs)  20.4 us
    ppermute x13, waiting for transfers between devices, across(): return lax.ppermute(x, 'heads', pairs)  14.9 us
    ppermute x11, waiting for transfers between devices, partner(): return lax.ppermute(x, 'views', [(i, i ^ mask) for i in range(peers)])  10.3 us
    pallas_call x3, Pallas kernels, attend(): pl.pallas_call(body, in_specs=[SMEM_SPEC, SMEM_SPEC] + many(VMEM_SPEC, he...  8.17 us
    pallas_call x1, Pallas kernels, project_views(): pl.pallas_call(body, in_specs=[SMEM_SPEC] + many(ANY_SPEC, 4), out_specs=...  6.79 us
    ppermute x4, starting transfers between devices, along(): lax.ppermute(x, 'views', [(i, (i + by) % peers) for i in range(peers)])  5.85 us
    ppermute x4, waiting for transfers between devices, along(): lax.ppermute(x, 'views', [(i, (i + by) % peers) for i in range(peers)])  5.05 us
  transfers between devices with their start and end apart: 28, of which 10 were waited for; matrix products, arithmetic and copies ran while one was open for 0% of the time, Pallas kernels for 13%

profile of v2, /device:TPU:0, one launch (start us, length us, event | category | flops | bytes accessed | tf_op | source)
XLA Modules:
  0.0 119.6 jit_solution(12802069091104291132)
XLA Ops:
  0.0 0.7 copy-done.3
  0.7 6.8 %project_views.1 = (bf16[256,256]{1,0:T(8,128)(2,1)S(1)}, bf16[2,256,256]{2,1,0:T(8,128)(2,1)S(1)}, bf16[256,256]{1,0:T(8,128)(2,1)S(1)}, bf16[2,256,256]{2,1,0:...) custom-call(s32[4]{0:T(128)S(1)} %compare_select_fusion.1.meta_ref, ...), custom_call_target="tpu_custom_call" | custom-call | flops 1610612736 | bytes 5242880 | tf_op jit(solution)/shard_map/project_views/pallas_call | solution.py:109
  7.5 3.4 %collective-permute-start = (bf16[2,256,256]{2,1,0:T(8,128)(2,1)S(1)}, bf16[2,256,256]{2,1,0:T(8,128)(2,1)S(1)}, u32[]{:S(2)}, u32[]{:S(2)}) collective-permute-start(bf16[2,256,256]{2,1,0:T(8,128)(2,1)S(1)} %get-tuple-element.56.refs_2_.refs_4_), channel_id=1, source_target_pairs={{0,28},{4,0},{8,4},{12,8},{16,12},{20,16},{24,20},{28,24},{1,29},{... | collective-permute-start | bytes 786440 | tf_op jit(solution)/shard_map/ppermute | solution.py:547
  10.9 3.5 %collective-permute-start.5 = (bf16[128,1024]{1,0:T(8,128)(2,1)S(1)}, bf16[128,1024]{1,0:T(8,128)(2,1)S(1)}, u32[]{:S(2)}, u32[]{:S(2)}) collective-permute-start(bf16[128,1024]{1,0:T(8,128)(2,1)S(1)} %get-tuple-element.68), channel_id=1, source_target_pairs={{0,1},{3,2},{4,5},{7,6},{8,9},{11,10},{12,13},{15,14},{16,17},{19,... | collective-permute-start | bytes 786440 | tf_op jit(solution)/shard_map/ppermute | solution.py:553
  14.4 2.9 %attend_local.1 = (f32[2,320,256]{2,1,0:T(8,128)S(1)}, f32[2,4,256]{2,1,0:T(4,128)S(1)}) custom-call(s32[4]{0:T(128)S(1)} %compare_select_fusion.1.meta_ref, s32[2,32]{1,0:T(2,128)S(1)} %bitcast.6, bf16[256,256]{1,0:T(8,128)(2,1)S(1)} %get-tuple-element.54.refs_0_.refs_2_, bf16[256,256]{1,0:T(8,128)(2,1)S(1)} %get-tuple-element.55.refs_1_.refs_3_, ...), custom_call_target="tpu_custom_call" | custom-call | flops 1073741824 | bytes 4194304 | tf_op jit(solution)/shard_map/attend_local/pallas_call | solution.py:278
  17.4 2.4 %collective-permute-start.2 = (bf16[2,256,256]{2,1,0:T(8,128)(2,1)S(1)}, bf16[2,256,256]{2,1,0:T(8,128)(2,1)S(1)}, u32[]{:S(2)}, u32[]{:S(2)}) collective-permute-start(bf16[2,256,256]{2,1,0:T(8,128)(2,1)S(1)} %get-tuple-element.65.refs_3_.refs_5_), channel_id=1, source_target_pairs={{0,28},{4,0},{8,4},{12,8},{16,12},{20,16},{24,20},{28,24},{1,29},{... | collective-permute-start | bytes 786440 | tf_op jit(solution)/shard_map/ppermute | solution.py:547
  19.8 1.7 %attend.2 = (bf16[256,256]{1,0:T(8,128)(2,1)S(1)}, bf16[256,256]{1,0:T(8,128)(2,1)S(1)}) custom-call(s32[4]{0:T(128)S(1)} %compare_select_fusion.1.meta_ref, s32[2,32]{1,0:T(2,128)S(1)} %bitcast.7, f32[2,320,256]{2,1,0:T(8,128)S(1)} %get-tuple-element.60.refs_0_, f32[2,4,256]{2,1,0:T(4,128)S(1)} %get-tuple-element.61.refs_1_, ...), custom_call_target="tpu_custom_call" | custom-call | flops 268435456 | bytes 1048576 | tf_op jit(solution)/shard_map/attend/pallas_call | solution.py:278
  21.6 3.1 %collective-permute-done.2.refs_7_ = bf16[2,256,256]{2,1,0:T(8,128)(2,1)S(1)} collective-permute-done((bf16[2,256,256]{2,1,0:T(8,128)(2,1)S(1)}, bf16[2,256,256]{2,1,0:T(8,128)(2,1)S(1)}, u32[]{:S(2)}, u32[]{:S(2)}) %collective-permute-start.2) | collective-permute-done | bytes 262176 | tf_op jit(solution)/shard_map/ppermute | solution.py:547
  24.7 2.0 %collective-permute-done.3.refs_9_ = bf16[2,256,256]{2,1,0:T(8,128)(2,1)S(1)} collective-permute-done((bf16[2,256,256]{2,1,0:T(8,128)(2,1)S(1)}, bf16[2,256,256]{2,1,0:T(8,128)(2,1)S(1)}, u32[]{:S(2)}, u32[]{:S(2)}) %collective-permute-start.3) | collective-permute-done | bytes 262176 | tf_op jit(solution)/shard_map/ppermute | solution.py:547
  26.7 3.5 %attend.3 = (bf16[256,256]{1,0:T(8,128)(2,1)S(1)}, bf16[256,256]{1,0:T(8,128)(2,1)S(1)}) custom-call(s32[4]{0:T(128)S(1)} %compare_select_fusion.1.meta_ref, s32[2,32]{1,0:T(2,128)S(1)} %bitcast.8, bf16[256,256]{1,0:T(8,128)(2,1)S(1)} %get-tuple-element.63.refs_0_, bf16[256,256]{1,0:T(8,128)(2,1)S(1)} %get-tuple-element.64.refs_1_, ...), custom_call_target="tpu_custom_call" | custom-call | flops 1342177280 | bytes 5242880 | tf_op jit(solution)/shard_map/attend/pallas_call | solution.py:278
  30.2 5.2 %collective-permute-start.4 = (bf16[256,256]{1,0:T(8,128)(2,1)S(1)}, bf16[256,256]{1,0:T(8,128)(2,1)S(1)}, u32[]{:S(2)}, u32[]{:S(2)}) collective-permute-start(bf16[256,256]{1,0:T(8,128)(2,1)S(1)} %get-tuple-element.67.att), channel_id=1, source_target_pairs={{0,1},{3,2},{4,5},{7,6},{8,9},{11,10},{12,13},{15,14},{16,17},{19,... | collective-permute-start | bytes 393224 | tf_op jit(solution)/shard_map/ppermute | solution.py:553
  35.4 1.3 %collective-permute-start.10 = (bf16[256,256]{1,0:T(8,128)(2,1)S(1)}, bf16[256,256]{1,0:T(8,128)(2,1)S(1)}, u32[]{:S(2)}, u32[]{:S(2)}) collective-permute-start(bf16[256,256]{1,0:T(8,128)(2,1)S(1)} %get-tuple-element.75.att), channel_id=1, source_target_pairs={{0,1},{3,2},{4,5},{7,6},{8,9},{11,10},{12,13},{15,14},{16,17},{19,... | collective-permute-start | bytes 393224 | tf_op jit(solution)/shard_map/ppermute | solution.py:553
  36.7 1.3 %collective-permute-start.13 = (bf16[256,256]{1,0:T(8,128)(2,1)S(1)}, bf16[256,256]{1,0:T(8,128)(2,1)S(1)}, u32[]{:S(2)}, u32[]{:S(2)}) collective-permute-start(bf16[256,256]{1,0:T(8,128)(2,1)S(1)} %get-tuple-element.62.att), channel_id=1, source_target_pairs={{0,1},{3,2},{4,5},{7,6},{8,9},{11,10},{12,13},{15,14},{16,17},{19,... | collective-permute-start | bytes 393224 | tf_op jit(solution)/shard_map/ppermute | solution.py:553
  38.0 1.3 %collective-permute-start.16 = (bf16[256,256]{1,0:T(8,128)(2,1)S(1)}, bf16[256,256]{1,0:T(8,128)(2,1)S(1)}, u32[]{:S(2)}, u32[]{:S(2)}) collective-permute-start(bf16[256,256]{1,0:T(8,128)(2,1)S(1)} %get-tuple-element.84.att), channel_id=1, source_target_pairs={{0,1},{3,2},{4,5},{7,6},{8,9},{11,10},{12,13},{15,14},{16,17},{19,... | collective-permute-start | bytes 393224 | tf_op jit(solution)/shard_map/ppermute | solution.py:553
  39.3 1.0 partial_out.4
  40.3 0.7 prepare_requests.1
  41.0 11.1 %collective-permute-start.7 = (s32[8,256]{1,0:T(8,128)S(1)}, s32[8,256]{1,0:T(8,128)S(1)}, u32[]{:S(2)}, u32[]{:S(2)}) collective-permute-start(s32[8,256]{1,0:T(8,128)S(1)} %get-tuple-element.74), channel_id=1, source_target_pairs={{0,4},{4,0},{8,12},{12,8},{16,20},{20,16},{24,28},{28,24},{1,5},{5... | collective-permute-start | bytes 24584 | tf_op jit(solution)/shard_map/ppermute | solution.py:550
  52.1 1.0 partial_out.5
  53.1 0.7 collective-permute-start.11
  53.8 1.0 partial_out.6
  54.8 0.7 collective-permute-start.14
  55.5 1.0 partial_out.7
  56.5 0.7 collective-permute-start.17
  57.2 0.7 collective-permute-start.19
  57.9 0.8 collective-permute-start.8
  58.8 3.0 %collective-permute-done.8 = s32[16,256]{1,0:T(8,128)S(1)} collective-permute-done((s32[16,256]{1,0:T(8,128)S(1)}, s32[16,256]{1,0:T(8,128)S(1)}, u32[]{:S(2)}, u32[]{:S(2)}) %collective-permute-start.8) | collective-permute-done | bytes 16416 | tf_op jit(solution)/shard_map/ppermute | solution.py:550
  61.7 13.5 %collective-permute-start.9 = (s32[32,256]{1,0:T(8,128)S(1)}, s32[32,256]{1,0:T(8,128)S(1)}, u32[]{:S(2)}, u32[]{:S(2)}) collective-permute-start(s32[32,256]{1,0:T(8,128)S(1)} %pad_add_fusion.1), channel_id=1, source_target_pairs={{0,16},{4,20},{8,24},{12,28},{16,0},{20,4},{24,8},{28,12},{1,17},{... | collective-permute-start | bytes 98312 | tf_op jit(solution)/shard_map/ppermute | solution.py:550
  75.2 0.6 merge_out.4
  75.9 1.3 %collective-permute-start.12 = (bf16[256,256]{1,0:T(8,128)(2,1)S(1)}, bf16[256,256]{1,0:T(8,128)(2,1)S(1)}, u32[]{:S(2)}, u32[]{:S(2)}) collective-permute-start(bf16[256,256]{1,0:T(8,128)(2,1)S(1)} %get-tuple-element.79), channel_id=1, source_target_pairs={{1,0},{2,3},{5,4},{6,7},{9,8},{10,11},{13,12},{14,15},{17,16},{18,... | collective-permute-start | bytes 393224 | tf_op jit(solution)/shard_map/ppermute | solution.py:553
  77.2 0.6 merge_out.5
  77.8 1.3 %collective-permute-start.15 = (bf16[256,256]{1,0:T(8,128)(2,1)S(1)}, bf16[256,256]{1,0:T(8,128)(2,1)S(1)}, u32[]{:S(2)}, u32[]{:S(2)}) collective-permute-start(bf16[256,256]{1,0:T(8,128)(2,1)S(1)} %get-tuple-element.83), channel_id=1, source_target_pairs={{1,0},{2,3},{5,4},{6,7},{9,8},{10,11},{13,12},{14,15},{17,16},{18,... | collective-permute-start | bytes 393224 | tf_op jit(solution)/shard_map/ppermute | solution.py:553
  79.1 0.6 merge_out.6
  79.7 1.3 %collective-permute-start.18 = (bf16[256,256]{1,0:T(8,128)(2,1)S(1)}, bf16[256,256]{1,0:T(8,128)(2,1)S(1)}, u32[]{:S(2)}, u32[]{:S(2)}) collective-permute-start(bf16[256,256]{1,0:T(8,128)(2,1)S(1)} %get-tuple-element.88), channel_id=1, source_target_pairs={{1,0},{2,3},{5,4},{6,7},{9,8},{10,11},{13,12},{14,15},{17,16},{18,... | collective-permute-start | bytes 393224 | tf_op jit(solution)/shard_map/ppermute | solution.py:553
  81.0 0.6 merge_out.7
  81.6 1.3 %collective-permute-start.20 = (bf16[256,256]{1,0:T(8,128)(2,1)S(1)}, bf16[256,256]{1,0:T(8,128)(2,1)S(1)}, u32[]{:S(2)}, u32[]{:S(2)}) collective-permute-start(bf16[256,256]{1,0:T(8,128)(2,1)S(1)} %get-tuple-element.91), channel_id=1, source_target_pairs={{1,0},{2,3},{5,4},{6,7},{9,8},{10,11},{13,12},{14,15},{17,16},{18,... | collective-permute-start | bytes 393224 | tf_op jit(solution)/shard_map/ppermute | solution.py:553
  83.0 7.5 %collective-permute-done.12.refs_1_ = bf16[256,256]{1,0:T(8,128)(2,1)S(1)} collective-permute-done((bf16[256,256]{1,0:T(8,128)(2,1)S(1)}, bf16[256,256]{1,0:T(8,128)(2,1)S(1)}, u32[]{:S(2)}, u32[]{:S(2)}) %collective-permute-start.12) | collective-permute-done | bytes 131104 | tf_op jit(solution)/shard_map/ppermute | solution.py:553
  90.5 2.8 %collective-permute-done.15.refs_3_ = bf16[256,256]{1,0:T(8,128)(2,1)S(1)} collective-permute-done((bf16[256,256]{1,0:T(8,128)(2,1)S(1)}, bf16[256,256]{1,0:T(8,128)(2,1)S(1)}, u32[]{:S(2)}, u32[]{:S(2)}) %collective-permute-start.15) | collective-permute-done | bytes 131104 | tf_op jit(solution)/shard_map/ppermute | solution.py:553
  93.3 2.8 %collective-permute-done.18.refs_5_ = bf16[256,256]{1,0:T(8,128)(2,1)S(1)} collective-permute-done((bf16[256,256]{1,0:T(8,128)(2,1)S(1)}, bf16[256,256]{1,0:T(8,128)(2,1)S(1)}, u32[]{:S(2)}, u32[]{:S(2)}) %collective-permute-start.18) | collective-permute-done | bytes 131104 | tf_op jit(solution)/shard_map/ppermute | solution.py:553
  96.1 1.7 %collective-permute-done.20.refs_7_ = bf16[256,256]{1,0:T(8,128)(2,1)S(1)} collective-permute-done((bf16[256,256]{1,0:T(8,128)(2,1)S(1)}, bf16[256,256]{1,0:T(8,128)(2,1)S(1)}, u32[]{:S(2)}, u32[]{:S(2)}) %collective-permute-start.20) | collective-permute-done | bytes 131104 | tf_op jit(solution)/shard_map/ppermute | solution.py:553
  97.9 2.1 %gather_rows.1 = (bf16[1024,256]{1,0:T(8,128)(2,1)S(1)}, bf16[256,256]{1,0:T(8,128)(2,1)S(1)}, bf16[256,256]{1,0:T(8,128)(2,1)S(1)}, bf16[256,256]{1,0:T(8,128)(...) custom-call(s32[4]{0:T(128)S(1)} %compare_select_fusion.1.meta_ref, ...), custom_call_target="tpu_custom_call" | custom-call | flops 1073741824 | bytes 3145728 | tf_op jit(solution)/shard_map/gather_rows/pallas_call | solution.py:462
  100.0 2.1 %collective-permute-start.22 = (bf16[256,256]{1,0:T(8,128)(2,1)S(1)}, bf16[256,256]{1,0:T(8,128)(2,1)S(1)}, u32[]{:S(2)}, u32[]{:S(2)}) collective-permute-start(bf16[256,256]{1,0:T(8,128)(2,1)S(1)} %get-tuple-element.95), channel_id=1, source_target_pairs={{0,8},{4,12},{8,0},{12,4},{16,24},{20,28},{24,16},{28,20},{1,9},{5... | collective-permute-start | bytes 393224 | tf_op jit(solution)/shard_map/ppermute | solution.py:550
  102.1 2.7 %collective-permute-start.24 = (bf16[256,256]{1,0:T(8,128)(2,1)S(1)}, bf16[256,256]{1,0:T(8,128)(2,1)S(1)}, u32[]{:S(2)}, u32[]{:S(2)}) collective-permute-start(bf16[256,256]{1,0:T(8,128)(2,1)S(1)} %get-tuple-element.97), channel_id=1, source_target_pairs={{0,16},{4,20},{8,24},{12,28},{16,0},{20,4},{24,8},{28,12},{1,17},{... | collective-permute-start | bytes 393224 | tf_op jit(solution)/shard_map/ppermute | solution.py:550
  104.8 2.9 %collective-permute-start.26 = (bf16[256,256]{1,0:T(8,128)(2,1)S(1)}, bf16[256,256]{1,0:T(8,128)(2,1)S(1)}, u32[]{:S(2)}, u32[]{:S(2)}) collective-permute-start(bf16[256,256]{1,0:T(8,128)(2,1)S(1)} %get-tuple-element.99), channel_id=1, source_target_pairs={{0,24},{4,28},{8,16},{12,20},{16,8},{20,12},{24,0},{28,4},{1,25},{... | collective-permute-start | bytes 393224 | tf_op jit(solution)/shard_map/ppermute | solution.py:550
  107.7 1.5 %collective-permute-start.27 = (bf16[256,256]{1,0:T(8,128)(2,1)S(1)}, bf16[256,256]{1,0:T(8,128)(2,1)S(1)}, u32[]{:S(2)}, u32[]{:S(2)}) collective-permute-start(bf16[256,256]{1,0:T(8,128)(2,1)S(1)} %get-tuple-element.100), channel_id=1, source_target_pairs={{0,28},{4,24},{8,20},{12,16},{16,12},{20,8},{24,4},{28,0},{1,29},{... | collective-permute-start | bytes 393224 | tf_op jit(solution)/shard_map/ppermute | solution.py:550
  109.2 5.0 %collective-permute-done.24.refs_4_ = bf16[256,256]{1,0:T(8,128)(2,1)S(1)} collective-permute-done((bf16[256,256]{1,0:T(8,128)(2,1)S(1)}, bf16[256,256]{1,0:T(8,128)(2,1)S(1)}, u32[]{:S(2)}, u32[]{:S(2)}) %collective-permute-start.24) | collective-permute-done | bytes 131104 | tf_op jit(solution)/shard_map/ppermute | solution.py:550
  114.2 2.1 %collective-permute-done.25.refs_5_ = bf16[256,256]{1,0:T(8,128)(2,1)S(1)} collective-permute-done((bf16[256,256]{1,0:T(8,128)(2,1)S(1)}, bf16[256,256]{1,0:T(8,128)(2,1)S(1)}, u32[]{:S(2)}, u32[]{:S(2)}) %collective-permute-start.25) | collective-permute-done | bytes 131104 | tf_op jit(solution)/shard_map/ppermute | solution.py:550
  116.3 0.2 collective-permute-done.27.refs_7_
  116.5 2.9 %finish_rows.1 = f32[1024,256]{1,0:T(8,128)} custom-call(s32[4]{0:T(128)S(1)} %compare_select_fusion.1.meta_ref, s32[8,128]{1,0:T(8,128)S(1)} %get-tuple-element.73.code_ref, f32[8,128]{1,0:T(8,128)S(1)} %bitcast.12, bf16[1024,256]{1,0:T(8,128)(2,1)S(1)} %get-tuple-element.92.layer_ref, bf16[256,256]{1,0:T(8,128)(2,1)S(1)} %get-tuple-element.93.refs_0_, ...), custom_call_target="tpu_custom_call" | custom-call | flops 1073741824 | bytes 2621440 | tf_op jit(solution)/shard_map/finish_rows/pallas_call | solution.py:518
  (41 shorter events, 0.3 us)
Async XLA Ops:
  0.0 0.7 copy-start.3
  0.7 13.7 %copy-start.2 = (s32[32,2]{0,1:T(2,128)S(1)}, s32[32,2]{0,1:T(2,128)}, u32[]{:S(2)}) copy-start(s32[32,2]{0,1:T(2,128)} %param.12) | copy-start | bytes 772
  7.5 12.3 %collective-permute-start = (bf16[2,256,256]{2,1,0:T(8,128)(2,1)S(1)}, bf16[2,256,256]{2,1,0:T(8,128)(2,1)S(1)}, u32[]{:S(2)}, u32[]{:S(2)}) collective-permute-start(bf16[2,256,256]{2,1,0:T(8,128)(2,1)S(1)} %get-tuple-element.56.refs_2_.refs_4_), channel_id=1, source_target_pairs={{0,28},{4,0},{8,4},{12,8},{16,12},{20,16},{24,20},{28,24},{1,29},{... | collective-permute-start | bytes 786440 | tf_op jit(solution)/shard_map/ppermute | solution.py:547
  10.9 8.9 %collective-permute-start.1 = (bf16[2,256,256]{2,1,0:T(8,128)(2,1)S(1)}, bf16[2,256,256]{2,1,0:T(8,128)(2,1)S(1)}, u32[]{:S(2)}, u32[]{:S(2)}) collective-permute-start(bf16[2,256,256]{2,1,0:T(8,128)(2,1)S(1)} %get-tuple-element.59.refs_5_.refs_7_), channel_id=1, source_target_pairs={{0,4},{4,8},{8,12},{12,16},{16,20},{20,24},{24,28},{28,0},{1,5},{5... | collective-permute-start | bytes 786440 | tf_op jit(solution)/shard_map/ppermute | solution.py:547
  10.9 10.6 %collective-permute-start.5 = (bf16[128,1024]{1,0:T(8,128)(2,1)S(1)}, bf16[128,1024]{1,0:T(8,128)(2,1)S(1)}, u32[]{:S(2)}, u32[]{:S(2)}) collective-permute-start(bf16[128,1024]{1,0:T(8,128)(2,1)S(1)} %get-tuple-element.68), channel_id=1, source_target_pairs={{0,1},{3,2},{4,5},{7,6},{8,9},{11,10},{12,13},{15,14},{16,17},{19,... | collective-permute-start | bytes 786440 | tf_op jit(solution)/shard_map/ppermute | solution.py:553
  17.4 7.3 %collective-permute-start.2 = (bf16[2,256,256]{2,1,0:T(8,128)(2,1)S(1)}, bf16[2,256,256]{2,1,0:T(8,128)(2,1)S(1)}, u32[]{:S(2)}, u32[]{:S(2)}) collective-permute-start(bf16[2,256,256]{2,1,0:T(8,128)(2,1)S(1)} %get-tuple-element.65.refs_3_.refs_5_), channel_id=1, source_target_pairs={{0,28},{4,0},{8,4},{12,8},{16,12},{20,16},{24,20},{28,24},{1,29},{... | collective-permute-start | bytes 786440 | tf_op jit(solution)/shard_map/ppermute | solution.py:547
  19.8 6.9 %collective-permute-start.3 = (bf16[2,256,256]{2,1,0:T(8,128)(2,1)S(1)}, bf16[2,256,256]{2,1,0:T(8,128)(2,1)S(1)}, u32[]{:S(2)}, u32[]{:S(2)}) collective-permute-start(bf16[2,256,256]{2,1,0:T(8,128)(2,1)S(1)} %get-tuple-element.66.refs_4_.refs_6_), channel_id=1, source_target_pairs={{0,4},{4,8},{8,12},{12,16},{16,20},{20,24},{24,28},{28,0},{1,5},{5... | collective-permute-start | bytes 786440 | tf_op jit(solution)/shard_map/ppermute | solution.py:547
  21.5 17.8 %collective-permute-start.6 = (bf16[128,1024]{1,0:T(8,128)(2,1)S(1)}, bf16[128,1024]{1,0:T(8,128)(2,1)S(1)}, u32[]{:S(2)}, u32[]{:S(2)}) collective-permute-start(bf16[128,1024]{1,0:T(8,128)(2,1)S(1)} %collective-permute-done.5.mine_ref), channel_id=1, source_target_pairs={{0,4},{4,0},{8,12},{12,8},{16,20},{20,16},{24,28},{28,24},{1,5},{5... | collective-permute-start | bytes 786440 | tf_op jit(solution)/shard_map/ppermute | solution.py:550
  26.7 12.6 %copy-start = (bf16[4,256,512]{2,1,0:T(8,128)(2,1)S(1)}, bf16[4,256,512]{2,1,0:T(8,128)(2,1)}, u32[]{:S(2)}) copy-start(bf16[4,256,512]{2,1,0:T(8,128)(2,1)} %get-tuple-element.70.halves_ref) | copy-start | bytes 3145732
  26.7 12.7 %copy-start.1 = (bf16[256,1024]{1,0:T(8,128)(2,1)S(1)}, bf16[256,1024]{1,0:T(8,128)(2,1)}, u32[]{:S(2)}) copy-start(bf16[256,1024]{1,0:T(8,128)(2,1)} %own_ref.7) | copy-start | bytes 1572868
  30.2 10.1 %copy-start.4 = (s32[1024,1]{0,1:T(1,128)S(1)}, s32[1024,1]{0,1:T(1,128)}, u32[]{:S(2)}) copy-start(s32[1024,1]{0,1:T(1,128)} %param.13) | copy-start | bytes 12292
  30.2 10.1 %copy-start.5 = (s32[1024]{0:T(1024)S(1)}, s32[1024]{0:T(1024)}, u32[]{:S(2)}) copy-start(s32[1024]{0:T(1024)} %param.14) | copy-start | bytes 12292
  30.2 9.1 %collective-permute-start.4 = (bf16[256,256]{1,0:T(8,128)(2,1)S(1)}, bf16[256,256]{1,0:T(8,128)(2,1)S(1)}, u32[]{:S(2)}, u32[]{:S(2)}) collective-permute-start(bf16[256,256]{1,0:T(8,128)(2,1)S(1)} %get-tuple-element.67.att), channel_id=1, source_target_pairs={{0,1},{3,2},{4,5},{7,6},{8,9},{11,10},{12,13},{15,14},{16,17},{19,... | collective-permute-start | bytes 393224 | tf_op jit(solution)/shard_map/ppermute | solution.py:553
  35.4 16.8 %collective-permute-start.10 = (bf16[256,256]{1,0:T(8,128)(2,1)S(1)}, bf16[256,256]{1,0:T(8,128)(2,1)S(1)}, u32[]{:S(2)}, u32[]{:S(2)}) collective-permute-start(bf16[256,256]{1,0:T(8,128)(2,1)S(1)} %get-tuple-element.75.att), channel_id=1, source_target_pairs={{0,1},{3,2},{4,5},{7,6},{8,9},{11,10},{12,13},{15,14},{16,17},{19,... | collective-permute-start | bytes 393224 | tf_op jit(solution)/shard_map/ppermute | solution.py:553
  36.7 17.1 %collective-permute-start.13 = (bf16[256,256]{1,0:T(8,128)(2,1)S(1)}, bf16[256,256]{1,0:T(8,128)(2,1)S(1)}, u32[]{:S(2)}, u32[]{:S(2)}) collective-permute-start(bf16[256,256]{1,0:T(8,128)(2,1)S(1)} %get-tuple-element.62.att), channel_id=1, source_target_pairs={{0,1},{3,2},{4,5},{7,6},{8,9},{11,10},{12,13},{15,14},{16,17},{19,... | collective-permute-start | bytes 393224 | tf_op jit(solution)/shard_map/ppermute | solution.py:553
  38.0 17.5 %collective-permute-start.16 = (bf16[256,256]{1,0:T(8,128)(2,1)S(1)}, bf16[256,256]{1,0:T(8,128)(2,1)S(1)}, u32[]{:S(2)}, u32[]{:S(2)}) collective-permute-start(bf16[256,256]{1,0:T(8,128)(2,1)S(1)} %get-tuple-element.84.att), channel_id=1, source_target_pairs={{0,1},{3,2},{4,5},{7,6},{8,9},{11,10},{12,13},{15,14},{16,17},{19,... | collective-permute-start | bytes 393224 | tf_op jit(solution)/shard_map/ppermute | solution.py:553
  41.0 16.8 %collective-permute-start.7 = (s32[8,256]{1,0:T(8,128)S(1)}, s32[8,256]{1,0:T(8,128)S(1)}, u32[]{:S(2)}, u32[]{:S(2)}) collective-permute-start(s32[8,256]{1,0:T(8,128)S(1)} %get-tuple-element.74), channel_id=1, source_target_pairs={{0,4},{4,0},{8,12},{12,8},{16,20},{20,16},{24,28},{28,24},{1,5},{5... | collective-permute-start | bytes 24584 | tf_op jit(solution)/shard_map/ppermute | solution.py:550
  53.1 22.1 %collective-permute-start.11 = (bf16[256,512]{1,0:T(8,128)(2,1)S(1)}, bf16[256,512]{1,0:T(8,128)(2,1)S(1)}, u32[]{:S(2)}, u32[]{:S(2)}) collective-permute-start(bf16[256,512]{1,0:T(8,128)(2,1)S(1)} %get-tuple-element.77), channel_id=1, source_target_pairs={{1,2},{2,1},{5,6},{6,5},{9,10},{10,9},{13,14},{14,13},{17,18},{18,... | collective-permute-start | bytes 786440 | tf_op jit(solution)/shard_map/ppermute | solution.py:553
  54.8 22.3 %collective-permute-start.14 = (bf16[256,512]{1,0:T(8,128)(2,1)S(1)}, bf16[256,512]{1,0:T(8,128)(2,1)S(1)}, u32[]{:S(2)}, u32[]{:S(2)}) collective-permute-start(bf16[256,512]{1,0:T(8,128)(2,1)S(1)} %get-tuple-element.81), channel_id=1, source_target_pairs={{1,2},{2,1},{5,6},{6,5},{9,10},{10,9},{13,14},{14,13},{17,18},{18,... | collective-permute-start | bytes 786440 | tf_op jit(solution)/shard_map/ppermute | solution.py:553
  56.5 22.6 %collective-permute-start.17 = (bf16[256,512]{1,0:T(8,128)(2,1)S(1)}, bf16[256,512]{1,0:T(8,128)(2,1)S(1)}, u32[]{:S(2)}, u32[]{:S(2)}) collective-permute-start(bf16[256,512]{1,0:T(8,128)(2,1)S(1)} %get-tuple-element.86), channel_id=1, source_target_pairs={{1,2},{2,1},{5,6},{6,5},{9,10},{10,9},{13,14},{14,13},{17,18},{18,... | collective-permute-start | bytes 786440 | tf_op jit(solution)/shard_map/ppermute | solution.py:553
  57.2 23.8 %collective-permute-start.19 = (bf16[256,512]{1,0:T(8,128)(2,1)S(1)}, bf16[256,512]{1,0:T(8,128)(2,1)S(1)}, u32[]{:S(2)}, u32[]{:S(2)}) collective-permute-start(bf16[256,512]{1,0:T(8,128)(2,1)S(1)} %get-tuple-element.71), channel_id=1, source_target_pairs={{1,2},{2,1},{5,6},{6,5},{9,10},{10,9},{13,14},{14,13},{17,18},{18,... | collective-permute-start | bytes 786440 | tf_op jit(solution)/shard_map/ppermute | solution.py:553
  57.9 3.8 %collective-permute-start.8 = (s32[16,256]{1,0:T(8,128)S(1)}, s32[16,256]{1,0:T(8,128)S(1)}, u32[]{:S(2)}, u32[]{:S(2)}) collective-permute-start(s32[16,256]{1,0:T(8,128)S(1)} %pad_add_fusion.2), channel_id=1, source_target_pairs={{0,8},{4,12},{8,0},{12,4},{16,24},{20,28},{24,16},{28,20},{1,9},{5... | collective-permute-start | bytes 49160 | tf_op jit(solution)/shard_map/ppermute | solution.py:550
  61.7 21.2 %collective-permute-start.9 = (s32[32,256]{1,0:T(8,128)S(1)}, s32[32,256]{1,0:T(8,128)S(1)}, u32[]{:S(2)}, u32[]{:S(2)}) collective-permute-start(s32[32,256]{1,0:T(8,128)S(1)} %pad_add_fusion.1), channel_id=1, source_target_pairs={{0,16},{4,20},{8,24},{12,28},{16,0},{20,4},{24,8},{28,12},{1,17},{... | collective-permute-start | bytes 98312 | tf_op jit(solution)/shard_map/ppermute | solution.py:550
  75.9 14.6 %collective-permute-start.12 = (bf16[256,256]{1,0:T(8,128)(2,1)S(1)}, bf16[256,256]{1,0:T(8,128)(2,1)S(1)}, u32[]{:S(2)}, u32[]{:S(2)}) collective-permute-start(bf16[256,256]{1,0:T(8,128)(2,1)S(1)} %get-tuple-element.79), channel_id=1, source_target_pairs={{1,0},{2,3},{5,4},{6,7},{9,8},{10,11},{13,12},{14,15},{17,16},{18,... | collective-permute-start | bytes 393224 | tf_op jit(solution)/shard_map/ppermute | solution.py:553
  77.8 15.5 %collective-permute-start.15 = (bf16[256,256]{1,0:T(8,128)(2,1)S(1)}, bf16[256,256]{1,0:T(8,128)(2,1)S(1)}, u32[]{:S(2)}, u32[]{:S(2)}) collective-permute-start(bf16[256,256]{1,0:T(8,128)(2,1)S(1)} %get-tuple-element.83), channel_id=1, source_target_pairs={{1,0},{2,3},{5,4},{6,7},{9,8},{10,11},{13,12},{14,15},{17,16},{18,... | collective-permute-start | bytes 393224 | tf_op jit(solution)/shard_map/ppermute | solution.py:553
  79.7 16.4 %collective-permute-start.18 = (bf16[256,256]{1,0:T(8,128)(2,1)S(1)}, bf16[256,256]{1,0:T(8,128)(2,1)S(1)}, u32[]{:S(2)}, u32[]{:S(2)}) collective-permute-start(bf16[256,256]{1,0:T(8,128)(2,1)S(1)} %get-tuple-element.88), channel_id=1, source_target_pairs={{1,0},{2,3},{5,4},{6,7},{9,8},{10,11},{13,12},{14,15},{17,16},{18,... | collective-permute-start | bytes 393224 | tf_op jit(solution)/shard_map/ppermute | solution.py:553
  81.6 34.9 %copy-start.6 = (f32[1024]{0:T(1024)S(1)}, f32[1024]{0:T(1024)}, u32[]{:S(2)}) copy-start(f32[1024]{0:T(1024)} %param.15) | copy-start | bytes 12292
  81.6 16.2 %collective-permute-start.20 = (bf16[256,256]{1,0:T(8,128)(2,1)S(1)}, bf16[256,256]{1,0:T(8,128)(2,1)S(1)}, u32[]{:S(2)}, u32[]{:S(2)}) collective-permute-start(bf16[256,256]{1,0:T(8,128)(2,1)S(1)} %get-tuple-element.91), channel_id=1, source_target_pairs={{1,0},{2,3},{5,4},{6,7},{9,8},{10,11},{13,12},{14,15},{17,16},{18,... | collective-permute-start | bytes 393224 | tf_op jit(solution)/shard_map/ppermute | solution.py:553
  99.9 4.9 %collective-permute-start.21 = (bf16[256,256]{1,0:T(8,128)(2,1)S(1)}, bf16[256,256]{1,0:T(8,128)(2,1)S(1)}, u32[]{:S(2)}, u32[]{:S(2)}) collective-permute-start(bf16[256,256]{1,0:T(8,128)(2,1)S(1)} %get-tuple-element.94), channel_id=1, source_target_pairs={{0,4},{4,0},{8,12},{12,8},{16,20},{20,16},{24,28},{28,24},{1,5},{5... | collective-permute-start | bytes 393224 | tf_op jit(solution)/shard_map/ppermute | solution.py:550
  100.0 7.7 %collective-permute-start.22 = (bf16[256,256]{1,0:T(8,128)(2,1)S(1)}, bf16[256,256]{1,0:T(8,128)(2,1)S(1)}, u32[]{:S(2)}, u32[]{:S(2)}) collective-permute-start(bf16[256,256]{1,0:T(8,128)(2,1)S(1)} %get-tuple-element.95), channel_id=1, source_target_pairs={{0,8},{4,12},{8,0},{12,4},{16,24},{20,28},{24,16},{28,20},{1,9},{5... | collective-permute-start | bytes 393224 | tf_op jit(solution)/shard_map/ppermute | solution.py:550
  102.1 7.1 %collective-permute-start.23 = (bf16[256,256]{1,0:T(8,128)(2,1)S(1)}, bf16[256,256]{1,0:T(8,128)(2,1)S(1)}, u32[]{:S(2)}, u32[]{:S(2)}) collective-permute-start(bf16[256,256]{1,0:T(8,128)(2,1)S(1)} %get-tuple-element.96), channel_id=1, source_target_pairs={{0,12},{4,8},{8,4},{12,0},{16,28},{20,24},{24,20},{28,16},{1,13},{... | collective-permute-start | bytes 393224 | tf_op jit(solution)/shard_map/ppermute | solution.py:550
  102.1 12.0 %collective-permute-start.24 = (bf16[256,256]{1,0:T(8,128)(2,1)S(1)}, bf16[256,256]{1,0:T(8,128)(2,1)S(1)}, u32[]{:S(2)}, u32[]{:S(2)}) collective-permute-start(bf16[256,256]{1,0:T(8,128)(2,1)S(1)} %get-tuple-element.97), channel_id=1, source_target_pairs={{0,16},{4,20},{8,24},{12,28},{16,0},{20,4},{24,8},{28,12},{1,17},{... | collective-permute-start | bytes 393224 | tf_op jit(solution)/shard_map/ppermute | solution.py:550
  104.8 11.5 %collective-permute-start.25 = (bf16[256,256]{1,0:T(8,128)(2,1)S(1)}, bf16[256,256]{1,0:T(8,128)(2,1)S(1)}, u32[]{:S(2)}, u32[]{:S(2)}) collective-permute-start(bf16[256,256]{1,0:T(8,128)(2,1)S(1)} %get-tuple-element.98), channel_id=1, source_target_pairs={{0,20},{4,16},{8,28},{12,24},{16,4},{20,0},{24,12},{28,8},{1,21},{... | collective-permute-start | bytes 393224 | tf_op jit(solution)/shard_map/ppermute | solution.py:550
  104.8 11.5 %collective-permute-start.26 = (bf16[256,256]{1,0:T(8,128)(2,1)S(1)}, bf16[256,256]{1,0:T(8,128)(2,1)S(1)}, u32[]{:S(2)}, u32[]{:S(2)}) collective-permute-start(bf16[256,256]{1,0:T(8,128)(2,1)S(1)} %get-tuple-element.99), channel_id=1, source_target_pairs={{0,24},{4,28},{8,16},{12,20},{16,8},{20,12},{24,0},{28,4},{1,25},{... | collective-permute-start | bytes 393224 | tf_op jit(solution)/shard_map/ppermute | solution.py:550
  107.7 8.9 %collective-permute-start.27 = (bf16[256,256]{1,0:T(8,128)(2,1)S(1)}, bf16[256,256]{1,0:T(8,128)(2,1)S(1)}, u32[]{:S(2)}, u32[]{:S(2)}) collective-permute-start(bf16[256,256]{1,0:T(8,128)(2,1)S(1)} %get-tuple-element.100), channel_id=1, source_target_pairs={{0,28},{4,24},{8,20},{12,16},{16,12},{20,8},{24,4},{28,0},{1,29},{... | collective-permute-start | bytes 393224 | tf_op jit(solution)/shard_map/ppermute | solution.py:550

commit v3 on v2

--- a/solution.py
+++ b/solution.py
@@ -67,33 +67,29 @@
             part: pltpu.make_async_copy(w_hbm.at[part], ws.at[part], sems.at[count + 1 + part])
             for part in order
         }
-        for copy in copies[:2] + [gain_copy] + [w_copies[p] for p in order] + copies[2:] + [w_copy]:
+        for copy in [gain_copy, copies[0]] + [w_copies[p] for p in order] + copies[1:] + [w_copy]:
             copy.start()
-        for i in range(0, count, 2):
-            normed = []
-            for j in (i, i + 1):
-                copies[j].wait()
-                kept[j].start()
-                if j == 0:
-                    gain_copy.wait()
-                wide = buffer[j].astype(f32)
-                mean_square = jnp.mean(wide * wide, axis=-1, keepdims=True)
-                normed.append((wide * lax.rsqrt(mean_square + epsilon) * gains[...]).astype(bf16))
-            normed = jnp.concatenate(normed, axis=0)
-            if i == 0:
-                w_copies[2].wait()
+
+        def load_norm(i):
+            copies[i].wait()
+            kept[i].start()
+            wide = buffer[i].astype(f32)
+            mean_square = jnp.mean(wide * wide, axis=-1, keepdims=True)
+            return (wide * lax.rsqrt(mean_square + epsilon) * gains[...]).astype(bf16)
+
+        gain_copy.wait()
+        following = load_norm(0)
+        for part in order:
+            w_copies[part].wait()
+        for i in range(count):
+            normed = following
+            if i + 1 < count:
+                following = load_norm(i + 1)
             values = dot(normed, ws[2])
-            if i == 0:
-                w_copies[0].wait()
             queries = dot(normed, ws[0])
-            if i == 0:
-                w_copies[1].wait()
-            keys = dot(normed, ws[1]).astype(bf16)
-            for j in (i, i + 1):
-                at = slice((j - i) * tokens, (j - i + 1) * tokens)
-                outs[2 * j + 1][1] = jnp.transpose(values[at]).astype(bf16)
-                outs[2 * j][...] = jnp.transpose(queries[at]).astype(bf16) * jnp.asarray(scale, bf16)
-                outs[2 * j + 1][0] = keys[at]
+            outs[2 * i + 1][0] = dot(normed, ws[1]).astype(bf16)
+            outs[2 * i + 1][1] = jnp.transpose(values).astype(bf16)
+            outs[2 * i][...] = jnp.transpose(queries).astype(bf16) * jnp.asarray(scale, bf16)
         w_copy.wait()
         for copy in kept:
             copy.wait()
@@ -428,84 +424,127 @@
     )(block_rows, token_rows)
 
 
-def picks(offsets, width):
-    clamped = jnp.minimum(jnp.maximum(offsets, -1.0), float(width)).astype(bf16)
-    place = lax.broadcasted_iota(jnp.int32, (offsets.shape[0], width), 1).astype(f32).astype(bf16)
-    spread = jnp.broadcast_to(clamped, place.shape)
-    return jnp.where(spread == place, jnp.ones_like(place), jnp.zeros_like(place))
-
-
-def gather_rows(meta, wanted, pieces):
+def spread_picks(spread, shift, width):
+    clamped = jnp.minimum(jnp.maximum(spread - shift, -1.0), float(width)).astype(bf16)
+    wide = jnp.concatenate([clamped] * (width // LANES), axis=1) if width > LANES else clamped[:, :width]
+    place = lax.broadcasted_iota(jnp.int32, wide.shape, 1).astype(f32).astype(bf16)
+    return jnp.where(wide == place, jnp.ones_like(place), jnp.zeros_like(place))
+
+
+def gather_rows(meta, wanted, pieces, masks, tokens):
     peers, capacity = int(round(wanted.shape[0] ** 0.5)), wanted.shape[1]
-    tokens, sub = pieces[0][0].shape
-    local_views = len(pieces)
-    rows = local_views * tokens
-    flat = [p for pair in pieces for p in pair]
+    whole = not isinstance(pieces, list)
+    flat = [pieces] if whole else [p for pair in pieces for p in pair]
+    sub = flat[0].shape[1]
+    rows = flat[0].shape[0] if whole else len(pieces) * tokens
+    local_views = rows // tokens
 
     def body(meta_ref, wanted_ref, *refs):
-        ins = refs[: len(flat)]
-        layer, outs = refs[len(flat)], refs[len(flat) + 1 :]
-        end = jnp.logical_or(meta_ref[1] == 0, meta_ref[1] == meta_ref[2] - 1)
-        for v in range(local_views):
-            layer[v * tokens : (v + 1) * tokens, :] = jnp.where(
-                end, ins[2 * v + 1][...], ins[2 * v][...]
+        ins, outs = refs[: len(flat)], refs[len(flat) :]
+        if whole:
+            layer = ins[0]
+        else:
+            layer, outs = outs[0], outs[1:]
+            end = jnp.logical_or(meta_ref[1] == 0, meta_ref[1] == meta_ref[2] - 1)
+            for v in range(local_views):
+                layer[v * tokens : (v + 1) * tokens, :] = jnp.where(
+                    end, ins[2 * v + 1][...], ins[2 * v][...]
+                )
+        lines = [wanted_ref[pl.ds(m * peers + meta_ref[0], 1), :] for m in masks]
+        lines += [lines[0]] * (-len(lines) % 8)
+        columns = jnp.transpose(jnp.concatenate(lines, axis=0).astype(f32))
+        for n in range(len(masks)):
+            spread = jnp.broadcast_to(columns[:, n : n + 1], (capacity, LANES))
+            pick = jnp.concatenate(
+                [spread_picks(spread, float(v * tokens), tokens) for v in range(local_views)], axis=1
             )
-        lines = [wanted_ref[pl.ds(m * peers + meta_ref[0], 1), :] for m in range(peers)]
-        columns = jnp.transpose(jnp.concatenate(lines, axis=0).astype(f32))
-        for mask in range(peers):
-            column = columns[:, mask : mask + 1]
-            pick = jnp.concatenate(
-                [picks(column - float(v * tokens), tokens) for v in range(local_views)], axis=1
-            )
-            outs[mask][...] = dot(pick, layer[...]).astype(bf16)
-
+            outs[n][...] = dot(pick, layer[...]).astype(bf16)
+
+    out_shape = [jax.ShapeDtypeStruct((capacity, sub), bf16)] * len(masks)
+    if not whole:
+        out_shape = [jax.ShapeDtypeStruct((rows, sub), bf16)] + out_shape
     return pl.pallas_call(
         body,
         in_specs=[SMEM_SPEC] + many(VMEM_SPEC, 1 + len(flat)),
-        out_specs=many(VMEM_SPEC, 1 + peers),
-        out_shape=[jax.ShapeDtypeStruct((rows, sub), bf16)]
-        + [jax.ShapeDtypeStruct((capacity, sub), bf16)] * peers,
+        out_specs=many(VMEM_SPEC, len(out_shape)),
+        out_shape=out_shape,
         name="gather_rows",
         compiler_params=grant(12),
-        cost_estimate=cost(2 * peers * capacity * rows * sub, 2 * (rows + peers * capacity) * sub * 2),
+        cost_estimate=cost(
+            2 * len(masks) * capacity * rows * sub, 2 * (rows + len(masks) * capacity) * sub * 2
+        ),
     )(meta, wanted, *flat)
 
 
-def finish_rows(meta, code, confidence, layer, replies, tokens):
+def fetched_part(meta_ref, code_spread, masks, reps, capacity):
+    pick = jnp.concatenate(
+        [
+            spread_picks(
+                code_spread, (lax.bitwise_xor(meta_ref[0], mask) * capacity).astype(f32), capacity
+            )
+            for mask in masks
+        ],
+        axis=1,
+    )
+    return dot(pick, jnp.concatenate([r[...] for r in reps], axis=0))
+
+
+def spread_column(turned, g, per, lanes):
+    return jnp.concatenate(
+        [
+            jnp.broadcast_to(turned[:, g * per + j : g * per + j + 1], (lanes, LANES))
+            for j in range(per)
+        ],
+        axis=0,
+    )
+
+
+def first_replies(meta, code, replies, tokens):
+    masks = sorted(replies)
+    capacity, sub = replies[masks[0]].shape
+    strips, lanes = code.shape
+    rows = strips * lanes
+    per = tokens // lanes
+
+    def body(meta_ref, code_ref, *refs):
+        codes = jnp.transpose(code_ref[...].astype(f32))
+        for g in range(rows // tokens):
+            refs[-1][g * tokens : (g + 1) * tokens, :] = fetched_part(
+                meta_ref, spread_column(codes, g, per, lanes), masks, refs[:-1], capacity
+            ).astype(bf16)
+
+    return pl.pallas_call(
+        body,
+        in_specs=[SMEM_SPEC] + many(VMEM_SPEC, 1 + len(masks)),
+        out_specs=VMEM_SPEC,
+        out_shape=jax.ShapeDtypeStruct((rows, sub), bf16),
+        name="first_replies",
+        compiler_params=grant(12),
+        cost_estimate=cost(2 * len(masks) * capacity * rows * sub, rows * sub * 4),
+    )(meta, code, *[replies[m] for m in masks])
+
+
+def finish_rows(meta, code, confidence, layer, early, replies, tokens):
     rows, sub = layer.shape
-    peers = len(replies)
-    capacity = replies[0].shape[0]
+    masks = sorted(replies)
+    capacity = replies[masks[0]].shape[0]
     _, lanes = code.shape
     blocks = rows // tokens
     per = tokens // lanes
 
-    def body(meta_ref, code_ref, conf_ref, layer_ref, *refs):
-        reps, (out_hbm, buffer, sems) = refs[:peers], refs[peers:]
+    def body(meta_ref, code_ref, conf_ref, layer_ref, early_ref, *refs):
+        reps, (out_hbm, buffer, sems) = refs[: len(masks)], refs[len(masks) :]
         codes = jnp.transpose(code_ref[...].astype(f32))
         confs = jnp.transpose(conf_ref[...]) * coupling
         copies = []
         for g in range(blocks):
-
-            def column(turned):
-                return jnp.concatenate(
-                    [turned[:, g * per + j : g * per + j + 1] for j in range(per)], axis=0
-                )
-
-            code_column = column(codes)
-            pick = jnp.concatenate(
-                [
-                    picks(
-                        code_column
-                        - (lax.bitwise_xor(meta_ref[0], mask) * capacity).astype(f32),
-                        capacity,
-                    )
-                    for mask in range(peers)
-                ],
-                axis=1,
+            at = slice(g * tokens, (g + 1) * tokens)
+            fetched = early_ref[at, :].astype(f32) + fetched_part(
+                meta_ref, spread_column(codes, g, per, lanes), masks, reps, capacity
             )
-            fetched = dot(pick, jnp.concatenate([r[...] for r in reps], axis=0))
-            wide = layer_ref[g * tokens : (g + 1) * tokens, :].astype(f32)
-            buffer[g] = wide + column(confs) * (fetched - wide)
+            wide = layer_ref[at, :].astype(f32)
+            weight = jnp.concatenate([spread_column(confs, g, per, lanes)] * (sub // LANES), axis=1)
+            buffer[g] = wide + weight * (fetched - wide)
             copies.append(
                 pltpu.make_async_copy(
                     buffer.at[g], out_hbm.at[pl.ds(g * tokens, tokens), :], sems.at[g]
@@ -517,7 +556,7 @@
 
     return pl.pallas_call(
         body,
-        in_specs=[SMEM_SPEC] + many(VMEM_SPEC, 3 + peers),
+        in_specs=[SMEM_SPEC] + many(VMEM_SPEC, 4 + len(masks)),
         out_specs=ANY_SPEC,
         out_shape=jax.ShapeDtypeStruct((rows, sub), f32),
         scratch_shapes=[
@@ -526,8 +565,8 @@
         ],
         name="finish_rows",
         compiler_params=grant(12),
-        cost_estimate=cost(2 * peers * capacity * rows * sub, rows * sub * 6 + peers * capacity * sub * 2),
-    )(meta, code, confidence, layer, *replies)
+        cost_estimate=cost(2 * len(masks) * capacity * rows * sub, rows * sub * 8),
+    )(meta, code, confidence, layer, early, *[replies[m] for m in masks])
 
 
 def per_device(latents, norm_gain, w_qkv, w_out, intersection, match_block, match_row, confidence):
@@ -577,25 +616,41 @@
     inner = attend(
         meta, inter, inner_queries, blocks, remote, inner_plan, window, earlier=tuple(local)
     )
-    remote.update(prev_second=prev_second, next_second=next_second)
-    outer_plan = [
-        (0, [("prev_last", -1, 0), ("prev_second", -2, 1)]),
-        (3, [("next_first", 3, 0), ("next_second", 3, 1)]),
-    ]
-    outer_queries = [after(queries[0], inner[0]), queries[3]]
-    outer = attend(meta, inter, outer_queries, blocks, remote, outer_plan, window)
-    attended = {1: inner[0], 2: inner[1], 0: outer[0], 3: outer[1]}
     w_theirs = partner(after(w_mine, inner[0]), 1)
+    sent = {}
+
+    def attend_outer(view, sources, done):
+        (result,) = attend(
+            meta,
+            inter,
+            [after(queries[view], done)],
+            blocks,
+            {k: x for k, x in halo.items() if k in [s[0] for s in sources]},
+            [(view, sources)],
+            window,
+        )
+        return result
+
+    halo = dict(remote, prev_second=prev_second, next_second=next_second)
+    attended = {1: inner[0], 2: inner[1]}
+    attended[0] = attend_outer(0, [("prev_last", -1, 0), ("prev_second", -2, 1)], inner[0])
     keep, got, formed = {}, {}, {}
-    for v in VIEW_ORDER:
+
+    def pass_on(v):
         near = across(attended[v], beside)
-        keep[v], send = partial_out(
+        keep[v], sent[v] = partial_out(
             meta, attended[v], near, w_out, w_mine, w_theirs, halves, loaded.index(v)
         )
-        got[v] = across(send, middle)
+        got[v] = across(sent[v], middle)
+
+    pass_on(1)
+    pass_on(2)
+    attended[3] = attend_outer(3, [("next_first", 3, 0), ("next_second", 3, 1)], sent[2])
+    pass_on(0)
+    pass_on(3)
     strips = rows // LANES
     wanted, code = prepare_requests(
-        after(match_block.reshape(strips, LANES), send),
+        after(match_block.reshape(strips, LANES), sent[3]),
         match_row.reshape(strips, LANES),
         peers,
         capacity,
@@ -609,14 +664,38 @@
         formed[v] = (own, across(other, back))
 
     pieces = [formed[v] for v in range(local_views)]
-    layer, *outgoing = gather_rows(meta, wanted, pieces)
-    replies = [outgoing[0]]
-    for mask in range(1, peers):
-        replies.append(partner(outgoing[mask], mask))
+    first_masks, last_masks = reply_order(peers)
+    replies = {}
+
+    def reply(masks, outgoing):
+        for mask, rows_out in zip(masks, outgoing):
+            replies[mask] = partner(rows_out, mask)
+
+    layer, *outgoing = gather_rows(meta, wanted, pieces, first_masks, tokens)
+    reply(first_masks, outgoing)
+    *outgoing, own_rows = gather_rows(meta, wanted, layer, last_masks + [0], tokens)
+    reply(last_masks, outgoing)
+    late = [m for m in last_masks if m > 1]
+    early = first_replies(
+        meta, code, {0: own_rows, **{m: r for m, r in replies.items() if m not in late}}, tokens
+    )
     refined = finish_rows(
-        meta, code, confidence.reshape(strips, LANES), layer, replies, tokens
+        meta,
+        code,
+        confidence.reshape(strips, LANES),
+        layer,
+        early,
+        {m: replies[m] for m in late},
+        tokens,
     )
     return refined.reshape(local_views, tokens, sub)
+
+
+def reply_order(peers):
+    far_half = list(range(peers // 2, peers))
+    far_half = far_half[len(far_half) // 2 :] + far_half[: len(far_half) // 2]
+    pairs = zip(far_half[: len(far_half) // 2], far_half[len(far_half) // 2 :])
+    return [m for pair in pairs for m in pair], list(range(2, peers // 2)) + [1]
 
 
 def solution(mesh):

time: 120 us -> 118 us (0.983)
  starting transfers between devices: 61.1 us -> 52.7 us
  waiting for transfers between devices: 30.3 us -> 35.2 us
  Pallas kernels: 26.9 us -> 28.8 us
    ppermute x11, starting transfers between devices: 34.8 us -> 10.7 us  [partner(): return lax.ppermute(x, 'views', [(i, i ^ mask) for i in range(peers)])]
    ppermute x4, starting transfers between devices: 5.85 us -> 21 us  [along(): lax.ppermute(x, 'views', [(i, (i + by) % peers) for i in range(peers)])]
    ppermute x13, waiting for transfers between devices: 14.9 us -> 21 us  [across(): return lax.ppermute(x, 'heads', pairs)]
    ppermute x4, waiting for transfers between devices: 5.05 us -> 1.18 us  [along(): lax.ppermute(x, 'views', [(i, (i + by) % peers) for i in range(peers)])]
    ppermute x11, waiting for transfers between devices: 10.3 us -> 13 us  [partner(): return lax.ppermute(x, 'views', [(i, i ^ mask) for i in range(peers)])]
    pallas_call x1 -> x2, Pallas kernels: 2.05 us -> 3.01 us  [gather_rows(): pl.pallas_call(body, in_specs=[SMEM_SPEC] + many(VMEM_SPEC, 1 + len(flat)...]
    pallas_call x1 -> x2, Pallas kernels: 2.86 us -> 3.79 us  [the longest x1 2.12 us: finish_rows(): pl.pallas_call(body, in_specs=[SMEM_SPEC] + many(VMEM_SPEC, 4 + len(masks...]
    pallas_call x3 -> x4, Pallas kernels: 8.17 us -> 9.05 us  [attend(): pl.pallas_call(body, in_specs=[SMEM_SPEC, SMEM_SPEC] + many(VMEM_SPEC, he...]
  transfers between devices with their start and end apart: 28 -> 28, of which waited for: 10 -> 10; matrix products, arithmetic and copies ran while one was open for 0% -> 0% of each run, Pallas kernels for 13% -> 16%
where the time goes in v3:
time: 118 us
  starting transfers between devices  52.7 us (45%)
  waiting for transfers between devices  35.2 us (30%)
  Pallas kernels  28.8 us (24%)
    ppermute x13, starting transfers between devices, across(): return lax.ppermute(x, 'heads', pairs)  21.1 us
    ppermute x13, waiting for transfers between devices, across(): return lax.ppermute(x, 'heads', pairs)  21 us
    ppermute x4, starting transfers between devices, along(): lax.ppermute(x, 'views', [(i, (i + by) % peers) for i in range(peers)])  21 us
    ppermute x11, waiting for transfers between devices, partner(): return lax.ppermute(x, 'views', [(i, i ^ mask) for i in range(peers)])  13 us
    ppermute x11, starting transfers between devices, partner(): return lax.ppermute(x, 'views', [(i, i ^ mask) for i in range(peers)])  10.7 us
    pallas_call x4, Pallas kernels, attend(): pl.pallas_call(body, in_specs=[SMEM_SPEC, SMEM_SPEC] + many(VMEM_SPEC, he...  9.05 us
    pallas_call x1, Pallas kernels, project_views(): pl.pallas_call(body, in_specs=[SMEM_SPEC] + many(ANY_SPEC, 4), out_specs=...  5.85 us
    pallas_call x4, Pallas kernels, partial_out(): pl.pallas_call(body, in_specs=[SMEM_SPEC] + many(VMEM_SPEC, 6), out_specs...  3.97 us
  transfers between devices with their start and end apart: 28, of which 10 were waited for; matrix products, arithmetic and copies ran while one was open for 0% of the time, Pallas kernels for 16%

profile of v3, /device:TPU:0, one launch (start us, length us, event | category | flops | bytes accessed | tf_op | source)
XLA Modules:
  0.0 118.1 jit_solution(5906631979047041153)
XLA Ops:
  0.0 0.7 copy-done.4
  0.7 5.9 %project_views.1 = (bf16[256,256]{1,0:T(8,128)(2,1)S(1)}, bf16[2,256,256]{2,1,0:T(8,128)(2,1)S(1)}, bf16[256,256]{1,0:T(8,128)(2,1)S(1)}, bf16[2,256,256]{2,1,0:...) custom-call(s32[4]{0:T(128)S(1)} %compare_select_fusion.1.meta_ref, ...), custom_call_target="tpu_custom_call" | custom-call | flops 1610612736 | bytes 5242880 | tf_op jit(solution)/shard_map/project_views/pallas_call | solution.py:105
  6.6 3.4 %collective-permute-start = (bf16[2,256,256]{2,1,0:T(8,128)(2,1)S(1)}, bf16[2,256,256]{2,1,0:T(8,128)(2,1)S(1)}, u32[]{:S(2)}, u32[]{:S(2)}) collective-permute-start(bf16[2,256,256]{2,1,0:T(8,128)(2,1)S(1)} %get-tuple-element.55.refs_2_.refs_4_.refs_1_), channel_id=1, source_target_pairs={{0,28},{4,0},{8,4},{12,8},{16,12},{20,16},{24,20},{28,24},{1,29},{... | collective-permute-start | bytes 786440 | tf_op jit(solution)/shard_map/ppermute | solution.py:586
  10.0 3.5 %collective-permute-start.3 = (bf16[128,1024]{1,0:T(8,128)(2,1)S(1)}, bf16[128,1024]{1,0:T(8,128)(2,1)S(1)}, u32[]{:S(2)}, u32[]{:S(2)}) collective-permute-start(bf16[128,1024]{1,0:T(8,128)(2,1)S(1)} %get-tuple-element.62), channel_id=1, source_target_pairs={{0,1},{3,2},{4,5},{7,6},{8,9},{11,10},{12,13},{15,14},{16,17},{19,... | collective-permute-start | bytes 786440 | tf_op jit(solution)/shard_map/ppermute | solution.py:592
  13.5 3.0 %attend_local.1 = (f32[2,320,256]{2,1,0:T(8,128)S(1)}, f32[2,4,256]{2,1,0:T(4,128)S(1)}) custom-call(s32[4]{0:T(128)S(1)} %compare_select_fusion.1.meta_ref, s32[2,32]{1,0:T(2,128)S(1)} %bitcast.7, bf16[256,256]{1,0:T(8,128)(2,1)S(1)} %get-tuple-element.53.refs_0_.refs_2_, bf16[256,256]{1,0:T(8,128)(2,1)S(1)} %get-tuple-element.54.refs_1_.refs_3_, ...), custom_call_target="tpu_custom_call" | custom-call | flops 1073741824 | bytes 4194304 | tf_op jit(solution)/shard_map/attend_local/pallas_call | solution.py:274
  16.5 1.2 collective-permute-done.1.refs_9_.refs_5_
  17.7 1.7 %attend.3 = (bf16[256,256]{1,0:T(8,128)(2,1)S(1)}, bf16[256,256]{1,0:T(8,128)(2,1)S(1)}) custom-call(s32[4]{0:T(128)S(1)} %compare_select_fusion.1.meta_ref, s32[2,32]{1,0:T(2,128)S(1)} %bitcast.8, f32[2,320,256]{2,1,0:T(8,128)S(1)} %get-tuple-element.59.refs_0_, f32[2,4,256]{2,1,0:T(4,128)S(1)} %get-tuple-element.60.refs_1_, ...), custom_call_target="tpu_custom_call" | custom-call | flops 268435456 | bytes 1048576 | tf_op jit(solution)/shard_map/attend/pallas_call | solution.py:274
  19.5 17.5 %collective-permute-start.5 = (bf16[2,256,256]{2,1,0:T(8,128)(2,1)S(1)}, bf16[2,256,256]{2,1,0:T(8,128)(2,1)S(1)}, u32[]{:S(2)}, u32[]{:S(2)}) collective-permute-start(bf16[2,256,256]{2,1,0:T(8,128)(2,1)S(1)} %get-tuple-element.68.refs_3_.refs_5_.refs_2_), channel_id=1, source_target_pairs={{0,28},{4,0},{8,4},{12,8},{16,12},{20,16},{24,20},{28,24},{1,29},{... | collective-permute-start | bytes 786440 | tf_op jit(solution)/shard_map/ppermute | solution.py:586
  37.0 3.8 %collective-permute-start.2 = (bf16[256,256]{1,0:T(8,128)(2,1)S(1)}, bf16[256,256]{1,0:T(8,128)(2,1)S(1)}, u32[]{:S(2)}, u32[]{:S(2)}) collective-permute-start(bf16[256,256]{1,0:T(8,128)(2,1)S(1)} %get-tuple-element.61.att), channel_id=1, source_target_pairs={{0,1},{3,2},{4,5},{7,6},{8,9},{11,10},{12,13},{15,14},{16,17},{19,... | collective-permute-start | bytes 393224 | tf_op jit(solution)/shard_map/ppermute | solution.py:592
  40.8 1.3 %collective-permute-start.14 = (bf16[256,256]{1,0:T(8,128)(2,1)S(1)}, bf16[256,256]{1,0:T(8,128)(2,1)S(1)}, u32[]{:S(2)}, u32[]{:S(2)}) collective-permute-start(bf16[256,256]{1,0:T(8,128)(2,1)S(1)} %get-tuple-element.63.att), channel_id=1, source_target_pairs={{0,1},{3,2},{4,5},{7,6},{8,9},{11,10},{12,13},{15,14},{16,17},{19,... | collective-permute-start | bytes 393224 | tf_op jit(solution)/shard_map/ppermute | solution.py:592
  42.1 2.2 %attend.5.att = bf16[256,256]{1,0:T(8,128)(2,1)S(1)} custom-call(s32[4]{0:T(128)S(1)} %compare_select_fusion.1.meta_ref, s32[2,32]{1,0:T(2,128)S(1)} %bitcast.9, bf16[256,256]{1,0:T(8,128)(2,1)S(1)} %get-tuple-element.74.refs_0_, bf16[2,256,256]{2,1,0:T(8,128)(2,1)S(1)} %get-tuple-element.55.refs_2_.refs_4_.refs_1_, ...), custom_call_target="tpu_custom_call" | custom-call | flops 671088640 | bytes 2621440 | tf_op jit(solution)/shard_map/attend/pallas_call | solution.py:274
  44.3 1.5 %collective-permute-start.11 = (bf16[256,256]{1,0:T(8,128)(2,1)S(1)}, bf16[256,256]{1,0:T(8,128)(2,1)S(1)}, u32[]{:S(2)}, u32[]{:S(2)}) collective-permute-start(bf16[256,256]{1,0:T(8,128)(2,1)S(1)} %attend.5.att), channel_id=1, source_target_pairs={{0,1},{3,2},{4,5},{7,6},{8,9},{11,10},{12,13},{15,14},{16,17},{19,... | collective-permute-start | bytes 393224 | tf_op jit(solution)/shard_map/ppermute | solution.py:592
  45.8 1.0 partial_out.4
  46.9 2.2 %attend.4.att = bf16[256,256]{1,0:T(8,128)(2,1)S(1)} custom-call(s32[4]{0:T(128)S(1)} %compare_select_fusion.1.meta_ref, s32[2,32]{1,0:T(2,128)S(1)} %bitcast.10, bf16[256,256]{1,0:T(8,128)(2,1)S(1)} %get-tuple-element.67.refs_0_, bf16[2,256,256]{2,1,0:T(8,128)(2,1)S(1)} %get-tuple-element.55.refs_2_.refs_4_.refs_1_, ...), custom_call_target="tpu_custom_call" | custom-call | flops 671088640 | bytes 2621440 | tf_op jit(solution)/shard_map/attend/pallas_call | solution.py:274
  49.0 3.2 %collective-permute-start.6 = (bf16[256,256]{1,0:T(8,128)(2,1)S(1)}, bf16[256,256]{1,0:T(8,128)(2,1)S(1)}, u32[]{:S(2)}, u32[]{:S(2)}) collective-permute-start(bf16[256,256]{1,0:T(8,128)(2,1)S(1)} %attend.4.att), channel_id=1, source_target_pairs={{0,1},{3,2},{4,5},{7,6},{8,9},{11,10},{12,13},{15,14},{16,17},{19,... | collective-permute-start | bytes 393224 | tf_op jit(solution)/shard_map/ppermute | solution.py:592
  52.2 0.7 collective-permute-start.17
  52.9 1.0 partial_out.7
  53.9 0.7 collective-permute-start.15
  54.6 1.0 partial_out.6
  55.6 0.7 collective-permute-start.12
  56.3 1.0 partial_out.5
  57.3 0.7 prepare_requests.1
  58.1 0.7 collective-permute-start.19
  59.2 3.7 %collective-permute-done.8 = s32[16,256]{1,0:T(8,128)S(1)} collective-permute-done((s32[16,256]{1,0:T(8,128)S(1)}, s32[16,256]{1,0:T(8,128)S(1)}, u32[]{:S(2)}, u32[]{:S(2)}) %collective-permute-start.8) | collective-permute-done | bytes 16416 | tf_op jit(solution)/shard_map/ppermute | solution.py:589
  63.0 3.5 %collective-permute-start.9 = (s32[32,256]{1,0:T(8,128)S(1)}, s32[32,256]{1,0:T(8,128)S(1)}, u32[]{:S(2)}, u32[]{:S(2)}) collective-permute-start(s32[32,256]{1,0:T(8,128)S(1)} %pad_add_fusion), channel_id=1, source_target_pairs={{0,16},{4,20},{8,24},{12,28},{16,0},{20,4},{24,8},{28,12},{1,17},{... | collective-permute-start | bytes 98312 | tf_op jit(solution)/shard_map/ppermute | solution.py:589
  66.4 0.6 merge_out.5
  67.0 1.3 %collective-permute-start.16 = (bf16[256,256]{1,0:T(8,128)(2,1)S(1)}, bf16[256,256]{1,0:T(8,128)(2,1)S(1)}, u32[]{:S(2)}, u32[]{:S(2)}) collective-permute-start(bf16[256,256]{1,0:T(8,128)(2,1)S(1)} %get-tuple-element.83), channel_id=1, source_target_pairs={{1,0},{2,3},{5,4},{6,7},{9,8},{10,11},{13,12},{14,15},{17,16},{18,... | collective-permute-start | bytes 393224 | tf_op jit(solution)/shard_map/ppermute | solution.py:592
  68.4 0.6 merge_out.4
  69.0 1.3 %collective-permute-start.13 = (bf16[256,256]{1,0:T(8,128)(2,1)S(1)}, bf16[256,256]{1,0:T(8,128)(2,1)S(1)}, u32[]{:S(2)}, u32[]{:S(2)}) collective-permute-start(bf16[256,256]{1,0:T(8,128)(2,1)S(1)} %get-tuple-element.79), channel_id=1, source_target_pairs={{1,0},{2,3},{5,4},{6,7},{9,8},{10,11},{13,12},{14,15},{17,16},{18,... | collective-permute-start | bytes 393224 | tf_op jit(solution)/shard_map/ppermute | solution.py:592
  70.3 0.6 merge_out.6
  70.9 1.3 %collective-permute-start.18 = (bf16[256,256]{1,0:T(8,128)(2,1)S(1)}, bf16[256,256]{1,0:T(8,128)(2,1)S(1)}, u32[]{:S(2)}, u32[]{:S(2)}) collective-permute-start(bf16[256,256]{1,0:T(8,128)(2,1)S(1)} %get-tuple-element.86), channel_id=1, source_target_pairs={{1,0},{2,3},{5,4},{6,7},{9,8},{10,11},{13,12},{14,15},{17,16},{18,... | collective-permute-start | bytes 393224 | tf_op jit(solution)/shard_map/ppermute | solution.py:592
  72.2 0.6 merge_out.7
  72.8 1.3 %collective-permute-start.20 = (bf16[256,256]{1,0:T(8,128)(2,1)S(1)}, bf16[256,256]{1,0:T(8,128)(2,1)S(1)}, u32[]{:S(2)}, u32[]{:S(2)}) collective-permute-start(bf16[256,256]{1,0:T(8,128)(2,1)S(1)} %get-tuple-element.89), channel_id=1, source_target_pairs={{1,0},{2,3},{5,4},{6,7},{9,8},{10,11},{13,12},{14,15},{17,16},{18,... | collective-permute-start | bytes 393224 | tf_op jit(solution)/shard_map/ppermute | solution.py:592
  74.1 13.9 %collective-permute-done.16.refs_3_ = bf16[256,256]{1,0:T(8,128)(2,1)S(1)} collective-permute-done((bf16[256,256]{1,0:T(8,128)(2,1)S(1)}, bf16[256,256]{1,0:T(8,128)(2,1)S(1)}, u32[]{:S(2)}, u32[]{:S(2)}) %collective-permute-start.16) | collective-permute-done | bytes 131104 | tf_op jit(solution)/shard_map/ppermute | solution.py:592
  88.0 2.8 %collective-permute-done.13.refs_1_ = bf16[256,256]{1,0:T(8,128)(2,1)S(1)} collective-permute-done((bf16[256,256]{1,0:T(8,128)(2,1)S(1)}, bf16[256,256]{1,0:T(8,128)(2,1)S(1)}, u32[]{:S(2)}, u32[]{:S(2)}) %collective-permute-start.13) | collective-permute-done | bytes 131104 | tf_op jit(solution)/shard_map/ppermute | solution.py:592
  90.8 2.8 %collective-permute-done.18.refs_5_ = bf16[256,256]{1,0:T(8,128)(2,1)S(1)} collective-permute-done((bf16[256,256]{1,0:T(8,128)(2,1)S(1)}, bf16[256,256]{1,0:T(8,128)(2,1)S(1)}, u32[]{:S(2)}, u32[]{:S(2)}) %collective-permute-start.18) | collective-permute-done | bytes 131104 | tf_op jit(solution)/shard_map/ppermute | solution.py:592
  93.6 1.5 %collective-permute-done.20.refs_7_ = bf16[256,256]{1,0:T(8,128)(2,1)S(1)} collective-permute-done((bf16[256,256]{1,0:T(8,128)(2,1)S(1)}, bf16[256,256]{1,0:T(8,128)(2,1)S(1)}, u32[]{:S(2)}, u32[]{:S(2)}) %collective-permute-start.20) | collective-permute-done | bytes 131104 | tf_op jit(solution)/shard_map/ppermute | solution.py:592
  95.2 1.5 %gather_rows.2 = (bf16[1024,256]{1,0:T(8,128)(2,1)S(1)}, bf16[256,256]{1,0:T(8,128)(2,1)S(1)}, bf16[256,256]{1,0:T(8,128)(2,1)S(1)}, bf16[256,256]{1,0:T(8,128)(2,1)S(1)}, bf16[256,256]{1,0:T(8,128)(2,1)S(1)}) custom-call(s32[4]{0:T(128)S(1)} %compare_select_fusion.1.meta_ref, s32[64,256]{1,0:T(8,128)S(1)} %constant_dynamic-update-slice_fusion.wanted_ref, ...), custom_call_target="tpu_custom_call" | custom-call | flops 536870912 | bytes 2097152 | tf_op jit(solution)/shard_map/gather_rows/pallas_call | solution.py:466
  96.9 2.9 %collective-permute-start.24 = (bf16[256,256]{1,0:T(8,128)(2,1)S(1)}, bf16[256,256]{1,0:T(8,128)(2,1)S(1)}, u32[]{:S(2)}, u32[]{:S(2)}) collective-permute-start(bf16[256,256]{1,0:T(8,128)(2,1)S(1)} %get-tuple-element.95), channel_id=1, source_target_pairs={{0,24},{4,28},{8,16},{12,20},{16,8},{20,12},{24,0},{28,4},{1,25},{... | collective-permute-start | bytes 393224 | tf_op jit(solution)/shard_map/ppermute | solution.py:589
  99.8 1.4 %collective-permute-start.25 = (bf16[256,256]{1,0:T(8,128)(2,1)S(1)}, bf16[256,256]{1,0:T(8,128)(2,1)S(1)}, u32[]{:S(2)}, u32[]{:S(2)}) collective-permute-start(bf16[256,256]{1,0:T(8,128)(2,1)S(1)} %get-tuple-element.96), channel_id=1, source_target_pairs={{0,28},{4,24},{8,20},{12,16},{16,12},{20,8},{24,4},{28,0},{1,29},{... | collective-permute-start | bytes 393224 | tf_op jit(solution)/shard_map/ppermute | solution.py:589
  101.1 1.5 %gather_rows.3 = (bf16[256,256]{1,0:T(8,128)(2,1)S(1)}, bf16[256,256]{1,0:T(8,128)(2,1)S(1)}, bf16[256,256]{1,0:T(8,128)(2,1)S(1)}, bf16[256,256]{1,0:T(8,128)(2,1)S(1)}) custom-call(s32[4]{0:T(128)S(1)} %compare_select_fusion.1.meta_ref, s32[64,256]{1,0:T(8,128)S(1)} %constant_dynamic-update-slice_fusion.wanted_ref, ...), custom_call_target="tpu_custom_call" | custom-call | flops 536870912 | bytes 2097152 | tf_op jit(solution)/shard_map/gather_rows/pallas_call | solution.py:466
  102.7 5.5 %collective-permute-done.22.refs_2_ = bf16[256,256]{1,0:T(8,128)(2,1)S(1)} collective-permute-done((bf16[256,256]{1,0:T(8,128)(2,1)S(1)}, bf16[256,256]{1,0:T(8,128)(2,1)S(1)}, u32[]{:S(2)}, u32[]{:S(2)}) %collective-permute-start.22) | collective-permute-done | bytes 131104 | tf_op jit(solution)/shard_map/ppermute | solution.py:589
  108.2 1.8 %collective-permute-start.26 = (bf16[256,256]{1,0:T(8,128)(2,1)S(1)}, bf16[256,256]{1,0:T(8,128)(2,1)S(1)}, u32[]{:S(2)}, u32[]{:S(2)}) collective-permute-start(bf16[256,256]{1,0:T(8,128)(2,1)S(1)} %get-tuple-element.97), channel_id=1, source_target_pairs={{0,8},{4,12},{8,0},{12,4},{16,24},{20,28},{24,16},{28,20},{1,9},{5... | collective-permute-start | bytes 393224 | tf_op jit(solution)/shard_map/ppermute | solution.py:589
  110.0 0.8 collective-permute-start.27
  110.9 1.7 %first_replies.1.early_ref = bf16[1024,256]{1,0:T(8,128)(2,1)S(1)} custom-call(s32[4]{0:T(128)S(1)} %compare_select_fusion.1.meta_ref, s32[8,128]{1,0:T(8,128)S(1)} %get-tuple-element.71.code_ref, bf16[256,256]{1,0:T(8,128)(2,1)S(1)} %get-tuple-element.91.refs_0_, bf16[256,256]{1,0:T(8,128)(2,1)S(1)} %collective-permute-done.21.refs_1_, ...), custom_call_target="tpu_custom_call" | custom-call | flops 805306368 | bytes 1048576 | tf_op jit(solution)/shard_map/first_replies/pallas_call | solution.py:516
  112.5 1.0 collective-permute-done.26.refs_0_
  113.6 2.2 %collective-permute-done.27.refs_1_ = bf16[256,256]{1,0:T(8,128)(2,1)S(1)} collective-permute-done((bf16[256,256]{1,0:T(8,128)(2,1)S(1)}, bf16[256,256]{1,0:T(8,128)(2,1)S(1)}, u32[]{:S(2)}, u32[]{:S(2)}) %collective-permute-start.27) | collective-permute-done | bytes 131104 | tf_op jit(solution)/shard_map/ppermute | solution.py:589
  115.8 2.1 %finish_rows.1 = f32[1024,256]{1,0:T(8,128)} custom-call(s32[4]{0:T(128)S(1)} %compare_select_fusion.1.meta_ref, s32[8,128]{1,0:T(8,128)S(1)} %get-tuple-element.71.code_ref, f32[8,128]{1,0:T(8,128)S(1)} %bitcast.6, bf16[1024,256]{1,0:T(8,128)(2,1)S(1)} %get-tuple-element.90.refs_0_.layer_ref, bf16[1024,256]{1,0:T(8,128)(2,1)S(1)} %first_replies.1.early_ref, ...), custom_call_target="tpu_custom_call" | custom-call | flops 268435456 | bytes 2097152 | tf_op jit(solution)/shard_map/finish_rows/pallas_call | solution.py:557
  (47 shorter events, 1.0 us)
Async XLA Ops:
  0.0 0.7 copy-start.4
  0.7 12.8 %copy-start.3 = (s32[32,2]{0,1:T(2,128)S(1)}, s32[32,2]{0,1:T(2,128)}, u32[]{:S(2)}) copy-start(s32[32,2]{0,1:T(2,128)} %param.12) | copy-start | bytes 772
  6.6 10.0 %collective-permute-start = (bf16[2,256,256]{2,1,0:T(8,128)(2,1)S(1)}, bf16[2,256,256]{2,1,0:T(8,128)(2,1)S(1)}, u32[]{:S(2)}, u32[]{:S(2)}) collective-permute-start(bf16[2,256,256]{2,1,0:T(8,128)(2,1)S(1)} %get-tuple-element.55.refs_2_.refs_4_.refs_1_), channel_id=1, source_target_pairs={{0,28},{4,0},{8,4},{12,8},{16,12},{20,16},{24,20},{28,24},{1,29},{... | collective-permute-start | bytes 786440 | tf_op jit(solution)/shard_map/ppermute | solution.py:586
  10.0 7.7 %collective-permute-start.1 = (bf16[2,256,256]{2,1,0:T(8,128)(2,1)S(1)}, bf16[2,256,256]{2,1,0:T(8,128)(2,1)S(1)}, u32[]{:S(2)}, u32[]{:S(2)}) collective-permute-start(bf16[2,256,256]{2,1,0:T(8,128)(2,1)S(1)} %get-tuple-element.58.refs_5_.refs_7_.refs_4_), channel_id=1, source_target_pairs={{0,4},{4,8},{8,12},{12,16},{16,20},{20,24},{24,28},{28,0},{1,5},{5... | collective-permute-start | bytes 786440 | tf_op jit(solution)/shard_map/ppermute | solution.py:586
  10.0 9.5 %collective-permute-start.3 = (bf16[128,1024]{1,0:T(8,128)(2,1)S(1)}, bf16[128,1024]{1,0:T(8,128)(2,1)S(1)}, u32[]{:S(2)}, u32[]{:S(2)}) collective-permute-start(bf16[128,1024]{1,0:T(8,128)(2,1)S(1)} %get-tuple-element.62), channel_id=1, source_target_pairs={{0,1},{3,2},{4,5},{7,6},{8,9},{11,10},{12,13},{15,14},{16,17},{19,... | collective-permute-start | bytes 786440 | tf_op jit(solution)/shard_map/ppermute | solution.py:592
  16.4 25.7 %collective-permute-start.10 = (bf16[2,256,256]{2,1,0:T(8,128)(2,1)S(1)}, bf16[2,256,256]{2,1,0:T(8,128)(2,1)S(1)}, u32[]{:S(2)}, u32[]{:S(2)}) collective-permute-start(bf16[2,256,256]{2,1,0:T(8,128)(2,1)S(1)} %get-tuple-element.75.refs_4_.refs_6_.refs_3_), channel_id=1, source_target_pairs={{0,4},{4,8},{8,12},{12,16},{16,20},{20,24},{24,28},{28,0},{1,5},{5... | collective-permute-start | bytes 786440 | tf_op jit(solution)/shard_map/ppermute | solution.py:586
  17.7 28.1 %copy-start = (bf16[4,256,512]{2,1,0:T(8,128)(2,1)S(1)}, bf16[4,256,512]{2,1,0:T(8,128)(2,1)}, u32[]{:S(2)}) copy-start(bf16[4,256,512]{2,1,0:T(8,128)(2,1)} %get-tuple-element.65.halves_ref) | copy-start | bytes 3145732
  17.7 28.1 %copy-start.1 = (bf16[256,1024]{1,0:T(8,128)(2,1)S(1)}, bf16[256,1024]{1,0:T(8,128)(2,1)}, u32[]{:S(2)}) copy-start(bf16[256,1024]{1,0:T(8,128)(2,1)} %own_ref.7) | copy-start | bytes 1572868
  19.4 26.4 %collective-permute-start.4 = (bf16[128,1024]{1,0:T(8,128)(2,1)S(1)}, bf16[128,1024]{1,0:T(8,128)(2,1)S(1)}, u32[]{:S(2)}, u32[]{:S(2)}) collective-permute-start(bf16[128,1024]{1,0:T(8,128)(2,1)S(1)} %collective-permute-done.3.mine_ref), channel_id=1, source_target_pairs={{0,4},{4,0},{8,12},{12,8},{16,20},{20,16},{24,28},{28,24},{1,5},{5... | collective-permute-start | bytes 786440 | tf_op jit(solution)/shard_map/ppermute | solution.py:589
  19.5 27.3 %collective-permute-start.5 = (bf16[2,256,256]{2,1,0:T(8,128)(2,1)S(1)}, bf16[2,256,256]{2,1,0:T(8,128)(2,1)S(1)}, u32[]{:S(2)}, u32[]{:S(2)}) collective-permute-start(bf16[2,256,256]{2,1,0:T(8,128)(2,1)S(1)} %get-tuple-element.68.refs_3_.refs_5_.refs_2_), channel_id=1, source_target_pairs={{0,28},{4,0},{8,4},{12,8},{16,12},{20,16},{24,20},{28,24},{1,29},{... | collective-permute-start | bytes 786440 | tf_op jit(solution)/shard_map/ppermute | solution.py:586
  37.0 8.8 %collective-permute-start.2 = (bf16[256,256]{1,0:T(8,128)(2,1)S(1)}, bf16[256,256]{1,0:T(8,128)(2,1)S(1)}, u32[]{:S(2)}, u32[]{:S(2)}) collective-permute-start(bf16[256,256]{1,0:T(8,128)(2,1)S(1)} %get-tuple-element.61.att), channel_id=1, source_target_pairs={{0,1},{3,2},{4,5},{7,6},{8,9},{11,10},{12,13},{15,14},{16,17},{19,... | collective-permute-start | bytes 393224 | tf_op jit(solution)/shard_map/ppermute | solution.py:592
  40.8 12.1 %collective-permute-start.14 = (bf16[256,256]{1,0:T(8,128)(2,1)S(1)}, bf16[256,256]{1,0:T(8,128)(2,1)S(1)}, u32[]{:S(2)}, u32[]{:S(2)}) collective-permute-start(bf16[256,256]{1,0:T(8,128)(2,1)S(1)} %get-tuple-element.63.att), channel_id=1, source_target_pairs={{0,1},{3,2},{4,5},{7,6},{8,9},{11,10},{12,13},{15,14},{16,17},{19,... | collective-permute-start | bytes 393224 | tf_op jit(solution)/shard_map/ppermute | solution.py:592
  44.3 10.3 %collective-permute-start.11 = (bf16[256,256]{1,0:T(8,128)(2,1)S(1)}, bf16[256,256]{1,0:T(8,128)(2,1)S(1)}, u32[]{:S(2)}, u32[]{:S(2)}) collective-permute-start(bf16[256,256]{1,0:T(8,128)(2,1)S(1)} %attend.5.att), channel_id=1, source_target_pairs={{0,1},{3,2},{4,5},{7,6},{8,9},{11,10},{12,13},{15,14},{16,17},{19,... | collective-permute-start | bytes 393224 | tf_op jit(solution)/shard_map/ppermute | solution.py:592
  49.0 7.3 %collective-permute-start.6 = (bf16[256,256]{1,0:T(8,128)(2,1)S(1)}, bf16[256,256]{1,0:T(8,128)(2,1)S(1)}, u32[]{:S(2)}, u32[]{:S(2)}) collective-permute-start(bf16[256,256]{1,0:T(8,128)(2,1)S(1)} %attend.4.att), channel_id=1, source_target_pairs={{0,1},{3,2},{4,5},{7,6},{8,9},{11,10},{12,13},{15,14},{16,17},{19,... | collective-permute-start | bytes 393224 | tf_op jit(solution)/shard_map/ppermute | solution.py:592
  52.2 18.1 %collective-permute-start.17 = (bf16[256,512]{1,0:T(8,128)(2,1)S(1)}, bf16[256,512]{1,0:T(8,128)(2,1)S(1)}, u32[]{:S(2)}, u32[]{:S(2)}) collective-permute-start(bf16[256,512]{1,0:T(8,128)(2,1)S(1)} %get-tuple-element.66), channel_id=1, source_target_pairs={{1,2},{2,1},{5,6},{6,5},{9,10},{10,9},{13,14},{14,13},{17,18},{18,... | collective-permute-start | bytes 786440 | tf_op jit(solution)/shard_map/ppermute | solution.py:592
  53.9 3.4 %copy-start.5 = (s32[1024,1]{0,1:T(1,128)S(1)}, s32[1024,1]{0,1:T(1,128)}, u32[]{:S(2)}) copy-start(s32[1024,1]{0,1:T(1,128)} %param.13) | copy-start | bytes 12292
  53.9 3.4 %copy-start.6 = (s32[1024]{0:T(1024)S(1)}, s32[1024]{0:T(1024)}, u32[]{:S(2)}) copy-start(s32[1024]{0:T(1024)} %param.14) | copy-start | bytes 12292
  53.9 12.5 %collective-permute-start.15 = (bf16[256,512]{1,0:T(8,128)(2,1)S(1)}, bf16[256,512]{1,0:T(8,128)(2,1)S(1)}, u32[]{:S(2)}, u32[]{:S(2)}) collective-permute-start(bf16[256,512]{1,0:T(8,128)(2,1)S(1)} %get-tuple-element.81), channel_id=1, source_target_pairs={{1,2},{2,1},{5,6},{6,5},{9,10},{10,9},{13,14},{14,13},{17,18},{18,... | collective-permute-start | bytes 786440 | tf_op jit(solution)/shard_map/ppermute | solution.py:592
  55.6 12.7 %collective-permute-start.12 = (bf16[256,512]{1,0:T(8,128)(2,1)S(1)}, bf16[256,512]{1,0:T(8,128)(2,1)S(1)}, u32[]{:S(2)}, u32[]{:S(2)}) collective-permute-start(bf16[256,512]{1,0:T(8,128)(2,1)S(1)} %get-tuple-element.77), channel_id=1, source_target_pairs={{1,2},{2,1},{5,6},{6,5},{9,10},{10,9},{13,14},{14,13},{17,18},{18,... | collective-permute-start | bytes 786440 | tf_op jit(solution)/shard_map/ppermute | solution.py:592
  58.0 1.2 %collective-permute-start.7 = (s32[8,256]{1,0:T(8,128)S(1)}, s32[8,256]{1,0:T(8,128)S(1)}, u32[]{:S(2)}, u32[]{:S(2)}) collective-permute-start(s32[8,256]{1,0:T(8,128)S(1)} %get-tuple-element.72), channel_id=1, source_target_pairs={{0,4},{4,0},{8,12},{12,8},{16,20},{20,16},{24,28},{28,24},{1,5},{5... | collective-permute-start | bytes 24584 | tf_op jit(solution)/shard_map/ppermute | solution.py:589
  58.1 14.1 %collective-permute-start.19 = (bf16[256,512]{1,0:T(8,128)(2,1)S(1)}, bf16[256,512]{1,0:T(8,128)(2,1)S(1)}, u32[]{:S(2)}, u32[]{:S(2)}) collective-permute-start(bf16[256,512]{1,0:T(8,128)(2,1)S(1)} %get-tuple-element.69), channel_id=1, source_target_pairs={{1,2},{2,1},{5,6},{6,5},{9,10},{10,9},{13,14},{14,13},{17,18},{18,... | collective-permute-start | bytes 786440 | tf_op jit(solution)/shard_map/ppermute | solution.py:592
  59.2 3.7 %collective-permute-start.8 = (s32[16,256]{1,0:T(8,128)S(1)}, s32[16,256]{1,0:T(8,128)S(1)}, u32[]{:S(2)}, u32[]{:S(2)}) collective-permute-start(s32[16,256]{1,0:T(8,128)S(1)} %pad_add_fusion.1), channel_id=1, source_target_pairs={{0,8},{4,12},{8,0},{12,4},{16,24},{20,28},{24,16},{28,20},{1,9},{5... | collective-permute-start | bytes 49160 | tf_op jit(solution)/shard_map/ppermute | solution.py:589
  63.0 11.2 %collective-permute-start.9 = (s32[32,256]{1,0:T(8,128)S(1)}, s32[32,256]{1,0:T(8,128)S(1)}, u32[]{:S(2)}, u32[]{:S(2)}) collective-permute-start(s32[32,256]{1,0:T(8,128)S(1)} %pad_add_fusion), channel_id=1, source_target_pairs={{0,16},{4,20},{8,24},{12,28},{16,0},{20,4},{24,8},{28,12},{1,17},{... | collective-permute-start | bytes 98312 | tf_op jit(solution)/shard_map/ppermute | solution.py:589
  67.0 21.0 %collective-permute-start.16 = (bf16[256,256]{1,0:T(8,128)(2,1)S(1)}, bf16[256,256]{1,0:T(8,128)(2,1)S(1)}, u32[]{:S(2)}, u32[]{:S(2)}) collective-permute-start(bf16[256,256]{1,0:T(8,128)(2,1)S(1)} %get-tuple-element.83), channel_id=1, source_target_pairs={{1,0},{2,3},{5,4},{6,7},{9,8},{10,11},{13,12},{14,15},{17,16},{18,... | collective-permute-start | bytes 393224 | tf_op jit(solution)/shard_map/ppermute | solution.py:592
  69.0 21.9 %collective-permute-start.13 = (bf16[256,256]{1,0:T(8,128)(2,1)S(1)}, bf16[256,256]{1,0:T(8,128)(2,1)S(1)}, u32[]{:S(2)}, u32[]{:S(2)}) collective-permute-start(bf16[256,256]{1,0:T(8,128)(2,1)S(1)} %get-tuple-element.79), channel_id=1, source_target_pairs={{1,0},{2,3},{5,4},{6,7},{9,8},{10,11},{13,12},{14,15},{17,16},{18,... | collective-permute-start | bytes 393224 | tf_op jit(solution)/shard_map/ppermute | solution.py:592
  70.9 22.7 %collective-permute-start.18 = (bf16[256,256]{1,0:T(8,128)(2,1)S(1)}, bf16[256,256]{1,0:T(8,128)(2,1)S(1)}, u32[]{:S(2)}, u32[]{:S(2)}) collective-permute-start(bf16[256,256]{1,0:T(8,128)(2,1)S(1)} %get-tuple-element.86), channel_id=1, source_target_pairs={{1,0},{2,3},{5,4},{6,7},{9,8},{10,11},{13,12},{14,15},{17,16},{18,... | collective-permute-start | bytes 393224 | tf_op jit(solution)/shard_map/ppermute | solution.py:592
  72.8 22.4 %collective-permute-start.20 = (bf16[256,256]{1,0:T(8,128)(2,1)S(1)}, bf16[256,256]{1,0:T(8,128)(2,1)S(1)}, u32[]{:S(2)}, u32[]{:S(2)}) collective-permute-start(bf16[256,256]{1,0:T(8,128)(2,1)S(1)} %get-tuple-element.89), channel_id=1, source_target_pairs={{1,0},{2,3},{5,4},{6,7},{9,8},{10,11},{13,12},{14,15},{17,16},{18,... | collective-permute-start | bytes 393224 | tf_op jit(solution)/shard_map/ppermute | solution.py:592
  96.7 11.6 %collective-permute-start.22 = (bf16[256,256]{1,0:T(8,128)(2,1)S(1)}, bf16[256,256]{1,0:T(8,128)(2,1)S(1)}, u32[]{:S(2)}, u32[]{:S(2)}) collective-permute-start(bf16[256,256]{1,0:T(8,128)(2,1)S(1)} %get-tuple-element.93), channel_id=1, source_target_pairs={{0,16},{4,20},{8,24},{12,28},{16,0},{20,4},{24,8},{28,12},{1,17},{... | collective-permute-start | bytes 393224 | tf_op jit(solution)/shard_map/ppermute | solution.py:589
  96.8 13.3 %collective-permute-start.23 = (bf16[256,256]{1,0:T(8,128)(2,1)S(1)}, bf16[256,256]{1,0:T(8,128)(2,1)S(1)}, u32[]{:S(2)}, u32[]{:S(2)}) collective-permute-start(bf16[256,256]{1,0:T(8,128)(2,1)S(1)} %get-tuple-element.94), channel_id=1, source_target_pairs={{0,20},{4,16},{8,28},{12,24},{16,4},{20,0},{24,12},{28,8},{1,21},{... | collective-permute-start | bytes 393224 | tf_op jit(solution)/shard_map/ppermute | solution.py:589
  96.9 13.9 %collective-permute-start.24 = (bf16[256,256]{1,0:T(8,128)(2,1)S(1)}, bf16[256,256]{1,0:T(8,128)(2,1)S(1)}, u32[]{:S(2)}, u32[]{:S(2)}) collective-permute-start(bf16[256,256]{1,0:T(8,128)(2,1)S(1)} %get-tuple-element.95), channel_id=1, source_target_pairs={{0,24},{4,28},{8,16},{12,20},{16,8},{20,12},{24,0},{28,4},{1,25},{... | collective-permute-start | bytes 393224 | tf_op jit(solution)/shard_map/ppermute | solution.py:589
  99.8 11.1 %collective-permute-start.25 = (bf16[256,256]{1,0:T(8,128)(2,1)S(1)}, bf16[256,256]{1,0:T(8,128)(2,1)S(1)}, u32[]{:S(2)}, u32[]{:S(2)}) collective-permute-start(bf16[256,256]{1,0:T(8,128)(2,1)S(1)} %get-tuple-element.96), channel_id=1, source_target_pairs={{0,28},{4,24},{8,20},{12,16},{16,12},{20,8},{24,4},{28,0},{1,29},{... | collective-permute-start | bytes 393224 | tf_op jit(solution)/shard_map/ppermute | solution.py:589
  101.1 14.7 %copy-start.2 = (f32[1024]{0:T(1024)S(1)}, f32[1024]{0:T(1024)}, u32[]{:S(2)}) copy-start(f32[1024]{0:T(1024)} %param.15) | copy-start | bytes 12292
  102.7 8.2 %collective-permute-start.21 = (bf16[256,256]{1,0:T(8,128)(2,1)S(1)}, bf16[256,256]{1,0:T(8,128)(2,1)S(1)}, u32[]{:S(2)}, u32[]{:S(2)}) collective-permute-start(bf16[256,256]{1,0:T(8,128)(2,1)S(1)} %get-tuple-element.92), channel_id=1, source_target_pairs={{0,4},{4,0},{8,12},{12,8},{16,20},{20,16},{24,28},{28,24},{1,5},{5... | collective-permute-start | bytes 393224 | tf_op jit(solution)/shard_map/ppermute | solution.py:589
  108.2 5.3 %collective-permute-start.26 = (bf16[256,256]{1,0:T(8,128)(2,1)S(1)}, bf16[256,256]{1,0:T(8,128)(2,1)S(1)}, u32[]{:S(2)}, u32[]{:S(2)}) collective-permute-start(bf16[256,256]{1,0:T(8,128)(2,1)S(1)} %get-tuple-element.97), channel_id=1, source_target_pairs={{0,8},{4,12},{8,0},{12,4},{16,24},{20,28},{24,16},{28,20},{1,9},{5... | collective-permute-start | bytes 393224 | tf_op jit(solution)/shard_map/ppermute | solution.py:589
  110.0 5.8 %collective-permute-start.27 = (bf16[256,256]{1,0:T(8,128)(2,1)S(1)}, bf16[256,256]{1,0:T(8,128)(2,1)S(1)}, u32[]{:S(2)}, u32[]{:S(2)}) collective-permute-start(bf16[256,256]{1,0:T(8,128)(2,1)S(1)} %get-tuple-element.98), channel_id=1, source_target_pairs={{0,12},{4,8},{8,4},{12,0},{16,28},{20,24},{24,20},{28,16},{1,13},{... | collective-permute-start | bytes 393224 | tf_op jit(solution)/shard_map/ppermute | solution.py:589

commit v4 on v3

--- a/solution.py
+++ b/solution.py
@@ -6,9 +6,10 @@
 from jax.sharding import PartitionSpec as P
 
 
+VIEWS, HEADS = "views", "heads"
 HEAD_DIM = 64
 LANES = 128
-VIEW_ORDER = (1, 2, 0, 3)
+CHUNKS = dict(a=(1, 2), b=(0,), c=(3,))
 
 coupling = 0.5
 epsilon = 1e-06
@@ -79,14 +80,19 @@
 
         gain_copy.wait()
         following = load_norm(0)
-        for part in order:
-            w_copies[part].wait()
         for i in range(count):
             normed = following
-            if i + 1 < count:
+            if i == 0:
+                w_copies[2].wait()
+            elif i + 1 < count:
                 following = load_norm(i + 1)
             values = dot(normed, ws[2])
+            if i == 0:
+                w_copies[0].wait()
             queries = dot(normed, ws[0])
+            if i == 0:
+                w_copies[1].wait()
+                following = load_norm(i + 1)
             outs[2 * i + 1][0] = dot(normed, ws[1]).astype(bf16)
             outs[2 * i + 1][1] = jnp.transpose(values).astype(bf16)
             outs[2 * i][...] = jnp.transpose(queries).astype(bf16) * jnp.asarray(scale, bf16)
@@ -113,7 +119,7 @@
             pltpu.VMEM((3, width, sub), bf16),
             pltpu.SemaphoreType.DMA((2 * count + 5,)),
         ],
-        name="project_views",
+        name="proj",
         compiler_params=grant(52),
         cost_estimate=cost(
             count * 6 * tokens * width * sub, count * tokens * (width + 3 * sub) * 2 + 6 * width * sub
@@ -278,7 +284,7 @@
         out_specs=many(VMEM_SPEC, len(out_shape)),
         out_shape=out_shape,
         scratch_shapes=scratch,
-        name="attend" if last else "attend_local",
+        name="att",
         compiler_params=grant(12),
         cost_estimate=attention_cost(tokens, sub, pairs),
     )(
@@ -321,8 +327,9 @@
     lax.fori_loop(0, heads, one_head, 0)
 
 
-def partial_out(meta, attended, near, w_own, w_mine, w_theirs, halves, place):
-    tokens, sub = attended.shape
+def partial_out(meta, attended, near, w_own, w_mine, w_theirs, halves, places):
+    sub = attended.shape[-1]
+    rows_all = attended.size // sub
     width = w_own.shape[1]
     half = width // 2
 
@@ -332,33 +339,37 @@
         away = pl.ds(pl.multiple_of((1 - side) * half, half), half)
         second = meta_ref[0] % 2
         strip = sub // 2
-        mine = near_ref[:, pl.ds(pl.multiple_of(second * strip, strip), strip)]
-        theirs = near_ref[:, pl.ds(pl.multiple_of((1 - second) * strip, strip), strip)]
-        rows = jnp.concatenate([att[...], mine, theirs], axis=1)
+        lead = (slice(None),) * (len(attended.shape) - 1)
+        mine = near_ref[lead + (pl.ds(pl.multiple_of(second * strip, strip), strip),)]
+        theirs = near_ref[lead + (pl.ds(pl.multiple_of((1 - second) * strip, strip), strip),)]
+        rows = jnp.concatenate(
+            [x.reshape(rows_all, x.shape[-1]) for x in (att[...], mine, theirs)], axis=1
+        )
 
         def columns(at):
             return jnp.concatenate([own_ref[:, at], mine_ref[:, at], theirs_ref[:, at]], axis=0)
 
         send[...] = dot(rows, columns(away)).astype(bf16)
         total = dot(rows, columns(here))
-        keep[...] = halves_ref[place].astype(f32) + total
+        base = jnp.concatenate([halves_ref[p] for p in places], axis=0)
+        keep[...] = base.astype(f32) + total
 
     return pl.pallas_call(
         body,
         in_specs=[SMEM_SPEC] + many(VMEM_SPEC, 6),
         out_specs=many(VMEM_SPEC, 2),
         out_shape=[
-            jax.ShapeDtypeStruct((tokens, half), f32),
-            jax.ShapeDtypeStruct((tokens, half), bf16),
+            jax.ShapeDtypeStruct((rows_all, half), f32),
+            jax.ShapeDtypeStruct((rows_all, half), bf16),
         ],
-        name="partial_out",
+        name="part",
         compiler_params=grant(12),
-        cost_estimate=cost(4 * tokens * sub * width, 4 * sub * width + tokens * width * 6),
+        cost_estimate=cost(4 * rows_all * sub * width, 4 * sub * width + rows_all * width * 6),
     )(meta, attended, near, w_own, w_mine, w_theirs, halves)
 
 
 def merge_out(meta, keep, got):
-    tokens, half = keep.shape
+    rows_all, half = keep.shape
     sub = half // 2
 
     def body(meta_ref, keep_ref, got_ref, own, other):
@@ -372,10 +383,10 @@
         body,
         in_specs=[SMEM_SPEC] + many(VMEM_SPEC, 2),
         out_specs=many(VMEM_SPEC, 2),
-        out_shape=[jax.ShapeDtypeStruct((tokens, sub), bf16)] * 2,
-        name="merge_out",
+        out_shape=[jax.ShapeDtypeStruct((rows_all, sub), bf16)] * 2,
+        name="merge",
         compiler_params=grant(8),
-        cost_estimate=cost(tokens * half * 2, tokens * half * 8),
+        cost_estimate=cost(rows_all * half * 2, rows_all * half * 8),
     )(meta, keep, got)
 
 
@@ -418,7 +429,7 @@
             jax.ShapeDtypeStruct((peers, capacity), jnp.int32),
             jax.ShapeDtypeStruct((strips, lanes), jnp.int32),
         ],
-        name="prepare_requests",
+        name="prep",
         compiler_params=grant(8),
         cost_estimate=cost(2 * strips * lanes * lanes * capacity, 3 * strips * lanes * 4),
     )(block_rows, token_rows)
@@ -434,9 +445,9 @@
 def gather_rows(meta, wanted, pieces, masks, tokens):
     peers, capacity = int(round(wanted.shape[0] ** 0.5)), wanted.shape[1]
     whole = not isinstance(pieces, list)
-    flat = [pieces] if whole else [p for pair in pieces for p in pair]
+    flat = [pieces] if whole else [p for _, *pair in pieces for p in pair]
     sub = flat[0].shape[1]
-    rows = flat[0].shape[0] if whole else len(pieces) * tokens
+    rows = flat[0].shape[0] if whole else sum(p.shape[0] for p in flat[::2])
     local_views = rows // tokens
 
     def body(meta_ref, wanted_ref, *refs):
@@ -446,10 +457,12 @@
         else:
             layer, outs = outs[0], outs[1:]
             end = jnp.logical_or(meta_ref[1] == 0, meta_ref[1] == meta_ref[2] - 1)
-            for v in range(local_views):
-                layer[v * tokens : (v + 1) * tokens, :] = jnp.where(
-                    end, ins[2 * v + 1][...], ins[2 * v][...]
-                )
+            for c, (views, _, _) in enumerate(pieces):
+                for i, v in enumerate(views):
+                    at = slice(i * tokens, (i + 1) * tokens)
+                    layer[v * tokens : (v + 1) * tokens, :] = jnp.where(
+                        end, ins[2 * c + 1][at, :], ins[2 * c][at, :]
+                    )
         lines = [wanted_ref[pl.ds(m * peers + meta_ref[0], 1), :] for m in masks]
         lines += [lines[0]] * (-len(lines) % 8)
         columns = jnp.transpose(jnp.concatenate(lines, axis=0).astype(f32))
@@ -468,7 +481,7 @@
         in_specs=[SMEM_SPEC] + many(VMEM_SPEC, 1 + len(flat)),
         out_specs=many(VMEM_SPEC, len(out_shape)),
         out_shape=out_shape,
-        name="gather_rows",
+        name="gath",
         compiler_params=grant(12),
         cost_estimate=cost(
             2 * len(masks) * capacity * rows * sub, 2 * (rows + len(masks) * capacity) * sub * 2
@@ -518,7 +531,7 @@
         in_specs=[SMEM_SPEC] + many(VMEM_SPEC, 1 + len(masks)),
         out_specs=VMEM_SPEC,
         out_shape=jax.ShapeDtypeStruct((rows, sub), bf16),
-        name="first_replies",
+        name="first",
         compiler_params=grant(12),
         cost_estimate=cost(2 * len(masks) * capacity * rows * sub, rows * sub * 4),
     )(meta, code, *[replies[m] for m in masks])
@@ -563,7 +576,7 @@
             pltpu.VMEM((blocks, tokens, sub), f32),
             pltpu.SemaphoreType.DMA((blocks,)),
         ],
-        name="finish_rows",
+        name="fin",
         compiler_params=grant(12),
         cost_estimate=cost(2 * len(masks) * capacity * rows * sub, rows * sub * 8),
     )(meta, code, confidence, layer, early, *[replies[m] for m in masks])
@@ -573,23 +586,23 @@
     local_views, tokens, width = latents.shape
     window = intersection.shape[1]
     sub = w_qkv.shape[2]
-    peers = lax.axis_size("views")
-    ends = lax.axis_size("heads")
+    peers = lax.axis_size(VIEWS)
+    ends = lax.axis_size(HEADS)
     rows = local_views * tokens
     capacity = 2 * rows // peers
     assert local_views == 4 and window == 2 and ends == 4 and tokens == sub
-    view_at, head_at = lax.axis_index("views"), lax.axis_index("heads")
+    view_at, head_at = lax.axis_index(VIEWS), lax.axis_index(HEADS)
     spot = jnp.arange(4, dtype=jnp.int32)
     meta = jnp.where(spot == 0, view_at, jnp.where(spot == 1, head_at, ends)).astype(jnp.int32)
 
     def along(x, by):
-        return lax.ppermute(x, "views", [(i, (i + by) % peers) for i in range(peers)])
+        return lax.ppermute(x, VIEWS, [(i, (i + by) % peers) for i in range(peers)])
 
     def partner(x, mask):
-        return lax.ppermute(x, "views", [(i, i ^ mask) for i in range(peers)])
+        return lax.ppermute(x, VIEWS, [(i, i ^ mask) for i in range(peers)])
 
     def across(x, pairs):
-        return lax.ppermute(x, "heads", pairs)
+        return lax.ppermute(x, HEADS, pairs)
 
     def after(x, done):
         return lax.optimization_barrier((x, done))[0]
@@ -597,27 +610,36 @@
     beside, middle, back = [(0, 1), (3, 2)], [(1, 2), (2, 1)], [(1, 0), (2, 3)]
     gain = norm_gain.reshape(1, width)
     inter = intersection.T
-    loaded = (0, local_views - 1, 1, 2)
+    loaded = (0, 3, 1, 2)
     projected, halves, w_half = project_views(meta, latents, gain, w_qkv, w_out, loaded)
     queries = {v: projected[v][0] for v in range(local_views)}
     blocks = {v: projected[v][1] for v in range(local_views)}
-    next_first = along(blocks[0], -1)
-    prev_last = along(blocks[3], 1)
+    far = {}
+    far["n1"] = along(blocks[0], -1)
+    far["p1"] = along(blocks[3], 1)
     w_mine = across(w_half, beside)
 
-    inner_plan = [(1, [("prev_last", -1, 1)]), (2, [("next_first", 2, 1)])]
+    inner_plan = [(1, [("p1", -1, 1)]), (2, [("n1", 2, 1)])]
     inner_queries = [queries[1], queries[2]]
     local = attend(
         meta, inter, inner_queries, blocks, {}, [(v, []) for v, _ in inner_plan], window, last=False
     )
-    next_second = along(after(blocks[1], local[0]), -1)
-    prev_second = along(after(blocks[2], local[0]), 1)
-    remote = dict(prev_last=prev_last, next_first=next_first)
-    inner = attend(
-        meta, inter, inner_queries, blocks, remote, inner_plan, window, earlier=tuple(local)
-    )
-    w_theirs = partner(after(w_mine, inner[0]), 1)
-    sent = {}
+    inner_far = dict(far)
+    far["n2"] = along(after(blocks[1], local[0]), -1)
+    far["p2"] = along(after(blocks[2], local[0]), 1)
+    attended = {}
+    (attended["a"],) = attend(
+        meta,
+        inter,
+        inner_queries,
+        blocks,
+        inner_far,
+        inner_plan,
+        window,
+        earlier=tuple(local),
+        merged=True,
+    )
+    w_theirs = partner(after(w_mine, attended["a"]), 1)
 
     def attend_outer(view, sources, done):
         (result,) = attend(
@@ -625,32 +647,36 @@
             inter,
             [after(queries[view], done)],
             blocks,
-            {k: x for k, x in halo.items() if k in [s[0] for s in sources]},
+            {s[0]: far[s[0]] for s in sources},
             [(view, sources)],
             window,
         )
         return result
 
-    halo = dict(remote, prev_second=prev_second, next_second=next_second)
-    attended = {1: inner[0], 2: inner[1]}
-    attended[0] = attend_outer(0, [("prev_last", -1, 0), ("prev_second", -2, 1)], inner[0])
-    keep, got, formed = {}, {}, {}
-
-    def pass_on(v):
-        near = across(attended[v], beside)
-        keep[v], sent[v] = partial_out(
-            meta, attended[v], near, w_out, w_mine, w_theirs, halves, loaded.index(v)
+    keep, sent, got = {}, {}, {}
+
+    def pass_on(c):
+        near = across(attended[c], beside)
+        keep[c], sent[c] = partial_out(
+            meta,
+            attended[c],
+            near,
+            w_out,
+            w_mine,
+            w_theirs,
+            halves,
+            [loaded.index(v) for v in CHUNKS[c]],
         )
-        got[v] = across(sent[v], middle)
-
-    pass_on(1)
-    pass_on(2)
-    attended[3] = attend_outer(3, [("next_first", 3, 0), ("next_second", 3, 1)], sent[2])
-    pass_on(0)
-    pass_on(3)
+        got[c] = across(sent[c], middle)
+
+    attended["b"] = attend_outer(0, [("p1", -1, 0), ("p2", -2, 1)], attended["a"])
+    pass_on("a")
+    attended["c"] = attend_outer(3, [("n1", 3, 0), ("n2", 3, 1)], sent["a"])
+    pass_on("b")
+    pass_on("c")
     strips = rows // LANES
     wanted, code = prepare_requests(
-        after(match_block.reshape(strips, LANES), sent[3]),
+        after(match_block.reshape(strips, LANES), sent["c"]),
         match_row.reshape(strips, LANES),
         peers,
         capacity,
@@ -659,11 +685,11 @@
     while mask < peers:
         wanted = jnp.concatenate([wanted, partner(wanted, mask)], axis=0)
         mask *= 2
-    for v in VIEW_ORDER:
-        own, other = merge_out(meta, keep[v], got[v])
-        formed[v] = (own, across(other, back))
-
-    pieces = [formed[v] for v in range(local_views)]
+    pieces = []
+    for c in CHUNKS:
+        own, other = merge_out(meta, keep[c], got[c])
+        pieces.append((CHUNKS[c], own, across(other, back)))
+
     first_masks, last_masks = reply_order(peers)
     replies = {}
 
@@ -700,16 +726,16 @@
 
 def solution(mesh):
     in_specs = (
-        P("views", None, None),
+        P(VIEWS, None, None),
         P(),
-        P(None, None, "heads"),
-        P("heads", None),
+        P(None, None, HEADS),
+        P(HEADS, None),
         P(),
-        P("views", None),
-        P("views"),
-        P("views"),
-    )
-    out_specs = P("views", None, "heads")
+        P(VIEWS, None),
+        P(VIEWS),
+        P(VIEWS),
+    )
+    out_specs = P(VIEWS, None, HEADS)
     return jax.shard_map(
         per_device, mesh=mesh, in_specs=in_specs, out_specs=out_specs, check_vma=False
     )

time: 118 us -> 111 us (0.941)
  waiting for transfers between devices: 35.2 us -> 27 us
  starting transfers between devices: 52.7 us -> 55.2 us
    ppermute x28 -> x25, waiting for transfers between devices: 35.2 us -> 27 us  [the longest x10 15.1 us: across(): return lax.ppermute(x, HEADS, pairs)]
    ppermute x28 -> x25, starting transfers between devices: 52.7 us -> 55.2 us  [the longest x10 25.8 us: across(): return lax.ppermute(x, HEADS, pairs)]
    pallas_call x4 -> x3, Pallas kernels: 3.97 us -> 3.24 us  [partial_out(): pl.pallas_call(body, in_specs=[SMEM_SPEC] + many(VMEM_SPEC, 6), out_specs...]
    pallas_call x4 -> x3, Pallas kernels: 2.42 us -> 1.88 us  [merge_out(): pl.pallas_call(body, in_specs=[SMEM_SPEC] + many(VMEM_SPEC, 2), out_specs...]
  transfers between devices with their start and end apart: 28 -> 25, of which waited for: 10 -> 9; matrix products, arithmetic and copies ran while one was open for 0% -> 0% of each run, Pallas kernels for 16% -> 16%
where the time goes in v4:
time: 111 us
  starting transfers between devices  55.2 us (50%)
  Pallas kernels  27.7 us (25%)
  waiting for transfers between devices  27 us (24%)
    ppermute x10, starting transfers between devices, across(): return lax.ppermute(x, HEADS, pairs)  25.8 us
    ppermute x11, starting transfers between devices, partner(): return lax.ppermute(x, VIEWS, [(i, i ^ mask) for i in range(peers)])  15.5 us
    ppermute x10, waiting for transfers between devices, across(): return lax.ppermute(x, HEADS, pairs)  15.1 us
    ppermute x4, starting transfers between devices, along(): return lax.ppermute(x, VIEWS, [(i, (i + by) % peers) for i in range(peers)])  13.9 us
    ppermute x11, waiting for transfers between devices, partner(): return lax.ppermute(x, VIEWS, [(i, i ^ mask) for i in range(peers)])  10.7 us
    pallas_call x4, Pallas kernels, attend(): pl.pallas_call(body, in_specs=[SMEM_SPEC, SMEM_SPEC] + many(VMEM_SPEC, he...  9.01 us
    pallas_call x1, Pallas kernels, project_views(): pl.pallas_call(body, in_specs=[SMEM_SPEC] + many(ANY_SPEC, 4), out_specs=...  6.02 us
    pallas_call x3, Pallas kernels, partial_out(): pl.pallas_call(body, in_specs=[SMEM_SPEC] + many(VMEM_SPEC, 6), out_specs...  3.24 us
  transfers between devices with their start and end apart: 25, of which 9 were waited for; matrix products, arithmetic and copies ran while one was open for 0% of the time, Pallas kernels for 16%

profile of v4, /device:TPU:0, one launch (start us, length us, event | category | flops | bytes accessed | tf_op | source)
XLA Modules:
  0.0 111.1 jit_solution(18124695671599504254)
XLA Ops:
  0.0 0.7 copy-done.4
  0.7 6.0 %proj.1 = (bf16[256,256]{1,0:T(8,128)(2,1)S(1)}, bf16[2,256,256]{2,1,0:T(8,128)(2,1)S(1)}, bf16[256,256]{1,0:T(8,128)(2,1)S(1)}, bf16[2,256,256]{2,1,0:T(8,128)(...) custom-call(s32[4]{0:T(128)S(1)} %compare_select_fusion.1.meta_ref, ...), custom_call_target="tpu_custom_call" | custom-call | flops 1610612736 | bytes 5242880 | tf_op jit(solution)/shard_map/proj/pallas_call | solution.py:111
  6.7 3.4 %collective-permute-start = (bf16[2,256,256]{2,1,0:T(8,128)(2,1)S(1)}, bf16[2,256,256]{2,1,0:T(8,128)(2,1)S(1)}, u32[]{:S(2)}, u32[]{:S(2)}) collective-permute-start(bf16[2,256,256]{2,1,0:T(8,128)(2,1)S(1)} %get-tuple-element.49.refs_2_.refs_4_.refs_1_), channel_id=1, source_target_pairs={{0,28},{4,0},{8,4},{12,8},{16,12},{20,16},{24,20},{28,24},{1,29},{... | collective-permute-start | bytes 786440 | tf_op jit(solution)/shard_map/ppermute | solution.py:599
  10.1 3.5 %collective-permute-start.3 = (bf16[128,1024]{1,0:T(8,128)(2,1)S(1)}, bf16[128,1024]{1,0:T(8,128)(2,1)S(1)}, u32[]{:S(2)}, u32[]{:S(2)}) collective-permute-start(bf16[128,1024]{1,0:T(8,128)(2,1)S(1)} %get-tuple-element.55), channel_id=1, source_target_pairs={{0,1},{3,2},{4,5},{7,6},{8,9},{11,10},{12,13},{15,14},{16,17},{19,... | collective-permute-start | bytes 786440 | tf_op jit(solution)/shard_map/ppermute | solution.py:605
  13.6 2.9 %att.4 = (f32[2,320,256]{2,1,0:T(8,128)S(1)}, f32[2,4,256]{2,1,0:T(4,128)S(1)}) custom-call(s32[4]{0:T(128)S(1)} %compare_select_fusion.1.meta_ref, s32[2,32]{1,0:T(2,128)S(1)} %bitcast.7, bf16[256,256]{1,0:T(8,128)(2,1)S(1)} %get-tuple-element.47.refs_0_.refs_2_, bf16[256,256]{1,0:T(8,128)(2,1)S(1)} %get-tuple-element.48.refs_1_.refs_3_, ...), custom_call_target="tpu_custom_call" | custom-call | flops 1073741824 | bytes 4194304 | tf_op jit(solution)/shard_map/att/pallas_call | solution.py:280
  16.6 0.1 collective-permute-start.12
  16.7 1.2 %collective-permute-done.1.refs_9_.refs_5_ = bf16[2,256,256]{2,1,0:T(8,128)(2,1)S(1)} collective-permute-done((bf16[2,256,256]{2,1,0:T(8,128)(2,1)S(1)}, bf16[2,256,256]{2,1,0:T(8,128)(2,1)S(1)}, u32[]{:S(2)}, u32[]{:S(2)}) %collective-permute-start.1) | collective-permute-done | bytes 262176 | tf_op jit(solution)/shard_map/ppermute | solution.py:599
  17.9 1.7 %att.5 = bf16[2,256,256]{2,1,0:T(8,128)(2,1)S(1)} custom-call(s32[4]{0:T(128)S(1)} %compare_select_fusion.1.meta_ref, s32[2,32]{1,0:T(2,128)S(1)} %bitcast.8, f32[2,320,256]{2,1,0:T(8,128)S(1)} %get-tuple-element.53.refs_0_, f32[2,4,256]{2,1,0:T(4,128)S(1)} %get-tuple-element.54.refs_1_, bf16[256,256]{1,0:T(8,128)(2,1)S(1)} %get-tuple-element.47.refs_0_.refs_2_, ...), custom_call_target="tpu_custom_call" | custom-call | flops 268435456 | bytes 1048576 | tf_op jit(solution)/shard_map/att/pallas_call | solution.py:280
  19.6 0.1 collective-permute-start.4
  19.7 10.6 %collective-permute-start.2 = (bf16[2,256,256]{2,1,0:T(8,128)(2,1)S(1)}, bf16[2,256,256]{2,1,0:T(8,128)(2,1)S(1)}, u32[]{:S(2)}, u32[]{:S(2)}) collective-permute-start(bf16[2,256,256]{2,1,0:T(8,128)(2,1)S(1)} %att.5), channel_id=1, source_target_pairs={{0,1},{3,2},{4,5},{7,6},{8,9},{11,10},{12,13},{15,14},{16,17},{19,... | collective-permute-start | bytes 786440 | tf_op jit(solution)/shard_map/ppermute | solution.py:605
  30.3 10.4 %collective-permute-start.5 = (bf16[2,256,256]{2,1,0:T(8,128)(2,1)S(1)}, bf16[2,256,256]{2,1,0:T(8,128)(2,1)S(1)}, u32[]{:S(2)}, u32[]{:S(2)}) collective-permute-start(bf16[2,256,256]{2,1,0:T(8,128)(2,1)S(1)} %get-tuple-element.60.refs_3_.refs_5_.refs_2_), channel_id=1, source_target_pairs={{0,28},{4,0},{8,4},{12,8},{16,12},{20,16},{24,20},{28,24},{1,29},{... | collective-permute-start | bytes 786440 | tf_op jit(solution)/shard_map/ppermute | solution.py:599
  40.7 2.2 %att.7 = bf16[256,256]{1,0:T(8,128)(2,1)S(1)} custom-call(s32[4]{0:T(128)S(1)} %compare_select_fusion.1.meta_ref, s32[2,32]{1,0:T(2,128)S(1)} %bitcast.9, bf16[256,256]{1,0:T(8,128)(2,1)S(1)} %get-tuple-element.69.refs_0_, bf16[2,256,256]{2,1,0:T(8,128)(2,1)S(1)} %get-tuple-element.49.refs_2_.refs_4_.refs_1_, ...), custom_call_target="tpu_custom_call" | custom-call | flops 671088640 | bytes 2621440 | tf_op jit(solution)/shard_map/att/pallas_call | solution.py:280
  42.9 1.6 %collective-permute-start.13 = (bf16[256,256]{1,0:T(8,128)(2,1)S(1)}, bf16[256,256]{1,0:T(8,128)(2,1)S(1)}, u32[]{:S(2)}, u32[]{:S(2)}) collective-permute-start(bf16[256,256]{1,0:T(8,128)(2,1)S(1)} %att.7), channel_id=1, source_target_pairs={{0,1},{3,2},{4,5},{7,6},{8,9},{11,10},{12,13},{15,14},{16,17},{19,... | collective-permute-start | bytes 393224 | tf_op jit(solution)/shard_map/ppermute | solution.py:605
  44.5 1.3 %part.3 = (f32[512,512]{1,0:T(8,128)S(1)}, bf16[512,512]{1,0:T(8,128)(2,1)S(1)}) custom-call(s32[4]{0:T(128)S(1)} %compare_select_fusion.1.meta_ref, bf16[2,256,256]{2,1,0:T(8,128)(2,1)S(1)} %att.5, bf16[2,256,256]{2,1,0:T(8,128)(2,1)S(1)} %collective-permute-done.2.near_ref, bf16[256,1024]{1,0:T(8,128)(2,1)S(1)} %copy-done.1, ...), custom_call_target="tpu_custom_call" | custom-call | flops 536870912 | bytes 4194304 | tf_op jit(solution)/shard_map/part/pallas_call | solution.py:357
  45.8 0.9 collective-permute-start.10
  46.7 2.2 %att.6 = bf16[256,256]{1,0:T(8,128)(2,1)S(1)} custom-call(s32[4]{0:T(128)S(1)} %compare_select_fusion.1.meta_ref, s32[2,32]{1,0:T(2,128)S(1)} %bitcast.10, bf16[256,256]{1,0:T(8,128)(2,1)S(1)} %get-tuple-element.59.refs_0_, bf16[2,256,256]{2,1,0:T(8,128)(2,1)S(1)} %get-tuple-element.49.refs_2_.refs_4_.refs_1_, ...), custom_call_target="tpu_custom_call" | custom-call | flops 671088640 | bytes 2621440 | tf_op jit(solution)/shard_map/att/pallas_call | solution.py:280
  48.9 0.0 copy-start.6
  48.9 4.1 %collective-permute-start.6 = (bf16[256,256]{1,0:T(8,128)(2,1)S(1)}, bf16[256,256]{1,0:T(8,128)(2,1)S(1)}, u32[]{:S(2)}, u32[]{:S(2)}) collective-permute-start(bf16[256,256]{1,0:T(8,128)(2,1)S(1)} %att.6), channel_id=1, source_target_pairs={{0,1},{3,2},{4,5},{7,6},{8,9},{11,10},{12,13},{15,14},{16,17},{19,... | collective-permute-start | bytes 393224 | tf_op jit(solution)/shard_map/ppermute | solution.py:605
  53.0 1.0 part.5
  54.0 0.7 collective-permute-start.14
  54.7 0.8 collective-permute-done.6.near_ref
  55.5 1.0 part.4
  56.5 0.7 prep.1
  57.2 0.7 collective-permute-start.16
  57.9 0.5 collective-permute-done.7
  58.4 3.4 %collective-permute-start.8 = (s32[16,256]{1,0:T(8,128)S(1)}, s32[16,256]{1,0:T(8,128)S(1)}, u32[]{:S(2)}, u32[]{:S(2)}) collective-permute-start(s32[16,256]{1,0:T(8,128)S(1)} %pad_add_fusion.1), channel_id=1, source_target_pairs={{0,8},{4,12},{8,0},{12,4},{16,24},{20,28},{24,16},{28,20},{1,9},{5... | collective-permute-start | bytes 49160 | tf_op jit(solution)/shard_map/ppermute | solution.py:602
  61.8 0.7 merge.3
  62.5 1.3 %collective-permute-start.11 = (bf16[512,256]{1,0:T(8,128)(2,1)S(1)}, bf16[512,256]{1,0:T(8,128)(2,1)S(1)}, u32[]{:S(2)}, u32[]{:S(2)}) collective-permute-start(bf16[512,256]{1,0:T(8,128)(2,1)S(1)} %get-tuple-element.67), channel_id=1, source_target_pairs={{1,0},{2,3},{5,4},{6,7},{9,8},{10,11},{13,12},{14,15},{17,16},{18,... | collective-permute-start | bytes 786440 | tf_op jit(solution)/shard_map/ppermute | solution.py:605
  63.8 4.7 %collective-permute-start.9 = (s32[32,256]{1,0:T(8,128)S(1)}, s32[32,256]{1,0:T(8,128)S(1)}, u32[]{:S(2)}, u32[]{:S(2)}) collective-permute-start(s32[32,256]{1,0:T(8,128)S(1)} %pad_add_fusion), channel_id=1, source_target_pairs={{0,16},{4,20},{8,24},{12,28},{16,0},{20,4},{24,8},{28,12},{1,17},{... | collective-permute-start | bytes 98312 | tf_op jit(solution)/shard_map/ppermute | solution.py:602
  68.4 0.6 merge.4
  69.1 1.3 %collective-permute-start.15 = (bf16[256,256]{1,0:T(8,128)(2,1)S(1)}, bf16[256,256]{1,0:T(8,128)(2,1)S(1)}, u32[]{:S(2)}, u32[]{:S(2)}) collective-permute-start(bf16[256,256]{1,0:T(8,128)(2,1)S(1)} %get-tuple-element.74), channel_id=1, source_target_pairs={{1,0},{2,3},{5,4},{6,7},{9,8},{10,11},{13,12},{14,15},{17,16},{18,... | collective-permute-start | bytes 393224 | tf_op jit(solution)/shard_map/ppermute | solution.py:605
  70.4 0.6 merge.5
  71.0 1.3 %collective-permute-start.17 = (bf16[256,256]{1,0:T(8,128)(2,1)S(1)}, bf16[256,256]{1,0:T(8,128)(2,1)S(1)}, u32[]{:S(2)}, u32[]{:S(2)}) collective-permute-start(bf16[256,256]{1,0:T(8,128)(2,1)S(1)} %get-tuple-element.77), channel_id=1, source_target_pairs={{1,0},{2,3},{5,4},{6,7},{9,8},{10,11},{13,12},{14,15},{17,16},{18,... | collective-permute-start | bytes 393224 | tf_op jit(solution)/shard_map/ppermute | solution.py:605
  72.3 12.4 %collective-permute-done.15.refs_3_ = bf16[256,256]{1,0:T(8,128)(2,1)S(1)} collective-permute-done((bf16[256,256]{1,0:T(8,128)(2,1)S(1)}, bf16[256,256]{1,0:T(8,128)(2,1)S(1)}, u32[]{:S(2)}, u32[]{:S(2)}) %collective-permute-start.15) | collective-permute-done | bytes 131104 | tf_op jit(solution)/shard_map/ppermute | solution.py:605
  84.8 1.8 %collective-permute-done.17.refs_5_ = bf16[256,256]{1,0:T(8,128)(2,1)S(1)} collective-permute-done((bf16[256,256]{1,0:T(8,128)(2,1)S(1)}, bf16[256,256]{1,0:T(8,128)(2,1)S(1)}, u32[]{:S(2)}, u32[]{:S(2)}) %collective-permute-start.17) | collective-permute-done | bytes 131104 | tf_op jit(solution)/shard_map/ppermute | solution.py:605
  86.6 1.5 %gath.2 = (bf16[1024,256]{1,0:T(8,128)(2,1)S(1)}, bf16[256,256]{1,0:T(8,128)(2,1)S(1)}, bf16[256,256]{1,0:T(8,128)(2,1)S(1)}, bf16[256,256]{1,0:T(8,128)(2,1)S(1)}, bf16[256,256]{1,0:T(8,128)(2,1)S(1)}) custom-call(s32[4]{0:T(128)S(1)} %compare_select_fusion.1.meta_ref, s32[64,256]{1,0:T(8,128)S(1)} %constant_dynamic-update-slice_fusion.wanted_ref, ...), custom_call_target="tpu_custom_call" | custom-call | flops 536870912 | bytes 2097152 | tf_op jit(solution)/shard_map/gath/pallas_call | solution.py:479
  88.1 3.8 %collective-permute-start.19 = (bf16[256,256]{1,0:T(8,128)(2,1)S(1)}, bf16[256,256]{1,0:T(8,128)(2,1)S(1)}, u32[]{:S(2)}, u32[]{:S(2)}) collective-permute-start(bf16[256,256]{1,0:T(8,128)(2,1)S(1)} %get-tuple-element.81), channel_id=1, source_target_pairs={{0,16},{4,20},{8,24},{12,28},{16,0},{20,4},{24,8},{28,12},{1,17},{... | collective-permute-start | bytes 393224 | tf_op jit(solution)/shard_map/ppermute | solution.py:602
  91.9 0.3 collective-permute-start.21
  92.2 2.2 %collective-permute-start.22 = (bf16[256,256]{1,0:T(8,128)(2,1)S(1)}, bf16[256,256]{1,0:T(8,128)(2,1)S(1)}, u32[]{:S(2)}, u32[]{:S(2)}) collective-permute-start(bf16[256,256]{1,0:T(8,128)(2,1)S(1)} %get-tuple-element.84), channel_id=1, source_target_pairs={{0,28},{4,24},{8,20},{12,16},{16,12},{20,8},{24,4},{28,0},{1,29},{... | collective-permute-start | bytes 393224 | tf_op jit(solution)/shard_map/ppermute | solution.py:602
  94.4 1.5 %gath.3 = (bf16[256,256]{1,0:T(8,128)(2,1)S(1)}, bf16[256,256]{1,0:T(8,128)(2,1)S(1)}, bf16[256,256]{1,0:T(8,128)(2,1)S(1)}, bf16[256,256]{1,0:T(8,128)(2,1)S(1)}) custom-call(s32[4]{0:T(128)S(1)} %compare_select_fusion.1.meta_ref, s32[64,256]{1,0:T(8,128)S(1)} %constant_dynamic-update-slice_fusion.wanted_ref, ...), custom_call_target="tpu_custom_call" | custom-call | flops 536870912 | bytes 2097152 | tf_op jit(solution)/shard_map/gath/pallas_call | solution.py:479
  95.9 0.7 collective-permute-start.18
  96.6 4.4 %collective-permute-done.19.refs_2_ = bf16[256,256]{1,0:T(8,128)(2,1)S(1)} collective-permute-done((bf16[256,256]{1,0:T(8,128)(2,1)S(1)}, bf16[256,256]{1,0:T(8,128)(2,1)S(1)}, u32[]{:S(2)}, u32[]{:S(2)}) %collective-permute-start.19) | collective-permute-done | bytes 131104 | tf_op jit(solution)/shard_map/ppermute | solution.py:602
  101.0 0.4 collective-permute-start.23
  101.4 2.0 %collective-permute-done.20.refs_3_ = bf16[256,256]{1,0:T(8,128)(2,1)S(1)} collective-permute-done((bf16[256,256]{1,0:T(8,128)(2,1)S(1)}, bf16[256,256]{1,0:T(8,128)(2,1)S(1)}, u32[]{:S(2)}, u32[]{:S(2)}) %collective-permute-start.20) | collective-permute-done | bytes 131104 | tf_op jit(solution)/shard_map/ppermute | solution.py:602
  103.3 1.7 %first.1.early_ref = bf16[1024,256]{1,0:T(8,128)(2,1)S(1)} custom-call(s32[4]{0:T(128)S(1)} %compare_select_fusion.1.meta_ref, s32[8,128]{1,0:T(8,128)S(1)} %get-tuple-element.63.code_ref, bf16[256,256]{1,0:T(8,128)(2,1)S(1)} %get-tuple-element.79.refs_0_, bf16[256,256]{1,0:T(8,128)(2,1)S(1)} %collective-permute-done.18.refs_1_, ...), custom_call_target="tpu_custom_call" | custom-call | flops 805306368 | bytes 1048576 | tf_op jit(solution)/shard_map/first/pallas_call | solution.py:529
  105.0 0.9 collective-permute-done.23.refs_0_
  105.9 2.9 %collective-permute-done.24.refs_1_ = bf16[256,256]{1,0:T(8,128)(2,1)S(1)} collective-permute-done((bf16[256,256]{1,0:T(8,128)(2,1)S(1)}, bf16[256,256]{1,0:T(8,128)(2,1)S(1)}, u32[]{:S(2)}, u32[]{:S(2)}) %collective-permute-start.24) | collective-permute-done | bytes 131104 | tf_op jit(solution)/shard_map/ppermute | solution.py:602
  108.9 2.1 %fin.1 = f32[1024,256]{1,0:T(8,128)} custom-call(s32[4]{0:T(128)S(1)} %compare_select_fusion.1.meta_ref, s32[8,128]{1,0:T(8,128)S(1)} %get-tuple-element.63.code_ref, f32[8,128]{1,0:T(8,128)S(1)} %bitcast.6, bf16[1024,256]{1,0:T(8,128)(2,1)S(1)} %get-tuple-element.78.refs_0_.layer_ref, bf16[1024,256]{1,0:T(8,128)(2,1)S(1)} %first.1.early_ref, ...), custom_call_target="tpu_custom_call" | custom-call | flops 268435456 | bytes 2097152 | tf_op jit(solution)/shard_map/fin/pallas_call | solution.py:570
  (39 shorter events, 0.1 us)
Async XLA Ops:
  0.0 0.7 copy-start.4
  0.7 12.9 %copy-start.3 = (s32[32,2]{0,1:T(2,128)S(1)}, s32[32,2]{0,1:T(2,128)}, u32[]{:S(2)}) copy-start(s32[32,2]{0,1:T(2,128)} %param.12) | copy-start | bytes 772
  6.7 9.9 %collective-permute-start = (bf16[2,256,256]{2,1,0:T(8,128)(2,1)S(1)}, bf16[2,256,256]{2,1,0:T(8,128)(2,1)S(1)}, u32[]{:S(2)}, u32[]{:S(2)}) collective-permute-start(bf16[2,256,256]{2,1,0:T(8,128)(2,1)S(1)} %get-tuple-element.49.refs_2_.refs_4_.refs_1_), channel_id=1, source_target_pairs={{0,28},{4,0},{8,4},{12,8},{16,12},{20,16},{24,20},{28,24},{1,29},{... | collective-permute-start | bytes 786440 | tf_op jit(solution)/shard_map/ppermute | solution.py:599
  10.1 7.7 %collective-permute-start.1 = (bf16[2,256,256]{2,1,0:T(8,128)(2,1)S(1)}, bf16[2,256,256]{2,1,0:T(8,128)(2,1)S(1)}, u32[]{:S(2)}, u32[]{:S(2)}) collective-permute-start(bf16[2,256,256]{2,1,0:T(8,128)(2,1)S(1)} %get-tuple-element.52.refs_5_.refs_7_.refs_4_), channel_id=1, source_target_pairs={{0,4},{4,8},{8,12},{12,16},{16,20},{20,24},{24,28},{28,0},{1,5},{5... | collective-permute-start | bytes 786440 | tf_op jit(solution)/shard_map/ppermute | solution.py:599
  10.1 9.5 %collective-permute-start.3 = (bf16[128,1024]{1,0:T(8,128)(2,1)S(1)}, bf16[128,1024]{1,0:T(8,128)(2,1)S(1)}, u32[]{:S(2)}, u32[]{:S(2)}) collective-permute-start(bf16[128,1024]{1,0:T(8,128)(2,1)S(1)} %get-tuple-element.55), channel_id=1, source_target_pairs={{0,1},{3,2},{4,5},{7,6},{8,9},{11,10},{12,13},{15,14},{16,17},{19,... | collective-permute-start | bytes 786440 | tf_op jit(solution)/shard_map/ppermute | solution.py:605
  16.6 24.1 %collective-permute-start.12 = (bf16[2,256,256]{2,1,0:T(8,128)(2,1)S(1)}, bf16[2,256,256]{2,1,0:T(8,128)(2,1)S(1)}, u32[]{:S(2)}, u32[]{:S(2)}) collective-permute-start(bf16[2,256,256]{2,1,0:T(8,128)(2,1)S(1)} %get-tuple-element.70.refs_4_.refs_6_.refs_3_), channel_id=1, source_target_pairs={{0,4},{4,8},{8,12},{12,16},{16,20},{20,24},{24,28},{28,0},{1,5},{5... | collective-permute-start | bytes 786440 | tf_op jit(solution)/shard_map/ppermute | solution.py:599
  17.9 26.6 %copy-start = (bf16[4,256,512]{2,1,0:T(8,128)(2,1)S(1)}, bf16[4,256,512]{2,1,0:T(8,128)(2,1)}, u32[]{:S(2)}) copy-start(bf16[4,256,512]{2,1,0:T(8,128)(2,1)} %get-tuple-element.57.halves_ref) | copy-start | bytes 3145732
  17.9 26.6 %copy-start.1 = (bf16[256,1024]{1,0:T(8,128)(2,1)S(1)}, bf16[256,1024]{1,0:T(8,128)(2,1)}, u32[]{:S(2)}) copy-start(bf16[256,1024]{1,0:T(8,128)(2,1)} %own_ref.5) | copy-start | bytes 1572868
  19.6 24.9 %collective-permute-start.4 = (bf16[128,1024]{1,0:T(8,128)(2,1)S(1)}, bf16[128,1024]{1,0:T(8,128)(2,1)S(1)}, u32[]{:S(2)}, u32[]{:S(2)}) collective-permute-start(bf16[128,1024]{1,0:T(8,128)(2,1)S(1)} %collective-permute-done.3.mine_ref), channel_id=1, source_target_pairs={{0,4},{4,0},{8,12},{12,8},{16,20},{20,16},{24,28},{28,24},{1,5},{5... | collective-permute-start | bytes 786440 | tf_op jit(solution)/shard_map/ppermute | solution.py:602
  19.7 24.8 %collective-permute-start.2 = (bf16[2,256,256]{2,1,0:T(8,128)(2,1)S(1)}, bf16[2,256,256]{2,1,0:T(8,128)(2,1)S(1)}, u32[]{:S(2)}, u32[]{:S(2)}) collective-permute-start(bf16[2,256,256]{2,1,0:T(8,128)(2,1)S(1)} %att.5), channel_id=1, source_target_pairs={{0,1},{3,2},{4,5},{7,6},{8,9},{11,10},{12,13},{15,14},{16,17},{19,... | collective-permute-start | bytes 786440 | tf_op jit(solution)/shard_map/ppermute | solution.py:605
  30.3 16.4 %collective-permute-start.5 = (bf16[2,256,256]{2,1,0:T(8,128)(2,1)S(1)}, bf16[2,256,256]{2,1,0:T(8,128)(2,1)S(1)}, u32[]{:S(2)}, u32[]{:S(2)}) collective-permute-start(bf16[2,256,256]{2,1,0:T(8,128)(2,1)S(1)} %get-tuple-element.60.refs_3_.refs_5_.refs_2_), channel_id=1, source_target_pairs={{0,28},{4,0},{8,4},{12,8},{16,12},{20,16},{24,20},{28,24},{1,29},{... | collective-permute-start | bytes 786440 | tf_op jit(solution)/shard_map/ppermute | solution.py:599
  42.9 10.1 %collective-permute-start.13 = (bf16[256,256]{1,0:T(8,128)(2,1)S(1)}, bf16[256,256]{1,0:T(8,128)(2,1)S(1)}, u32[]{:S(2)}, u32[]{:S(2)}) collective-permute-start(bf16[256,256]{1,0:T(8,128)(2,1)S(1)} %att.7), channel_id=1, source_target_pairs={{0,1},{3,2},{4,5},{7,6},{8,9},{11,10},{12,13},{15,14},{16,17},{19,... | collective-permute-start | bytes 393224 | tf_op jit(solution)/shard_map/ppermute | solution.py:605
  45.8 16.0 %collective-permute-start.10 = (bf16[512,512]{1,0:T(8,128)(2,1)S(1)}, bf16[512,512]{1,0:T(8,128)(2,1)S(1)}, u32[]{:S(2)}, u32[]{:S(2)}) collective-permute-start(bf16[512,512]{1,0:T(8,128)(2,1)S(1)} %get-tuple-element.58), channel_id=1, source_target_pairs={{1,2},{2,1},{5,6},{6,5},{9,10},{10,9},{13,14},{14,13},{17,18},{18,... | collective-permute-start | bytes 1572872 | tf_op jit(solution)/shard_map/ppermute | solution.py:605
  48.8 7.6 %copy-start.5 = (s32[1024,1]{0,1:T(1,128)S(1)}, s32[1024,1]{0,1:T(1,128)}, u32[]{:S(2)}) copy-start(s32[1024,1]{0,1:T(1,128)} %param.13) | copy-start | bytes 12292
  48.9 7.6 %copy-start.6 = (s32[1024]{0:T(1024)S(1)}, s32[1024]{0:T(1024)}, u32[]{:S(2)}) copy-start(s32[1024]{0:T(1024)} %param.14) | copy-start | bytes 12292
  48.9 6.6 %collective-permute-start.6 = (bf16[256,256]{1,0:T(8,128)(2,1)S(1)}, bf16[256,256]{1,0:T(8,128)(2,1)S(1)}, u32[]{:S(2)}, u32[]{:S(2)}) collective-permute-start(bf16[256,256]{1,0:T(8,128)(2,1)S(1)} %att.6), channel_id=1, source_target_pairs={{0,1},{3,2},{4,5},{7,6},{8,9},{11,10},{12,13},{15,14},{16,17},{19,... | collective-permute-start | bytes 393224 | tf_op jit(solution)/shard_map/ppermute | solution.py:605
  54.0 14.5 %collective-permute-start.14 = (bf16[256,512]{1,0:T(8,128)(2,1)S(1)}, bf16[256,512]{1,0:T(8,128)(2,1)S(1)}, u32[]{:S(2)}, u32[]{:S(2)}) collective-permute-start(bf16[256,512]{1,0:T(8,128)(2,1)S(1)} %get-tuple-element.72), channel_id=1, source_target_pairs={{1,2},{2,1},{5,6},{6,5},{9,10},{10,9},{13,14},{14,13},{17,18},{18,... | collective-permute-start | bytes 786440 | tf_op jit(solution)/shard_map/ppermute | solution.py:605
  57.2 1.2 %collective-permute-start.7 = (s32[8,256]{1,0:T(8,128)S(1)}, s32[8,256]{1,0:T(8,128)S(1)}, u32[]{:S(2)}, u32[]{:S(2)}) collective-permute-start(s32[8,256]{1,0:T(8,128)S(1)} %get-tuple-element.64), channel_id=1, source_target_pairs={{0,4},{4,0},{8,12},{12,8},{16,20},{20,16},{24,28},{28,24},{1,5},{5... | collective-permute-start | bytes 24584 | tf_op jit(solution)/shard_map/ppermute | solution.py:602
  57.2 13.2 %collective-permute-start.16 = (bf16[256,512]{1,0:T(8,128)(2,1)S(1)}, bf16[256,512]{1,0:T(8,128)(2,1)S(1)}, u32[]{:S(2)}, u32[]{:S(2)}) collective-permute-start(bf16[256,512]{1,0:T(8,128)(2,1)S(1)} %get-tuple-element.61), channel_id=1, source_target_pairs={{1,2},{2,1},{5,6},{6,5},{9,10},{10,9},{13,14},{14,13},{17,18},{18,... | collective-permute-start | bytes 786440 | tf_op jit(solution)/shard_map/ppermute | solution.py:605
  58.4 5.4 %collective-permute-start.8 = (s32[16,256]{1,0:T(8,128)S(1)}, s32[16,256]{1,0:T(8,128)S(1)}, u32[]{:S(2)}, u32[]{:S(2)}) collective-permute-start(s32[16,256]{1,0:T(8,128)S(1)} %pad_add_fusion.1), channel_id=1, source_target_pairs={{0,8},{4,12},{8,0},{12,4},{16,24},{20,28},{24,16},{28,20},{1,9},{5... | collective-permute-start | bytes 49160 | tf_op jit(solution)/shard_map/ppermute | solution.py:602
  62.5 24.1 %collective-permute-start.11 = (bf16[512,256]{1,0:T(8,128)(2,1)S(1)}, bf16[512,256]{1,0:T(8,128)(2,1)S(1)}, u32[]{:S(2)}, u32[]{:S(2)}) collective-permute-start(bf16[512,256]{1,0:T(8,128)(2,1)S(1)} %get-tuple-element.67), channel_id=1, source_target_pairs={{1,0},{2,3},{5,4},{6,7},{9,8},{10,11},{13,12},{14,15},{17,16},{18,... | collective-permute-start | bytes 786440 | tf_op jit(solution)/shard_map/ppermute | solution.py:605
  63.8 8.5 %collective-permute-start.9 = (s32[32,256]{1,0:T(8,128)S(1)}, s32[32,256]{1,0:T(8,128)S(1)}, u32[]{:S(2)}, u32[]{:S(2)}) collective-permute-start(s32[32,256]{1,0:T(8,128)S(1)} %pad_add_fusion), channel_id=1, source_target_pairs={{0,16},{4,20},{8,24},{12,28},{16,0},{20,4},{24,8},{28,12},{1,17},{... | collective-permute-start | bytes 98312 | tf_op jit(solution)/shard_map/ppermute | solution.py:602
  69.1 15.7 %collective-permute-start.15 = (bf16[256,256]{1,0:T(8,128)(2,1)S(1)}, bf16[256,256]{1,0:T(8,128)(2,1)S(1)}, u32[]{:S(2)}, u32[]{:S(2)}) collective-permute-start(bf16[256,256]{1,0:T(8,128)(2,1)S(1)} %get-tuple-element.74), channel_id=1, source_target_pairs={{1,0},{2,3},{5,4},{6,7},{9,8},{10,11},{13,12},{14,15},{17,16},{18,... | collective-permute-start | bytes 393224 | tf_op jit(solution)/shard_map/ppermute | solution.py:605
  71.0 15.6 %collective-permute-start.17 = (bf16[256,256]{1,0:T(8,128)(2,1)S(1)}, bf16[256,256]{1,0:T(8,128)(2,1)S(1)}, u32[]{:S(2)}, u32[]{:S(2)}) collective-permute-start(bf16[256,256]{1,0:T(8,128)(2,1)S(1)} %get-tuple-element.77), channel_id=1, source_target_pairs={{1,0},{2,3},{5,4},{6,7},{9,8},{10,11},{13,12},{14,15},{17,16},{18,... | collective-permute-start | bytes 393224 | tf_op jit(solution)/shard_map/ppermute | solution.py:605
  88.1 12.8 %collective-permute-start.19 = (bf16[256,256]{1,0:T(8,128)(2,1)S(1)}, bf16[256,256]{1,0:T(8,128)(2,1)S(1)}, u32[]{:S(2)}, u32[]{:S(2)}) collective-permute-start(bf16[256,256]{1,0:T(8,128)(2,1)S(1)} %get-tuple-element.81), channel_id=1, source_target_pairs={{0,16},{4,20},{8,24},{12,28},{16,0},{20,4},{24,8},{28,12},{1,17},{... | collective-permute-start | bytes 393224 | tf_op jit(solution)/shard_map/ppermute | solution.py:602
  91.9 11.4 %collective-permute-start.20 = (bf16[256,256]{1,0:T(8,128)(2,1)S(1)}, bf16[256,256]{1,0:T(8,128)(2,1)S(1)}, u32[]{:S(2)}, u32[]{:S(2)}) collective-permute-start(bf16[256,256]{1,0:T(8,128)(2,1)S(1)} %get-tuple-element.82), channel_id=1, source_target_pairs={{0,20},{4,16},{8,28},{12,24},{16,4},{20,0},{24,12},{28,8},{1,21},{... | collective-permute-start | bytes 393224 | tf_op jit(solution)/shard_map/ppermute | solution.py:602
  91.9 11.4 %collective-permute-start.21 = (bf16[256,256]{1,0:T(8,128)(2,1)S(1)}, bf16[256,256]{1,0:T(8,128)(2,1)S(1)}, u32[]{:S(2)}, u32[]{:S(2)}) collective-permute-start(bf16[256,256]{1,0:T(8,128)(2,1)S(1)} %get-tuple-element.83), channel_id=1, source_target_pairs={{0,24},{4,28},{8,16},{12,20},{16,8},{20,12},{24,0},{28,4},{1,25},{... | collective-permute-start | bytes 393224 | tf_op jit(solution)/shard_map/ppermute | solution.py:602
  92.2 11.1 %collective-permute-start.22 = (bf16[256,256]{1,0:T(8,128)(2,1)S(1)}, bf16[256,256]{1,0:T(8,128)(2,1)S(1)}, u32[]{:S(2)}, u32[]{:S(2)}) collective-permute-start(bf16[256,256]{1,0:T(8,128)(2,1)S(1)} %get-tuple-element.84), channel_id=1, source_target_pairs={{0,28},{4,24},{8,20},{12,16},{16,12},{20,8},{24,4},{28,0},{1,29},{... | collective-permute-start | bytes 393224 | tf_op jit(solution)/shard_map/ppermute | solution.py:602
  94.4 14.5 %copy-start.2 = (f32[1024]{0:T(1024)S(1)}, f32[1024]{0:T(1024)}, u32[]{:S(2)}) copy-start(f32[1024]{0:T(1024)} %param.15) | copy-start | bytes 12292
  95.9 7.4 %collective-permute-start.18 = (bf16[256,256]{1,0:T(8,128)(2,1)S(1)}, bf16[256,256]{1,0:T(8,128)(2,1)S(1)}, u32[]{:S(2)}, u32[]{:S(2)}) collective-permute-start(bf16[256,256]{1,0:T(8,128)(2,1)S(1)} %get-tuple-element.80), channel_id=1, source_target_pairs={{0,4},{4,0},{8,12},{12,8},{16,20},{20,16},{24,28},{28,24},{1,5},{5... | collective-permute-start | bytes 393224 | tf_op jit(solution)/shard_map/ppermute | solution.py:602
  101.0 5.0 %collective-permute-start.23 = (bf16[256,256]{1,0:T(8,128)(2,1)S(1)}, bf16[256,256]{1,0:T(8,128)(2,1)S(1)}, u32[]{:S(2)}, u32[]{:S(2)}) collective-permute-start(bf16[256,256]{1,0:T(8,128)(2,1)S(1)} %get-tuple-element.85), channel_id=1, source_target_pairs={{0,8},{4,12},{8,0},{12,4},{16,24},{20,28},{24,16},{28,20},{1,9},{5... | collective-permute-start | bytes 393224 | tf_op jit(solution)/shard_map/ppermute | solution.py:602
  103.3 5.5 %collective-permute-start.24 = (bf16[256,256]{1,0:T(8,128)(2,1)S(1)}, bf16[256,256]{1,0:T(8,128)(2,1)S(1)}, u32[]{:S(2)}, u32[]{:S(2)}) collective-permute-start(bf16[256,256]{1,0:T(8,128)(2,1)S(1)} %get-tuple-element.86), channel_id=1, source_target_pairs={{0,12},{4,8},{8,4},{12,0},{16,28},{20,24},{24,20},{28,16},{1,13},{... | collective-permute-start | bytes 393224 | tf_op jit(solution)/shard_map/ppermute | solution.py:602

commit v5 on v4

--- a/solution.py
+++ b/solution.py
@@ -9,7 +9,7 @@
 VIEWS, HEADS = "views", "heads"
 HEAD_DIM = 64
 LANES = 128
-CHUNKS = dict(a=(1, 2), b=(0,), c=(3,))
+CHUNKS = dict(a=(1,), b=(2, 0), c=(3,))
 
 coupling = 0.5
 epsilon = 1e-06
@@ -171,7 +171,7 @@
 
 
 def attend(
-    meta, inter, queries, blocks, remote, plan, window, earlier=None, last=True, merged=False
+    meta, inter, queries, blocks, remote, plan, window, earlier=None, last=True, carry=None
 ):
     local_views = len(blocks)
     sub, tokens = queries[0].shape
@@ -200,8 +200,11 @@
                 keys += [(kvs[t], source, o) for t, source, o in sources_of(view, local_views, window)]
             return keys + [(far_kvs[name], source, o) for name, source, o in sources]
 
-        if last:
-            outs = [refs[0].at[i] for i in range(count)] if merged else refs[:count]
+        if last and carry is not None:
+            refs[1][0] = refs[0][...]
+            outs, refs = [refs[1].at[1 + i] for i in range(count)], refs[1:]
+        elif last:
+            outs = refs[:count]
         units = [(i, h, k) for i in range(count) for h in range(heads) for k in keys_of(i)]
         far = {}
         for _, _, (_, source, o) in units:
@@ -265,8 +268,8 @@
 
     if last:
         out_shape = [jax.ShapeDtypeStruct((tokens, sub), bf16)] * count
-        if merged:
-            out_shape = [jax.ShapeDtypeStruct((count, tokens, sub), bf16)]
+        if carry is not None:
+            out_shape = [jax.ShapeDtypeStruct((1 + count, tokens, sub), bf16)]
         scratch = [pltpu.VMEM((sub, tokens), f32), pltpu.VMEM((heads, 8, tokens), f32)]
     else:
         out_shape = [
@@ -280,7 +283,7 @@
     return pl.pallas_call(
         body,
         in_specs=[SMEM_SPEC, SMEM_SPEC]
-        + many(VMEM_SPEC, held + count + local_views + len(names)),
+        + many(VMEM_SPEC, held + count + local_views + len(names) + (carry is not None)),
         out_specs=many(VMEM_SPEC, len(out_shape)),
         out_shape=out_shape,
         scratch_shapes=scratch,
@@ -294,6 +297,7 @@
         *queries,
         *[blocks[v] for v in range(local_views)],
         *[remote[name] for name in names],
+        *(() if carry is None else (carry,)),
     )
 
 
@@ -628,20 +632,12 @@
     far["n2"] = along(after(blocks[1], local[0]), -1)
     far["p2"] = along(after(blocks[2], local[0]), 1)
     attended = {}
-    (attended["a"],) = attend(
-        meta,
-        inter,
-        inner_queries,
-        blocks,
-        inner_far,
-        inner_plan,
-        window,
-        earlier=tuple(local),
-        merged=True,
+    attended["a"], second = attend(
+        meta, inter, inner_queries, blocks, inner_far, inner_plan, window, earlier=tuple(local)
     )
     w_theirs = partner(after(w_mine, attended["a"]), 1)
 
-    def attend_outer(view, sources, done):
+    def attend_outer(view, sources, done, carry=None):
         (result,) = attend(
             meta,
             inter,
@@ -650,6 +646,7 @@
             {s[0]: far[s[0]] for s in sources},
             [(view, sources)],
             window,
+            carry=carry,
         )
         return result
 
@@ -669,7 +666,7 @@
         )
         got[c] = across(sent[c], middle)
 
-    attended["b"] = attend_outer(0, [("p1", -1, 0), ("p2", -2, 1)], attended["a"])
+    attended["b"] = attend_outer(0, [("p1", -1, 0), ("p2", -2, 1)], attended["a"], second)
     pass_on("a")
     attended["c"] = attend_outer(3, [("n1", 3, 0), ("n2", 3, 1)], sent["a"])
     pass_on("b")

time: 111 us -> 123 us (1.11)
  waiting for transfers between devices: 27 us -> 36.4 us
  starting transfers between devices: 55.2 us -> 57.2 us
    ppermute x4, starting transfers between devices: 13.9 us -> 18.7 us  [along(): return lax.ppermute(x, VIEWS, [(i, (i + by) % peers) for i in range(peers)])]
    ppermute x4, waiting for transfers between devices: 1.19 us -> 5.91 us  [along(): return lax.ppermute(x, VIEWS, [(i, (i + by) % peers) for i in range(peers)])]
    ppermute x10, waiting for transfers between devices: 15.1 us -> 19.5 us  [across(): return lax.ppermute(x, HEADS, pairs)]
    ppermute x11, starting transfers between devices: 15.5 us -> 11.3 us  [partner(): return lax.ppermute(x, VIEWS, [(i, i ^ mask) for i in range(peers)])]
    ppermute x10, starting transfers between devices: 25.8 us -> 27.2 us  [across(): return lax.ppermute(x, HEADS, pairs)]
  transfers between devices with their start and end apart: 25 -> 25, of which waited for: 9 -> 13; matrix products, arithmetic and copies ran while one was open for 0% -> 0% of each run, Pallas kernels for 16% -> 15%
where the time goes in v5:
time: 123 us; the launch traced here: 122 us
  starting transfers between devices  57.2 us (47%)
  waiting for transfers between devices  36.4 us (30%)
  Pallas kernels  27.7 us (23%)
    ppermute x10, starting transfers between devices, across(): return lax.ppermute(x, HEADS, pairs)  27.2 us
    ppermute x10, waiting for transfers between devices, across(): return lax.ppermute(x, HEADS, pairs)  19.5 us
    ppermute x4, starting transfers between devices, along(): return lax.ppermute(x, VIEWS, [(i, (i + by) % peers) for i in range(peers)])  18.7 us
    ppermute x11, starting transfers between devices, partner(): return lax.ppermute(x, VIEWS, [(i, i ^ mask) for i in range(peers)])  11.3 us
    ppermute x11, waiting for transfers between devices, partner(): return lax.ppermute(x, VIEWS, [(i, i ^ mask) for i in range(peers)])  10.9 us
    pallas_call x4, Pallas kernels, attend(): pl.pallas_call(body, in_specs=[SMEM_SPEC, SMEM_SPEC] + many(VMEM_SPEC, he...  9.05 us
    pallas_call x1, Pallas kernels, project_views(): pl.pallas_call(body, in_specs=[SMEM_SPEC] + many(ANY_SPEC, 4), out_specs=...  6.02 us
    ppermute x4, waiting for transfers between devices, along(): return lax.ppermute(x, VIEWS, [(i, (i + by) % peers) for i in range(peers)])  5.91 us
  transfers between devices with their start and end apart: 25, of which 13 were waited for; matrix products, arithmetic and copies ran while one was open for 0% of the time, Pallas kernels for 15%

profile of v5, /device:TPU:0, one launch (start us, length us, event | category | flops | bytes accessed | tf_op | source)
XLA Modules:
  0.0 122.5 jit_solution(14405367436463892928)
XLA Ops:
  0.0 0.7 copy-done.4
  0.7 6.0 %proj.1 = (bf16[256,256]{1,0:T(8,128)(2,1)S(1)}, bf16[2,256,256]{2,1,0:T(8,128)(2,1)S(1)}, bf16[256,256]{1,0:T(8,128)(2,1)S(1)}, bf16[2,256,256]{2,1,0:T(8,128)(...) custom-call(s32[4]{0:T(128)S(1)} %compare_select_fusion.1.meta_ref, ...), custom_call_target="tpu_custom_call" | custom-call | flops 1610612736 | bytes 5242880 | tf_op jit(solution)/shard_map/proj/pallas_call | solution.py:111
  6.7 5.0 %collective-permute-start.3 = (bf16[128,1024]{1,0:T(8,128)(2,1)S(1)}, bf16[128,1024]{1,0:T(8,128)(2,1)S(1)}, u32[]{:S(2)}, u32[]{:S(2)}) collective-permute-start(bf16[128,1024]{1,0:T(8,128)(2,1)S(1)} %get-tuple-element.58), channel_id=1, source_target_pairs={{0,1},{3,2},{4,5},{7,6},{8,9},{11,10},{12,13},{15,14},{16,17},{19,... | collective-permute-start | bytes 786440 | tf_op jit(solution)/shard_map/ppermute | solution.py:609
  11.7 1.7 %collective-permute-start = (bf16[2,256,256]{2,1,0:T(8,128)(2,1)S(1)}, bf16[2,256,256]{2,1,0:T(8,128)(2,1)S(1)}, u32[]{:S(2)}, u32[]{:S(2)}) collective-permute-start(bf16[2,256,256]{2,1,0:T(8,128)(2,1)S(1)} %get-tuple-element.51.refs_2_.refs_4_.refs_1_), channel_id=1, source_target_pairs={{0,28},{4,0},{8,4},{12,8},{16,12},{20,16},{24,20},{28,24},{1,29},{... | collective-permute-start | bytes 786440 | tf_op jit(solution)/shard_map/ppermute | solution.py:603
  13.4 2.9 %att.4 = (f32[2,320,256]{2,1,0:T(8,128)S(1)}, f32[2,4,256]{2,1,0:T(4,128)S(1)}) custom-call(s32[4]{0:T(128)S(1)} %compare_select_fusion.1.meta_ref, s32[2,32]{1,0:T(2,128)S(1)} %bitcast.7, bf16[256,256]{1,0:T(8,128)(2,1)S(1)} %get-tuple-element.49.refs_0_.refs_2_, bf16[256,256]{1,0:T(8,128)(2,1)S(1)} %get-tuple-element.50.refs_1_.refs_3_, ...), custom_call_target="tpu_custom_call" | custom-call | flops 1073741824 | bytes 4194304 | tf_op jit(solution)/shard_map/att/pallas_call | solution.py:283
  16.4 3.6 %collective-permute-done.refs_8_.refs_5_ = bf16[2,256,256]{2,1,0:T(8,128)(2,1)S(1)} collective-permute-done((bf16[2,256,256]{2,1,0:T(8,128)(2,1)S(1)}, bf16[2,256,256]{2,1,0:T(8,128)(2,1)S(1)}, u32[]{:S(2)}, u32[]{:S(2)}) %collective-permute-start) | collective-permute-done | bytes 262176 | tf_op jit(solution)/shard_map/ppermute | solution.py:603
  20.1 1.3 %collective-permute-done.1.refs_9_.refs_5_ = bf16[2,256,256]{2,1,0:T(8,128)(2,1)S(1)} collective-permute-done((bf16[2,256,256]{2,1,0:T(8,128)(2,1)S(1)}, bf16[2,256,256]{2,1,0:T(8,128)(2,1)S(1)}, u32[]{:S(2)}, u32[]{:S(2)}) %collective-permute-start.1) | collective-permute-done | bytes 262176 | tf_op jit(solution)/shard_map/ppermute | solution.py:603
  21.4 1.7 %att.5 = (bf16[256,256]{1,0:T(8,128)(2,1)S(1)}, bf16[256,256]{1,0:T(8,128)(2,1)S(1)}) custom-call(s32[4]{0:T(128)S(1)} %compare_select_fusion.1.meta_ref, s32[2,32]{1,0:T(2,128)S(1)} %bitcast.8, f32[2,320,256]{2,1,0:T(8,128)S(1)} %get-tuple-element.55.refs_0_, f32[2,4,256]{2,1,0:T(4,128)S(1)} %get-tuple-element.56.refs_1_, ...), custom_call_target="tpu_custom_call" | custom-call | flops 268435456 | bytes 1048576 | tf_op jit(solution)/shard_map/att/pallas_call | solution.py:283
  23.2 1.0 collective-permute-done.12.refs_6_
  24.2 2.2 %att.7 = bf16[2,256,256]{2,1,0:T(8,128)(2,1)S(1)} custom-call(s32[4]{0:T(128)S(1)} %compare_select_fusion.1.meta_ref, s32[2,32]{1,0:T(2,128)S(1)} %bitcast.9, bf16[256,256]{1,0:T(8,128)(2,1)S(1)} %get-tuple-element.72.refs_0_, bf16[2,256,256]{2,1,0:T(8,128)(2,1)S(1)} %get-tuple-element.51.refs_2_.refs_4_.refs_1_, ...), custom_call_target="tpu_custom_call" | custom-call | flops 671088640 | bytes 2621440 | tf_op jit(solution)/shard_map/att/pallas_call | solution.py:283
  26.4 7.4 %collective-permute-start.13 = (bf16[2,256,256]{2,1,0:T(8,128)(2,1)S(1)}, bf16[2,256,256]{2,1,0:T(8,128)(2,1)S(1)}, u32[]{:S(2)}, u32[]{:S(2)}) collective-permute-start(bf16[2,256,256]{2,1,0:T(8,128)(2,1)S(1)} %att.7), channel_id=1, source_target_pairs={{0,1},{3,2},{4,5},{7,6},{8,9},{11,10},{12,13},{15,14},{16,17},{19,... | collective-permute-start | bytes 786440 | tf_op jit(solution)/shard_map/ppermute | solution.py:609
  33.8 16.9 %collective-permute-start.5 = (bf16[2,256,256]{2,1,0:T(8,128)(2,1)S(1)}, bf16[2,256,256]{2,1,0:T(8,128)(2,1)S(1)}, u32[]{:S(2)}, u32[]{:S(2)}) collective-permute-start(bf16[2,256,256]{2,1,0:T(8,128)(2,1)S(1)} %get-tuple-element.63.refs_3_.refs_5_.refs_2_), channel_id=1, source_target_pairs={{0,28},{4,0},{8,4},{12,8},{16,12},{20,16},{24,20},{28,24},{1,29},{... | collective-permute-start | bytes 786440 | tf_op jit(solution)/shard_map/ppermute | solution.py:603
  50.7 1.6 %collective-permute-start.2 = (bf16[256,256]{1,0:T(8,128)(2,1)S(1)}, bf16[256,256]{1,0:T(8,128)(2,1)S(1)}, u32[]{:S(2)}, u32[]{:S(2)}) collective-permute-start(bf16[256,256]{1,0:T(8,128)(2,1)S(1)} %get-tuple-element.57.att), channel_id=1, source_target_pairs={{0,1},{3,2},{4,5},{7,6},{8,9},{11,10},{12,13},{15,14},{16,17},{19,... | collective-permute-start | bytes 393224 | tf_op jit(solution)/shard_map/ppermute | solution.py:609
  52.3 2.5 %collective-permute-done.2.near_ref = bf16[256,256]{1,0:T(8,128)(2,1)S(1)} collective-permute-done((bf16[256,256]{1,0:T(8,128)(2,1)S(1)}, bf16[256,256]{1,0:T(8,128)(2,1)S(1)}, u32[]{:S(2)}, u32[]{:S(2)}) %collective-permute-start.2) | collective-permute-done | bytes 131104 | tf_op jit(solution)/shard_map/ppermute | solution.py:609
  54.8 1.0 part.3
  55.8 1.3 %part.5 = (f32[512,512]{1,0:T(8,128)S(1)}, bf16[512,512]{1,0:T(8,128)(2,1)S(1)}) custom-call(s32[4]{0:T(128)S(1)} %compare_select_fusion.1.meta_ref, bf16[2,256,256]{2,1,0:T(8,128)(2,1)S(1)} %att.7, bf16[2,256,256]{2,1,0:T(8,128)(2,1)S(1)} %collective-permute-done.13.near_ref, bf16[256,1024]{1,0:T(8,128)(2,1)S(1)} %copy-done.1, ...), custom_call_target="tpu_custom_call" | custom-call | flops 536870912 | bytes 4194304 | tf_op jit(solution)/shard_map/part/pallas_call | solution.py:361
  57.1 0.9 collective-permute-start.14
  58.0 2.2 %att.6 = bf16[256,256]{1,0:T(8,128)(2,1)S(1)} custom-call(s32[4]{0:T(128)S(1)} %compare_select_fusion.1.meta_ref, s32[2,32]{1,0:T(2,128)S(1)} %bitcast.10, bf16[256,256]{1,0:T(8,128)(2,1)S(1)} %get-tuple-element.62.refs_0_, bf16[2,256,256]{2,1,0:T(8,128)(2,1)S(1)} %get-tuple-element.51.refs_2_.refs_4_.refs_1_, ...), custom_call_target="tpu_custom_call" | custom-call | flops 671088640 | bytes 2621440 | tf_op jit(solution)/shard_map/att/pallas_call | solution.py:283
  60.2 7.2 %collective-permute-start.6 = (bf16[256,256]{1,0:T(8,128)(2,1)S(1)}, bf16[256,256]{1,0:T(8,128)(2,1)S(1)}, u32[]{:S(2)}, u32[]{:S(2)}) collective-permute-start(bf16[256,256]{1,0:T(8,128)(2,1)S(1)} %att.6), channel_id=1, source_target_pairs={{0,1},{3,2},{4,5},{7,6},{8,9},{11,10},{12,13},{15,14},{16,17},{19,... | collective-permute-start | bytes 393224 | tf_op jit(solution)/shard_map/ppermute | solution.py:609
  67.3 0.7 collective-permute-start.10
  68.0 1.8 %collective-permute-done.6.near_ref = bf16[256,256]{1,0:T(8,128)(2,1)S(1)} collective-permute-done((bf16[256,256]{1,0:T(8,128)(2,1)S(1)}, bf16[256,256]{1,0:T(8,128)(2,1)S(1)}, u32[]{:S(2)}, u32[]{:S(2)}) %collective-permute-start.6) | collective-permute-done | bytes 131104 | tf_op jit(solution)/shard_map/ppermute | solution.py:609
  69.8 1.0 part.4
  70.8 0.7 prep.1
  71.6 0.7 collective-permute-start.16
  72.2 0.5 collective-permute-done.7
  72.7 1.5 %collective-permute-start.8 = (s32[16,256]{1,0:T(8,128)S(1)}, s32[16,256]{1,0:T(8,128)S(1)}, u32[]{:S(2)}, u32[]{:S(2)}) collective-permute-start(s32[16,256]{1,0:T(8,128)S(1)} %pad_add_fusion.1), channel_id=1, source_target_pairs={{0,8},{4,12},{8,0},{12,4},{16,24},{20,28},{24,16},{28,20},{1,9},{5... | collective-permute-start | bytes 49160 | tf_op jit(solution)/shard_map/ppermute | solution.py:606
  74.2 0.7 merge.4
  74.9 1.3 %collective-permute-start.15 = (bf16[512,256]{1,0:T(8,128)(2,1)S(1)}, bf16[512,256]{1,0:T(8,128)(2,1)S(1)}, u32[]{:S(2)}, u32[]{:S(2)}) collective-permute-start(bf16[512,256]{1,0:T(8,128)(2,1)S(1)} %get-tuple-element.78), channel_id=1, source_target_pairs={{1,0},{2,3},{5,4},{6,7},{9,8},{10,11},{13,12},{14,15},{17,16},{18,... | collective-permute-start | bytes 786440 | tf_op jit(solution)/shard_map/ppermute | solution.py:609
  76.5 4.0 %collective-permute-start.9 = (s32[32,256]{1,0:T(8,128)S(1)}, s32[32,256]{1,0:T(8,128)S(1)}, u32[]{:S(2)}, u32[]{:S(2)}) collective-permute-start(s32[32,256]{1,0:T(8,128)S(1)} %pad_add_fusion), channel_id=1, source_target_pairs={{0,16},{4,20},{8,24},{12,28},{16,0},{20,4},{24,8},{28,12},{1,17},{... | collective-permute-start | bytes 98312 | tf_op jit(solution)/shard_map/ppermute | solution.py:606
  80.5 0.6 merge.3
  81.1 1.3 %collective-permute-start.11 = (bf16[256,256]{1,0:T(8,128)(2,1)S(1)}, bf16[256,256]{1,0:T(8,128)(2,1)S(1)}, u32[]{:S(2)}, u32[]{:S(2)}) collective-permute-start(bf16[256,256]{1,0:T(8,128)(2,1)S(1)} %get-tuple-element.70), channel_id=1, source_target_pairs={{1,0},{2,3},{5,4},{6,7},{9,8},{10,11},{13,12},{14,15},{17,16},{18,... | collective-permute-start | bytes 393224 | tf_op jit(solution)/shard_map/ppermute | solution.py:609
  82.4 0.6 merge.5
  83.0 1.3 %collective-permute-start.17 = (bf16[256,256]{1,0:T(8,128)(2,1)S(1)}, bf16[256,256]{1,0:T(8,128)(2,1)S(1)}, u32[]{:S(2)}, u32[]{:S(2)}) collective-permute-start(bf16[256,256]{1,0:T(8,128)(2,1)S(1)} %get-tuple-element.81), channel_id=1, source_target_pairs={{1,0},{2,3},{5,4},{6,7},{9,8},{10,11},{13,12},{14,15},{17,16},{18,... | collective-permute-start | bytes 393224 | tf_op jit(solution)/shard_map/ppermute | solution.py:609
  84.3 13.1 %collective-permute-done.11.refs_1_ = bf16[256,256]{1,0:T(8,128)(2,1)S(1)} collective-permute-done((bf16[256,256]{1,0:T(8,128)(2,1)S(1)}, bf16[256,256]{1,0:T(8,128)(2,1)S(1)}, u32[]{:S(2)}, u32[]{:S(2)}) %collective-permute-start.11) | collective-permute-done | bytes 131104 | tf_op jit(solution)/shard_map/ppermute | solution.py:609
  97.5 2.1 %collective-permute-done.17.refs_5_ = bf16[256,256]{1,0:T(8,128)(2,1)S(1)} collective-permute-done((bf16[256,256]{1,0:T(8,128)(2,1)S(1)}, bf16[256,256]{1,0:T(8,128)(2,1)S(1)}, u32[]{:S(2)}, u32[]{:S(2)}) %collective-permute-start.17) | collective-permute-done | bytes 131104 | tf_op jit(solution)/shard_map/ppermute | solution.py:609
  99.5 1.5 %gath.2 = (bf16[1024,256]{1,0:T(8,128)(2,1)S(1)}, bf16[256,256]{1,0:T(8,128)(2,1)S(1)}, bf16[256,256]{1,0:T(8,128)(2,1)S(1)}, bf16[256,256]{1,0:T(8,128)(2,1)S(1)}, bf16[256,256]{1,0:T(8,128)(2,1)S(1)}) custom-call(s32[4]{0:T(128)S(1)} %compare_select_fusion.1.meta_ref, s32[64,256]{1,0:T(8,128)S(1)} %constant_dynamic-update-slice_fusion.wanted_ref, ...), custom_call_target="tpu_custom_call" | custom-call | flops 536870912 | bytes 2097152 | tf_op jit(solution)/shard_map/gath/pallas_call | solution.py:483
  101.1 2.2 %collective-permute-start.19 = (bf16[256,256]{1,0:T(8,128)(2,1)S(1)}, bf16[256,256]{1,0:T(8,128)(2,1)S(1)}, u32[]{:S(2)}, u32[]{:S(2)}) collective-permute-start(bf16[256,256]{1,0:T(8,128)(2,1)S(1)} %get-tuple-element.85), channel_id=1, source_target_pairs={{0,16},{4,20},{8,24},{12,28},{16,0},{20,4},{24,8},{28,12},{1,17},{... | collective-permute-start | bytes 393224 | tf_op jit(solution)/shard_map/ppermute | solution.py:606
  103.3 0.3 collective-permute-start.21
  103.5 2.2 %collective-permute-start.22 = (bf16[256,256]{1,0:T(8,128)(2,1)S(1)}, bf16[256,256]{1,0:T(8,128)(2,1)S(1)}, u32[]{:S(2)}, u32[]{:S(2)}) collective-permute-start(bf16[256,256]{1,0:T(8,128)(2,1)S(1)} %get-tuple-element.88), channel_id=1, source_target_pairs={{0,28},{4,24},{8,20},{12,16},{16,12},{20,8},{24,4},{28,0},{1,29},{... | collective-permute-start | bytes 393224 | tf_op jit(solution)/shard_map/ppermute | solution.py:606
  105.7 1.5 %gath.3 = (bf16[256,256]{1,0:T(8,128)(2,1)S(1)}, bf16[256,256]{1,0:T(8,128)(2,1)S(1)}, bf16[256,256]{1,0:T(8,128)(2,1)S(1)}, bf16[256,256]{1,0:T(8,128)(2,1)S(1)}) custom-call(s32[4]{0:T(128)S(1)} %compare_select_fusion.1.meta_ref, s32[64,256]{1,0:T(8,128)S(1)} %constant_dynamic-update-slice_fusion.wanted_ref, ...), custom_call_target="tpu_custom_call" | custom-call | flops 536870912 | bytes 2097152 | tf_op jit(solution)/shard_map/gath/pallas_call | solution.py:483
  107.2 0.7 collective-permute-start.18
  107.9 4.4 %collective-permute-done.19.refs_2_ = bf16[256,256]{1,0:T(8,128)(2,1)S(1)} collective-permute-done((bf16[256,256]{1,0:T(8,128)(2,1)S(1)}, bf16[256,256]{1,0:T(8,128)(2,1)S(1)}, u32[]{:S(2)}, u32[]{:S(2)}) %collective-permute-start.19) | collective-permute-done | bytes 131104 | tf_op jit(solution)/shard_map/ppermute | solution.py:606
  112.3 0.4 collective-permute-start.23
  112.7 2.0 %collective-permute-done.20.refs_3_ = bf16[256,256]{1,0:T(8,128)(2,1)S(1)} collective-permute-done((bf16[256,256]{1,0:T(8,128)(2,1)S(1)}, bf16[256,256]{1,0:T(8,128)(2,1)S(1)}, u32[]{:S(2)}, u32[]{:S(2)}) %collective-permute-start.20) | collective-permute-done | bytes 131104 | tf_op jit(solution)/shard_map/ppermute | solution.py:606
  114.6 1.7 %first.1.early_ref = bf16[1024,256]{1,0:T(8,128)(2,1)S(1)} custom-call(s32[4]{0:T(128)S(1)} %compare_select_fusion.1.meta_ref, s32[8,128]{1,0:T(8,128)S(1)} %get-tuple-element.66.code_ref, bf16[256,256]{1,0:T(8,128)(2,1)S(1)} %get-tuple-element.83.refs_0_, bf16[256,256]{1,0:T(8,128)(2,1)S(1)} %collective-permute-done.18.refs_1_, ...), custom_call_target="tpu_custom_call" | custom-call | flops 805306368 | bytes 1048576 | tf_op jit(solution)/shard_map/first/pallas_call | solution.py:533
  116.3 0.9 collective-permute-done.23.refs_0_
  117.2 2.9 %collective-permute-done.24.refs_1_ = bf16[256,256]{1,0:T(8,128)(2,1)S(1)} collective-permute-done((bf16[256,256]{1,0:T(8,128)(2,1)S(1)}, bf16[256,256]{1,0:T(8,128)(2,1)S(1)}, u32[]{:S(2)}, u32[]{:S(2)}) %collective-permute-start.24) | collective-permute-done | bytes 131104 | tf_op jit(solution)/shard_map/ppermute | solution.py:606
  120.2 2.1 %fin.1 = f32[1024,256]{1,0:T(8,128)} custom-call(s32[4]{0:T(128)S(1)} %compare_select_fusion.1.meta_ref, s32[8,128]{1,0:T(8,128)S(1)} %get-tuple-element.66.code_ref, f32[8,128]{1,0:T(8,128)S(1)} %bitcast.6, bf16[1024,256]{1,0:T(8,128)(2,1)S(1)} %get-tuple-element.82.refs_0_.layer_ref, bf16[1024,256]{1,0:T(8,128)(2,1)S(1)} %first.1.early_ref, ...), custom_call_target="tpu_custom_call" | custom-call | flops 268435456 | bytes 2097152 | tf_op jit(solution)/shard_map/fin/pallas_call | solution.py:574
  (39 shorter events, 0.5 us)
Async XLA Ops:
  0.0 0.7 copy-start.4
  0.7 12.7 %copy-start.3 = (s32[32,2]{0,1:T(2,128)S(1)}, s32[32,2]{0,1:T(2,128)}, u32[]{:S(2)}) copy-start(s32[32,2]{0,1:T(2,128)} %param.12) | copy-start | bytes 772
  6.7 16.4 %collective-permute-start.3 = (bf16[128,1024]{1,0:T(8,128)(2,1)S(1)}, bf16[128,1024]{1,0:T(8,128)(2,1)S(1)}, u32[]{:S(2)}, u32[]{:S(2)}) collective-permute-start(bf16[128,1024]{1,0:T(8,128)(2,1)S(1)} %get-tuple-element.58), channel_id=1, source_target_pairs={{0,1},{3,2},{4,5},{7,6},{8,9},{11,10},{12,13},{15,14},{16,17},{19,... | collective-permute-start | bytes 786440 | tf_op jit(solution)/shard_map/ppermute | solution.py:609
  11.7 8.4 %collective-permute-start = (bf16[2,256,256]{2,1,0:T(8,128)(2,1)S(1)}, bf16[2,256,256]{2,1,0:T(8,128)(2,1)S(1)}, u32[]{:S(2)}, u32[]{:S(2)}) collective-permute-start(bf16[2,256,256]{2,1,0:T(8,128)(2,1)S(1)} %get-tuple-element.51.refs_2_.refs_4_.refs_1_), channel_id=1, source_target_pairs={{0,28},{4,0},{8,4},{12,8},{16,12},{20,16},{24,20},{28,24},{1,29},{... | collective-permute-start | bytes 786440 | tf_op jit(solution)/shard_map/ppermute | solution.py:603
  13.4 8.0 %collective-permute-start.1 = (bf16[2,256,256]{2,1,0:T(8,128)(2,1)S(1)}, bf16[2,256,256]{2,1,0:T(8,128)(2,1)S(1)}, u32[]{:S(2)}, u32[]{:S(2)}) collective-permute-start(bf16[2,256,256]{2,1,0:T(8,128)(2,1)S(1)} %get-tuple-element.54.refs_5_.refs_7_.refs_4_), channel_id=1, source_target_pairs={{0,4},{4,8},{8,12},{12,16},{16,20},{20,24},{24,28},{28,0},{1,5},{5... | collective-permute-start | bytes 786440 | tf_op jit(solution)/shard_map/ppermute | solution.py:603
  16.3 7.9 %collective-permute-start.12 = (bf16[2,256,256]{2,1,0:T(8,128)(2,1)S(1)}, bf16[2,256,256]{2,1,0:T(8,128)(2,1)S(1)}, u32[]{:S(2)}, u32[]{:S(2)}) collective-permute-start(bf16[2,256,256]{2,1,0:T(8,128)(2,1)S(1)} %get-tuple-element.73.refs_4_.refs_6_.refs_3_), channel_id=1, source_target_pairs={{0,4},{4,8},{8,12},{12,16},{16,20},{20,24},{24,28},{28,0},{1,5},{5... | collective-permute-start | bytes 786440 | tf_op jit(solution)/shard_map/ppermute | solution.py:603
  21.4 33.4 %copy-start = (bf16[4,256,512]{2,1,0:T(8,128)(2,1)S(1)}, bf16[4,256,512]{2,1,0:T(8,128)(2,1)}, u32[]{:S(2)}) copy-start(bf16[4,256,512]{2,1,0:T(8,128)(2,1)} %get-tuple-element.60.halves_ref) | copy-start | bytes 3145732
  21.4 33.4 %copy-start.1 = (bf16[256,1024]{1,0:T(8,128)(2,1)S(1)}, bf16[256,1024]{1,0:T(8,128)(2,1)}, u32[]{:S(2)}) copy-start(bf16[256,1024]{1,0:T(8,128)(2,1)} %own_ref.5) | copy-start | bytes 1572868
  23.1 31.7 %collective-permute-start.4 = (bf16[128,1024]{1,0:T(8,128)(2,1)S(1)}, bf16[128,1024]{1,0:T(8,128)(2,1)S(1)}, u32[]{:S(2)}, u32[]{:S(2)}) collective-permute-start(bf16[128,1024]{1,0:T(8,128)(2,1)S(1)} %collective-permute-done.3.mine_ref), channel_id=1, source_target_pairs={{0,4},{4,0},{8,12},{12,8},{16,20},{20,16},{24,28},{28,24},{1,5},{5... | collective-permute-start | bytes 786440 | tf_op jit(solution)/shard_map/ppermute | solution.py:606
  26.4 29.4 %collective-permute-start.13 = (bf16[2,256,256]{2,1,0:T(8,128)(2,1)S(1)}, bf16[2,256,256]{2,1,0:T(8,128)(2,1)S(1)}, u32[]{:S(2)}, u32[]{:S(2)}) collective-permute-start(bf16[2,256,256]{2,1,0:T(8,128)(2,1)S(1)} %att.7), channel_id=1, source_target_pairs={{0,1},{3,2},{4,5},{7,6},{8,9},{11,10},{12,13},{15,14},{16,17},{19,... | collective-permute-start | bytes 786440 | tf_op jit(solution)/shard_map/ppermute | solution.py:609
  33.8 24.2 %collective-permute-start.5 = (bf16[2,256,256]{2,1,0:T(8,128)(2,1)S(1)}, bf16[2,256,256]{2,1,0:T(8,128)(2,1)S(1)}, u32[]{:S(2)}, u32[]{:S(2)}) collective-permute-start(bf16[2,256,256]{2,1,0:T(8,128)(2,1)S(1)} %get-tuple-element.63.refs_3_.refs_5_.refs_2_), channel_id=1, source_target_pairs={{0,28},{4,0},{8,4},{12,8},{16,12},{20,16},{24,20},{28,24},{1,29},{... | collective-permute-start | bytes 786440 | tf_op jit(solution)/shard_map/ppermute | solution.py:603
  50.7 4.1 %collective-permute-start.2 = (bf16[256,256]{1,0:T(8,128)(2,1)S(1)}, bf16[256,256]{1,0:T(8,128)(2,1)S(1)}, u32[]{:S(2)}, u32[]{:S(2)}) collective-permute-start(bf16[256,256]{1,0:T(8,128)(2,1)S(1)} %get-tuple-element.57.att), channel_id=1, source_target_pairs={{0,1},{3,2},{4,5},{7,6},{8,9},{11,10},{12,13},{15,14},{16,17},{19,... | collective-permute-start | bytes 393224 | tf_op jit(solution)/shard_map/ppermute | solution.py:609
  57.1 13.8 %copy-start.5 = (s32[1024,1]{0,1:T(1,128)S(1)}, s32[1024,1]{0,1:T(1,128)}, u32[]{:S(2)}) copy-start(s32[1024,1]{0,1:T(1,128)} %param.13) | copy-start | bytes 12292
  57.1 13.8 %copy-start.6 = (s32[1024]{0:T(1024)S(1)}, s32[1024]{0:T(1024)}, u32[]{:S(2)}) copy-start(s32[1024]{0:T(1024)} %param.14) | copy-start | bytes 12292
  57.1 17.2 %collective-permute-start.14 = (bf16[512,512]{1,0:T(8,128)(2,1)S(1)}, bf16[512,512]{1,0:T(8,128)(2,1)S(1)}, u32[]{:S(2)}, u32[]{:S(2)}) collective-permute-start(bf16[512,512]{1,0:T(8,128)(2,1)S(1)} %get-tuple-element.76), channel_id=1, source_target_pairs={{1,2},{2,1},{5,6},{6,5},{9,10},{10,9},{13,14},{14,13},{17,18},{18,... | collective-permute-start | bytes 1572872 | tf_op jit(solution)/shard_map/ppermute | solution.py:609
  60.2 9.7 %collective-permute-start.6 = (bf16[256,256]{1,0:T(8,128)(2,1)S(1)}, bf16[256,256]{1,0:T(8,128)(2,1)S(1)}, u32[]{:S(2)}, u32[]{:S(2)}) collective-permute-start(bf16[256,256]{1,0:T(8,128)(2,1)S(1)} %att.6), channel_id=1, source_target_pairs={{0,1},{3,2},{4,5},{7,6},{8,9},{11,10},{12,13},{15,14},{16,17},{19,... | collective-permute-start | bytes 393224 | tf_op jit(solution)/shard_map/ppermute | solution.py:609
  67.3 13.1 %collective-permute-start.10 = (bf16[256,512]{1,0:T(8,128)(2,1)S(1)}, bf16[256,512]{1,0:T(8,128)(2,1)S(1)}, u32[]{:S(2)}, u32[]{:S(2)}) collective-permute-start(bf16[256,512]{1,0:T(8,128)(2,1)S(1)} %get-tuple-element.61), channel_id=1, source_target_pairs={{1,2},{2,1},{5,6},{6,5},{9,10},{10,9},{13,14},{14,13},{17,18},{18,... | collective-permute-start | bytes 786440 | tf_op jit(solution)/shard_map/ppermute | solution.py:609
  71.5 1.2 collective-permute-start.7
  71.6 10.8 %collective-permute-start.16 = (bf16[256,512]{1,0:T(8,128)(2,1)S(1)}, bf16[256,512]{1,0:T(8,128)(2,1)S(1)}, u32[]{:S(2)}, u32[]{:S(2)}) collective-permute-start(bf16[256,512]{1,0:T(8,128)(2,1)S(1)} %get-tuple-element.64), channel_id=1, source_target_pairs={{1,2},{2,1},{5,6},{6,5},{9,10},{10,9},{13,14},{14,13},{17,18},{18,... | collective-permute-start | bytes 786440 | tf_op jit(solution)/shard_map/ppermute | solution.py:609
  72.7 3.7 %collective-permute-start.8 = (s32[16,256]{1,0:T(8,128)S(1)}, s32[16,256]{1,0:T(8,128)S(1)}, u32[]{:S(2)}, u32[]{:S(2)}) collective-permute-start(s32[16,256]{1,0:T(8,128)S(1)} %pad_add_fusion.1), channel_id=1, source_target_pairs={{0,8},{4,12},{8,0},{12,4},{16,24},{20,28},{24,16},{28,20},{1,9},{5... | collective-permute-start | bytes 49160 | tf_op jit(solution)/shard_map/ppermute | solution.py:606
  74.9 24.6 %collective-permute-start.15 = (bf16[512,256]{1,0:T(8,128)(2,1)S(1)}, bf16[512,256]{1,0:T(8,128)(2,1)S(1)}, u32[]{:S(2)}, u32[]{:S(2)}) collective-permute-start(bf16[512,256]{1,0:T(8,128)(2,1)S(1)} %get-tuple-element.78), channel_id=1, source_target_pairs={{1,0},{2,3},{5,4},{6,7},{9,8},{10,11},{13,12},{14,15},{17,16},{18,... | collective-permute-start | bytes 786440 | tf_op jit(solution)/shard_map/ppermute | solution.py:609
  76.5 7.8 %collective-permute-start.9 = (s32[32,256]{1,0:T(8,128)S(1)}, s32[32,256]{1,0:T(8,128)S(1)}, u32[]{:S(2)}, u32[]{:S(2)}) collective-permute-start(s32[32,256]{1,0:T(8,128)S(1)} %pad_add_fusion), channel_id=1, source_target_pairs={{0,16},{4,20},{8,24},{12,28},{16,0},{20,4},{24,8},{28,12},{1,17},{... | collective-permute-start | bytes 98312 | tf_op jit(solution)/shard_map/ppermute | solution.py:606
  81.1 16.4 %collective-permute-start.11 = (bf16[256,256]{1,0:T(8,128)(2,1)S(1)}, bf16[256,256]{1,0:T(8,128)(2,1)S(1)}, u32[]{:S(2)}, u32[]{:S(2)}) collective-permute-start(bf16[256,256]{1,0:T(8,128)(2,1)S(1)} %get-tuple-element.70), channel_id=1, source_target_pairs={{1,0},{2,3},{5,4},{6,7},{9,8},{10,11},{13,12},{14,15},{17,16},{18,... | collective-permute-start | bytes 393224 | tf_op jit(solution)/shard_map/ppermute | solution.py:609
  83.0 16.5 %collective-permute-start.17 = (bf16[256,256]{1,0:T(8,128)(2,1)S(1)}, bf16[256,256]{1,0:T(8,128)(2,1)S(1)}, u32[]{:S(2)}, u32[]{:S(2)}) collective-permute-start(bf16[256,256]{1,0:T(8,128)(2,1)S(1)} %get-tuple-element.81), channel_id=1, source_target_pairs={{1,0},{2,3},{5,4},{6,7},{9,8},{10,11},{13,12},{14,15},{17,16},{18,... | collective-permute-start | bytes 393224 | tf_op jit(solution)/shard_map/ppermute | solution.py:609
  101.1 11.2 %collective-permute-start.19 = (bf16[256,256]{1,0:T(8,128)(2,1)S(1)}, bf16[256,256]{1,0:T(8,128)(2,1)S(1)}, u32[]{:S(2)}, u32[]{:S(2)}) collective-permute-start(bf16[256,256]{1,0:T(8,128)(2,1)S(1)} %get-tuple-element.85), channel_id=1, source_target_pairs={{0,16},{4,20},{8,24},{12,28},{16,0},{20,4},{24,8},{28,12},{1,17},{... | collective-permute-start | bytes 393224 | tf_op jit(solution)/shard_map/ppermute | solution.py:606
  103.3 11.4 %collective-permute-start.20 = (bf16[256,256]{1,0:T(8,128)(2,1)S(1)}, bf16[256,256]{1,0:T(8,128)(2,1)S(1)}, u32[]{:S(2)}, u32[]{:S(2)}) collective-permute-start(bf16[256,256]{1,0:T(8,128)(2,1)S(1)} %get-tuple-element.86), channel_id=1, source_target_pairs={{0,20},{4,16},{8,28},{12,24},{16,4},{20,0},{24,12},{28,8},{1,21},{... | collective-permute-start | bytes 393224 | tf_op jit(solution)/shard_map/ppermute | solution.py:606
  103.3 11.4 %collective-permute-start.21 = (bf16[256,256]{1,0:T(8,128)(2,1)S(1)}, bf16[256,256]{1,0:T(8,128)(2,1)S(1)}, u32[]{:S(2)}, u32[]{:S(2)}) collective-permute-start(bf16[256,256]{1,0:T(8,128)(2,1)S(1)} %get-tuple-element.87), channel_id=1, source_target_pairs={{0,24},{4,28},{8,16},{12,20},{16,8},{20,12},{24,0},{28,4},{1,25},{... | collective-permute-start | bytes 393224 | tf_op jit(solution)/shard_map/ppermute | solution.py:606
  103.5 11.1 %collective-permute-start.22 = (bf16[256,256]{1,0:T(8,128)(2,1)S(1)}, bf16[256,256]{1,0:T(8,128)(2,1)S(1)}, u32[]{:S(2)}, u32[]{:S(2)}) collective-permute-start(bf16[256,256]{1,0:T(8,128)(2,1)S(1)} %get-tuple-element.88), channel_id=1, source_target_pairs={{0,28},{4,24},{8,20},{12,16},{16,12},{20,8},{24,4},{28,0},{1,29},{... | collective-permute-start | bytes 393224 | tf_op jit(solution)/shard_map/ppermute | solution.py:606
  105.7 14.5 %copy-start.2 = (f32[1024]{0:T(1024)S(1)}, f32[1024]{0:T(1024)}, u32[]{:S(2)}) copy-start(f32[1024]{0:T(1024)} %param.15) | copy-start | bytes 12292
  107.2 7.4 %collective-permute-start.18 = (bf16[256,256]{1,0:T(8,128)(2,1)S(1)}, bf16[256,256]{1,0:T(8,128)(2,1)S(1)}, u32[]{:S(2)}, u32[]{:S(2)}) collective-permute-start(bf16[256,256]{1,0:T(8,128)(2,1)S(1)} %get-tuple-element.84), channel_id=1, source_target_pairs={{0,4},{4,0},{8,12},{12,8},{16,20},{20,16},{24,28},{28,24},{1,5},{5... | collective-permute-start | bytes 393224 | tf_op jit(solution)/shard_map/ppermute | solution.py:606
  112.3 5.0 %collective-permute-start.23 = (bf16[256,256]{1,0:T(8,128)(2,1)S(1)}, bf16[256,256]{1,0:T(8,128)(2,1)S(1)}, u32[]{:S(2)}, u32[]{:S(2)}) collective-permute-start(bf16[256,256]{1,0:T(8,128)(2,1)S(1)} %get-tuple-element.89), channel_id=1, source_target_pairs={{0,8},{4,12},{8,0},{12,4},{16,24},{20,28},{24,16},{28,20},{1,9},{5... | collective-permute-start | bytes 393224 | tf_op jit(solution)/shard_map/ppermute | solution.py:606
  114.6 5.5 %collective-permute-start.24 = (bf16[256,256]{1,0:T(8,128)(2,1)S(1)}, bf16[256,256]{1,0:T(8,128)(2,1)S(1)}, u32[]{:S(2)}, u32[]{:S(2)}) collective-permute-start(bf16[256,256]{1,0:T(8,128)(2,1)S(1)} %get-tuple-element.90), channel_id=1, source_target_pairs={{0,12},{4,8},{8,4},{12,0},{16,28},{20,24},{24,20},{28,16},{1,13},{... | collective-permute-start | bytes 393224 | tf_op jit(solution)/shard_map/ppermute | solution.py:606

commit v6 on v5

--- a/solution.py
+++ b/solution.py
@@ -9,6 +9,7 @@
 VIEWS, HEADS = "views", "heads"
 HEAD_DIM = 64
 LANES = 128
+STAGED = 4
 CHUNKS = dict(a=(1,), b=(2, 0), c=(3,))
 
 coupling = 0.5
@@ -41,19 +42,15 @@
     return [spec] * count
 
 
-def project_views(meta, latents, gain, w_qkv, w_out, which):
+def project_views(meta, latents, gain, w_qkv, which):
     _, tokens, width = latents.shape
     sub = w_qkv.shape[2]
     count = len(which)
     scale = HEAD_DIM ** (-0.5)
     order = (2, 0, 1)
 
-    strip = sub // 2
-
-    def body(meta_ref, lat_hbm, gain_hbm, w_hbm, w_out_hbm, *refs):
-        outs, (halves, w_half, buffer, gains, ws, sems) = refs[: 2 * count], refs[2 * count :]
-        mine = pl.ds(pl.multiple_of((meta_ref[0] % 2) * strip, strip), strip)
-        w_copy = pltpu.make_async_copy(w_out_hbm.at[mine], w_half, sems.at[2 * count + 4])
+    def body(meta_ref, lat_hbm, gain_hbm, w_hbm, *refs):
+        outs, (halves, buffer, gains, ws, sems) = refs[: 2 * count], refs[2 * count :]
         here = pl.ds(pl.multiple_of((meta_ref[1] // 2) * (width // 2), width // 2), width // 2)
         kept = [
             pltpu.make_async_copy(buffer.at[i, :, here], halves.at[i], sems.at[count + 4 + i])
@@ -68,35 +65,42 @@
             part: pltpu.make_async_copy(w_hbm.at[part], ws.at[part], sems.at[count + 1 + part])
             for part in order
         }
-        for copy in [gain_copy, copies[0]] + [w_copies[p] for p in order] + copies[1:] + [w_copy]:
+        queue = [copies[0], gain_copy, w_copies[2], w_copies[0], w_copies[1]] + copies[1:]
+        for copy in queue[:STAGED]:
             copy.start()
+        waiting = queue[STAGED:]
+
+        def arrive(copy):
+            copy.wait()
+            if waiting:
+                waiting.pop(0).start()
 
         def load_norm(i):
-            copies[i].wait()
+            arrive(copies[i])
             kept[i].start()
+            if i == 0:
+                arrive(gain_copy)
             wide = buffer[i].astype(f32)
             mean_square = jnp.mean(wide * wide, axis=-1, keepdims=True)
             return (wide * lax.rsqrt(mean_square + epsilon) * gains[...]).astype(bf16)
 
-        gain_copy.wait()
         following = load_norm(0)
         for i in range(count):
             normed = following
             if i == 0:
-                w_copies[2].wait()
+                arrive(w_copies[2])
             elif i + 1 < count:
                 following = load_norm(i + 1)
             values = dot(normed, ws[2])
             if i == 0:
-                w_copies[0].wait()
+                arrive(w_copies[0])
             queries = dot(normed, ws[0])
             if i == 0:
-                w_copies[1].wait()
+                arrive(w_copies[1])
                 following = load_norm(i + 1)
             outs[2 * i + 1][0] = dot(normed, ws[1]).astype(bf16)
             outs[2 * i + 1][1] = jnp.transpose(values).astype(bf16)
             outs[2 * i][...] = jnp.transpose(queries).astype(bf16) * jnp.asarray(scale, bf16)
-        w_copy.wait()
         for copy in kept:
             copy.wait()
 
@@ -107,25 +111,24 @@
             jax.ShapeDtypeStruct((2, tokens, sub), bf16),
         ]
     out_shape.append(jax.ShapeDtypeStruct((count, tokens, width // 2), bf16))
-    out_shape.append(jax.ShapeDtypeStruct((strip, w_out.shape[1]), bf16))
     outs = pl.pallas_call(
         body,
-        in_specs=[SMEM_SPEC] + many(ANY_SPEC, 4),
+        in_specs=[SMEM_SPEC] + many(ANY_SPEC, 3),
         out_specs=many(VMEM_SPEC, len(out_shape)),
         out_shape=out_shape,
         scratch_shapes=[
             pltpu.VMEM((count, tokens, width), bf16),
             pltpu.VMEM((1, width), f32),
             pltpu.VMEM((3, width, sub), bf16),
-            pltpu.SemaphoreType.DMA((2 * count + 5,)),
+            pltpu.SemaphoreType.DMA((2 * count + 4,)),
         ],
         name="proj",
-        compiler_params=grant(52),
+        compiler_params=grant(50),
         cost_estimate=cost(
             count * 6 * tokens * width * sub, count * tokens * (width + 3 * sub) * 2 + 6 * width * sub
         ),
-    )(meta, latents, gain, w_qkv, w_out)
-    return {v: (outs[2 * i], outs[2 * i + 1]) for i, v in enumerate(which)}, outs[-2], outs[-1]
+    )(meta, latents, gain, w_qkv)
+    return {v: (outs[2 * i], outs[2 * i + 1]) for i, v in enumerate(which)}, outs[-1]
 
 
 ONES = 16
@@ -331,27 +334,20 @@
     lax.fori_loop(0, heads, one_head, 0)
 
 
-def partial_out(meta, attended, near, w_own, w_mine, w_theirs, halves, places):
+def partial_out(meta, attended, near, w_own, w_near, halves, places):
     sub = attended.shape[-1]
     rows_all = attended.size // sub
     width = w_own.shape[1]
     half = width // 2
 
-    def body(meta_ref, att, near_ref, own_ref, mine_ref, theirs_ref, halves_ref, keep, send):
+    def body(meta_ref, att, near_ref, own_ref, near_w_ref, halves_ref, keep, send):
         side = meta_ref[1] // 2
         here = pl.ds(pl.multiple_of(side * half, half), half)
         away = pl.ds(pl.multiple_of((1 - side) * half, half), half)
-        second = meta_ref[0] % 2
-        strip = sub // 2
-        lead = (slice(None),) * (len(attended.shape) - 1)
-        mine = near_ref[lead + (pl.ds(pl.multiple_of(second * strip, strip), strip),)]
-        theirs = near_ref[lead + (pl.ds(pl.multiple_of((1 - second) * strip, strip), strip),)]
-        rows = jnp.concatenate(
-            [x.reshape(rows_all, x.shape[-1]) for x in (att[...], mine, theirs)], axis=1
-        )
+        rows = jnp.concatenate([x[...].reshape(rows_all, sub) for x in (att, near_ref)], axis=1)
 
         def columns(at):
-            return jnp.concatenate([own_ref[:, at], mine_ref[:, at], theirs_ref[:, at]], axis=0)
+            return jnp.concatenate([own_ref[:, at], near_w_ref[:, at]], axis=0)
 
         send[...] = dot(rows, columns(away)).astype(bf16)
         total = dot(rows, columns(here))
@@ -360,7 +356,7 @@
 
     return pl.pallas_call(
         body,
-        in_specs=[SMEM_SPEC] + many(VMEM_SPEC, 6),
+        in_specs=[SMEM_SPEC] + many(VMEM_SPEC, 5),
         out_specs=many(VMEM_SPEC, 2),
         out_shape=[
             jax.ShapeDtypeStruct((rows_all, half), f32),
@@ -369,7 +365,7 @@
         name="part",
         compiler_params=grant(12),
         cost_estimate=cost(4 * rows_all * sub * width, 4 * sub * width + rows_all * width * 6),
-    )(meta, attended, near, w_own, w_mine, w_theirs, halves)
+    )(meta, attended, near, w_own, w_near, halves)
 
 
 def merge_out(meta, keep, got):
@@ -615,13 +611,13 @@
     gain = norm_gain.reshape(1, width)
     inter = intersection.T
     loaded = (0, 3, 1, 2)
-    projected, halves, w_half = project_views(meta, latents, gain, w_qkv, w_out, loaded)
+    w_near = across(w_out, beside)
+    projected, halves = project_views(meta, latents, gain, w_qkv, loaded)
     queries = {v: projected[v][0] for v in range(local_views)}
     blocks = {v: projected[v][1] for v in range(local_views)}
     far = {}
     far["n1"] = along(blocks[0], -1)
     far["p1"] = along(blocks[3], 1)
-    w_mine = across(w_half, beside)
 
     inner_plan = [(1, [("p1", -1, 1)]), (2, [("n1", 2, 1)])]
     inner_queries = [queries[1], queries[2]]
@@ -635,7 +631,6 @@
     attended["a"], second = attend(
         meta, inter, inner_queries, blocks, inner_far, inner_plan, window, earlier=tuple(local)
     )
-    w_theirs = partner(after(w_mine, attended["a"]), 1)
 
     def attend_outer(view, sources, done, carry=None):
         (result,) = attend(
@@ -659,8 +654,7 @@
             attended[c],
             near,
             w_out,
-            w_mine,
-            w_theirs,
+            w_near,
             halves,
             [loaded.index(v) for v in CHUNKS[c]],
         )

time: 123 us -> 118 us (0.959)
  starting transfers between devices: 57.2 us -> 54.1 us
  waiting for transfers between devices: 36.4 us -> 34.8 us
    ppermute x4, starting transfers between devices: 18.7 us -> 26.4 us  [along(): return lax.ppermute(x, VIEWS, [(i, (i + by) % peers) for i in range(peers)])]
    ppermute x11 -> x10, starting transfers between devices: 11.3 us -> 5.86 us  [partner(): return lax.ppermute(x, VIEWS, [(i, i ^ mask) for i in range(peers)])]
    ppermute x10, starting transfers between devices: 27.2 us -> 21.8 us  [across(): return lax.ppermute(x, HEADS, pairs)]
    ppermute x4, waiting for transfers between devices: 5.91 us -> 2.25 us  [along(): return lax.ppermute(x, VIEWS, [(i, (i + by) % peers) for i in range(peers)])]
    ppermute x10, waiting for transfers between devices: 19.5 us -> 21.1 us  [across(): return lax.ppermute(x, HEADS, pairs)]
    ppermute x11 -> x10, waiting for transfers between devices: 10.9 us -> 11.4 us  [partner(): return lax.ppermute(x, VIEWS, [(i, i ^ mask) for i in range(peers)])]
  transfers between devices with their start and end apart: 25 -> 24, of which waited for: 13 -> 14; matrix products, arithmetic and copies ran while one was open for 0% -> 0% of each run, Pallas kernels for 15% -> 15%
where the time goes in v6:
time: 118 us; the launch traced here: 117 us
  starting transfers between devices  54.1 us (46%)
  waiting for transfers between devices  34.8 us (29%)
  Pallas kernels  26.9 us (23%)
    ppermute x4, starting transfers between devices, along(): return lax.ppermute(x, VIEWS, [(i, (i + by) % peers) for i in range(peers)])  26.4 us
    ppermute x10, starting transfers between devices, across(): return lax.ppermute(x, HEADS, pairs)  21.8 us
    ppermute x10, waiting for transfers between devices, across(): return lax.ppermute(x, HEADS, pairs)  21.1 us
    ppermute x10, waiting for transfers between devices, partner(): return lax.ppermute(x, VIEWS, [(i, i ^ mask) for i in range(peers)])  11.4 us
    pallas_call x4, Pallas kernels, attend(): pl.pallas_call(body, in_specs=[SMEM_SPEC, SMEM_SPEC] + many(VMEM_SPEC, he...  9.05 us
    ppermute x10, starting transfers between devices, partner(): return lax.ppermute(x, VIEWS, [(i, i ^ mask) for i in range(peers)])  5.86 us
    pallas_call x1, Pallas kernels, project_views(): pl.pallas_call(body, in_specs=[SMEM_SPEC] + many(ANY_SPEC, 3), out_specs=...  5.22 us
    pallas_call x3, Pallas kernels, partial_out(): pl.pallas_call(body, in_specs=[SMEM_SPEC] + many(VMEM_SPEC, 5), out_specs...  3.25 us
  transfers between devices with their start and end apart: 24, of which 14 were waited for; matrix products, arithmetic and copies ran while one was open for 0% of the time, Pallas kernels for 15%

profile of v6, /device:TPU:0, one launch (start us, length us, event | category | flops | bytes accessed | tf_op | source)
XLA Modules:
  0.0 117.0 jit_solution(10096957500621200816)
XLA Ops:
  0.0 0.7 copy-done.3
  0.7 5.2 %proj.1 = (bf16[256,256]{1,0:T(8,128)(2,1)S(1)}, bf16[2,256,256]{2,1,0:T(8,128)(2,1)S(1)}, bf16[256,256]{1,0:T(8,128)(2,1)S(1)}, bf16[2,256,256]{2,1,0:T(8,128)(...) custom-call(s32[4]{0:T(128)S(1)} %compare_select_fusion.1.meta_ref, ...), custom_call_target="tpu_custom_call" | custom-call | flops 1610612736 | bytes 5242880 | tf_op jit(solution)/shard_map/proj/pallas_call | solution.py:114
  5.9 3.4 %collective-permute-start = (bf16[2,256,256]{2,1,0:T(8,128)(2,1)S(1)}, bf16[2,256,256]{2,1,0:T(8,128)(2,1)S(1)}, u32[]{:S(2)}, u32[]{:S(2)}) collective-permute-start(bf16[2,256,256]{2,1,0:T(8,128)(2,1)S(1)} %get-tuple-element.49.refs_2_.refs_4_.refs_1_), channel_id=1, source_target_pairs={{0,28},{4,0},{8,4},{12,8},{16,12},{20,16},{24,20},{28,24},{1,29},{... | collective-permute-start | bytes 786440 | tf_op jit(solution)/shard_map/ppermute | solution.py:599
  9.4 3.0 %att.4 = (f32[2,320,256]{2,1,0:T(8,128)S(1)}, f32[2,4,256]{2,1,0:T(4,128)S(1)}) custom-call(s32[4]{0:T(128)S(1)} %compare_select_fusion.1.meta_ref, s32[2,32]{1,0:T(2,128)S(1)} %bitcast.7, bf16[256,256]{1,0:T(8,128)(2,1)S(1)} %get-tuple-element.47.refs_0_.refs_2_, bf16[256,256]{1,0:T(8,128)(2,1)S(1)} %get-tuple-element.48.refs_1_.refs_3_, ...), custom_call_target="tpu_custom_call" | custom-call | flops 1073741824 | bytes 4194304 | tf_op jit(solution)/shard_map/att/pallas_call | solution.py:286
  12.4 3.5 %collective-permute-start.3 = (bf16[256,1024]{1,0:T(8,128)(2,1)S(1)}, bf16[256,1024]{1,0:T(8,128)(2,1)S(1)}, u32[]{:S(2)}, u32[]{:S(2)}) collective-permute-start(bf16[256,1024]{1,0:T(8,128)(2,1)S(1)} %copy-done), channel_id=1, source_target_pairs={{0,1},{3,2},{4,5},{7,6},{8,9},{11,10},{12,13},{15,14},{16,17},{19,... | collective-permute-start | bytes 1572872 | tf_op jit(solution)/shard_map/ppermute | solution.py:605
  15.9 0.1 collective-permute-done.refs_8_.refs_5_
  16.0 1.0 collective-permute-done.1.refs_9_.refs_5_
  17.1 1.7 %att.5 = (bf16[256,256]{1,0:T(8,128)(2,1)S(1)}, bf16[256,256]{1,0:T(8,128)(2,1)S(1)}) custom-call(s32[4]{0:T(128)S(1)} %compare_select_fusion.1.meta_ref, s32[2,32]{1,0:T(2,128)S(1)} %bitcast.8, f32[2,320,256]{2,1,0:T(8,128)S(1)} %get-tuple-element.53.refs_0_, f32[2,4,256]{2,1,0:T(4,128)S(1)} %get-tuple-element.54.refs_1_, ...), custom_call_target="tpu_custom_call" | custom-call | flops 268435456 | bytes 1048576 | tf_op jit(solution)/shard_map/att/pallas_call | solution.py:286
  18.8 1.1 collective-permute-done.11.refs_6_
  19.9 2.2 %att.7 = bf16[2,256,256]{2,1,0:T(8,128)(2,1)S(1)} custom-call(s32[4]{0:T(128)S(1)} %compare_select_fusion.1.meta_ref, s32[2,32]{1,0:T(2,128)S(1)} %bitcast.9, bf16[256,256]{1,0:T(8,128)(2,1)S(1)} %get-tuple-element.68.refs_0_, bf16[2,256,256]{2,1,0:T(8,128)(2,1)S(1)} %get-tuple-element.49.refs_2_.refs_4_.refs_1_, ...), custom_call_target="tpu_custom_call" | custom-call | flops 671088640 | bytes 2621440 | tf_op jit(solution)/shard_map/att/pallas_call | solution.py:286
  22.1 3.5 %collective-permute-start.12 = (bf16[2,256,256]{2,1,0:T(8,128)(2,1)S(1)}, bf16[2,256,256]{2,1,0:T(8,128)(2,1)S(1)}, u32[]{:S(2)}, u32[]{:S(2)}) collective-permute-start(bf16[2,256,256]{2,1,0:T(8,128)(2,1)S(1)} %att.7), channel_id=1, source_target_pairs={{0,1},{3,2},{4,5},{7,6},{8,9},{11,10},{12,13},{15,14},{16,17},{19,... | collective-permute-start | bytes 786440 | tf_op jit(solution)/shard_map/ppermute | solution.py:605
  25.6 22.9 %collective-permute-start.4 = (bf16[2,256,256]{2,1,0:T(8,128)(2,1)S(1)}, bf16[2,256,256]{2,1,0:T(8,128)(2,1)S(1)}, u32[]{:S(2)}, u32[]{:S(2)}) collective-permute-start(bf16[2,256,256]{2,1,0:T(8,128)(2,1)S(1)} %get-tuple-element.59.refs_3_.refs_5_.refs_2_), channel_id=1, source_target_pairs={{0,28},{4,0},{8,4},{12,8},{16,12},{20,16},{24,20},{28,24},{1,29},{... | collective-permute-start | bytes 786440 | tf_op jit(solution)/shard_map/ppermute | solution.py:599
  48.5 1.6 %collective-permute-start.2 = (bf16[256,256]{1,0:T(8,128)(2,1)S(1)}, bf16[256,256]{1,0:T(8,128)(2,1)S(1)}, u32[]{:S(2)}, u32[]{:S(2)}) collective-permute-start(bf16[256,256]{1,0:T(8,128)(2,1)S(1)} %get-tuple-element.55.att), channel_id=1, source_target_pairs={{0,1},{3,2},{4,5},{7,6},{8,9},{11,10},{12,13},{15,14},{16,17},{19,... | collective-permute-start | bytes 393224 | tf_op jit(solution)/shard_map/ppermute | solution.py:605
  50.1 2.5 %collective-permute-done.2.near_ref = bf16[256,256]{1,0:T(8,128)(2,1)S(1)} collective-permute-done((bf16[256,256]{1,0:T(8,128)(2,1)S(1)}, bf16[256,256]{1,0:T(8,128)(2,1)S(1)}, u32[]{:S(2)}, u32[]{:S(2)}) %collective-permute-start.2) | collective-permute-done | bytes 131104 | tf_op jit(solution)/shard_map/ppermute | solution.py:605
  52.6 1.0 part.3
  53.6 1.3 %part.5 = (f32[512,512]{1,0:T(8,128)S(1)}, bf16[512,512]{1,0:T(8,128)(2,1)S(1)}) custom-call(s32[4]{0:T(128)S(1)} %compare_select_fusion.1.meta_ref, bf16[2,256,256]{2,1,0:T(8,128)(2,1)S(1)} %att.7, bf16[2,256,256]{2,1,0:T(8,128)(2,1)S(1)} %collective-permute-done.12.near_ref, bf16[256,1024]{1,0:T(8,128)(2,1)S(1)} %copy-done, ...), custom_call_target="tpu_custom_call" | custom-call | flops 536870912 | bytes 4194304 | tf_op jit(solution)/shard_map/part/pallas_call | solution.py:357
  54.9 0.9 collective-permute-start.13
  55.8 2.2 %att.6 = bf16[256,256]{1,0:T(8,128)(2,1)S(1)} custom-call(s32[4]{0:T(128)S(1)} %compare_select_fusion.1.meta_ref, s32[2,32]{1,0:T(2,128)S(1)} %bitcast.10, bf16[256,256]{1,0:T(8,128)(2,1)S(1)} %get-tuple-element.58.refs_0_, bf16[2,256,256]{2,1,0:T(8,128)(2,1)S(1)} %get-tuple-element.49.refs_2_.refs_4_.refs_1_, ...), custom_call_target="tpu_custom_call" | custom-call | flops 671088640 | bytes 2621440 | tf_op jit(solution)/shard_map/att/pallas_call | solution.py:286
  58.0 7.2 %collective-permute-start.5 = (bf16[256,256]{1,0:T(8,128)(2,1)S(1)}, bf16[256,256]{1,0:T(8,128)(2,1)S(1)}, u32[]{:S(2)}, u32[]{:S(2)}) collective-permute-start(bf16[256,256]{1,0:T(8,128)(2,1)S(1)} %att.6), channel_id=1, source_target_pairs={{0,1},{3,2},{4,5},{7,6},{8,9},{11,10},{12,13},{15,14},{16,17},{19,... | collective-permute-start | bytes 393224 | tf_op jit(solution)/shard_map/ppermute | solution.py:605
  65.1 0.7 collective-permute-start.9
  65.8 1.8 %collective-permute-done.5.near_ref = bf16[256,256]{1,0:T(8,128)(2,1)S(1)} collective-permute-done((bf16[256,256]{1,0:T(8,128)(2,1)S(1)}, bf16[256,256]{1,0:T(8,128)(2,1)S(1)}, u32[]{:S(2)}, u32[]{:S(2)}) %collective-permute-start.5) | collective-permute-done | bytes 131104 | tf_op jit(solution)/shard_map/ppermute | solution.py:605
  67.6 1.0 part.4
  68.6 0.7 prep.1
  69.4 0.7 collective-permute-start.15
  70.0 0.5 collective-permute-done.6
  70.5 0.7 merge.4
  71.2 1.3 %collective-permute-start.14 = (bf16[512,256]{1,0:T(8,128)(2,1)S(1)}, bf16[512,256]{1,0:T(8,128)(2,1)S(1)}, u32[]{:S(2)}, u32[]{:S(2)}) collective-permute-start(bf16[512,256]{1,0:T(8,128)(2,1)S(1)} %get-tuple-element.74), channel_id=1, source_target_pairs={{1,0},{2,3},{5,4},{6,7},{9,8},{10,11},{13,12},{14,15},{17,16},{18,... | collective-permute-start | bytes 786440 | tf_op jit(solution)/shard_map/ppermute | solution.py:605
  72.5 1.7 %collective-permute-done.7 = s32[16,256]{1,0:T(8,128)S(1)} collective-permute-done((s32[16,256]{1,0:T(8,128)S(1)}, s32[16,256]{1,0:T(8,128)S(1)}, u32[]{:S(2)}, u32[]{:S(2)}) %collective-permute-start.7) | collective-permute-done | bytes 16416 | tf_op jit(solution)/shard_map/ppermute | solution.py:602
  74.3 0.6 merge.3
  74.9 1.3 %collective-permute-start.10 = (bf16[256,256]{1,0:T(8,128)(2,1)S(1)}, bf16[256,256]{1,0:T(8,128)(2,1)S(1)}, u32[]{:S(2)}, u32[]{:S(2)}) collective-permute-start(bf16[256,256]{1,0:T(8,128)(2,1)S(1)} %get-tuple-element.66), channel_id=1, source_target_pairs={{1,0},{2,3},{5,4},{6,7},{9,8},{10,11},{13,12},{14,15},{17,16},{18,... | collective-permute-start | bytes 393224 | tf_op jit(solution)/shard_map/ppermute | solution.py:605
  76.2 0.6 merge.5
  76.8 1.3 %collective-permute-start.16 = (bf16[256,256]{1,0:T(8,128)(2,1)S(1)}, bf16[256,256]{1,0:T(8,128)(2,1)S(1)}, u32[]{:S(2)}, u32[]{:S(2)}) collective-permute-start(bf16[256,256]{1,0:T(8,128)(2,1)S(1)} %get-tuple-element.77), channel_id=1, source_target_pairs={{1,0},{2,3},{5,4},{6,7},{9,8},{10,11},{13,12},{14,15},{17,16},{18,... | collective-permute-start | bytes 393224 | tf_op jit(solution)/shard_map/ppermute | solution.py:605
  78.2 14.7 %collective-permute-done.10.refs_1_ = bf16[256,256]{1,0:T(8,128)(2,1)S(1)} collective-permute-done((bf16[256,256]{1,0:T(8,128)(2,1)S(1)}, bf16[256,256]{1,0:T(8,128)(2,1)S(1)}, u32[]{:S(2)}, u32[]{:S(2)}) %collective-permute-start.10) | collective-permute-done | bytes 131104 | tf_op jit(solution)/shard_map/ppermute | solution.py:605
  92.9 2.1 %collective-permute-done.16.refs_5_ = bf16[256,256]{1,0:T(8,128)(2,1)S(1)} collective-permute-done((bf16[256,256]{1,0:T(8,128)(2,1)S(1)}, bf16[256,256]{1,0:T(8,128)(2,1)S(1)}, u32[]{:S(2)}, u32[]{:S(2)}) %collective-permute-start.16) | collective-permute-done | bytes 131104 | tf_op jit(solution)/shard_map/ppermute | solution.py:605
  95.0 1.5 %gath.2 = (bf16[1024,256]{1,0:T(8,128)(2,1)S(1)}, bf16[256,256]{1,0:T(8,128)(2,1)S(1)}, bf16[256,256]{1,0:T(8,128)(2,1)S(1)}, bf16[256,256]{1,0:T(8,128)(2,1)S(1)}, bf16[256,256]{1,0:T(8,128)(2,1)S(1)}) custom-call(s32[4]{0:T(128)S(1)} %compare_select_fusion.1.meta_ref, s32[64,256]{1,0:T(8,128)S(1)} %constant_dynamic-update-slice_fusion.wanted_ref, ...), custom_call_target="tpu_custom_call" | custom-call | flops 536870912 | bytes 2097152 | tf_op jit(solution)/shard_map/gath/pallas_call | solution.py:479
  96.5 1.0 collective-permute-start.18
  97.5 0.9 collective-permute-start.20
  98.3 2.6 %collective-permute-start.21 = (bf16[256,256]{1,0:T(8,128)(2,1)S(1)}, bf16[256,256]{1,0:T(8,128)(2,1)S(1)}, u32[]{:S(2)}, u32[]{:S(2)}) collective-permute-start(bf16[256,256]{1,0:T(8,128)(2,1)S(1)} %get-tuple-element.84), channel_id=1, source_target_pairs={{0,28},{4,24},{8,20},{12,16},{16,12},{20,8},{24,4},{28,0},{1,29},{... | collective-permute-start | bytes 393224 | tf_op jit(solution)/shard_map/ppermute | solution.py:602
  101.0 1.5 %gath.3 = (bf16[256,256]{1,0:T(8,128)(2,1)S(1)}, bf16[256,256]{1,0:T(8,128)(2,1)S(1)}, bf16[256,256]{1,0:T(8,128)(2,1)S(1)}, bf16[256,256]{1,0:T(8,128)(2,1)S(1)}) custom-call(s32[4]{0:T(128)S(1)} %compare_select_fusion.1.meta_ref, s32[64,256]{1,0:T(8,128)S(1)} %constant_dynamic-update-slice_fusion.wanted_ref, ...), custom_call_target="tpu_custom_call" | custom-call | flops 536870912 | bytes 2097152 | tf_op jit(solution)/shard_map/gath/pallas_call | solution.py:479
  102.5 0.1 collective-permute-start.17
  102.6 5.7 %collective-permute-done.18.refs_2_ = bf16[256,256]{1,0:T(8,128)(2,1)S(1)} collective-permute-done((bf16[256,256]{1,0:T(8,128)(2,1)S(1)}, bf16[256,256]{1,0:T(8,128)(2,1)S(1)}, u32[]{:S(2)}, u32[]{:S(2)}) %collective-permute-start.18) | collective-permute-done | bytes 131104 | tf_op jit(solution)/shard_map/ppermute | solution.py:602
  108.2 0.5 collective-permute-start.22
  108.7 0.2 collective-permute-done.19.refs_3_
  108.9 0.9 collective-permute-start.23
  109.8 1.7 %first.1.early_ref = bf16[1024,256]{1,0:T(8,128)(2,1)S(1)} custom-call(s32[4]{0:T(128)S(1)} %compare_select_fusion.1.meta_ref, s32[8,128]{1,0:T(8,128)S(1)} %get-tuple-element.62.code_ref, bf16[256,256]{1,0:T(8,128)(2,1)S(1)} %get-tuple-element.79.refs_0_, bf16[256,256]{1,0:T(8,128)(2,1)S(1)} %collective-permute-done.17.refs_1_, ...), custom_call_target="tpu_custom_call" | custom-call | flops 805306368 | bytes 1048576 | tf_op jit(solution)/shard_map/first/pallas_call | solution.py:529
  111.5 3.0 %collective-permute-done.22.refs_0_ = bf16[256,256]{1,0:T(8,128)(2,1)S(1)} collective-permute-done((bf16[256,256]{1,0:T(8,128)(2,1)S(1)}, bf16[256,256]{1,0:T(8,128)(2,1)S(1)}, u32[]{:S(2)}, u32[]{:S(2)}) %collective-permute-start.22) | collective-permute-done | bytes 131104 | tf_op jit(solution)/shard_map/ppermute | solution.py:602
  114.5 0.2 collective-permute-done.23.refs_1_
  114.7 2.1 %fin.1 = f32[1024,256]{1,0:T(8,128)} custom-call(s32[4]{0:T(128)S(1)} %compare_select_fusion.1.meta_ref, s32[8,128]{1,0:T(8,128)S(1)} %get-tuple-element.62.code_ref, f32[8,128]{1,0:T(8,128)S(1)} %bitcast.6, bf16[1024,256]{1,0:T(8,128)(2,1)S(1)} %get-tuple-element.78.refs_0_.layer_ref, bf16[1024,256]{1,0:T(8,128)(2,1)S(1)} %first.1.early_ref, ...), custom_call_target="tpu_custom_call" | custom-call | flops 268435456 | bytes 2097152 | tf_op jit(solution)/shard_map/fin/pallas_call | solution.py:570
  (35 shorter events, 0.2 us)
Async XLA Ops:
  0.0 0.7 copy-start.3
  0.7 8.7 %copy-start.2 = (s32[32,2]{0,1:T(2,128)S(1)}, s32[32,2]{0,1:T(2,128)}, u32[]{:S(2)}) copy-start(s32[32,2]{0,1:T(2,128)} %param.12) | copy-start | bytes 772
  5.9 6.5 %copy-start = (bf16[256,1024]{1,0:T(8,128)(2,1)S(1)}, bf16[256,1024]{1,0:T(8,128)(2,1)}, u32[]{:S(2)}) copy-start(bf16[256,1024]{1,0:T(8,128)(2,1)} %own_ref.5) | copy-start | bytes 1572868
  5.9 10.1 %collective-permute-start = (bf16[2,256,256]{2,1,0:T(8,128)(2,1)S(1)}, bf16[2,256,256]{2,1,0:T(8,128)(2,1)S(1)}, u32[]{:S(2)}, u32[]{:S(2)}) collective-permute-start(bf16[2,256,256]{2,1,0:T(8,128)(2,1)S(1)} %get-tuple-element.49.refs_2_.refs_4_.refs_1_), channel_id=1, source_target_pairs={{0,28},{4,0},{8,4},{12,8},{16,12},{20,16},{24,20},{28,24},{1,29},{... | collective-permute-start | bytes 786440 | tf_op jit(solution)/shard_map/ppermute | solution.py:599
  9.3 7.7 %collective-permute-start.1 = (bf16[2,256,256]{2,1,0:T(8,128)(2,1)S(1)}, bf16[2,256,256]{2,1,0:T(8,128)(2,1)S(1)}, u32[]{:S(2)}, u32[]{:S(2)}) collective-permute-start(bf16[2,256,256]{2,1,0:T(8,128)(2,1)S(1)} %get-tuple-element.52.refs_5_.refs_7_.refs_4_), channel_id=1, source_target_pairs={{0,4},{4,8},{8,12},{12,16},{16,20},{20,24},{24,28},{28,0},{1,5},{5... | collective-permute-start | bytes 786440 | tf_op jit(solution)/shard_map/ppermute | solution.py:599
  12.3 7.6 %collective-permute-start.11 = (bf16[2,256,256]{2,1,0:T(8,128)(2,1)S(1)}, bf16[2,256,256]{2,1,0:T(8,128)(2,1)S(1)}, u32[]{:S(2)}, u32[]{:S(2)}) collective-permute-start(bf16[2,256,256]{2,1,0:T(8,128)(2,1)S(1)} %get-tuple-element.69.refs_4_.refs_6_.refs_3_), channel_id=1, source_target_pairs={{0,4},{4,8},{8,12},{12,16},{16,20},{20,24},{24,28},{28,0},{1,5},{5... | collective-permute-start | bytes 786440 | tf_op jit(solution)/shard_map/ppermute | solution.py:599
  12.4 40.2 %collective-permute-start.3 = (bf16[256,1024]{1,0:T(8,128)(2,1)S(1)}, bf16[256,1024]{1,0:T(8,128)(2,1)S(1)}, u32[]{:S(2)}, u32[]{:S(2)}) collective-permute-start(bf16[256,1024]{1,0:T(8,128)(2,1)S(1)} %copy-done), channel_id=1, source_target_pairs={{0,1},{3,2},{4,5},{7,6},{8,9},{11,10},{12,13},{15,14},{16,17},{19,... | collective-permute-start | bytes 1572872 | tf_op jit(solution)/shard_map/ppermute | solution.py:605
  22.1 31.5 %collective-permute-start.12 = (bf16[2,256,256]{2,1,0:T(8,128)(2,1)S(1)}, bf16[2,256,256]{2,1,0:T(8,128)(2,1)S(1)}, u32[]{:S(2)}, u32[]{:S(2)}) collective-permute-start(bf16[2,256,256]{2,1,0:T(8,128)(2,1)S(1)} %att.7), channel_id=1, source_target_pairs={{0,1},{3,2},{4,5},{7,6},{8,9},{11,10},{12,13},{15,14},{16,17},{19,... | collective-permute-start | bytes 786440 | tf_op jit(solution)/shard_map/ppermute | solution.py:605
  25.6 30.2 %collective-permute-start.4 = (bf16[2,256,256]{2,1,0:T(8,128)(2,1)S(1)}, bf16[2,256,256]{2,1,0:T(8,128)(2,1)S(1)}, u32[]{:S(2)}, u32[]{:S(2)}) collective-permute-start(bf16[2,256,256]{2,1,0:T(8,128)(2,1)S(1)} %get-tuple-element.59.refs_3_.refs_5_.refs_2_), channel_id=1, source_target_pairs={{0,28},{4,0},{8,4},{12,8},{16,12},{20,16},{24,20},{28,24},{1,29},{... | collective-permute-start | bytes 786440 | tf_op jit(solution)/shard_map/ppermute | solution.py:599
  48.5 4.1 %collective-permute-start.2 = (bf16[256,256]{1,0:T(8,128)(2,1)S(1)}, bf16[256,256]{1,0:T(8,128)(2,1)S(1)}, u32[]{:S(2)}, u32[]{:S(2)}) collective-permute-start(bf16[256,256]{1,0:T(8,128)(2,1)S(1)} %get-tuple-element.55.att), channel_id=1, source_target_pairs={{0,1},{3,2},{4,5},{7,6},{8,9},{11,10},{12,13},{15,14},{16,17},{19,... | collective-permute-start | bytes 393224 | tf_op jit(solution)/shard_map/ppermute | solution.py:605
  54.9 13.8 %copy-start.4 = (s32[1024,1]{0,1:T(1,128)S(1)}, s32[1024,1]{0,1:T(1,128)}, u32[]{:S(2)}) copy-start(s32[1024,1]{0,1:T(1,128)} %param.13) | copy-start | bytes 12292
  54.9 13.8 %copy-start.5 = (s32[1024]{0:T(1024)S(1)}, s32[1024]{0:T(1024)}, u32[]{:S(2)}) copy-start(s32[1024]{0:T(1024)} %param.14) | copy-start | bytes 12292
  54.9 15.7 %collective-permute-start.13 = (bf16[512,512]{1,0:T(8,128)(2,1)S(1)}, bf16[512,512]{1,0:T(8,128)(2,1)S(1)}, u32[]{:S(2)}, u32[]{:S(2)}) collective-permute-start(bf16[512,512]{1,0:T(8,128)(2,1)S(1)} %get-tuple-element.72), channel_id=1, source_target_pairs={{1,2},{2,1},{5,6},{6,5},{9,10},{10,9},{13,14},{14,13},{17,18},{18,... | collective-permute-start | bytes 1572872 | tf_op jit(solution)/shard_map/ppermute | solution.py:605
  58.0 9.7 %collective-permute-start.5 = (bf16[256,256]{1,0:T(8,128)(2,1)S(1)}, bf16[256,256]{1,0:T(8,128)(2,1)S(1)}, u32[]{:S(2)}, u32[]{:S(2)}) collective-permute-start(bf16[256,256]{1,0:T(8,128)(2,1)S(1)} %att.6), channel_id=1, source_target_pairs={{0,1},{3,2},{4,5},{7,6},{8,9},{11,10},{12,13},{15,14},{16,17},{19,... | collective-permute-start | bytes 393224 | tf_op jit(solution)/shard_map/ppermute | solution.py:605
  65.1 9.1 %collective-permute-start.9 = (bf16[256,512]{1,0:T(8,128)(2,1)S(1)}, bf16[256,512]{1,0:T(8,128)(2,1)S(1)}, u32[]{:S(2)}, u32[]{:S(2)}) collective-permute-start(bf16[256,512]{1,0:T(8,128)(2,1)S(1)} %get-tuple-element.57), channel_id=1, source_target_pairs={{1,2},{2,1},{5,6},{6,5},{9,10},{10,9},{13,14},{14,13},{17,18},{18,... | collective-permute-start | bytes 786440 | tf_op jit(solution)/shard_map/ppermute | solution.py:605
  69.3 1.2 %collective-permute-start.6 = (s32[8,256]{1,0:T(8,128)S(1)}, s32[8,256]{1,0:T(8,128)S(1)}, u32[]{:S(2)}, u32[]{:S(2)}) collective-permute-start(s32[8,256]{1,0:T(8,128)S(1)} %get-tuple-element.63), channel_id=1, source_target_pairs={{0,4},{4,0},{8,12},{12,8},{16,20},{20,16},{24,28},{28,24},{1,5},{5... | collective-permute-start | bytes 24584 | tf_op jit(solution)/shard_map/ppermute | solution.py:602
  69.4 6.8 %collective-permute-start.15 = (bf16[256,512]{1,0:T(8,128)(2,1)S(1)}, bf16[256,512]{1,0:T(8,128)(2,1)S(1)}, u32[]{:S(2)}, u32[]{:S(2)}) collective-permute-start(bf16[256,512]{1,0:T(8,128)(2,1)S(1)} %get-tuple-element.60), channel_id=1, source_target_pairs={{1,2},{2,1},{5,6},{6,5},{9,10},{10,9},{13,14},{14,13},{17,18},{18,... | collective-permute-start | bytes 786440 | tf_op jit(solution)/shard_map/ppermute | solution.py:605
  70.5 3.7 %collective-permute-start.7 = (s32[16,256]{1,0:T(8,128)S(1)}, s32[16,256]{1,0:T(8,128)S(1)}, u32[]{:S(2)}, u32[]{:S(2)}) collective-permute-start(s32[16,256]{1,0:T(8,128)S(1)} %pad_add_fusion.1), channel_id=1, source_target_pairs={{0,8},{4,12},{8,0},{12,4},{16,24},{20,28},{24,16},{28,20},{1,9},{5... | collective-permute-start | bytes 49160 | tf_op jit(solution)/shard_map/ppermute | solution.py:602
  71.2 23.8 %collective-permute-start.14 = (bf16[512,256]{1,0:T(8,128)(2,1)S(1)}, bf16[512,256]{1,0:T(8,128)(2,1)S(1)}, u32[]{:S(2)}, u32[]{:S(2)}) collective-permute-start(bf16[512,256]{1,0:T(8,128)(2,1)S(1)} %get-tuple-element.74), channel_id=1, source_target_pairs={{1,0},{2,3},{5,4},{6,7},{9,8},{10,11},{13,12},{14,15},{17,16},{18,... | collective-permute-start | bytes 786440 | tf_op jit(solution)/shard_map/ppermute | solution.py:605
  74.3 3.9 %collective-permute-start.8 = (s32[32,256]{1,0:T(8,128)S(1)}, s32[32,256]{1,0:T(8,128)S(1)}, u32[]{:S(2)}, u32[]{:S(2)}) collective-permute-start(s32[32,256]{1,0:T(8,128)S(1)} %pad_add_fusion), channel_id=1, source_target_pairs={{0,16},{4,20},{8,24},{12,28},{16,0},{20,4},{24,8},{28,12},{1,17},{... | collective-permute-start | bytes 98312 | tf_op jit(solution)/shard_map/ppermute | solution.py:602
  74.9 18.0 %collective-permute-start.10 = (bf16[256,256]{1,0:T(8,128)(2,1)S(1)}, bf16[256,256]{1,0:T(8,128)(2,1)S(1)}, u32[]{:S(2)}, u32[]{:S(2)}) collective-permute-start(bf16[256,256]{1,0:T(8,128)(2,1)S(1)} %get-tuple-element.66), channel_id=1, source_target_pairs={{1,0},{2,3},{5,4},{6,7},{9,8},{10,11},{13,12},{14,15},{17,16},{18,... | collective-permute-start | bytes 393224 | tf_op jit(solution)/shard_map/ppermute | solution.py:605
  76.8 18.2 %collective-permute-start.16 = (bf16[256,256]{1,0:T(8,128)(2,1)S(1)}, bf16[256,256]{1,0:T(8,128)(2,1)S(1)}, u32[]{:S(2)}, u32[]{:S(2)}) collective-permute-start(bf16[256,256]{1,0:T(8,128)(2,1)S(1)} %get-tuple-element.77), channel_id=1, source_target_pairs={{1,0},{2,3},{5,4},{6,7},{9,8},{10,11},{13,12},{14,15},{17,16},{18,... | collective-permute-start | bytes 393224 | tf_op jit(solution)/shard_map/ppermute | solution.py:605
  96.5 11.7 %collective-permute-start.18 = (bf16[256,256]{1,0:T(8,128)(2,1)S(1)}, bf16[256,256]{1,0:T(8,128)(2,1)S(1)}, u32[]{:S(2)}, u32[]{:S(2)}) collective-permute-start(bf16[256,256]{1,0:T(8,128)(2,1)S(1)} %get-tuple-element.81), channel_id=1, source_target_pairs={{0,16},{4,20},{8,24},{12,28},{16,0},{20,4},{24,8},{28,12},{1,17},{... | collective-permute-start | bytes 393224 | tf_op jit(solution)/shard_map/ppermute | solution.py:602
  97.5 11.4 %collective-permute-start.19 = (bf16[256,256]{1,0:T(8,128)(2,1)S(1)}, bf16[256,256]{1,0:T(8,128)(2,1)S(1)}, u32[]{:S(2)}, u32[]{:S(2)}) collective-permute-start(bf16[256,256]{1,0:T(8,128)(2,1)S(1)} %get-tuple-element.82), channel_id=1, source_target_pairs={{0,20},{4,16},{8,28},{12,24},{16,4},{20,0},{24,12},{28,8},{1,21},{... | collective-permute-start | bytes 393224 | tf_op jit(solution)/shard_map/ppermute | solution.py:602
  97.5 12.3 %collective-permute-start.20 = (bf16[256,256]{1,0:T(8,128)(2,1)S(1)}, bf16[256,256]{1,0:T(8,128)(2,1)S(1)}, u32[]{:S(2)}, u32[]{:S(2)}) collective-permute-start(bf16[256,256]{1,0:T(8,128)(2,1)S(1)} %get-tuple-element.83), channel_id=1, source_target_pairs={{0,24},{4,28},{8,16},{12,20},{16,8},{20,12},{24,0},{28,4},{1,25},{... | collective-permute-start | bytes 393224 | tf_op jit(solution)/shard_map/ppermute | solution.py:602
  98.3 11.4 %collective-permute-start.21 = (bf16[256,256]{1,0:T(8,128)(2,1)S(1)}, bf16[256,256]{1,0:T(8,128)(2,1)S(1)}, u32[]{:S(2)}, u32[]{:S(2)}) collective-permute-start(bf16[256,256]{1,0:T(8,128)(2,1)S(1)} %get-tuple-element.84), channel_id=1, source_target_pairs={{0,28},{4,24},{8,20},{12,16},{16,12},{20,8},{24,4},{28,0},{1,29},{... | collective-permute-start | bytes 393224 | tf_op jit(solution)/shard_map/ppermute | solution.py:602
  101.0 13.7 %copy-start.1 = (f32[1024]{0:T(1024)S(1)}, f32[1024]{0:T(1024)}, u32[]{:S(2)}) copy-start(f32[1024]{0:T(1024)} %param.15) | copy-start | bytes 12292
  102.5 7.3 %collective-permute-start.17 = (bf16[256,256]{1,0:T(8,128)(2,1)S(1)}, bf16[256,256]{1,0:T(8,128)(2,1)S(1)}, u32[]{:S(2)}, u32[]{:S(2)}) collective-permute-start(bf16[256,256]{1,0:T(8,128)(2,1)S(1)} %get-tuple-element.80), channel_id=1, source_target_pairs={{0,4},{4,0},{8,12},{12,8},{16,20},{20,16},{24,28},{28,24},{1,5},{5... | collective-permute-start | bytes 393224 | tf_op jit(solution)/shard_map/ppermute | solution.py:602
  108.2 6.3 %collective-permute-start.22 = (bf16[256,256]{1,0:T(8,128)(2,1)S(1)}, bf16[256,256]{1,0:T(8,128)(2,1)S(1)}, u32[]{:S(2)}, u32[]{:S(2)}) collective-permute-start(bf16[256,256]{1,0:T(8,128)(2,1)S(1)} %get-tuple-element.85), channel_id=1, source_target_pairs={{0,8},{4,12},{8,0},{12,4},{16,24},{20,28},{24,16},{28,20},{1,9},{5... | collective-permute-start | bytes 393224 | tf_op jit(solution)/shard_map/ppermute | solution.py:602
  108.9 5.8 %collective-permute-start.23 = (bf16[256,256]{1,0:T(8,128)(2,1)S(1)}, bf16[256,256]{1,0:T(8,128)(2,1)S(1)}, u32[]{:S(2)}, u32[]{:S(2)}) collective-permute-start(bf16[256,256]{1,0:T(8,128)(2,1)S(1)} %get-tuple-element.86), channel_id=1, source_target_pairs={{0,12},{4,8},{8,4},{12,0},{16,28},{20,24},{24,20},{28,16},{1,13},{... | collective-permute-start | bytes 393224 | tf_op jit(solution)/shard_map/ppermute | solution.py:602

commit v7 on v6

--- a/solution.py
+++ b/solution.py
@@ -9,7 +9,8 @@
 VIEWS, HEADS = "views", "heads"
 HEAD_DIM = 64
 LANES = 128
-STAGED = 4
+STAGED = 3
+GRANT_A, GRANT_B = 50, 50
 CHUNKS = dict(a=(1,), b=(2, 0), c=(3,))
 
 coupling = 0.5
@@ -42,30 +43,32 @@
     return [spec] * count
 
 
-def project_views(meta, latents, gain, w_qkv, which):
+def project_views(meta, latents, gain, w_qkv, which, loaded=False):
     _, tokens, width = latents.shape
     sub = w_qkv.shape[2]
     count = len(which)
     scale = HEAD_DIM ** (-0.5)
-    order = (2, 0, 1)
-
-    def body(meta_ref, lat_hbm, gain_hbm, w_hbm, *refs):
-        outs, (halves, buffer, gains, ws, sems) = refs[: 2 * count], refs[2 * count :]
+
+    def body(meta_ref, lat_hbm, gain_ref, w_ref, *refs):
+        outs, refs = refs[: 2 * count], refs[2 * count :]
+        halves, refs = refs[0], refs[1:]
+        ws = w_ref if loaded else refs[0]
+        buffer, sems = refs[-2:]
         here = pl.ds(pl.multiple_of((meta_ref[1] // 2) * (width // 2), width // 2), width // 2)
         kept = [
-            pltpu.make_async_copy(buffer.at[i, :, here], halves.at[i], sems.at[count + 4 + i])
+            pltpu.make_async_copy(buffer.at[i, :, here], halves.at[i], sems.at[i])
             for i in range(count)
         ]
         copies = [
-            pltpu.make_async_copy(lat_hbm.at[v], buffer.at[i], sems.at[i])
+            pltpu.make_async_copy(lat_hbm.at[v], buffer.at[i], sems.at[count + i])
             for i, v in enumerate(which)
         ]
-        gain_copy = pltpu.make_async_copy(gain_hbm, gains, sems.at[count])
-        w_copies = {
-            part: pltpu.make_async_copy(w_hbm.at[part], ws.at[part], sems.at[count + 1 + part])
-            for part in order
-        }
-        queue = [copies[0], gain_copy, w_copies[2], w_copies[0], w_copies[1]] + copies[1:]
+        w_copies = []
+        if not loaded:
+            w_copies = [
+                pltpu.make_async_copy(w_ref.at[p], ws.at[p], sems.at[2 * count + p]) for p in range(3)
+            ]
+        queue = copies[:1] + w_copies[::-1] + copies[1:]
         for copy in queue[:STAGED]:
             copy.start()
         waiting = queue[STAGED:]
@@ -78,27 +81,26 @@
         def load_norm(i):
             arrive(copies[i])
             kept[i].start()
-            if i == 0:
-                arrive(gain_copy)
             wide = buffer[i].astype(f32)
             mean_square = jnp.mean(wide * wide, axis=-1, keepdims=True)
-            return (wide * lax.rsqrt(mean_square + epsilon) * gains[...]).astype(bf16)
+            return (wide * lax.rsqrt(mean_square + epsilon) * gain_ref[...]).astype(bf16)
 
         following = load_norm(0)
         for i in range(count):
             normed = following
-            if i == 0:
+            staged = i == 0 and not loaded
+            if staged:
                 arrive(w_copies[2])
             elif i + 1 < count:
                 following = load_norm(i + 1)
             values = dot(normed, ws[2])
-            if i == 0:
+            if staged:
+                arrive(w_copies[1])
+            outs[2 * i + 1][0] = dot(normed, ws[1]).astype(bf16)
+            if staged:
                 arrive(w_copies[0])
+                following = load_norm(i + 1)
             queries = dot(normed, ws[0])
-            if i == 0:
-                arrive(w_copies[1])
-                following = load_norm(i + 1)
-            outs[2 * i + 1][0] = dot(normed, ws[1]).astype(bf16)
             outs[2 * i + 1][1] = jnp.transpose(values).astype(bf16)
             outs[2 * i][...] = jnp.transpose(queries).astype(bf16) * jnp.asarray(scale, bf16)
         for copy in kept:
@@ -111,24 +113,25 @@
             jax.ShapeDtypeStruct((2, tokens, sub), bf16),
         ]
     out_shape.append(jax.ShapeDtypeStruct((count, tokens, width // 2), bf16))
+    if not loaded:
+        out_shape.append(jax.ShapeDtypeStruct(w_qkv.shape, bf16))
     outs = pl.pallas_call(
         body,
-        in_specs=[SMEM_SPEC] + many(ANY_SPEC, 3),
+        in_specs=[SMEM_SPEC, ANY_SPEC, VMEM_SPEC, VMEM_SPEC if loaded else ANY_SPEC],
         out_specs=many(VMEM_SPEC, len(out_shape)),
         out_shape=out_shape,
         scratch_shapes=[
             pltpu.VMEM((count, tokens, width), bf16),
-            pltpu.VMEM((1, width), f32),
-            pltpu.VMEM((3, width, sub), bf16),
-            pltpu.SemaphoreType.DMA((2 * count + 4,)),
+            pltpu.SemaphoreType.DMA((2 * count + 3,)),
         ],
         name="proj",
-        compiler_params=grant(50),
+        compiler_params=grant(GRANT_B if loaded else GRANT_A),
         cost_estimate=cost(
             count * 6 * tokens * width * sub, count * tokens * (width + 3 * sub) * 2 + 6 * width * sub
         ),
     )(meta, latents, gain, w_qkv)
-    return {v: (outs[2 * i], outs[2 * i + 1]) for i, v in enumerate(which)}, outs[-1]
+    views = {v: (outs[2 * i], outs[2 * i + 1]) for i, v in enumerate(which)}
+    return views, outs[2 * count], outs[-1]
 
 
 ONES = 16
@@ -334,13 +337,14 @@
     lax.fori_loop(0, heads, one_head, 0)
 
 
-def partial_out(meta, attended, near, w_own, w_near, halves, places):
+def partial_out(meta, attended, near, w_own, w_near, base):
     sub = attended.shape[-1]
     rows_all = attended.size // sub
     width = w_own.shape[1]
     half = width // 2
 
-    def body(meta_ref, att, near_ref, own_ref, near_w_ref, halves_ref, keep, send):
+    def body(meta_ref, att, near_ref, own_ref, near_w_ref, *refs):
+        keep, send = refs[-2:]
         side = meta_ref[1] // 2
         here = pl.ds(pl.multiple_of(side * half, half), half)
         away = pl.ds(pl.multiple_of((1 - side) * half, half), half)
@@ -351,12 +355,12 @@
 
         send[...] = dot(rows, columns(away)).astype(bf16)
         total = dot(rows, columns(here))
-        base = jnp.concatenate([halves_ref[p] for p in places], axis=0)
-        keep[...] = base.astype(f32) + total
+        start = jnp.concatenate([ref[place] for ref, (_, place) in zip(refs, base)], axis=0)
+        keep[...] = start.astype(f32) + total
 
     return pl.pallas_call(
         body,
-        in_specs=[SMEM_SPEC] + many(VMEM_SPEC, 5),
+        in_specs=[SMEM_SPEC] + many(VMEM_SPEC, 4 + len(base)),
         out_specs=many(VMEM_SPEC, 2),
         out_shape=[
             jax.ShapeDtypeStruct((rows_all, half), f32),
@@ -365,7 +369,7 @@
         name="part",
         compiler_params=grant(12),
         cost_estimate=cost(4 * rows_all * sub * width, 4 * sub * width + rows_all * width * 6),
-    )(meta, attended, near, w_own, w_near, halves)
+    )(meta, attended, near, w_own, w_near, *[array for array, _ in base])
 
 
 def merge_out(meta, keep, got):
@@ -610,23 +614,25 @@
     beside, middle, back = [(0, 1), (3, 2)], [(1, 2), (2, 1)], [(1, 0), (2, 3)]
     gain = norm_gain.reshape(1, width)
     inter = intersection.T
-    loaded = (0, 3, 1, 2)
     w_near = across(w_out, beside)
-    projected, halves = project_views(meta, latents, gain, w_qkv, loaded)
+    far = {}
+    projected, edge_halves, weights = project_views(meta, latents, gain, w_qkv, (0, 3))
+    far["n1"] = along(projected[0][1], -1)
+    far["p1"] = along(projected[3][1], 1)
+    more, inner_halves, _ = project_views(meta, latents, gain, weights, (1, 2), loaded=True)
+    projected.update(more)
     queries = {v: projected[v][0] for v in range(local_views)}
     blocks = {v: projected[v][1] for v in range(local_views)}
-    far = {}
-    far["n1"] = along(blocks[0], -1)
-    far["p1"] = along(blocks[3], 1)
+    inner_far = dict(far)
+    far["n2"] = along(blocks[1], -1)
+    far["p2"] = along(blocks[2], 1)
+    base = {0: (edge_halves, 0), 3: (edge_halves, 1), 1: (inner_halves, 0), 2: (inner_halves, 1)}
 
     inner_plan = [(1, [("p1", -1, 1)]), (2, [("n1", 2, 1)])]
     inner_queries = [queries[1], queries[2]]
     local = attend(
         meta, inter, inner_queries, blocks, {}, [(v, []) for v, _ in inner_plan], window, last=False
     )
-    inner_far = dict(far)
-    far["n2"] = along(after(blocks[1], local[0]), -1)
-    far["p2"] = along(after(blocks[2], local[0]), 1)
     attended = {}
     attended["a"], second = attend(
         meta, inter, inner_queries, blocks, inner_far, inner_plan, window, earlier=tuple(local)
@@ -655,8 +661,7 @@
             near,
             w_out,
             w_near,
-            halves,
-            [loaded.index(v) for v in CHUNKS[c]],
+            [base[v] for v in CHUNKS[c]],
         )
         got[c] = across(sent[c], middle)
 

time: 118 us -> 118 us (level)
  Pallas kernels: 26.9 us -> 28.6 us
    ppermute x4, waiting for transfers between devices: 2.25 us -> 0.01 us  [along(): return lax.ppermute(x, VIEWS, [(i, (i + by) % peers) for i in range(peers)])]
    pallas_call x4 -> x5, Pallas kernels: 8.47 us -> 10.2 us  [the longest x2 6.96 us: project_views(): pl.pallas_call(body, in_specs=[SMEM_SPEC, ANY_SPEC, VMEM_SPEC, VMEM_SPEC...]
    ppermute x10, waiting for transfers between devices: 21.1 us -> 22.6 us  [across(): return lax.ppermute(x, HEADS, pairs)]
  transfers between devices with their start and end apart: 24 -> 24, of which waited for: 14 -> 10; matrix products, arithmetic and copies ran while one was open for 0% -> 0% of each run, Pallas kernels for 15% -> 17%
where the time goes in v7:
time: 118 us
  starting transfers between devices  53.5 us (45%)
  waiting for transfers between devices  34.5 us (29%)
  Pallas kernels  28.6 us (24%)
    ppermute x4, starting transfers between devices, along(): return lax.ppermute(x, VIEWS, [(i, (i + by) % peers) for i in range(peers)])  27 us
    ppermute x10, waiting for transfers between devices, across(): return lax.ppermute(x, HEADS, pairs)  22.6 us
    ppermute x10, starting transfers between devices, across(): return lax.ppermute(x, HEADS, pairs)  21 us
    ppermute x10, waiting for transfers between devices, partner(): return lax.ppermute(x, VIEWS, [(i, i ^ mask) for i in range(peers)])  11.8 us
    pallas_call x4, Pallas kernels, attend(): pl.pallas_call(body, in_specs=[SMEM_SPEC, SMEM_SPEC] + many(VMEM_SPEC, he...  9.03 us
    pallas_call x2, Pallas kernels, project_views(): pl.pallas_call(body, in_specs=[SMEM_SPEC, ANY_SPEC, VMEM_SPEC, VMEM_SPEC...  6.96 us
    ppermute x10, starting transfers between devices, partner(): return lax.ppermute(x, VIEWS, [(i, i ^ mask) for i in range(peers)])  5.54 us
    pallas_call x3, Pallas kernels, partial_out(): pl.pallas_call(body, in_specs=[SMEM_SPEC] + many(VMEM_SPEC, 4 + len(base)...  3.27 us
  transfers between devices with their start and end apart: 24, of which 10 were waited for; matrix products, arithmetic and copies ran while one was open for 0% of the time, Pallas kernels for 17%

profile of v7, /device:TPU:0, one launch (start us, length us, event | category | flops | bytes accessed | tf_op | source)
XLA Modules:
  0.0 117.9 jit_solution(17440741009458167434)
XLA Ops:
  0.0 0.7 copy-done.1
  0.7 3.9 %proj.2 = (bf16[256,256]{1,0:T(8,128)(2,1)S(1)}, bf16[2,256,256]{2,1,0:T(8,128)(2,1)S(1)}, bf16[256,256]{1,0:T(8,128)(2,1)S(1)}, bf16[2,256,256]{2,1,0:T(8,128)(...) custom-call(s32[4]{0:T(128)S(1)} %compare_select_fusion.1.meta_ref, ...), custom_call_target="tpu_custom_call" | custom-call | flops 805306368 | bytes 3407872 | tf_op jit(solution)/shard_map/proj/pallas_call | solution.py:118
  4.6 3.4 %collective-permute-start = (bf16[2,256,256]{2,1,0:T(8,128)(2,1)S(1)}, bf16[2,256,256]{2,1,0:T(8,128)(2,1)S(1)}, u32[]{:S(2)}, u32[]{:S(2)}) collective-permute-start(bf16[2,256,256]{2,1,0:T(8,128)(2,1)S(1)} %get-tuple-element.50.refs_2_.refs_4_.refs_1_), channel_id=1, source_target_pairs={{0,28},{4,0},{8,4},{12,8},{16,12},{20,16},{24,20},{28,24},{1,29},{... | collective-permute-start | bytes 786440 | tf_op jit(solution)/shard_map/ppermute | solution.py:603
  8.0 3.0 %proj.3 = (bf16[256,256]{1,0:T(8,128)(2,1)S(1)}, bf16[2,256,256]{2,1,0:T(8,128)(2,1)S(1)}, bf16[256,256]{1,0:T(8,128)(2,1)S(1)}, bf16[2,256,256]{2,1,0:T(8,128)(2,1)S(1)}, bf16[2,256,512]{2,1,0:T(8,128)(2,1)S(1)}) custom-call(s32[4]{0:T(128)S(1)} %compare_select_fusion.1.meta_ref, bf16[4,256,1024]{2,1,0:T(8,128)(2,1)} %lat_hbm.3, f32[1,1024]{1,0:T(1,128)S(1)} %bitcast.7, ...), custom_call_target="tpu_custom_call" | custom-call | flops 805306368 | bytes 3407872 | tf_op jit(solution)/shard_map/proj/pallas_call | solution.py:118
  11.1 0.1 collective-permute-start.11
  11.2 3.5 %collective-permute-start.3 = (bf16[256,1024]{1,0:T(8,128)(2,1)S(1)}, bf16[256,1024]{1,0:T(8,128)(2,1)S(1)}, u32[]{:S(2)}, u32[]{:S(2)}) collective-permute-start(bf16[256,1024]{1,0:T(8,128)(2,1)S(1)} %copy-done), channel_id=1, source_target_pairs={{0,1},{3,2},{4,5},{7,6},{8,9},{11,10},{12,13},{15,14},{16,17},{19,... | collective-permute-start | bytes 1572872 | tf_op jit(solution)/shard_map/ppermute | solution.py:609
  14.7 2.9 %att.4 = (f32[2,320,256]{2,1,0:T(8,128)S(1)}, f32[2,4,256]{2,1,0:T(4,128)S(1)}) custom-call(s32[4]{0:T(128)S(1)} %compare_select_fusion.1.meta_ref, s32[2,32]{1,0:T(2,128)S(1)} %bitcast.9, bf16[256,256]{1,0:T(8,128)(2,1)S(1)} %get-tuple-element.48.refs_0_.refs_2_, bf16[256,256]{1,0:T(8,128)(2,1)S(1)} %get-tuple-element.49.refs_1_.refs_3_, ...), custom_call_target="tpu_custom_call" | custom-call | flops 1073741824 | bytes 4194304 | tf_op jit(solution)/shard_map/att/pallas_call | solution.py:289
  17.7 1.7 %att.5 = (bf16[256,256]{1,0:T(8,128)(2,1)S(1)}, bf16[256,256]{1,0:T(8,128)(2,1)S(1)}) custom-call(s32[4]{0:T(128)S(1)} %compare_select_fusion.1.meta_ref, s32[2,32]{1,0:T(2,128)S(1)} %bitcast.10, f32[2,320,256]{2,1,0:T(8,128)S(1)} %get-tuple-element.54.refs_0_, f32[2,4,256]{2,1,0:T(4,128)S(1)} %get-tuple-element.55.refs_1_, ...), custom_call_target="tpu_custom_call" | custom-call | flops 268435456 | bytes 1048576 | tf_op jit(solution)/shard_map/att/pallas_call | solution.py:289
  19.4 2.2 %att.7 = bf16[2,256,256]{2,1,0:T(8,128)(2,1)S(1)} custom-call(s32[4]{0:T(128)S(1)} %compare_select_fusion.1.meta_ref, s32[2,32]{1,0:T(2,128)S(1)} %bitcast.11, bf16[256,256]{1,0:T(8,128)(2,1)S(1)} %get-tuple-element.69.refs_0_, bf16[2,256,256]{2,1,0:T(8,128)(2,1)S(1)} %get-tuple-element.50.refs_2_.refs_4_.refs_1_, ...), custom_call_target="tpu_custom_call" | custom-call | flops 671088640 | bytes 2621440 | tf_op jit(solution)/shard_map/att/pallas_call | solution.py:289
  21.6 2.7 %collective-permute-start.12 = (bf16[2,256,256]{2,1,0:T(8,128)(2,1)S(1)}, bf16[2,256,256]{2,1,0:T(8,128)(2,1)S(1)}, u32[]{:S(2)}, u32[]{:S(2)}) collective-permute-start(bf16[2,256,256]{2,1,0:T(8,128)(2,1)S(1)} %att.7), channel_id=1, source_target_pairs={{0,1},{3,2},{4,5},{7,6},{8,9},{11,10},{12,13},{15,14},{16,17},{19,... | collective-permute-start | bytes 786440 | tf_op jit(solution)/shard_map/ppermute | solution.py:609
  24.3 23.5 %collective-permute-start.4 = (bf16[2,256,256]{2,1,0:T(8,128)(2,1)S(1)}, bf16[2,256,256]{2,1,0:T(8,128)(2,1)S(1)}, u32[]{:S(2)}, u32[]{:S(2)}) collective-permute-start(bf16[2,256,256]{2,1,0:T(8,128)(2,1)S(1)} %get-tuple-element.51.refs_3_.refs_5_.refs_2_), channel_id=1, source_target_pairs={{0,28},{4,0},{8,4},{12,8},{16,12},{20,16},{24,20},{28,24},{1,29},{... | collective-permute-start | bytes 786440 | tf_op jit(solution)/shard_map/ppermute | solution.py:603
  47.8 1.6 %collective-permute-start.2 = (bf16[256,256]{1,0:T(8,128)(2,1)S(1)}, bf16[256,256]{1,0:T(8,128)(2,1)S(1)}, u32[]{:S(2)}, u32[]{:S(2)}) collective-permute-start(bf16[256,256]{1,0:T(8,128)(2,1)S(1)} %get-tuple-element.56.att), channel_id=1, source_target_pairs={{0,1},{3,2},{4,5},{7,6},{8,9},{11,10},{12,13},{15,14},{16,17},{19,... | collective-permute-start | bytes 393224 | tf_op jit(solution)/shard_map/ppermute | solution.py:609
  49.3 2.5 %collective-permute-done.2.near_ref = bf16[256,256]{1,0:T(8,128)(2,1)S(1)} collective-permute-done((bf16[256,256]{1,0:T(8,128)(2,1)S(1)}, bf16[256,256]{1,0:T(8,128)(2,1)S(1)}, u32[]{:S(2)}, u32[]{:S(2)}) %collective-permute-start.2) | collective-permute-done | bytes 131104 | tf_op jit(solution)/shard_map/ppermute | solution.py:609
  51.8 1.0 part.3
  52.8 1.3 %part.5 = (f32[512,512]{1,0:T(8,128)S(1)}, bf16[512,512]{1,0:T(8,128)(2,1)S(1)}) custom-call(s32[4]{0:T(128)S(1)} %compare_select_fusion.1.meta_ref, bf16[2,256,256]{2,1,0:T(8,128)(2,1)S(1)} %att.7, bf16[2,256,256]{2,1,0:T(8,128)(2,1)S(1)} %collective-permute-done.12.near_ref, bf16[256,1024]{1,0:T(8,128)(2,1)S(1)} %copy-done, ...), custom_call_target="tpu_custom_call" | custom-call | flops 536870912 | bytes 4194304 | tf_op jit(solution)/shard_map/part/pallas_call | solution.py:361
  54.1 0.9 collective-permute-start.13
  55.0 2.2 %att.6 = bf16[256,256]{1,0:T(8,128)(2,1)S(1)} custom-call(s32[4]{0:T(128)S(1)} %compare_select_fusion.1.meta_ref, s32[2,32]{1,0:T(2,128)S(1)} %bitcast.12, bf16[256,256]{1,0:T(8,128)(2,1)S(1)} %get-tuple-element.59.refs_0_, bf16[2,256,256]{2,1,0:T(8,128)(2,1)S(1)} %get-tuple-element.50.refs_2_.refs_4_.refs_1_, ...), custom_call_target="tpu_custom_call" | custom-call | flops 671088640 | bytes 2621440 | tf_op jit(solution)/shard_map/att/pallas_call | solution.py:289
  57.2 7.2 %collective-permute-start.5 = (bf16[256,256]{1,0:T(8,128)(2,1)S(1)}, bf16[256,256]{1,0:T(8,128)(2,1)S(1)}, u32[]{:S(2)}, u32[]{:S(2)}) collective-permute-start(bf16[256,256]{1,0:T(8,128)(2,1)S(1)} %att.6), channel_id=1, source_target_pairs={{0,1},{3,2},{4,5},{7,6},{8,9},{11,10},{12,13},{15,14},{16,17},{19,... | collective-permute-start | bytes 393224 | tf_op jit(solution)/shard_map/ppermute | solution.py:609
  64.4 0.7 collective-permute-start.9
  65.1 1.8 %collective-permute-done.5.near_ref = bf16[256,256]{1,0:T(8,128)(2,1)S(1)} collective-permute-done((bf16[256,256]{1,0:T(8,128)(2,1)S(1)}, bf16[256,256]{1,0:T(8,128)(2,1)S(1)}, u32[]{:S(2)}, u32[]{:S(2)}) %collective-permute-start.5) | collective-permute-done | bytes 131104 | tf_op jit(solution)/shard_map/ppermute | solution.py:609
  66.9 1.0 part.4
  67.9 0.7 prep.1
  68.6 0.7 collective-permute-start.15
  69.3 0.5 collective-permute-done.6
  69.8 0.7 collective-permute-start.7
  70.5 0.7 merge.4
  71.2 1.3 %collective-permute-start.14 = (bf16[512,256]{1,0:T(8,128)(2,1)S(1)}, bf16[512,256]{1,0:T(8,128)(2,1)S(1)}, u32[]{:S(2)}, u32[]{:S(2)}) collective-permute-start(bf16[512,256]{1,0:T(8,128)(2,1)S(1)} %get-tuple-element.74), channel_id=1, source_target_pairs={{1,0},{2,3},{5,4},{6,7},{9,8},{10,11},{13,12},{14,15},{17,16},{18,... | collective-permute-start | bytes 786440 | tf_op jit(solution)/shard_map/ppermute | solution.py:609
  72.5 1.1 collective-permute-done.7
  73.5 0.6 merge.3
  74.1 1.3 %collective-permute-start.10 = (bf16[256,256]{1,0:T(8,128)(2,1)S(1)}, bf16[256,256]{1,0:T(8,128)(2,1)S(1)}, u32[]{:S(2)}, u32[]{:S(2)}) collective-permute-start(bf16[256,256]{1,0:T(8,128)(2,1)S(1)} %get-tuple-element.67), channel_id=1, source_target_pairs={{1,0},{2,3},{5,4},{6,7},{9,8},{10,11},{13,12},{14,15},{17,16},{18,... | collective-permute-start | bytes 393224 | tf_op jit(solution)/shard_map/ppermute | solution.py:609
  75.5 0.6 merge.5
  76.1 1.3 %collective-permute-start.16 = (bf16[256,256]{1,0:T(8,128)(2,1)S(1)}, bf16[256,256]{1,0:T(8,128)(2,1)S(1)}, u32[]{:S(2)}, u32[]{:S(2)}) collective-permute-start(bf16[256,256]{1,0:T(8,128)(2,1)S(1)} %get-tuple-element.77), channel_id=1, source_target_pairs={{1,0},{2,3},{5,4},{6,7},{9,8},{10,11},{13,12},{14,15},{17,16},{18,... | collective-permute-start | bytes 393224 | tf_op jit(solution)/shard_map/ppermute | solution.py:609
  77.4 0.1 collective-permute-done.8
  77.4 16.3 %collective-permute-done.10.refs_1_ = bf16[256,256]{1,0:T(8,128)(2,1)S(1)} collective-permute-done((bf16[256,256]{1,0:T(8,128)(2,1)S(1)}, bf16[256,256]{1,0:T(8,128)(2,1)S(1)}, u32[]{:S(2)}, u32[]{:S(2)}) %collective-permute-start.10) | collective-permute-done | bytes 131104 | tf_op jit(solution)/shard_map/ppermute | solution.py:609
  93.7 2.1 %collective-permute-done.16.refs_5_ = bf16[256,256]{1,0:T(8,128)(2,1)S(1)} collective-permute-done((bf16[256,256]{1,0:T(8,128)(2,1)S(1)}, bf16[256,256]{1,0:T(8,128)(2,1)S(1)}, u32[]{:S(2)}, u32[]{:S(2)}) %collective-permute-start.16) | collective-permute-done | bytes 131104 | tf_op jit(solution)/shard_map/ppermute | solution.py:609
  95.8 1.5 %gath.2 = (bf16[1024,256]{1,0:T(8,128)(2,1)S(1)}, bf16[256,256]{1,0:T(8,128)(2,1)S(1)}, bf16[256,256]{1,0:T(8,128)(2,1)S(1)}, bf16[256,256]{1,0:T(8,128)(2,1)S(1)}, bf16[256,256]{1,0:T(8,128)(2,1)S(1)}) custom-call(s32[4]{0:T(128)S(1)} %compare_select_fusion.1.meta_ref, s32[64,256]{1,0:T(8,128)S(1)} %constant_dynamic-update-slice_fusion.wanted_ref, ...), custom_call_target="tpu_custom_call" | custom-call | flops 536870912 | bytes 2097152 | tf_op jit(solution)/shard_map/gath/pallas_call | solution.py:483
  97.3 1.5 %gath.3 = (bf16[256,256]{1,0:T(8,128)(2,1)S(1)}, bf16[256,256]{1,0:T(8,128)(2,1)S(1)}, bf16[256,256]{1,0:T(8,128)(2,1)S(1)}, bf16[256,256]{1,0:T(8,128)(2,1)S(1)}) custom-call(s32[4]{0:T(128)S(1)} %compare_select_fusion.1.meta_ref, s32[64,256]{1,0:T(8,128)S(1)} %constant_dynamic-update-slice_fusion.wanted_ref, ...), custom_call_target="tpu_custom_call" | custom-call | flops 536870912 | bytes 2097152 | tf_op jit(solution)/shard_map/gath/pallas_call | solution.py:483
  98.8 0.1 collective-permute-start.17
  98.9 0.1 collective-permute-start.18
  99.0 1.8 %collective-permute-start.19 = (bf16[256,256]{1,0:T(8,128)(2,1)S(1)}, bf16[256,256]{1,0:T(8,128)(2,1)S(1)}, u32[]{:S(2)}, u32[]{:S(2)}) collective-permute-start(bf16[256,256]{1,0:T(8,128)(2,1)S(1)} %get-tuple-element.82), channel_id=1, source_target_pairs={{0,20},{4,16},{8,28},{12,24},{16,4},{20,0},{24,12},{28,8},{1,21},{... | collective-permute-start | bytes 393224 | tf_op jit(solution)/shard_map/ppermute | solution.py:606
  100.7 0.0 collective-permute-start.20
  100.8 2.6 %collective-permute-start.21 = (bf16[256,256]{1,0:T(8,128)(2,1)S(1)}, bf16[256,256]{1,0:T(8,128)(2,1)S(1)}, u32[]{:S(2)}, u32[]{:S(2)}) collective-permute-start(bf16[256,256]{1,0:T(8,128)(2,1)S(1)} %get-tuple-element.84), channel_id=1, source_target_pairs={{0,28},{4,24},{8,20},{12,16},{16,12},{20,8},{24,4},{28,0},{1,29},{... | collective-permute-start | bytes 393224 | tf_op jit(solution)/shard_map/ppermute | solution.py:606
  103.4 0.3 collective-permute-start.22
  103.7 7.3 %collective-permute-done.18.refs_2_ = bf16[256,256]{1,0:T(8,128)(2,1)S(1)} collective-permute-done((bf16[256,256]{1,0:T(8,128)(2,1)S(1)}, bf16[256,256]{1,0:T(8,128)(2,1)S(1)}, u32[]{:S(2)}, u32[]{:S(2)}) %collective-permute-start.18) | collective-permute-done | bytes 131104 | tf_op jit(solution)/shard_map/ppermute | solution.py:606
  111.0 1.7 %collective-permute-done.19.refs_3_ = bf16[256,256]{1,0:T(8,128)(2,1)S(1)} collective-permute-done((bf16[256,256]{1,0:T(8,128)(2,1)S(1)}, bf16[256,256]{1,0:T(8,128)(2,1)S(1)}, u32[]{:S(2)}, u32[]{:S(2)}) %collective-permute-start.19) | collective-permute-done | bytes 131104 | tf_op jit(solution)/shard_map/ppermute | solution.py:606
  112.7 1.7 %first.1.early_ref = bf16[1024,256]{1,0:T(8,128)(2,1)S(1)} custom-call(s32[4]{0:T(128)S(1)} %compare_select_fusion.1.meta_ref, s32[8,128]{1,0:T(8,128)S(1)} %get-tuple-element.63.code_ref, bf16[256,256]{1,0:T(8,128)(2,1)S(1)} %get-tuple-element.79.refs_0_, bf16[256,256]{1,0:T(8,128)(2,1)S(1)} %collective-permute-done.17.refs_1_, ...), custom_call_target="tpu_custom_call" | custom-call | flops 805306368 | bytes 1048576 | tf_op jit(solution)/shard_map/first/pallas_call | solution.py:533
  114.4 1.2 %collective-permute-done.23.refs_1_ = bf16[256,256]{1,0:T(8,128)(2,1)S(1)} collective-permute-done((bf16[256,256]{1,0:T(8,128)(2,1)S(1)}, bf16[256,256]{1,0:T(8,128)(2,1)S(1)}, u32[]{:S(2)}, u32[]{:S(2)}) %collective-permute-start.23) | collective-permute-done | bytes 131104 | tf_op jit(solution)/shard_map/ppermute | solution.py:606
  115.6 2.1 %fin.1 = f32[1024,256]{1,0:T(8,128)} custom-call(s32[4]{0:T(128)S(1)} %compare_select_fusion.1.meta_ref, s32[8,128]{1,0:T(8,128)S(1)} %get-tuple-element.63.code_ref, f32[8,128]{1,0:T(8,128)S(1)} %bitcast.8, bf16[1024,256]{1,0:T(8,128)(2,1)S(1)} %get-tuple-element.78.refs_0_.layer_ref, bf16[1024,256]{1,0:T(8,128)(2,1)S(1)} %first.1.early_ref, ...), custom_call_target="tpu_custom_call" | custom-call | flops 268435456 | bytes 2097152 | tf_op jit(solution)/shard_map/fin/pallas_call | solution.py:574
  (36 shorter events, 0.1 us)
Async XLA Ops:
  0.0 0.7 copy-start.1
  4.6 13.0 %collective-permute-start = (bf16[2,256,256]{2,1,0:T(8,128)(2,1)S(1)}, bf16[2,256,256]{2,1,0:T(8,128)(2,1)S(1)}, u32[]{:S(2)}, u32[]{:S(2)}) collective-permute-start(bf16[2,256,256]{2,1,0:T(8,128)(2,1)S(1)} %get-tuple-element.50.refs_2_.refs_4_.refs_1_), channel_id=1, source_target_pairs={{0,28},{4,0},{8,4},{12,8},{16,12},{20,16},{24,20},{28,24},{1,29},{... | collective-permute-start | bytes 786440 | tf_op jit(solution)/shard_map/ppermute | solution.py:603
  8.0 9.6 %collective-permute-start.1 = (bf16[2,256,256]{2,1,0:T(8,128)(2,1)S(1)}, bf16[2,256,256]{2,1,0:T(8,128)(2,1)S(1)}, u32[]{:S(2)}, u32[]{:S(2)}) collective-permute-start(bf16[2,256,256]{2,1,0:T(8,128)(2,1)S(1)} %get-tuple-element.53.refs_5_.refs_7_.refs_4_), channel_id=1, source_target_pairs={{0,4},{4,8},{8,12},{12,16},{16,20},{20,24},{24,28},{28,0},{1,5},{5... | collective-permute-start | bytes 786440 | tf_op jit(solution)/shard_map/ppermute | solution.py:603
  8.0 3.1 %copy-start = (bf16[256,1024]{1,0:T(8,128)(2,1)S(1)}, bf16[256,1024]{1,0:T(8,128)(2,1)}, u32[]{:S(2)}) copy-start(bf16[256,1024]{1,0:T(8,128)(2,1)} %own_ref.5) | copy-start | bytes 1572868
  8.0 6.6 %copy-start.3 = (s32[32,2]{0,1:T(2,128)S(1)}, s32[32,2]{0,1:T(2,128)}, u32[]{:S(2)}) copy-start(s32[32,2]{0,1:T(2,128)} %param.12) | copy-start | bytes 772
  11.1 8.3 %collective-permute-start.11 = (bf16[2,256,256]{2,1,0:T(8,128)(2,1)S(1)}, bf16[2,256,256]{2,1,0:T(8,128)(2,1)S(1)}, u32[]{:S(2)}, u32[]{:S(2)}) collective-permute-start(bf16[2,256,256]{2,1,0:T(8,128)(2,1)S(1)} %get-tuple-element.52.refs_4_.refs_6_.refs_3_), channel_id=1, source_target_pairs={{0,4},{4,8},{8,12},{12,16},{16,20},{20,24},{24,28},{28,0},{1,5},{5... | collective-permute-start | bytes 786440 | tf_op jit(solution)/shard_map/ppermute | solution.py:603
  11.2 40.7 %collective-permute-start.3 = (bf16[256,1024]{1,0:T(8,128)(2,1)S(1)}, bf16[256,1024]{1,0:T(8,128)(2,1)S(1)}, u32[]{:S(2)}, u32[]{:S(2)}) collective-permute-start(bf16[256,1024]{1,0:T(8,128)(2,1)S(1)} %copy-done), channel_id=1, source_target_pairs={{0,1},{3,2},{4,5},{7,6},{8,9},{11,10},{12,13},{15,14},{16,17},{19,... | collective-permute-start | bytes 1572872 | tf_op jit(solution)/shard_map/ppermute | solution.py:609
  21.6 31.2 %collective-permute-start.12 = (bf16[2,256,256]{2,1,0:T(8,128)(2,1)S(1)}, bf16[2,256,256]{2,1,0:T(8,128)(2,1)S(1)}, u32[]{:S(2)}, u32[]{:S(2)}) collective-permute-start(bf16[2,256,256]{2,1,0:T(8,128)(2,1)S(1)} %att.7), channel_id=1, source_target_pairs={{0,1},{3,2},{4,5},{7,6},{8,9},{11,10},{12,13},{15,14},{16,17},{19,... | collective-permute-start | bytes 786440 | tf_op jit(solution)/shard_map/ppermute | solution.py:609
  24.3 30.8 %collective-permute-start.4 = (bf16[2,256,256]{2,1,0:T(8,128)(2,1)S(1)}, bf16[2,256,256]{2,1,0:T(8,128)(2,1)S(1)}, u32[]{:S(2)}, u32[]{:S(2)}) collective-permute-start(bf16[2,256,256]{2,1,0:T(8,128)(2,1)S(1)} %get-tuple-element.51.refs_3_.refs_5_.refs_2_), channel_id=1, source_target_pairs={{0,28},{4,0},{8,4},{12,8},{16,12},{20,16},{24,20},{28,24},{1,29},{... | collective-permute-start | bytes 786440 | tf_op jit(solution)/shard_map/ppermute | solution.py:603
  47.8 4.1 %collective-permute-start.2 = (bf16[256,256]{1,0:T(8,128)(2,1)S(1)}, bf16[256,256]{1,0:T(8,128)(2,1)S(1)}, u32[]{:S(2)}, u32[]{:S(2)}) collective-permute-start(bf16[256,256]{1,0:T(8,128)(2,1)S(1)} %get-tuple-element.56.att), channel_id=1, source_target_pairs={{0,1},{3,2},{4,5},{7,6},{8,9},{11,10},{12,13},{15,14},{16,17},{19,... | collective-permute-start | bytes 393224 | tf_op jit(solution)/shard_map/ppermute | solution.py:609
  54.1 13.8 %copy-start.4 = (s32[1024,1]{0,1:T(1,128)S(1)}, s32[1024,1]{0,1:T(1,128)}, u32[]{:S(2)}) copy-start(s32[1024,1]{0,1:T(1,128)} %param.13) | copy-start | bytes 12292
  54.1 13.8 %copy-start.5 = (s32[1024]{0:T(1024)S(1)}, s32[1024]{0:T(1024)}, u32[]{:S(2)}) copy-start(s32[1024]{0:T(1024)} %param.14) | copy-start | bytes 12292
  54.1 16.4 %collective-permute-start.13 = (bf16[512,512]{1,0:T(8,128)(2,1)S(1)}, bf16[512,512]{1,0:T(8,128)(2,1)S(1)}, u32[]{:S(2)}, u32[]{:S(2)}) collective-permute-start(bf16[512,512]{1,0:T(8,128)(2,1)S(1)} %get-tuple-element.72), channel_id=1, source_target_pairs={{1,2},{2,1},{5,6},{6,5},{9,10},{10,9},{13,14},{14,13},{17,18},{18,... | collective-permute-start | bytes 1572872 | tf_op jit(solution)/shard_map/ppermute | solution.py:609
  57.2 9.7 %collective-permute-start.5 = (bf16[256,256]{1,0:T(8,128)(2,1)S(1)}, bf16[256,256]{1,0:T(8,128)(2,1)S(1)}, u32[]{:S(2)}, u32[]{:S(2)}) collective-permute-start(bf16[256,256]{1,0:T(8,128)(2,1)S(1)} %att.6), channel_id=1, source_target_pairs={{0,1},{3,2},{4,5},{7,6},{8,9},{11,10},{12,13},{15,14},{16,17},{19,... | collective-permute-start | bytes 393224 | tf_op jit(solution)/shard_map/ppermute | solution.py:609
  64.4 9.2 %collective-permute-start.9 = (bf16[256,512]{1,0:T(8,128)(2,1)S(1)}, bf16[256,512]{1,0:T(8,128)(2,1)S(1)}, u32[]{:S(2)}, u32[]{:S(2)}) collective-permute-start(bf16[256,512]{1,0:T(8,128)(2,1)S(1)} %get-tuple-element.58), channel_id=1, source_target_pairs={{1,2},{2,1},{5,6},{6,5},{9,10},{10,9},{13,14},{14,13},{17,18},{18,... | collective-permute-start | bytes 786440 | tf_op jit(solution)/shard_map/ppermute | solution.py:609
  68.6 1.2 %collective-permute-start.6 = (s32[8,256]{1,0:T(8,128)S(1)}, s32[8,256]{1,0:T(8,128)S(1)}, u32[]{:S(2)}, u32[]{:S(2)}) collective-permute-start(s32[8,256]{1,0:T(8,128)S(1)} %get-tuple-element.64), channel_id=1, source_target_pairs={{0,4},{4,0},{8,12},{12,8},{16,20},{20,16},{24,28},{28,24},{1,5},{5... | collective-permute-start | bytes 24584 | tf_op jit(solution)/shard_map/ppermute | solution.py:606
  68.6 6.8 %collective-permute-start.15 = (bf16[256,512]{1,0:T(8,128)(2,1)S(1)}, bf16[256,512]{1,0:T(8,128)(2,1)S(1)}, u32[]{:S(2)}, u32[]{:S(2)}) collective-permute-start(bf16[256,512]{1,0:T(8,128)(2,1)S(1)} %get-tuple-element.61), channel_id=1, source_target_pairs={{1,2},{2,1},{5,6},{6,5},{9,10},{10,9},{13,14},{14,13},{17,18},{18,... | collective-permute-start | bytes 786440 | tf_op jit(solution)/shard_map/ppermute | solution.py:609
  69.8 3.7 %collective-permute-start.7 = (s32[16,256]{1,0:T(8,128)S(1)}, s32[16,256]{1,0:T(8,128)S(1)}, u32[]{:S(2)}, u32[]{:S(2)}) collective-permute-start(s32[16,256]{1,0:T(8,128)S(1)} %pad_add_fusion.1), channel_id=1, source_target_pairs={{0,8},{4,12},{8,0},{12,4},{16,24},{20,28},{24,16},{28,20},{1,9},{5... | collective-permute-start | bytes 49160 | tf_op jit(solution)/shard_map/ppermute | solution.py:606
  71.2 24.6 %collective-permute-start.14 = (bf16[512,256]{1,0:T(8,128)(2,1)S(1)}, bf16[512,256]{1,0:T(8,128)(2,1)S(1)}, u32[]{:S(2)}, u32[]{:S(2)}) collective-permute-start(bf16[512,256]{1,0:T(8,128)(2,1)S(1)} %get-tuple-element.74), channel_id=1, source_target_pairs={{1,0},{2,3},{5,4},{6,7},{9,8},{10,11},{13,12},{14,15},{17,16},{18,... | collective-permute-start | bytes 786440 | tf_op jit(solution)/shard_map/ppermute | solution.py:609
  73.5 3.9 %collective-permute-start.8 = (s32[32,256]{1,0:T(8,128)S(1)}, s32[32,256]{1,0:T(8,128)S(1)}, u32[]{:S(2)}, u32[]{:S(2)}) collective-permute-start(s32[32,256]{1,0:T(8,128)S(1)} %pad_add_fusion), channel_id=1, source_target_pairs={{0,16},{4,20},{8,24},{12,28},{16,0},{20,4},{24,8},{28,12},{1,17},{... | collective-permute-start | bytes 98312 | tf_op jit(solution)/shard_map/ppermute | solution.py:606
  74.1 19.6 %collective-permute-start.10 = (bf16[256,256]{1,0:T(8,128)(2,1)S(1)}, bf16[256,256]{1,0:T(8,128)(2,1)S(1)}, u32[]{:S(2)}, u32[]{:S(2)}) collective-permute-start(bf16[256,256]{1,0:T(8,128)(2,1)S(1)} %get-tuple-element.67), channel_id=1, source_target_pairs={{1,0},{2,3},{5,4},{6,7},{9,8},{10,11},{13,12},{14,15},{17,16},{18,... | collective-permute-start | bytes 393224 | tf_op jit(solution)/shard_map/ppermute | solution.py:609
  76.1 19.7 %collective-permute-start.16 = (bf16[256,256]{1,0:T(8,128)(2,1)S(1)}, bf16[256,256]{1,0:T(8,128)(2,1)S(1)}, u32[]{:S(2)}, u32[]{:S(2)}) collective-permute-start(bf16[256,256]{1,0:T(8,128)(2,1)S(1)} %get-tuple-element.77), channel_id=1, source_target_pairs={{1,0},{2,3},{5,4},{6,7},{9,8},{10,11},{13,12},{14,15},{17,16},{18,... | collective-permute-start | bytes 393224 | tf_op jit(solution)/shard_map/ppermute | solution.py:609
  98.8 16.8 %copy-start.2 = (f32[1024]{0:T(1024)S(1)}, f32[1024]{0:T(1024)}, u32[]{:S(2)}) copy-start(f32[1024]{0:T(1024)} %param.15) | copy-start | bytes 12292
  98.8 4.5 %collective-permute-start.17 = (bf16[256,256]{1,0:T(8,128)(2,1)S(1)}, bf16[256,256]{1,0:T(8,128)(2,1)S(1)}, u32[]{:S(2)}, u32[]{:S(2)}) collective-permute-start(bf16[256,256]{1,0:T(8,128)(2,1)S(1)} %get-tuple-element.80), channel_id=1, source_target_pairs={{0,4},{4,0},{8,12},{12,8},{16,20},{20,16},{24,28},{28,24},{1,5},{5... | collective-permute-start | bytes 393224 | tf_op jit(solution)/shard_map/ppermute | solution.py:606
  98.9 12.1 %collective-permute-start.18 = (bf16[256,256]{1,0:T(8,128)(2,1)S(1)}, bf16[256,256]{1,0:T(8,128)(2,1)S(1)}, u32[]{:S(2)}, u32[]{:S(2)}) collective-permute-start(bf16[256,256]{1,0:T(8,128)(2,1)S(1)} %get-tuple-element.81), channel_id=1, source_target_pairs={{0,16},{4,20},{8,24},{12,28},{16,0},{20,4},{24,8},{28,12},{1,17},{... | collective-permute-start | bytes 393224 | tf_op jit(solution)/shard_map/ppermute | solution.py:606
  99.0 13.7 %collective-permute-start.19 = (bf16[256,256]{1,0:T(8,128)(2,1)S(1)}, bf16[256,256]{1,0:T(8,128)(2,1)S(1)}, u32[]{:S(2)}, u32[]{:S(2)}) collective-permute-start(bf16[256,256]{1,0:T(8,128)(2,1)S(1)} %get-tuple-element.82), channel_id=1, source_target_pairs={{0,20},{4,16},{8,28},{12,24},{16,4},{20,0},{24,12},{28,8},{1,21},{... | collective-permute-start | bytes 393224 | tf_op jit(solution)/shard_map/ppermute | solution.py:606
  100.7 11.9 %collective-permute-start.20 = (bf16[256,256]{1,0:T(8,128)(2,1)S(1)}, bf16[256,256]{1,0:T(8,128)(2,1)S(1)}, u32[]{:S(2)}, u32[]{:S(2)}) collective-permute-start(bf16[256,256]{1,0:T(8,128)(2,1)S(1)} %get-tuple-element.83), channel_id=1, source_target_pairs={{0,24},{4,28},{8,16},{12,20},{16,8},{20,12},{24,0},{28,4},{1,25},{... | collective-permute-start | bytes 393224 | tf_op jit(solution)/shard_map/ppermute | solution.py:606
  100.8 11.9 %collective-permute-start.21 = (bf16[256,256]{1,0:T(8,128)(2,1)S(1)}, bf16[256,256]{1,0:T(8,128)(2,1)S(1)}, u32[]{:S(2)}, u32[]{:S(2)}) collective-permute-start(bf16[256,256]{1,0:T(8,128)(2,1)S(1)} %get-tuple-element.84), channel_id=1, source_target_pairs={{0,28},{4,24},{8,20},{12,16},{16,12},{20,8},{24,4},{28,0},{1,29},{... | collective-permute-start | bytes 393224 | tf_op jit(solution)/shard_map/ppermute | solution.py:606
  103.4 11.0 %collective-permute-start.22 = (bf16[256,256]{1,0:T(8,128)(2,1)S(1)}, bf16[256,256]{1,0:T(8,128)(2,1)S(1)}, u32[]{:S(2)}, u32[]{:S(2)}) collective-permute-start(bf16[256,256]{1,0:T(8,128)(2,1)S(1)} %get-tuple-element.85), channel_id=1, source_target_pairs={{0,8},{4,12},{8,0},{12,4},{16,24},{20,28},{24,16},{28,20},{1,9},{5... | collective-permute-start | bytes 393224 | tf_op jit(solution)/shard_map/ppermute | solution.py:606
  110.9 4.7 %collective-permute-start.23 = (bf16[256,256]{1,0:T(8,128)(2,1)S(1)}, bf16[256,256]{1,0:T(8,128)(2,1)S(1)}, u32[]{:S(2)}, u32[]{:S(2)}) collective-permute-start(bf16[256,256]{1,0:T(8,128)(2,1)S(1)} %get-tuple-element.86), channel_id=1, source_target_pairs={{0,12},{4,8},{8,4},{12,0},{16,28},{20,24},{24,20},{28,16},{1,13},{... | collective-permute-start | bytes 393224 | tf_op jit(solution)/shard_map/ppermute | solution.py:606

commit v8 on v7

--- a/solution.py
+++ b/solution.py
@@ -10,7 +10,7 @@
 HEAD_DIM = 64
 LANES = 128
 STAGED = 3
-GRANT_A, GRANT_B = 50, 50
+GRANT_A, GRANT_B = 50, 40
 CHUNKS = dict(a=(1,), b=(2, 0), c=(3,))
 
 coupling = 0.5
@@ -43,32 +43,36 @@
     return [spec] * count
 
 
-def project_views(meta, latents, gain, w_qkv, which, loaded=False):
-    _, tokens, width = latents.shape
+def project_views(meta, latents, gain, w_qkv, which, following=()):
+    tokens, width = latents.shape[1:]
     sub = w_qkv.shape[2]
-    count = len(which)
+    count, ahead = len(which), len(following)
     scale = HEAD_DIM ** (-0.5)
 
-    def body(meta_ref, lat_hbm, gain_ref, w_ref, *refs):
+    def body(meta_ref, lat_ref, gain_ref, w_ref, *refs):
         outs, refs = refs[: 2 * count], refs[2 * count :]
         halves, refs = refs[0], refs[1:]
-        ws = w_ref if loaded else refs[0]
-        buffer, sems = refs[-2:]
+        ws, source = (refs[0], refs[2]) if ahead else (w_ref, lat_ref)
+        sems = refs[-1]
         here = pl.ds(pl.multiple_of((meta_ref[1] // 2) * (width // 2), width // 2), width // 2)
         kept = [
-            pltpu.make_async_copy(buffer.at[i, :, here], halves.at[i], sems.at[i])
+            pltpu.make_async_copy(source.at[i, :, here], halves.at[i], sems.at[i])
             for i in range(count)
         ]
-        copies = [
-            pltpu.make_async_copy(lat_hbm.at[v], buffer.at[i], sems.at[count + i])
-            for i, v in enumerate(which)
-        ]
-        w_copies = []
-        if not loaded:
-            w_copies = [
+        queue, loads, parts = [], [], []
+        if ahead:
+            loads = [
+                pltpu.make_async_copy(lat_ref.at[v], source.at[i], sems.at[count + i])
+                for i, v in enumerate(which)
+            ]
+            parts = [
                 pltpu.make_async_copy(w_ref.at[p], ws.at[p], sems.at[2 * count + p]) for p in range(3)
             ]
-        queue = copies[:1] + w_copies[::-1] + copies[1:]
+            later = [
+                pltpu.make_async_copy(lat_ref.at[v], refs[1].at[i], sems.at[2 * count + 3 + i])
+                for i, v in enumerate(following)
+            ]
+            queue = loads + [parts[2], parts[1], parts[0]] + later
         for copy in queue[:STAGED]:
             copy.start()
         waiting = queue[STAGED:]
@@ -78,32 +82,26 @@
             if waiting:
                 waiting.pop(0).start()
 
-        def load_norm(i):
-            arrive(copies[i])
+        normed = []
+        for i in range(count):
+            if ahead:
+                arrive(loads[i])
             kept[i].start()
-            wide = buffer[i].astype(f32)
+            wide = source[i].astype(f32)
             mean_square = jnp.mean(wide * wide, axis=-1, keepdims=True)
-            return (wide * lax.rsqrt(mean_square + epsilon) * gain_ref[...]).astype(bf16)
-
-        following = load_norm(0)
-        for i in range(count):
-            normed = following
-            staged = i == 0 and not loaded
-            if staged:
-                arrive(w_copies[2])
-            elif i + 1 < count:
-                following = load_norm(i + 1)
-            values = dot(normed, ws[2])
-            if staged:
-                arrive(w_copies[1])
-            outs[2 * i + 1][0] = dot(normed, ws[1]).astype(bf16)
-            if staged:
-                arrive(w_copies[0])
-                following = load_norm(i + 1)
-            queries = dot(normed, ws[0])
-            outs[2 * i + 1][1] = jnp.transpose(values).astype(bf16)
-            outs[2 * i][...] = jnp.transpose(queries).astype(bf16) * jnp.asarray(scale, bf16)
-        for copy in kept:
+            normed.append((wide * lax.rsqrt(mean_square + epsilon) * gain_ref[...]).astype(bf16))
+        for part in (2, 1, 0):
+            if ahead:
+                arrive(parts[part])
+            for i in range(count):
+                product = dot(normed[i], ws[part])
+                if part == 2:
+                    outs[2 * i + 1][1] = jnp.transpose(product).astype(bf16)
+                elif part == 1:
+                    outs[2 * i + 1][0] = product.astype(bf16)
+                else:
+                    outs[2 * i][...] = jnp.transpose(product).astype(bf16) * jnp.asarray(scale, bf16)
+        for copy in kept + (later if ahead else []):
             copy.wait()
 
     out_shape = []
@@ -113,25 +111,26 @@
             jax.ShapeDtypeStruct((2, tokens, sub), bf16),
         ]
     out_shape.append(jax.ShapeDtypeStruct((count, tokens, width // 2), bf16))
-    if not loaded:
+    scratch = [pltpu.SemaphoreType.DMA((2 * count + 3 + ahead,))]
+    if ahead:
         out_shape.append(jax.ShapeDtypeStruct(w_qkv.shape, bf16))
+        out_shape.append(jax.ShapeDtypeStruct((ahead, tokens, width), bf16))
+        scratch = [pltpu.VMEM((count, tokens, width), bf16)] + scratch
+    big = ANY_SPEC if ahead else VMEM_SPEC
     outs = pl.pallas_call(
         body,
-        in_specs=[SMEM_SPEC, ANY_SPEC, VMEM_SPEC, VMEM_SPEC if loaded else ANY_SPEC],
+        in_specs=[SMEM_SPEC, big, VMEM_SPEC, big],
         out_specs=many(VMEM_SPEC, len(out_shape)),
         out_shape=out_shape,
-        scratch_shapes=[
-            pltpu.VMEM((count, tokens, width), bf16),
-            pltpu.SemaphoreType.DMA((2 * count + 3,)),
-        ],
+        scratch_shapes=scratch,
         name="proj",
-        compiler_params=grant(GRANT_B if loaded else GRANT_A),
+        compiler_params=grant(GRANT_A if ahead else GRANT_B),
         cost_estimate=cost(
             count * 6 * tokens * width * sub, count * tokens * (width + 3 * sub) * 2 + 6 * width * sub
         ),
     )(meta, latents, gain, w_qkv)
     views = {v: (outs[2 * i], outs[2 * i + 1]) for i, v in enumerate(which)}
-    return views, outs[2 * count], outs[-1]
+    return views, *outs[2 * count :]
 
 
 ONES = 16
@@ -177,7 +176,7 @@
 
 
 def attend(
-    meta, inter, queries, blocks, remote, plan, window, earlier=None, last=True, carry=None
+    meta, inter, queries, blocks, remote, plan, window, earlier=None, last=True, carry=None, slot=0
 ):
     local_views = len(blocks)
     sub, tokens = queries[0].shape
@@ -224,7 +223,7 @@
             for h in range(heads):
                 keys = keys_of(i)
                 weights = []
-                top = before[1][i, h : h + 1, :] if held else None
+                top = before[1][slot + i, h : h + 1, :] if held else None
                 for _, source, o in keys:
                     scores = upcoming
                     n += 1
@@ -240,7 +239,7 @@
                 values = jnp.concatenate([head_values(k[0], h) for k in keys], axis=1)
                 sums = dot(values, jnp.concatenate(weights, axis=0))
                 if held:
-                    sums = sums + before[0][i, h * tall : (h + 1) * tall, :]
+                    sums = sums + before[0][slot + i, h * tall : (h + 1) * tall, :]
                 if not last:
                     refs[0][i, h * tall : (h + 1) * tall, :] = sums
                     refs[1][i, h : h + 1, :] = top
@@ -616,14 +615,15 @@
     inter = intersection.T
     w_near = across(w_out, beside)
     far = {}
-    projected, edge_halves, weights = project_views(meta, latents, gain, w_qkv, (0, 3))
+    projected, edge_halves, weights, inner_latents = project_views(
+        meta, latents, gain, w_qkv, (0, 3), (1, 2)
+    )
     far["n1"] = along(projected[0][1], -1)
     far["p1"] = along(projected[3][1], 1)
-    more, inner_halves, _ = project_views(meta, latents, gain, weights, (1, 2), loaded=True)
+    more, inner_halves = project_views(meta, inner_latents, gain, weights, (1, 2))
     projected.update(more)
     queries = {v: projected[v][0] for v in range(local_views)}
     blocks = {v: projected[v][1] for v in range(local_views)}
-    inner_far = dict(far)
     far["n2"] = along(blocks[1], -1)
     far["p2"] = along(blocks[2], 1)
     base = {0: (edge_halves, 0), 3: (edge_halves, 1), 1: (inner_halves, 0), 2: (inner_halves, 1)}
@@ -634,9 +634,22 @@
         meta, inter, inner_queries, blocks, {}, [(v, []) for v, _ in inner_plan], window, last=False
     )
     attended = {}
-    attended["a"], second = attend(
-        meta, inter, inner_queries, blocks, inner_far, inner_plan, window, earlier=tuple(local)
-    )
+    inner = []
+    for n in range(2):
+        view, sources = inner_plan[n]
+        query = inner_queries[n] if n == 0 else after(inner_queries[n], inner[0])
+        inner += attend(
+            meta,
+            inter,
+            [query],
+            blocks,
+            {s[0]: far[s[0]] for s in sources},
+            [(view, sources)],
+            window,
+            earlier=tuple(local),
+            slot=n,
+        )
+    attended["a"], second = inner
 
     def attend_outer(view, sources, done, carry=None):
         (result,) = attend(

time: 118 us -> 117 us (level)
  waiting for transfers between devices: 34.5 us -> 31.1 us
  starting transfers between devices: 53.5 us -> 55.8 us
    ppermute x10, waiting for transfers between devices: 22.6 us -> 18.3 us  [across(): return lax.ppermute(x, HEADS, pairs)]
    ppermute x10, starting transfers between devices: 5.54 us -> 7.16 us  [partner(): return lax.ppermute(x, VIEWS, [(i, i ^ mask) for i in range(peers)])]
    pallas_call x4 -> x5, Pallas kernels: 9.03 us -> 9.91 us  [attend(): pl.pallas_call(body, in_specs=[SMEM_SPEC, SMEM_SPEC] + many(VMEM_SPEC, he...]
where the time goes in v8:
time: 117 us
  starting transfers between devices  55.8 us (48%)
  waiting for transfers between devices  31.1 us (27%)
  Pallas kernels  28.5 us (24%)
    ppermute x4, starting transfers between devices, along(): return lax.ppermute(x, VIEWS, [(i, (i + by) % peers) for i in range(peers)])  27.8 us
    ppermute x10, starting transfers between devices, across(): return lax.ppermute(x, HEADS, pairs)  20.9 us
    ppermute x10, waiting for transfers between devices, across(): return lax.ppermute(x, HEADS, pairs)  18.3 us
    ppermute x10, waiting for transfers between devices, partner(): return lax.ppermute(x, VIEWS, [(i, i ^ mask) for i in range(peers)])  12.8 us
    pallas_call x5, Pallas kernels, attend(): pl.pallas_call(body, in_specs=[SMEM_SPEC, SMEM_SPEC] + many(VMEM_SPEC, he...  9.91 us
    ppermute x10, starting transfers between devices, partner(): return lax.ppermute(x, VIEWS, [(i, i ^ mask) for i in range(peers)])  7.16 us
    pallas_call x2, Pallas kernels, project_views(): pl.pallas_call(body, in_specs=[SMEM_SPEC, big, VMEM_SPEC, big], out_specs...  5.97 us
    pallas_call x3, Pallas kernels, partial_out(): pl.pallas_call(body, in_specs=[SMEM_SPEC] + many(VMEM_SPEC, 4 + len(base)...  3.26 us
  transfers between devices with their start and end apart: 24, of which 10 were waited for; matrix products, arithmetic and copies ran while one was open for 0% of the time, Pallas kernels for 17%

profile of v8, /device:TPU:0, one launch (start us, length us, event | category | flops | bytes accessed | tf_op | source)
XLA Modules:
  0.0 116.7 jit_solution(2961521323270050911)
XLA Ops:
  0.0 0.7 copy-done.1
  0.7 3.9 %proj.2 = (bf16[256,256]{1,0:T(8,128)(2,1)S(1)}, bf16[2,256,256]{2,1,0:T(8,128)(2,1)S(1)}, bf16[256,256]{1,0:T(8,128)(2,1)S(1)}, bf16[2,256,256]{2,1,0:T(8,128)(...) custom-call(s32[4]{0:T(128)S(1)} %compare_select_fusion.1.meta_ref, ...), custom_call_target="tpu_custom_call" | custom-call | flops 805306368 | bytes 3407872 | tf_op jit(solution)/shard_map/proj/pallas_call | solution.py:120
  4.6 0.5 collective-permute-start
  5.2 2.9 %collective-permute-start.3 = (bf16[2,256,256]{2,1,0:T(8,128)(2,1)S(1)}, bf16[2,256,256]{2,1,0:T(8,128)(2,1)S(1)}, u32[]{:S(2)}, u32[]{:S(2)}) collective-permute-start(bf16[2,256,256]{2,1,0:T(8,128)(2,1)S(1)} %get-tuple-element.51.refs_2_.refs_3_.refs_1_), channel_id=1, source_target_pairs={{0,28},{4,0},{8,4},{12,8},{16,12},{20,16},{24,20},{28,24},{1,29},{... | collective-permute-start | bytes 786440 | tf_op jit(solution)/shard_map/ppermute | solution.py:602
  8.1 2.1 %proj.3 = (bf16[256,256]{1,0:T(8,128)(2,1)S(1)}, bf16[2,256,256]{2,1,0:T(8,128)(2,1)S(1)}, bf16[256,256]{1,0:T(8,128)(2,1)S(1)}, bf16[2,256,256]{2,1,0:T(8,128)(2,1)S(1)}, bf16[2,256,512]{2,1,0:T(8,128)(2,1)S(1)}) custom-call(s32[4]{0:T(128)S(1)} %compare_select_fusion.1.meta_ref, bf16[2,256,1024]{2,1,0:T(8,128)(2,1)S(1)} %get-tuple-element.47.lat_ref, ...), custom_call_target="tpu_custom_call" | custom-call | flops 805306368 | bytes 3407872 | tf_op jit(solution)/shard_map/proj/pallas_call | solution.py:120
  10.2 0.1 collective-permute-start.11
  10.3 4.2 %collective-permute-start.2 = (bf16[256,1024]{1,0:T(8,128)(2,1)S(1)}, bf16[256,1024]{1,0:T(8,128)(2,1)S(1)}, u32[]{:S(2)}, u32[]{:S(2)}) collective-permute-start(bf16[256,1024]{1,0:T(8,128)(2,1)S(1)} %copy-done), channel_id=1, source_target_pairs={{0,1},{3,2},{4,5},{7,6},{8,9},{11,10},{12,13},{15,14},{16,17},{19,... | collective-permute-start | bytes 1572872 | tf_op jit(solution)/shard_map/ppermute | solution.py:608
  14.5 3.0 %att.5 = (f32[2,320,256]{2,1,0:T(8,128)S(1)}, f32[2,4,256]{2,1,0:T(4,128)S(1)}) custom-call(s32[4]{0:T(128)S(1)} %compare_select_fusion.1.meta_ref, s32[2,32]{1,0:T(2,128)S(1)} %bitcast.9, bf16[256,256]{1,0:T(8,128)(2,1)S(1)} %get-tuple-element.49.refs_0_.refs_2_, bf16[256,256]{1,0:T(8,128)(2,1)S(1)} %get-tuple-element.70.refs_1_.refs_2_, ...), custom_call_target="tpu_custom_call" | custom-call | flops 1073741824 | bytes 4194304 | tf_op jit(solution)/shard_map/att/pallas_call | solution.py:288
  17.5 1.3 %att.6 = bf16[256,256]{1,0:T(8,128)(2,1)S(1)} custom-call(s32[4]{0:T(128)S(1)} %compare_select_fusion.1.meta_ref, s32[2,32]{1,0:T(2,128)S(1)} %bitcast.10, f32[2,320,256]{2,1,0:T(8,128)S(1)} %get-tuple-element.55.refs_0_, f32[2,4,256]{2,1,0:T(4,128)S(1)} %get-tuple-element.56.refs_1_, bf16[256,256]{1,0:T(8,128)(2,1)S(1)} %get-tuple-element.49.refs_0_.refs_2_, ...), custom_call_target="tpu_custom_call" | custom-call | flops 134217728 | bytes 524288 | tf_op jit(solution)/shard_map/att/pallas_call | solution.py:288
  18.8 1.3 %att.8.refs_7_ = bf16[256,256]{1,0:T(8,128)(2,1)S(1)} custom-call(s32[4]{0:T(128)S(1)} %compare_select_fusion.1.meta_ref, s32[2,32]{1,0:T(2,128)S(1)} %bitcast.11, f32[2,320,256]{2,1,0:T(8,128)S(1)} %get-tuple-element.55.refs_0_, f32[2,4,256]{2,1,0:T(4,128)S(1)} %get-tuple-element.56.refs_1_, bf16[256,256]{1,0:T(8,128)(2,1)S(1)} %get-tuple-element.70.refs_1_.refs_2_, ...), custom_call_target="tpu_custom_call" | custom-call | flops 134217728 | bytes 524288 | tf_op jit(solution)/shard_map/att/pallas_call | solution.py:288
  20.1 2.2 %att.9 = bf16[2,256,256]{2,1,0:T(8,128)(2,1)S(1)} custom-call(s32[4]{0:T(128)S(1)} %compare_select_fusion.1.meta_ref, s32[2,32]{1,0:T(2,128)S(1)} %bitcast.12, bf16[256,256]{1,0:T(8,128)(2,1)S(1)} %get-tuple-element.69.refs_0_, bf16[2,256,256]{2,1,0:T(8,128)(2,1)S(1)} %get-tuple-element.51.refs_2_.refs_3_.refs_1_, ...), custom_call_target="tpu_custom_call" | custom-call | flops 671088640 | bytes 2621440 | tf_op jit(solution)/shard_map/att/pallas_call | solution.py:288
  22.3 1.9 %collective-permute-start.12 = (bf16[2,256,256]{2,1,0:T(8,128)(2,1)S(1)}, bf16[2,256,256]{2,1,0:T(8,128)(2,1)S(1)}, u32[]{:S(2)}, u32[]{:S(2)}) collective-permute-start(bf16[2,256,256]{2,1,0:T(8,128)(2,1)S(1)} %att.9), channel_id=1, source_target_pairs={{0,1},{3,2},{4,5},{7,6},{8,9},{11,10},{12,13},{15,14},{16,17},{19,... | collective-permute-start | bytes 786440 | tf_op jit(solution)/shard_map/ppermute | solution.py:608
  24.2 24.2 %collective-permute-start.4 = (bf16[2,256,256]{2,1,0:T(8,128)(2,1)S(1)}, bf16[2,256,256]{2,1,0:T(8,128)(2,1)S(1)}, u32[]{:S(2)}, u32[]{:S(2)}) collective-permute-start(bf16[2,256,256]{2,1,0:T(8,128)(2,1)S(1)} %get-tuple-element.52.refs_3_.refs_4_.refs_2_), channel_id=1, source_target_pairs={{0,28},{4,0},{8,4},{12,8},{16,12},{20,16},{24,20},{28,24},{1,29},{... | collective-permute-start | bytes 786440 | tf_op jit(solution)/shard_map/ppermute | solution.py:602
  48.4 1.6 %collective-permute-start.1 = (bf16[256,256]{1,0:T(8,128)(2,1)S(1)}, bf16[256,256]{1,0:T(8,128)(2,1)S(1)}, u32[]{:S(2)}, u32[]{:S(2)}) collective-permute-start(bf16[256,256]{1,0:T(8,128)(2,1)S(1)} %att.6), channel_id=1, source_target_pairs={{0,1},{3,2},{4,5},{7,6},{8,9},{11,10},{12,13},{15,14},{16,17},{19,... | collective-permute-start | bytes 393224 | tf_op jit(solution)/shard_map/ppermute | solution.py:608
  50.0 2.5 %collective-permute-done.1.near_ref = bf16[256,256]{1,0:T(8,128)(2,1)S(1)} collective-permute-done((bf16[256,256]{1,0:T(8,128)(2,1)S(1)}, bf16[256,256]{1,0:T(8,128)(2,1)S(1)}, u32[]{:S(2)}, u32[]{:S(2)}) %collective-permute-start.1) | collective-permute-done | bytes 131104 | tf_op jit(solution)/shard_map/ppermute | solution.py:608
  52.5 1.0 part.3
  53.5 1.3 %part.5 = (f32[512,512]{1,0:T(8,128)S(1)}, bf16[512,512]{1,0:T(8,128)(2,1)S(1)}) custom-call(s32[4]{0:T(128)S(1)} %compare_select_fusion.1.meta_ref, bf16[2,256,256]{2,1,0:T(8,128)(2,1)S(1)} %att.9, bf16[2,256,256]{2,1,0:T(8,128)(2,1)S(1)} %collective-permute-done.12.near_ref, bf16[256,1024]{1,0:T(8,128)(2,1)S(1)} %copy-done, ...), custom_call_target="tpu_custom_call" | custom-call | flops 536870912 | bytes 4194304 | tf_op jit(solution)/shard_map/part/pallas_call | solution.py:360
  54.8 0.9 collective-permute-start.13
  55.7 2.2 %att.7 = bf16[256,256]{1,0:T(8,128)(2,1)S(1)} custom-call(s32[4]{0:T(128)S(1)} %compare_select_fusion.1.meta_ref, s32[2,32]{1,0:T(2,128)S(1)} %bitcast.13, bf16[256,256]{1,0:T(8,128)(2,1)S(1)} %get-tuple-element.59.refs_0_, bf16[2,256,256]{2,1,0:T(8,128)(2,1)S(1)} %get-tuple-element.51.refs_2_.refs_3_.refs_1_, ...), custom_call_target="tpu_custom_call" | custom-call | flops 671088640 | bytes 2621440 | tf_op jit(solution)/shard_map/att/pallas_call | solution.py:288
  57.8 7.1 %collective-permute-start.5 = (bf16[256,256]{1,0:T(8,128)(2,1)S(1)}, bf16[256,256]{1,0:T(8,128)(2,1)S(1)}, u32[]{:S(2)}, u32[]{:S(2)}) collective-permute-start(bf16[256,256]{1,0:T(8,128)(2,1)S(1)} %att.7), channel_id=1, source_target_pairs={{0,1},{3,2},{4,5},{7,6},{8,9},{11,10},{12,13},{15,14},{16,17},{19,... | collective-permute-start | bytes 393224 | tf_op jit(solution)/shard_map/ppermute | solution.py:608
  65.0 0.7 collective-permute-start.9
  65.7 1.8 %collective-permute-done.5.near_ref = bf16[256,256]{1,0:T(8,128)(2,1)S(1)} collective-permute-done((bf16[256,256]{1,0:T(8,128)(2,1)S(1)}, bf16[256,256]{1,0:T(8,128)(2,1)S(1)}, u32[]{:S(2)}, u32[]{:S(2)}) %collective-permute-start.5) | collective-permute-done | bytes 131104 | tf_op jit(solution)/shard_map/ppermute | solution.py:608
  67.5 1.0 part.4
  68.5 0.7 prep.1
  69.2 0.7 collective-permute-start.15
  69.9 0.5 collective-permute-done.6
  70.4 0.7 merge.4
  71.1 1.3 %collective-permute-start.14 = (bf16[512,256]{1,0:T(8,128)(2,1)S(1)}, bf16[512,256]{1,0:T(8,128)(2,1)S(1)}, u32[]{:S(2)}, u32[]{:S(2)}) collective-permute-start(bf16[512,256]{1,0:T(8,128)(2,1)S(1)} %get-tuple-element.74), channel_id=1, source_target_pairs={{1,0},{2,3},{5,4},{6,7},{9,8},{10,11},{13,12},{14,15},{17,16},{18,... | collective-permute-start | bytes 786440 | tf_op jit(solution)/shard_map/ppermute | solution.py:608
  72.4 1.7 %collective-permute-done.7 = s32[16,256]{1,0:T(8,128)S(1)} collective-permute-done((s32[16,256]{1,0:T(8,128)S(1)}, s32[16,256]{1,0:T(8,128)S(1)}, u32[]{:S(2)}, u32[]{:S(2)}) %collective-permute-start.7) | collective-permute-done | bytes 16416 | tf_op jit(solution)/shard_map/ppermute | solution.py:605
  74.1 0.6 merge.3
  74.8 1.3 %collective-permute-start.10 = (bf16[256,256]{1,0:T(8,128)(2,1)S(1)}, bf16[256,256]{1,0:T(8,128)(2,1)S(1)}, u32[]{:S(2)}, u32[]{:S(2)}) collective-permute-start(bf16[256,256]{1,0:T(8,128)(2,1)S(1)} %get-tuple-element.67), channel_id=1, source_target_pairs={{1,0},{2,3},{5,4},{6,7},{9,8},{10,11},{13,12},{14,15},{17,16},{18,... | collective-permute-start | bytes 393224 | tf_op jit(solution)/shard_map/ppermute | solution.py:608
  76.1 0.6 merge.5
  76.7 1.3 %collective-permute-start.16 = (bf16[256,256]{1,0:T(8,128)(2,1)S(1)}, bf16[256,256]{1,0:T(8,128)(2,1)S(1)}, u32[]{:S(2)}, u32[]{:S(2)}) collective-permute-start(bf16[256,256]{1,0:T(8,128)(2,1)S(1)} %get-tuple-element.77), channel_id=1, source_target_pairs={{1,0},{2,3},{5,4},{6,7},{9,8},{10,11},{13,12},{14,15},{17,16},{18,... | collective-permute-start | bytes 393224 | tf_op jit(solution)/shard_map/ppermute | solution.py:608
  78.0 0.1 collective-permute-done.8
  78.1 12.1 %collective-permute-done.10.refs_1_ = bf16[256,256]{1,0:T(8,128)(2,1)S(1)} collective-permute-done((bf16[256,256]{1,0:T(8,128)(2,1)S(1)}, bf16[256,256]{1,0:T(8,128)(2,1)S(1)}, u32[]{:S(2)}, u32[]{:S(2)}) %collective-permute-start.10) | collective-permute-done | bytes 131104 | tf_op jit(solution)/shard_map/ppermute | solution.py:608
  90.2 1.8 %collective-permute-done.16.refs_5_ = bf16[256,256]{1,0:T(8,128)(2,1)S(1)} collective-permute-done((bf16[256,256]{1,0:T(8,128)(2,1)S(1)}, bf16[256,256]{1,0:T(8,128)(2,1)S(1)}, u32[]{:S(2)}, u32[]{:S(2)}) %collective-permute-start.16) | collective-permute-done | bytes 131104 | tf_op jit(solution)/shard_map/ppermute | solution.py:608
  92.0 1.5 %gath.2 = (bf16[1024,256]{1,0:T(8,128)(2,1)S(1)}, bf16[256,256]{1,0:T(8,128)(2,1)S(1)}, bf16[256,256]{1,0:T(8,128)(2,1)S(1)}, bf16[256,256]{1,0:T(8,128)(2,1)S(1)}, bf16[256,256]{1,0:T(8,128)(2,1)S(1)}) custom-call(s32[4]{0:T(128)S(1)} %compare_select_fusion.1.meta_ref, s32[64,256]{1,0:T(8,128)S(1)} %constant_dynamic-update-slice_fusion.wanted_ref, ...), custom_call_target="tpu_custom_call" | custom-call | flops 536870912 | bytes 2097152 | tf_op jit(solution)/shard_map/gath/pallas_call | solution.py:482
  93.5 1.5 %gath.3 = (bf16[256,256]{1,0:T(8,128)(2,1)S(1)}, bf16[256,256]{1,0:T(8,128)(2,1)S(1)}, bf16[256,256]{1,0:T(8,128)(2,1)S(1)}, bf16[256,256]{1,0:T(8,128)(2,1)S(1)}) custom-call(s32[4]{0:T(128)S(1)} %compare_select_fusion.1.meta_ref, s32[64,256]{1,0:T(8,128)S(1)} %constant_dynamic-update-slice_fusion.wanted_ref, ...), custom_call_target="tpu_custom_call" | custom-call | flops 536870912 | bytes 2097152 | tf_op jit(solution)/shard_map/gath/pallas_call | solution.py:482
  95.0 0.1 collective-permute-start.17
  95.1 3.8 %collective-permute-start.18 = (bf16[256,256]{1,0:T(8,128)(2,1)S(1)}, bf16[256,256]{1,0:T(8,128)(2,1)S(1)}, u32[]{:S(2)}, u32[]{:S(2)}) collective-permute-start(bf16[256,256]{1,0:T(8,128)(2,1)S(1)} %get-tuple-element.81), channel_id=1, source_target_pairs={{0,16},{4,20},{8,24},{12,28},{16,0},{20,4},{24,8},{28,12},{1,17},{... | collective-permute-start | bytes 393224 | tf_op jit(solution)/shard_map/ppermute | solution.py:605
  99.0 1.5 %collective-permute-start.20 = (bf16[256,256]{1,0:T(8,128)(2,1)S(1)}, bf16[256,256]{1,0:T(8,128)(2,1)S(1)}, u32[]{:S(2)}, u32[]{:S(2)}) collective-permute-start(bf16[256,256]{1,0:T(8,128)(2,1)S(1)} %get-tuple-element.83), channel_id=1, source_target_pairs={{0,24},{4,28},{8,16},{12,20},{16,8},{20,12},{24,0},{28,4},{1,25},{... | collective-permute-start | bytes 393224 | tf_op jit(solution)/shard_map/ppermute | solution.py:605
  100.5 0.9 collective-permute-start.21
  101.4 0.8 collective-permute-start.22
  102.2 6.5 %collective-permute-done.18.refs_2_ = bf16[256,256]{1,0:T(8,128)(2,1)S(1)} collective-permute-done((bf16[256,256]{1,0:T(8,128)(2,1)S(1)}, bf16[256,256]{1,0:T(8,128)(2,1)S(1)}, u32[]{:S(2)}, u32[]{:S(2)}) %collective-permute-start.18) | collective-permute-done | bytes 131104 | tf_op jit(solution)/shard_map/ppermute | solution.py:605
  108.7 2.5 %collective-permute-done.19.refs_3_ = bf16[256,256]{1,0:T(8,128)(2,1)S(1)} collective-permute-done((bf16[256,256]{1,0:T(8,128)(2,1)S(1)}, bf16[256,256]{1,0:T(8,128)(2,1)S(1)}, u32[]{:S(2)}, u32[]{:S(2)}) %collective-permute-start.19) | collective-permute-done | bytes 131104 | tf_op jit(solution)/shard_map/ppermute | solution.py:605
  111.2 1.7 %first.1.early_ref = bf16[1024,256]{1,0:T(8,128)(2,1)S(1)} custom-call(s32[4]{0:T(128)S(1)} %compare_select_fusion.1.meta_ref, s32[8,128]{1,0:T(8,128)S(1)} %get-tuple-element.63.code_ref, bf16[256,256]{1,0:T(8,128)(2,1)S(1)} %get-tuple-element.79.refs_0_, bf16[256,256]{1,0:T(8,128)(2,1)S(1)} %collective-permute-done.17.refs_1_, ...), custom_call_target="tpu_custom_call" | custom-call | flops 805306368 | bytes 1048576 | tf_op jit(solution)/shard_map/first/pallas_call | solution.py:532
  112.9 1.5 %collective-permute-done.23.refs_1_ = bf16[256,256]{1,0:T(8,128)(2,1)S(1)} collective-permute-done((bf16[256,256]{1,0:T(8,128)(2,1)S(1)}, bf16[256,256]{1,0:T(8,128)(2,1)S(1)}, u32[]{:S(2)}, u32[]{:S(2)}) %collective-permute-start.23) | collective-permute-done | bytes 131104 | tf_op jit(solution)/shard_map/ppermute | solution.py:605
  114.4 2.1 %fin.1 = f32[1024,256]{1,0:T(8,128)} custom-call(s32[4]{0:T(128)S(1)} %compare_select_fusion.1.meta_ref, s32[8,128]{1,0:T(8,128)S(1)} %get-tuple-element.63.code_ref, f32[8,128]{1,0:T(8,128)S(1)} %bitcast.8, bf16[1024,256]{1,0:T(8,128)(2,1)S(1)} %get-tuple-element.78.refs_0_.layer_ref, bf16[1024,256]{1,0:T(8,128)(2,1)S(1)} %first.1.early_ref, ...), custom_call_target="tpu_custom_call" | custom-call | flops 268435456 | bytes 2097152 | tf_op jit(solution)/shard_map/fin/pallas_call | solution.py:573
  (37 shorter events, 0.1 us)
Async XLA Ops:
  0.0 0.7 copy-start.1
  4.6 5.6 %copy-start = (bf16[256,1024]{1,0:T(8,128)(2,1)S(1)}, bf16[256,1024]{1,0:T(8,128)(2,1)}, u32[]{:S(2)}) copy-start(bf16[256,1024]{1,0:T(8,128)(2,1)} %own_ref.5) | copy-start | bytes 1572868
  4.6 9.8 %copy-start.3 = (s32[32,2]{0,1:T(2,128)S(1)}, s32[32,2]{0,1:T(2,128)}, u32[]{:S(2)}) copy-start(s32[32,2]{0,1:T(2,128)} %param.12) | copy-start | bytes 772
  4.6 12.8 %collective-permute-start = (bf16[2,256,256]{2,1,0:T(8,128)(2,1)S(1)}, bf16[2,256,256]{2,1,0:T(8,128)(2,1)S(1)}, u32[]{:S(2)}, u32[]{:S(2)}) collective-permute-start(bf16[2,256,256]{2,1,0:T(8,128)(2,1)S(1)} %get-tuple-element.54.refs_5_.refs_6_.refs_4_), channel_id=1, source_target_pairs={{0,4},{4,8},{8,12},{12,16},{16,20},{20,24},{24,28},{28,0},{1,5},{5... | collective-permute-start | bytes 786440 | tf_op jit(solution)/shard_map/ppermute | solution.py:602
  5.2 13.6 %collective-permute-start.3 = (bf16[2,256,256]{2,1,0:T(8,128)(2,1)S(1)}, bf16[2,256,256]{2,1,0:T(8,128)(2,1)S(1)}, u32[]{:S(2)}, u32[]{:S(2)}) collective-permute-start(bf16[2,256,256]{2,1,0:T(8,128)(2,1)S(1)} %get-tuple-element.51.refs_2_.refs_3_.refs_1_), channel_id=1, source_target_pairs={{0,28},{4,0},{8,4},{12,8},{16,12},{20,16},{24,20},{28,24},{1,29},{... | collective-permute-start | bytes 786440 | tf_op jit(solution)/shard_map/ppermute | solution.py:602
  10.2 9.9 %collective-permute-start.11 = (bf16[2,256,256]{2,1,0:T(8,128)(2,1)S(1)}, bf16[2,256,256]{2,1,0:T(8,128)(2,1)S(1)}, u32[]{:S(2)}, u32[]{:S(2)}) collective-permute-start(bf16[2,256,256]{2,1,0:T(8,128)(2,1)S(1)} %get-tuple-element.53.refs_4_.refs_5_.refs_3_), channel_id=1, source_target_pairs={{0,4},{4,8},{8,12},{12,16},{16,20},{20,24},{24,28},{28,0},{1,5},{5... | collective-permute-start | bytes 786440 | tf_op jit(solution)/shard_map/ppermute | solution.py:602
  10.3 42.2 %collective-permute-start.2 = (bf16[256,1024]{1,0:T(8,128)(2,1)S(1)}, bf16[256,1024]{1,0:T(8,128)(2,1)S(1)}, u32[]{:S(2)}, u32[]{:S(2)}) collective-permute-start(bf16[256,1024]{1,0:T(8,128)(2,1)S(1)} %copy-done), channel_id=1, source_target_pairs={{0,1},{3,2},{4,5},{7,6},{8,9},{11,10},{12,13},{15,14},{16,17},{19,... | collective-permute-start | bytes 1572872 | tf_op jit(solution)/shard_map/ppermute | solution.py:608
  22.3 31.2 %collective-permute-start.12 = (bf16[2,256,256]{2,1,0:T(8,128)(2,1)S(1)}, bf16[2,256,256]{2,1,0:T(8,128)(2,1)S(1)}, u32[]{:S(2)}, u32[]{:S(2)}) collective-permute-start(bf16[2,256,256]{2,1,0:T(8,128)(2,1)S(1)} %att.9), channel_id=1, source_target_pairs={{0,1},{3,2},{4,5},{7,6},{8,9},{11,10},{12,13},{15,14},{16,17},{19,... | collective-permute-start | bytes 786440 | tf_op jit(solution)/shard_map/ppermute | solution.py:608
  24.2 31.5 %collective-permute-start.4 = (bf16[2,256,256]{2,1,0:T(8,128)(2,1)S(1)}, bf16[2,256,256]{2,1,0:T(8,128)(2,1)S(1)}, u32[]{:S(2)}, u32[]{:S(2)}) collective-permute-start(bf16[2,256,256]{2,1,0:T(8,128)(2,1)S(1)} %get-tuple-element.52.refs_3_.refs_4_.refs_2_), channel_id=1, source_target_pairs={{0,28},{4,0},{8,4},{12,8},{16,12},{20,16},{24,20},{28,24},{1,29},{... | collective-permute-start | bytes 786440 | tf_op jit(solution)/shard_map/ppermute | solution.py:602
  48.4 4.1 %collective-permute-start.1 = (bf16[256,256]{1,0:T(8,128)(2,1)S(1)}, bf16[256,256]{1,0:T(8,128)(2,1)S(1)}, u32[]{:S(2)}, u32[]{:S(2)}) collective-permute-start(bf16[256,256]{1,0:T(8,128)(2,1)S(1)} %att.6), channel_id=1, source_target_pairs={{0,1},{3,2},{4,5},{7,6},{8,9},{11,10},{12,13},{15,14},{16,17},{19,... | collective-permute-start | bytes 393224 | tf_op jit(solution)/shard_map/ppermute | solution.py:608
  54.7 13.8 %copy-start.4 = (s32[1024,1]{0,1:T(1,128)S(1)}, s32[1024,1]{0,1:T(1,128)}, u32[]{:S(2)}) copy-start(s32[1024,1]{0,1:T(1,128)} %param.13) | copy-start | bytes 12292
  54.8 13.7 %copy-start.5 = (s32[1024]{0:T(1024)S(1)}, s32[1024]{0:T(1024)}, u32[]{:S(2)}) copy-start(s32[1024]{0:T(1024)} %param.14) | copy-start | bytes 12292
  54.8 15.6 %collective-permute-start.13 = (bf16[512,512]{1,0:T(8,128)(2,1)S(1)}, bf16[512,512]{1,0:T(8,128)(2,1)S(1)}, u32[]{:S(2)}, u32[]{:S(2)}) collective-permute-start(bf16[512,512]{1,0:T(8,128)(2,1)S(1)} %get-tuple-element.72), channel_id=1, source_target_pairs={{1,2},{2,1},{5,6},{6,5},{9,10},{10,9},{13,14},{14,13},{17,18},{18,... | collective-permute-start | bytes 1572872 | tf_op jit(solution)/shard_map/ppermute | solution.py:608
  57.8 9.6 %collective-permute-start.5 = (bf16[256,256]{1,0:T(8,128)(2,1)S(1)}, bf16[256,256]{1,0:T(8,128)(2,1)S(1)}, u32[]{:S(2)}, u32[]{:S(2)}) collective-permute-start(bf16[256,256]{1,0:T(8,128)(2,1)S(1)} %att.7), channel_id=1, source_target_pairs={{0,1},{3,2},{4,5},{7,6},{8,9},{11,10},{12,13},{15,14},{16,17},{19,... | collective-permute-start | bytes 393224 | tf_op jit(solution)/shard_map/ppermute | solution.py:608
  65.0 9.1 %collective-permute-start.9 = (bf16[256,512]{1,0:T(8,128)(2,1)S(1)}, bf16[256,512]{1,0:T(8,128)(2,1)S(1)}, u32[]{:S(2)}, u32[]{:S(2)}) collective-permute-start(bf16[256,512]{1,0:T(8,128)(2,1)S(1)} %get-tuple-element.58), channel_id=1, source_target_pairs={{1,2},{2,1},{5,6},{6,5},{9,10},{10,9},{13,14},{14,13},{17,18},{18,... | collective-permute-start | bytes 786440 | tf_op jit(solution)/shard_map/ppermute | solution.py:608
  69.2 1.2 %collective-permute-start.6 = (s32[8,256]{1,0:T(8,128)S(1)}, s32[8,256]{1,0:T(8,128)S(1)}, u32[]{:S(2)}, u32[]{:S(2)}) collective-permute-start(s32[8,256]{1,0:T(8,128)S(1)} %get-tuple-element.64), channel_id=1, source_target_pairs={{0,4},{4,0},{8,12},{12,8},{16,20},{20,16},{24,28},{28,24},{1,5},{5... | collective-permute-start | bytes 24584 | tf_op jit(solution)/shard_map/ppermute | solution.py:605
  69.2 6.8 %collective-permute-start.15 = (bf16[256,512]{1,0:T(8,128)(2,1)S(1)}, bf16[256,512]{1,0:T(8,128)(2,1)S(1)}, u32[]{:S(2)}, u32[]{:S(2)}) collective-permute-start(bf16[256,512]{1,0:T(8,128)(2,1)S(1)} %get-tuple-element.61), channel_id=1, source_target_pairs={{1,2},{2,1},{5,6},{6,5},{9,10},{10,9},{13,14},{14,13},{17,18},{18,... | collective-permute-start | bytes 786440 | tf_op jit(solution)/shard_map/ppermute | solution.py:608
  70.4 3.7 %collective-permute-start.7 = (s32[16,256]{1,0:T(8,128)S(1)}, s32[16,256]{1,0:T(8,128)S(1)}, u32[]{:S(2)}, u32[]{:S(2)}) collective-permute-start(s32[16,256]{1,0:T(8,128)S(1)} %pad_add_fusion.1), channel_id=1, source_target_pairs={{0,8},{4,12},{8,0},{12,4},{16,24},{20,28},{24,16},{28,20},{1,9},{5... | collective-permute-start | bytes 49160 | tf_op jit(solution)/shard_map/ppermute | solution.py:605
  71.1 20.9 %collective-permute-start.14 = (bf16[512,256]{1,0:T(8,128)(2,1)S(1)}, bf16[512,256]{1,0:T(8,128)(2,1)S(1)}, u32[]{:S(2)}, u32[]{:S(2)}) collective-permute-start(bf16[512,256]{1,0:T(8,128)(2,1)S(1)} %get-tuple-element.74), channel_id=1, source_target_pairs={{1,0},{2,3},{5,4},{6,7},{9,8},{10,11},{13,12},{14,15},{17,16},{18,... | collective-permute-start | bytes 786440 | tf_op jit(solution)/shard_map/ppermute | solution.py:608
  74.1 3.9 %collective-permute-start.8 = (s32[32,256]{1,0:T(8,128)S(1)}, s32[32,256]{1,0:T(8,128)S(1)}, u32[]{:S(2)}, u32[]{:S(2)}) collective-permute-start(s32[32,256]{1,0:T(8,128)S(1)} %pad_add_fusion), channel_id=1, source_target_pairs={{0,16},{4,20},{8,24},{12,28},{16,0},{20,4},{24,8},{28,12},{1,17},{... | collective-permute-start | bytes 98312 | tf_op jit(solution)/shard_map/ppermute | solution.py:605
  74.8 15.4 %collective-permute-start.10 = (bf16[256,256]{1,0:T(8,128)(2,1)S(1)}, bf16[256,256]{1,0:T(8,128)(2,1)S(1)}, u32[]{:S(2)}, u32[]{:S(2)}) collective-permute-start(bf16[256,256]{1,0:T(8,128)(2,1)S(1)} %get-tuple-element.67), channel_id=1, source_target_pairs={{1,0},{2,3},{5,4},{6,7},{9,8},{10,11},{13,12},{14,15},{17,16},{18,... | collective-permute-start | bytes 393224 | tf_op jit(solution)/shard_map/ppermute | solution.py:608
  76.7 15.3 %collective-permute-start.16 = (bf16[256,256]{1,0:T(8,128)(2,1)S(1)}, bf16[256,256]{1,0:T(8,128)(2,1)S(1)}, u32[]{:S(2)}, u32[]{:S(2)}) collective-permute-start(bf16[256,256]{1,0:T(8,128)(2,1)S(1)} %get-tuple-element.77), channel_id=1, source_target_pairs={{1,0},{2,3},{5,4},{6,7},{9,8},{10,11},{13,12},{14,15},{17,16},{18,... | collective-permute-start | bytes 393224 | tf_op jit(solution)/shard_map/ppermute | solution.py:608
  95.0 19.4 %copy-start.2 = (f32[1024]{0:T(1024)S(1)}, f32[1024]{0:T(1024)}, u32[]{:S(2)}) copy-start(f32[1024]{0:T(1024)} %param.15) | copy-start | bytes 12292
  95.0 6.4 %collective-permute-start.17 = (bf16[256,256]{1,0:T(8,128)(2,1)S(1)}, bf16[256,256]{1,0:T(8,128)(2,1)S(1)}, u32[]{:S(2)}, u32[]{:S(2)}) collective-permute-start(bf16[256,256]{1,0:T(8,128)(2,1)S(1)} %get-tuple-element.80), channel_id=1, source_target_pairs={{0,4},{4,0},{8,12},{12,8},{16,20},{20,16},{24,28},{28,24},{1,5},{5... | collective-permute-start | bytes 393224 | tf_op jit(solution)/shard_map/ppermute | solution.py:605
  95.1 13.6 %collective-permute-start.18 = (bf16[256,256]{1,0:T(8,128)(2,1)S(1)}, bf16[256,256]{1,0:T(8,128)(2,1)S(1)}, u32[]{:S(2)}, u32[]{:S(2)}) collective-permute-start(bf16[256,256]{1,0:T(8,128)(2,1)S(1)} %get-tuple-element.81), channel_id=1, source_target_pairs={{0,16},{4,20},{8,24},{12,28},{16,0},{20,4},{24,8},{28,12},{1,17},{... | collective-permute-start | bytes 393224 | tf_op jit(solution)/shard_map/ppermute | solution.py:605
  99.0 12.3 %collective-permute-start.19 = (bf16[256,256]{1,0:T(8,128)(2,1)S(1)}, bf16[256,256]{1,0:T(8,128)(2,1)S(1)}, u32[]{:S(2)}, u32[]{:S(2)}) collective-permute-start(bf16[256,256]{1,0:T(8,128)(2,1)S(1)} %get-tuple-element.82), channel_id=1, source_target_pairs={{0,20},{4,16},{8,28},{12,24},{16,4},{20,0},{24,12},{28,8},{1,21},{... | collective-permute-start | bytes 393224 | tf_op jit(solution)/shard_map/ppermute | solution.py:605
  99.0 12.2 %collective-permute-start.20 = (bf16[256,256]{1,0:T(8,128)(2,1)S(1)}, bf16[256,256]{1,0:T(8,128)(2,1)S(1)}, u32[]{:S(2)}, u32[]{:S(2)}) collective-permute-start(bf16[256,256]{1,0:T(8,128)(2,1)S(1)} %get-tuple-element.83), channel_id=1, source_target_pairs={{0,24},{4,28},{8,16},{12,20},{16,8},{20,12},{24,0},{28,4},{1,25},{... | collective-permute-start | bytes 393224 | tf_op jit(solution)/shard_map/ppermute | solution.py:605
  100.5 10.7 %collective-permute-start.21 = (bf16[256,256]{1,0:T(8,128)(2,1)S(1)}, bf16[256,256]{1,0:T(8,128)(2,1)S(1)}, u32[]{:S(2)}, u32[]{:S(2)}) collective-permute-start(bf16[256,256]{1,0:T(8,128)(2,1)S(1)} %get-tuple-element.84), channel_id=1, source_target_pairs={{0,28},{4,24},{8,20},{12,16},{16,12},{20,8},{24,4},{28,0},{1,29},{... | collective-permute-start | bytes 393224 | tf_op jit(solution)/shard_map/ppermute | solution.py:605
  101.4 11.5 %collective-permute-start.22 = (bf16[256,256]{1,0:T(8,128)(2,1)S(1)}, bf16[256,256]{1,0:T(8,128)(2,1)S(1)}, u32[]{:S(2)}, u32[]{:S(2)}) collective-permute-start(bf16[256,256]{1,0:T(8,128)(2,1)S(1)} %get-tuple-element.85), channel_id=1, source_target_pairs={{0,8},{4,12},{8,0},{12,4},{16,24},{20,28},{24,16},{28,20},{1,9},{5... | collective-permute-start | bytes 393224 | tf_op jit(solution)/shard_map/ppermute | solution.py:605
  108.7 5.7 %collective-permute-start.23 = (bf16[256,256]{1,0:T(8,128)(2,1)S(1)}, bf16[256,256]{1,0:T(8,128)(2,1)S(1)}, u32[]{:S(2)}, u32[]{:S(2)}) collective-permute-start(bf16[256,256]{1,0:T(8,128)(2,1)S(1)} %get-tuple-element.86), channel_id=1, source_target_pairs={{0,12},{4,8},{8,4},{12,0},{16,28},{20,24},{24,20},{28,16},{1,13},{... | collective-permute-start | bytes 393224 | tf_op jit(solution)/shard_map/ppermute | solution.py:605

commit v9 on v8

--- a/solution.py
+++ b/solution.py
@@ -176,7 +176,7 @@
 
 
 def attend(
-    meta, inter, queries, blocks, remote, plan, window, earlier=None, last=True, carry=None, slot=0
+    meta, inter, queries, blocks, remote, plan, window, earlier=None, last=True, carry=None
 ):
     local_views = len(blocks)
     sub, tokens = queries[0].shape
@@ -223,7 +223,7 @@
             for h in range(heads):
                 keys = keys_of(i)
                 weights = []
-                top = before[1][slot + i, h : h + 1, :] if held else None
+                top = before[1][i, h : h + 1, :] if held else None
                 for _, source, o in keys:
                     scores = upcoming
                     n += 1
@@ -239,7 +239,7 @@
                 values = jnp.concatenate([head_values(k[0], h) for k in keys], axis=1)
                 sums = dot(values, jnp.concatenate(weights, axis=0))
                 if held:
-                    sums = sums + before[0][slot + i, h * tall : (h + 1) * tall, :]
+                    sums = sums + before[0][i, h * tall : (h + 1) * tall, :]
                 if not last:
                     refs[0][i, h * tall : (h + 1) * tall, :] = sums
                     refs[1][i, h : h + 1, :] = top
@@ -634,22 +634,10 @@
         meta, inter, inner_queries, blocks, {}, [(v, []) for v, _ in inner_plan], window, last=False
     )
     attended = {}
-    inner = []
-    for n in range(2):
-        view, sources = inner_plan[n]
-        query = inner_queries[n] if n == 0 else after(inner_queries[n], inner[0])
-        inner += attend(
-            meta,
-            inter,
-            [query],
-            blocks,
-            {s[0]: far[s[0]] for s in sources},
-            [(view, sources)],
-            window,
-            earlier=tuple(local),
-            slot=n,
-        )
-    attended["a"], second = inner
+    attended["a"], second = attend(
+        meta, inter, inner_queries, blocks, dict(n1=far["n1"], p1=far["p1"]), inner_plan, window,
+        earlier=tuple(local),
+    )
 
     def attend_outer(view, sources, done, carry=None):
         (result,) = attend(
@@ -685,7 +673,7 @@
     pass_on("c")
     strips = rows // LANES
     wanted, code = prepare_requests(
-        after(match_block.reshape(strips, LANES), sent["c"]),
+        after(match_block.reshape(strips, LANES), sent["b"]),
         match_row.reshape(strips, LANES),
         peers,
         capacity,
@@ -699,21 +687,16 @@
         own, other = merge_out(meta, keep[c], got[c])
         pieces.append((CHUNKS[c], own, across(other, back)))
 
-    first_masks, last_masks = reply_order(peers)
-    replies = {}
-
-    def reply(masks, outgoing):
-        for mask, rows_out in zip(masks, outgoing):
-            replies[mask] = partner(rows_out, mask)
-
-    layer, *outgoing = gather_rows(meta, wanted, pieces, first_masks, tokens)
-    reply(first_masks, outgoing)
-    *outgoing, own_rows = gather_rows(meta, wanted, layer, last_masks + [0], tokens)
-    reply(last_masks, outgoing)
-    late = [m for m in last_masks if m > 1]
-    early = first_replies(
-        meta, code, {0: own_rows, **{m: r for m, r in replies.items() if m not in late}}, tokens
-    )
+    groups = reply_groups(peers)
+    replies, layer = {}, pieces
+    for n, masks in enumerate(groups):
+        found = gather_rows(meta, wanted, layer, masks, tokens)
+        if n == 0:
+            layer, *found = found
+        for mask, rows_out in zip(masks, found):
+            replies[mask] = partner(rows_out, mask) if mask else rows_out
+    late = late_masks(peers)
+    early = first_replies(meta, code, {m: r for m, r in replies.items() if m not in late}, tokens)
     refined = finish_rows(
         meta,
         code,
@@ -726,11 +709,14 @@
     return refined.reshape(local_views, tokens, sub)
 
 
-def reply_order(peers):
-    far_half = list(range(peers // 2, peers))
-    far_half = far_half[len(far_half) // 2 :] + far_half[: len(far_half) // 2]
-    pairs = zip(far_half[: len(far_half) // 2], far_half[len(far_half) // 2 :])
-    return [m for pair in pairs for m in pair], list(range(2, peers // 2)) + [1]
+def late_masks(peers):
+    return list(range(3 * peers // 4, peers))
+
+
+def reply_groups(peers):
+    quarter, half = list(range(peers // 4, peers // 2)), list(range(peers // 2, 3 * peers // 4))
+    pairs = [m for pair in zip(half, quarter) for m in pair]
+    return [pairs[: len(quarter)], pairs[len(quarter) :], late_masks(peers) + list(range(1, peers // 4)) + [0]]
 
 
 def solution(mesh):

time: 117 us -> 113 us (0.966)
  waiting for transfers between devices: 31.1 us -> 26.9 us
    ppermute x10, waiting for transfers between devices: 12.8 us -> 7.63 us  [partner(): return lax.ppermute(x, VIEWS, [(i, i ^ mask) for i in range(peers)])]
    ppermute x10, starting transfers between devices: 7.16 us -> 10.7 us  [partner(): return lax.ppermute(x, VIEWS, [(i, i ^ mask) for i in range(peers)])]
    ppermute x10, starting transfers between devices: 20.9 us -> 19 us  [across(): return lax.ppermute(x, HEADS, pairs)]
    ppermute x4, starting transfers between devices: 27.8 us -> 26.4 us  [along(): return lax.ppermute(x, VIEWS, [(i, (i + by) % peers) for i in range(peers)])]
    pallas_call x2 -> x3, Pallas kernels: 3.02 us -> 3.95 us  [gather_rows(): pl.pallas_call(body, in_specs=[SMEM_SPEC] + many(VMEM_SPEC, 1 + len(flat)...]
    pallas_call x5 -> x4, Pallas kernels: 9.91 us -> 9.04 us  [attend(): pl.pallas_call(body, in_specs=[SMEM_SPEC, SMEM_SPEC] + many(VMEM_SPEC, he...]
  transfers between devices with their start and end apart: 24 -> 24, of which waited for: 10 -> 7; matrix products, arithmetic and copies ran while one was open for 0% -> 0% of each run, Pallas kernels for 17% -> 18%
where the time goes in v9:
time: 113 us
  starting transfers between devices  56.2 us (50%)
  Pallas kernels  28.6 us (25%)
  waiting for transfers between devices  26.9 us (24%)
    ppermute x4, starting transfers between devices, along(): return lax.ppermute(x, VIEWS, [(i, (i + by) % peers) for i in range(peers)])  26.4 us
    ppermute x10, waiting for transfers between devices, across(): return lax.ppermute(x, HEADS, pairs)  19.1 us
    ppermute x10, starting transfers between devices, across(): return lax.ppermute(x, HEADS, pairs)  19 us
    ppermute x10, starting transfers between devices, partner(): return lax.ppermute(x, VIEWS, [(i, i ^ mask) for i in range(peers)])  10.7 us
    pallas_call x4, Pallas kernels, attend(): pl.pallas_call(body, in_specs=[SMEM_SPEC, SMEM_SPEC] + many(VMEM_SPEC, he...  9.04 us
    ppermute x10, waiting for transfers between devices, partner(): return lax.ppermute(x, VIEWS, [(i, i ^ mask) for i in range(peers)])  7.63 us
    pallas_call x2, Pallas kernels, project_views(): pl.pallas_call(body, in_specs=[SMEM_SPEC, big, VMEM_SPEC, big], out_specs...  5.97 us
    pallas_call x3, Pallas kernels, gather_rows(): pl.pallas_call(body, in_specs=[SMEM_SPEC] + many(VMEM_SPEC, 1 + len(flat)...  3.95 us
  transfers between devices with their start and end apart: 24, of which 7 were waited for; matrix products, arithmetic and copies ran while one was open for 0% of the time, Pallas kernels for 18%

profile of v9, /device:TPU:0, one launch (start us, length us, event | category | flops | bytes accessed | tf_op | source)
XLA Modules:
  0.0 113.0 jit_solution(13588969049175353067)
XLA Ops:
  0.0 0.7 copy-done.1
  0.7 3.9 %proj.2 = (bf16[256,256]{1,0:T(8,128)(2,1)S(1)}, bf16[2,256,256]{2,1,0:T(8,128)(2,1)S(1)}, bf16[256,256]{1,0:T(8,128)(2,1)S(1)}, bf16[2,256,256]{2,1,0:T(8,128)(...) custom-call(s32[4]{0:T(128)S(1)} %compare_select_fusion.1.meta_ref, ...), custom_call_target="tpu_custom_call" | custom-call | flops 805306368 | bytes 3407872 | tf_op jit(solution)/shard_map/proj/pallas_call | solution.py:120
  4.6 3.4 %collective-permute-start = (bf16[2,256,256]{2,1,0:T(8,128)(2,1)S(1)}, bf16[2,256,256]{2,1,0:T(8,128)(2,1)S(1)}, u32[]{:S(2)}, u32[]{:S(2)}) collective-permute-start(bf16[2,256,256]{2,1,0:T(8,128)(2,1)S(1)} %get-tuple-element.52.refs_2_.refs_4_.refs_1_), channel_id=1, source_target_pairs={{0,28},{4,0},{8,4},{12,8},{16,12},{20,16},{24,20},{28,24},{1,29},{... | collective-permute-start | bytes 786440 | tf_op jit(solution)/shard_map/ppermute | solution.py:602
  8.1 2.1 %proj.3 = (bf16[256,256]{1,0:T(8,128)(2,1)S(1)}, bf16[2,256,256]{2,1,0:T(8,128)(2,1)S(1)}, bf16[256,256]{1,0:T(8,128)(2,1)S(1)}, bf16[2,256,256]{2,1,0:T(8,128)(2,1)S(1)}, bf16[2,256,512]{2,1,0:T(8,128)(2,1)S(1)}) custom-call(s32[4]{0:T(128)S(1)} %compare_select_fusion.1.meta_ref, bf16[2,256,1024]{2,1,0:T(8,128)(2,1)S(1)} %get-tuple-element.48.lat_ref, ...), custom_call_target="tpu_custom_call" | custom-call | flops 805306368 | bytes 3407872 | tf_op jit(solution)/shard_map/proj/pallas_call | solution.py:120
  10.1 0.1 collective-permute-start.2
  10.2 3.5 %collective-permute-start.4 = (bf16[256,1024]{1,0:T(8,128)(2,1)S(1)}, bf16[256,1024]{1,0:T(8,128)(2,1)S(1)}, u32[]{:S(2)}, u32[]{:S(2)}) collective-permute-start(bf16[256,1024]{1,0:T(8,128)(2,1)S(1)} %copy-done), channel_id=1, source_target_pairs={{0,1},{3,2},{4,5},{7,6},{8,9},{11,10},{12,13},{15,14},{16,17},{19,... | collective-permute-start | bytes 1572872 | tf_op jit(solution)/shard_map/ppermute | solution.py:608
  13.7 2.9 %att.4 = (f32[2,320,256]{2,1,0:T(8,128)S(1)}, f32[2,4,256]{2,1,0:T(4,128)S(1)}) custom-call(s32[4]{0:T(128)S(1)} %compare_select_fusion.1.meta_ref, s32[2,32]{1,0:T(2,128)S(1)} %bitcast.9, bf16[256,256]{1,0:T(8,128)(2,1)S(1)} %get-tuple-element.50.refs_0_.refs_2_, bf16[256,256]{1,0:T(8,128)(2,1)S(1)} %get-tuple-element.51.refs_1_.refs_3_, ...), custom_call_target="tpu_custom_call" | custom-call | flops 1073741824 | bytes 4194304 | tf_op jit(solution)/shard_map/att/pallas_call | solution.py:288
  16.7 1.7 %att.5 = (bf16[256,256]{1,0:T(8,128)(2,1)S(1)}, bf16[256,256]{1,0:T(8,128)(2,1)S(1)}) custom-call(s32[4]{0:T(128)S(1)} %compare_select_fusion.1.meta_ref, s32[2,32]{1,0:T(2,128)S(1)} %bitcast.10, f32[2,320,256]{2,1,0:T(8,128)S(1)} %get-tuple-element.56.refs_0_, f32[2,4,256]{2,1,0:T(4,128)S(1)} %get-tuple-element.57.refs_1_, ...), custom_call_target="tpu_custom_call" | custom-call | flops 268435456 | bytes 1048576 | tf_op jit(solution)/shard_map/att/pallas_call | solution.py:288
  18.4 0.2 collective-permute-done.2.refs_6_
  18.6 2.2 %att.6 = bf16[2,256,256]{2,1,0:T(8,128)(2,1)S(1)} custom-call(s32[4]{0:T(128)S(1)} %compare_select_fusion.1.meta_ref, s32[2,32]{1,0:T(2,128)S(1)} %bitcast.11, bf16[256,256]{1,0:T(8,128)(2,1)S(1)} %get-tuple-element.59.refs_0_, bf16[2,256,256]{2,1,0:T(8,128)(2,1)S(1)} %get-tuple-element.52.refs_2_.refs_4_.refs_1_, ...), custom_call_target="tpu_custom_call" | custom-call | flops 671088640 | bytes 2621440 | tf_op jit(solution)/shard_map/att/pallas_call | solution.py:288
  20.8 3.5 %collective-permute-start.3 = (bf16[2,256,256]{2,1,0:T(8,128)(2,1)S(1)}, bf16[2,256,256]{2,1,0:T(8,128)(2,1)S(1)}, u32[]{:S(2)}, u32[]{:S(2)}) collective-permute-start(bf16[2,256,256]{2,1,0:T(8,128)(2,1)S(1)} %att.6), channel_id=1, source_target_pairs={{0,1},{3,2},{4,5},{7,6},{8,9},{11,10},{12,13},{15,14},{16,17},{19,... | collective-permute-start | bytes 786440 | tf_op jit(solution)/shard_map/ppermute | solution.py:608
  24.3 22.9 %collective-permute-start.13 = (bf16[2,256,256]{2,1,0:T(8,128)(2,1)S(1)}, bf16[2,256,256]{2,1,0:T(8,128)(2,1)S(1)}, u32[]{:S(2)}, u32[]{:S(2)}) collective-permute-start(bf16[2,256,256]{2,1,0:T(8,128)(2,1)S(1)} %get-tuple-element.53.refs_3_.refs_5_.refs_2_), channel_id=1, source_target_pairs={{0,28},{4,0},{8,4},{12,8},{16,12},{20,16},{24,20},{28,24},{1,29},{... | collective-permute-start | bytes 786440 | tf_op jit(solution)/shard_map/ppermute | solution.py:602
  47.2 1.6 %collective-permute-start.8 = (bf16[256,256]{1,0:T(8,128)(2,1)S(1)}, bf16[256,256]{1,0:T(8,128)(2,1)S(1)}, u32[]{:S(2)}, u32[]{:S(2)}) collective-permute-start(bf16[256,256]{1,0:T(8,128)(2,1)S(1)} %get-tuple-element.58.att), channel_id=1, source_target_pairs={{0,1},{3,2},{4,5},{7,6},{8,9},{11,10},{12,13},{15,14},{16,17},{19,... | collective-permute-start | bytes 393224 | tf_op jit(solution)/shard_map/ppermute | solution.py:608
  48.8 1.3 %part.3 = (f32[512,512]{1,0:T(8,128)S(1)}, bf16[512,512]{1,0:T(8,128)(2,1)S(1)}) custom-call(s32[4]{0:T(128)S(1)} %compare_select_fusion.1.meta_ref, bf16[2,256,256]{2,1,0:T(8,128)(2,1)S(1)} %att.6, bf16[2,256,256]{2,1,0:T(8,128)(2,1)S(1)} %collective-permute-done.3.near_ref, bf16[256,1024]{1,0:T(8,128)(2,1)S(1)} %copy-done, ...), custom_call_target="tpu_custom_call" | custom-call | flops 536870912 | bytes 4194304 | tf_op jit(solution)/shard_map/part/pallas_call | solution.py:360
  50.1 0.9 collective-permute-start.11
  51.0 0.3 collective-permute-done.8.near_ref
  51.3 1.0 part.4
  52.3 2.2 %att.7 = bf16[256,256]{1,0:T(8,128)(2,1)S(1)} custom-call(s32[4]{0:T(128)S(1)} %compare_select_fusion.1.meta_ref, s32[2,32]{1,0:T(2,128)S(1)} %bitcast.12, bf16[256,256]{1,0:T(8,128)(2,1)S(1)} %get-tuple-element.75.refs_0_, bf16[2,256,256]{2,1,0:T(8,128)(2,1)S(1)} %get-tuple-element.52.refs_2_.refs_4_.refs_1_, ...), custom_call_target="tpu_custom_call" | custom-call | flops 671088640 | bytes 2621440 | tf_op jit(solution)/shard_map/att/pallas_call | solution.py:288
  54.5 4.4 %collective-permute-start.14 = (bf16[256,256]{1,0:T(8,128)(2,1)S(1)}, bf16[256,256]{1,0:T(8,128)(2,1)S(1)}, u32[]{:S(2)}, u32[]{:S(2)}) collective-permute-start(bf16[256,256]{1,0:T(8,128)(2,1)S(1)} %att.7), channel_id=1, source_target_pairs={{0,1},{3,2},{4,5},{7,6},{8,9},{11,10},{12,13},{15,14},{16,17},{19,... | collective-permute-start | bytes 393224 | tf_op jit(solution)/shard_map/ppermute | solution.py:608
  58.9 0.7 collective-permute-start.9
  59.6 0.7 prep.1
  60.3 1.1 collective-permute-done.14.near_ref
  61.4 1.0 part.5
  62.4 0.7 collective-permute-start.15
  63.1 3.9 %collective-permute-start.6 = (s32[16,256]{1,0:T(8,128)S(1)}, s32[16,256]{1,0:T(8,128)S(1)}, u32[]{:S(2)}, u32[]{:S(2)}) collective-permute-start(s32[16,256]{1,0:T(8,128)S(1)} %pad_add_fusion.1), channel_id=1, source_target_pairs={{0,8},{4,12},{8,0},{12,4},{16,24},{20,28},{24,16},{28,20},{1,9},{5... | collective-permute-start | bytes 49160 | tf_op jit(solution)/shard_map/ppermute | solution.py:605
  67.0 0.7 merge.4
  67.7 1.3 %collective-permute-start.12 = (bf16[512,256]{1,0:T(8,128)(2,1)S(1)}, bf16[512,256]{1,0:T(8,128)(2,1)S(1)}, u32[]{:S(2)}, u32[]{:S(2)}) collective-permute-start(bf16[512,256]{1,0:T(8,128)(2,1)S(1)} %get-tuple-element.73), channel_id=1, source_target_pairs={{1,0},{2,3},{5,4},{6,7},{9,8},{10,11},{13,12},{14,15},{17,16},{18,... | collective-permute-start | bytes 786440 | tf_op jit(solution)/shard_map/ppermute | solution.py:608
  69.0 0.1 collective-permute-start.7
  69.1 0.6 merge.3
  69.7 1.3 %collective-permute-start.10 = (bf16[256,256]{1,0:T(8,128)(2,1)S(1)}, bf16[256,256]{1,0:T(8,128)(2,1)S(1)}, u32[]{:S(2)}, u32[]{:S(2)}) collective-permute-start(bf16[256,256]{1,0:T(8,128)(2,1)S(1)} %get-tuple-element.70), channel_id=1, source_target_pairs={{1,0},{2,3},{5,4},{6,7},{9,8},{10,11},{13,12},{14,15},{17,16},{18,... | collective-permute-start | bytes 393224 | tf_op jit(solution)/shard_map/ppermute | solution.py:608
  71.0 0.6 merge.5
  71.7 1.3 %collective-permute-start.16 = (bf16[256,256]{1,0:T(8,128)(2,1)S(1)}, bf16[256,256]{1,0:T(8,128)(2,1)S(1)}, u32[]{:S(2)}, u32[]{:S(2)}) collective-permute-start(bf16[256,256]{1,0:T(8,128)(2,1)S(1)} %get-tuple-element.79), channel_id=1, source_target_pairs={{1,0},{2,3},{5,4},{6,7},{9,8},{10,11},{13,12},{14,15},{17,16},{18,... | collective-permute-start | bytes 393224 | tf_op jit(solution)/shard_map/ppermute | solution.py:608
  73.0 16.2 %collective-permute-done.10.refs_1_ = bf16[256,256]{1,0:T(8,128)(2,1)S(1)} collective-permute-done((bf16[256,256]{1,0:T(8,128)(2,1)S(1)}, bf16[256,256]{1,0:T(8,128)(2,1)S(1)}, u32[]{:S(2)}, u32[]{:S(2)}) %collective-permute-start.10) | collective-permute-done | bytes 131104 | tf_op jit(solution)/shard_map/ppermute | solution.py:608
  89.3 1.4 %collective-permute-done.16.refs_5_ = bf16[256,256]{1,0:T(8,128)(2,1)S(1)} collective-permute-done((bf16[256,256]{1,0:T(8,128)(2,1)S(1)}, bf16[256,256]{1,0:T(8,128)(2,1)S(1)}, u32[]{:S(2)}, u32[]{:S(2)}) %collective-permute-start.16) | collective-permute-done | bytes 131104 | tf_op jit(solution)/shard_map/ppermute | solution.py:608
  90.7 1.2 %gath.3 = (bf16[1024,256]{1,0:T(8,128)(2,1)S(1)}, bf16[256,256]{1,0:T(8,128)(2,1)S(1)}, bf16[256,256]{1,0:T(8,128)(2,1)S(1)}) custom-call(s32[4]{0:T(128)S(1)} %compare_select_fusion.1.meta_ref, s32[64,256]{1,0:T(8,128)S(1)} %constant_dynamic-update-slice_fusion.wanted_ref, bf16[256,256]{1,0:T(8,128)(2,1)S(1)} %get-tuple-element.69.refs_0_, ...), custom_call_target="tpu_custom_call" | custom-call | flops 268435456 | bytes 1572864 | tf_op jit(solution)/shard_map/gath/pallas_call | solution.py:482
  91.9 1.2 %gath.5 = (bf16[256,256]{1,0:T(8,128)(2,1)S(1)}, bf16[256,256]{1,0:T(8,128)(2,1)S(1)}) custom-call(s32[4]{0:T(128)S(1)} %compare_select_fusion.1.meta_ref, s32[64,256]{1,0:T(8,128)S(1)} %constant_dynamic-update-slice_fusion.wanted_ref, bf16[1024,256]{1,0:T(8,128)(2,1)S(1)} %get-tuple-element.80.refs_0_.layer_ref), custom_call_target="tpu_custom_call" | custom-call | flops 268435456 | bytes 1572864 | tf_op jit(solution)/shard_map/gath/pallas_call | solution.py:482
  93.1 0.1 collective-permute-start.19
  93.2 1.6 %collective-permute-start.21 = (bf16[256,256]{1,0:T(8,128)(2,1)S(1)}, bf16[256,256]{1,0:T(8,128)(2,1)S(1)}, u32[]{:S(2)}, u32[]{:S(2)}) collective-permute-start(bf16[256,256]{1,0:T(8,128)(2,1)S(1)} %get-tuple-element.86), channel_id=1, source_target_pairs={{0,20},{4,16},{8,28},{12,24},{16,4},{20,0},{24,12},{28,8},{1,21},{... | collective-permute-start | bytes 393224 | tf_op jit(solution)/shard_map/ppermute | solution.py:605
  94.8 1.5 %gath.4 = (bf16[256,256]{1,0:T(8,128)(2,1)S(1)}, bf16[256,256]{1,0:T(8,128)(2,1)S(1)}, bf16[256,256]{1,0:T(8,128)(2,1)S(1)}, bf16[256,256]{1,0:T(8,128)(2,1)S(1)}) custom-call(s32[4]{0:T(128)S(1)} %compare_select_fusion.1.meta_ref, s32[64,256]{1,0:T(8,128)S(1)} %constant_dynamic-update-slice_fusion.wanted_ref, ...), custom_call_target="tpu_custom_call" | custom-call | flops 536870912 | bytes 2097152 | tf_op jit(solution)/shard_map/gath/pallas_call | solution.py:482
  96.3 0.1 collective-permute-start.17
  96.4 1.5 %collective-permute-start.18 = (bf16[256,256]{1,0:T(8,128)(2,1)S(1)}, bf16[256,256]{1,0:T(8,128)(2,1)S(1)}, u32[]{:S(2)}, u32[]{:S(2)}) collective-permute-start(bf16[256,256]{1,0:T(8,128)(2,1)S(1)} %get-tuple-element.83), channel_id=1, source_target_pairs={{0,8},{4,12},{8,0},{12,4},{16,24},{20,28},{24,16},{28,20},{1,9},{5... | collective-permute-start | bytes 393224 | tf_op jit(solution)/shard_map/ppermute | solution.py:605
  97.9 0.8 collective-permute-start.20
  98.6 1.6 %collective-permute-start.22 = (bf16[256,256]{1,0:T(8,128)(2,1)S(1)}, bf16[256,256]{1,0:T(8,128)(2,1)S(1)}, u32[]{:S(2)}, u32[]{:S(2)}) collective-permute-start(bf16[256,256]{1,0:T(8,128)(2,1)S(1)} %get-tuple-element.87), channel_id=1, source_target_pairs={{0,24},{4,28},{8,16},{12,20},{16,8},{20,12},{24,0},{28,4},{1,25},{... | collective-permute-start | bytes 393224 | tf_op jit(solution)/shard_map/ppermute | solution.py:605
  100.2 1.2 %collective-permute-start.23 = (bf16[256,256]{1,0:T(8,128)(2,1)S(1)}, bf16[256,256]{1,0:T(8,128)(2,1)S(1)}, u32[]{:S(2)}, u32[]{:S(2)}) collective-permute-start(bf16[256,256]{1,0:T(8,128)(2,1)S(1)} %get-tuple-element.88), channel_id=1, source_target_pairs={{0,28},{4,24},{8,20},{12,16},{16,12},{20,8},{24,4},{28,0},{1,29},{... | collective-permute-start | bytes 393224 | tf_op jit(solution)/shard_map/ppermute | solution.py:605
  101.4 0.8 collective-permute-done.18.refs_2_
  102.3 6.7 %collective-permute-done.20.refs_4_ = bf16[256,256]{1,0:T(8,128)(2,1)S(1)} collective-permute-done((bf16[256,256]{1,0:T(8,128)(2,1)S(1)}, bf16[256,256]{1,0:T(8,128)(2,1)S(1)}, u32[]{:S(2)}, u32[]{:S(2)}) %collective-permute-start.20) | collective-permute-done | bytes 131104 | tf_op jit(solution)/shard_map/ppermute | solution.py:605
  109.0 1.7 %first.1.early_ref = bf16[1024,256]{1,0:T(8,128)(2,1)S(1)} custom-call(s32[4]{0:T(128)S(1)} %compare_select_fusion.1.meta_ref, s32[8,128]{1,0:T(8,128)S(1)} %get-tuple-element.65.code_ref, bf16[256,256]{1,0:T(8,128)(2,1)S(1)} %get-tuple-element.81.refs_0_, bf16[256,256]{1,0:T(8,128)(2,1)S(1)} %collective-permute-done.17.refs_1_, ...), custom_call_target="tpu_custom_call" | custom-call | flops 805306368 | bytes 1048576 | tf_op jit(solution)/shard_map/first/pallas_call | solution.py:532
  110.7 2.1 %fin.1 = f32[1024,256]{1,0:T(8,128)} custom-call(s32[4]{0:T(128)S(1)} %compare_select_fusion.1.meta_ref, s32[8,128]{1,0:T(8,128)S(1)} %get-tuple-element.65.code_ref, f32[8,128]{1,0:T(8,128)S(1)} %bitcast.8, bf16[1024,256]{1,0:T(8,128)(2,1)S(1)} %get-tuple-element.80.refs_0_.layer_ref, bf16[1024,256]{1,0:T(8,128)(2,1)S(1)} %first.1.early_ref, ...), custom_call_target="tpu_custom_call" | custom-call | flops 268435456 | bytes 2097152 | tf_op jit(solution)/shard_map/fin/pallas_call | solution.py:573
  (37 shorter events, 0.2 us)
Async XLA Ops:
  0.0 0.7 copy-start.1
  4.6 5.6 %copy-start = (bf16[256,1024]{1,0:T(8,128)(2,1)S(1)}, bf16[256,1024]{1,0:T(8,128)(2,1)}, u32[]{:S(2)}) copy-start(bf16[256,1024]{1,0:T(8,128)(2,1)} %own_ref.5) | copy-start | bytes 1572868
  4.6 9.1 %copy-start.3 = (s32[32,2]{0,1:T(2,128)S(1)}, s32[32,2]{0,1:T(2,128)}, u32[]{:S(2)}) copy-start(s32[32,2]{0,1:T(2,128)} %param.12) | copy-start | bytes 772
  4.6 12.0 %collective-permute-start = (bf16[2,256,256]{2,1,0:T(8,128)(2,1)S(1)}, bf16[2,256,256]{2,1,0:T(8,128)(2,1)S(1)}, u32[]{:S(2)}, u32[]{:S(2)}) collective-permute-start(bf16[2,256,256]{2,1,0:T(8,128)(2,1)S(1)} %get-tuple-element.52.refs_2_.refs_4_.refs_1_), channel_id=1, source_target_pairs={{0,28},{4,0},{8,4},{12,8},{16,12},{20,16},{24,20},{28,24},{1,29},{... | collective-permute-start | bytes 786440 | tf_op jit(solution)/shard_map/ppermute | solution.py:602
  8.0 8.6 %collective-permute-start.1 = (bf16[2,256,256]{2,1,0:T(8,128)(2,1)S(1)}, bf16[2,256,256]{2,1,0:T(8,128)(2,1)S(1)}, u32[]{:S(2)}, u32[]{:S(2)}) collective-permute-start(bf16[2,256,256]{2,1,0:T(8,128)(2,1)S(1)} %get-tuple-element.55.refs_5_.refs_7_.refs_4_), channel_id=1, source_target_pairs={{0,4},{4,8},{8,12},{12,16},{16,20},{20,24},{24,28},{28,0},{1,5},{5... | collective-permute-start | bytes 786440 | tf_op jit(solution)/shard_map/ppermute | solution.py:602
  10.1 8.5 %collective-permute-start.2 = (bf16[2,256,256]{2,1,0:T(8,128)(2,1)S(1)}, bf16[2,256,256]{2,1,0:T(8,128)(2,1)S(1)}, u32[]{:S(2)}, u32[]{:S(2)}) collective-permute-start(bf16[2,256,256]{2,1,0:T(8,128)(2,1)S(1)} %get-tuple-element.54.refs_4_.refs_6_.refs_3_), channel_id=1, source_target_pairs={{0,4},{4,8},{8,12},{12,16},{16,20},{20,24},{24,28},{28,0},{1,5},{5... | collective-permute-start | bytes 786440 | tf_op jit(solution)/shard_map/ppermute | solution.py:602
  10.2 38.6 %collective-permute-start.4 = (bf16[256,1024]{1,0:T(8,128)(2,1)S(1)}, bf16[256,1024]{1,0:T(8,128)(2,1)S(1)}, u32[]{:S(2)}, u32[]{:S(2)}) collective-permute-start(bf16[256,1024]{1,0:T(8,128)(2,1)S(1)} %copy-done), channel_id=1, source_target_pairs={{0,1},{3,2},{4,5},{7,6},{8,9},{11,10},{12,13},{15,14},{16,17},{19,... | collective-permute-start | bytes 1572872 | tf_op jit(solution)/shard_map/ppermute | solution.py:608
  20.8 28.0 %collective-permute-start.3 = (bf16[2,256,256]{2,1,0:T(8,128)(2,1)S(1)}, bf16[2,256,256]{2,1,0:T(8,128)(2,1)S(1)}, u32[]{:S(2)}, u32[]{:S(2)}) collective-permute-start(bf16[2,256,256]{2,1,0:T(8,128)(2,1)S(1)} %att.6), channel_id=1, source_target_pairs={{0,1},{3,2},{4,5},{7,6},{8,9},{11,10},{12,13},{15,14},{16,17},{19,... | collective-permute-start | bytes 786440 | tf_op jit(solution)/shard_map/ppermute | solution.py:608
  24.3 28.0 %collective-permute-start.13 = (bf16[2,256,256]{2,1,0:T(8,128)(2,1)S(1)}, bf16[2,256,256]{2,1,0:T(8,128)(2,1)S(1)}, u32[]{:S(2)}, u32[]{:S(2)}) collective-permute-start(bf16[2,256,256]{2,1,0:T(8,128)(2,1)S(1)} %get-tuple-element.53.refs_3_.refs_5_.refs_2_), channel_id=1, source_target_pairs={{0,28},{4,0},{8,4},{12,8},{16,12},{20,16},{24,20},{28,24},{1,29},{... | collective-permute-start | bytes 786440 | tf_op jit(solution)/shard_map/ppermute | solution.py:602
  47.2 4.1 %collective-permute-start.8 = (bf16[256,256]{1,0:T(8,128)(2,1)S(1)}, bf16[256,256]{1,0:T(8,128)(2,1)S(1)}, u32[]{:S(2)}, u32[]{:S(2)}) collective-permute-start(bf16[256,256]{1,0:T(8,128)(2,1)S(1)} %get-tuple-element.58.att), channel_id=1, source_target_pairs={{0,1},{3,2},{4,5},{7,6},{8,9},{11,10},{12,13},{15,14},{16,17},{19,... | collective-permute-start | bytes 393224 | tf_op jit(solution)/shard_map/ppermute | solution.py:608
  50.1 16.9 %collective-permute-start.11 = (bf16[512,512]{1,0:T(8,128)(2,1)S(1)}, bf16[512,512]{1,0:T(8,128)(2,1)S(1)}, u32[]{:S(2)}, u32[]{:S(2)}) collective-permute-start(bf16[512,512]{1,0:T(8,128)(2,1)S(1)} %get-tuple-element.63), channel_id=1, source_target_pairs={{1,2},{2,1},{5,6},{6,5},{9,10},{10,9},{13,14},{14,13},{17,18},{18,... | collective-permute-start | bytes 1572872 | tf_op jit(solution)/shard_map/ppermute | solution.py:608
  52.3 7.3 %copy-start.4 = (s32[1024,1]{0,1:T(1,128)S(1)}, s32[1024,1]{0,1:T(1,128)}, u32[]{:S(2)}) copy-start(s32[1024,1]{0,1:T(1,128)} %param.13) | copy-start | bytes 12292
  52.3 7.3 %copy-start.5 = (s32[1024]{0:T(1024)S(1)}, s32[1024]{0:T(1024)}, u32[]{:S(2)}) copy-start(s32[1024]{0:T(1024)} %param.14) | copy-start | bytes 12292
  54.5 6.9 %collective-permute-start.14 = (bf16[256,256]{1,0:T(8,128)(2,1)S(1)}, bf16[256,256]{1,0:T(8,128)(2,1)S(1)}, u32[]{:S(2)}, u32[]{:S(2)}) collective-permute-start(bf16[256,256]{1,0:T(8,128)(2,1)S(1)} %att.7), channel_id=1, source_target_pairs={{0,1},{3,2},{4,5},{7,6},{8,9},{11,10},{12,13},{15,14},{16,17},{19,... | collective-permute-start | bytes 393224 | tf_op jit(solution)/shard_map/ppermute | solution.py:608
  58.9 10.2 %collective-permute-start.9 = (bf16[256,512]{1,0:T(8,128)(2,1)S(1)}, bf16[256,512]{1,0:T(8,128)(2,1)S(1)}, u32[]{:S(2)}, u32[]{:S(2)}) collective-permute-start(bf16[256,512]{1,0:T(8,128)(2,1)S(1)} %get-tuple-element.68), channel_id=1, source_target_pairs={{1,2},{2,1},{5,6},{6,5},{9,10},{10,9},{13,14},{14,13},{17,18},{18,... | collective-permute-start | bytes 786440 | tf_op jit(solution)/shard_map/ppermute | solution.py:608
  60.3 2.8 %collective-permute-start.5 = (s32[8,256]{1,0:T(8,128)S(1)}, s32[8,256]{1,0:T(8,128)S(1)}, u32[]{:S(2)}, u32[]{:S(2)}) collective-permute-start(s32[8,256]{1,0:T(8,128)S(1)} %get-tuple-element.66), channel_id=1, source_target_pairs={{0,4},{4,0},{8,12},{12,8},{16,20},{20,16},{24,28},{28,24},{1,5},{5... | collective-permute-start | bytes 24584 | tf_op jit(solution)/shard_map/ppermute | solution.py:605
  62.4 8.6 %collective-permute-start.15 = (bf16[256,512]{1,0:T(8,128)(2,1)S(1)}, bf16[256,512]{1,0:T(8,128)(2,1)S(1)}, u32[]{:S(2)}, u32[]{:S(2)}) collective-permute-start(bf16[256,512]{1,0:T(8,128)(2,1)S(1)} %get-tuple-element.77), channel_id=1, source_target_pairs={{1,2},{2,1},{5,6},{6,5},{9,10},{10,9},{13,14},{14,13},{17,18},{18,... | collective-permute-start | bytes 786440 | tf_op jit(solution)/shard_map/ppermute | solution.py:608
  63.1 5.9 %collective-permute-start.6 = (s32[16,256]{1,0:T(8,128)S(1)}, s32[16,256]{1,0:T(8,128)S(1)}, u32[]{:S(2)}, u32[]{:S(2)}) collective-permute-start(s32[16,256]{1,0:T(8,128)S(1)} %pad_add_fusion.1), channel_id=1, source_target_pairs={{0,8},{4,12},{8,0},{12,4},{16,24},{20,28},{24,16},{28,20},{1,9},{5... | collective-permute-start | bytes 49160 | tf_op jit(solution)/shard_map/ppermute | solution.py:605
  67.7 23.0 %collective-permute-start.12 = (bf16[512,256]{1,0:T(8,128)(2,1)S(1)}, bf16[512,256]{1,0:T(8,128)(2,1)S(1)}, u32[]{:S(2)}, u32[]{:S(2)}) collective-permute-start(bf16[512,256]{1,0:T(8,128)(2,1)S(1)} %get-tuple-element.73), channel_id=1, source_target_pairs={{1,0},{2,3},{5,4},{6,7},{9,8},{10,11},{13,12},{14,15},{17,16},{18,... | collective-permute-start | bytes 786440 | tf_op jit(solution)/shard_map/ppermute | solution.py:608
  69.0 4.0 %collective-permute-start.7 = (s32[32,256]{1,0:T(8,128)S(1)}, s32[32,256]{1,0:T(8,128)S(1)}, u32[]{:S(2)}, u32[]{:S(2)}) collective-permute-start(s32[32,256]{1,0:T(8,128)S(1)} %pad_add_fusion), channel_id=1, source_target_pairs={{0,16},{4,20},{8,24},{12,28},{16,0},{20,4},{24,8},{28,12},{1,17},{... | collective-permute-start | bytes 98312 | tf_op jit(solution)/shard_map/ppermute | solution.py:605
  69.7 19.5 %collective-permute-start.10 = (bf16[256,256]{1,0:T(8,128)(2,1)S(1)}, bf16[256,256]{1,0:T(8,128)(2,1)S(1)}, u32[]{:S(2)}, u32[]{:S(2)}) collective-permute-start(bf16[256,256]{1,0:T(8,128)(2,1)S(1)} %get-tuple-element.70), channel_id=1, source_target_pairs={{1,0},{2,3},{5,4},{6,7},{9,8},{10,11},{13,12},{14,15},{17,16},{18,... | collective-permute-start | bytes 393224 | tf_op jit(solution)/shard_map/ppermute | solution.py:608
  71.7 19.0 %collective-permute-start.16 = (bf16[256,256]{1,0:T(8,128)(2,1)S(1)}, bf16[256,256]{1,0:T(8,128)(2,1)S(1)}, u32[]{:S(2)}, u32[]{:S(2)}) collective-permute-start(bf16[256,256]{1,0:T(8,128)(2,1)S(1)} %get-tuple-element.79), channel_id=1, source_target_pairs={{1,0},{2,3},{5,4},{6,7},{9,8},{10,11},{13,12},{14,15},{17,16},{18,... | collective-permute-start | bytes 393224 | tf_op jit(solution)/shard_map/ppermute | solution.py:608
  93.1 5.5 %collective-permute-start.19 = (bf16[256,256]{1,0:T(8,128)(2,1)S(1)}, bf16[256,256]{1,0:T(8,128)(2,1)S(1)}, u32[]{:S(2)}, u32[]{:S(2)}) collective-permute-start(bf16[256,256]{1,0:T(8,128)(2,1)S(1)} %get-tuple-element.84), channel_id=1, source_target_pairs={{0,12},{4,8},{8,4},{12,0},{16,28},{20,24},{24,20},{28,16},{1,13},{... | collective-permute-start | bytes 393224 | tf_op jit(solution)/shard_map/ppermute | solution.py:605
  93.2 7.0 %collective-permute-start.21 = (bf16[256,256]{1,0:T(8,128)(2,1)S(1)}, bf16[256,256]{1,0:T(8,128)(2,1)S(1)}, u32[]{:S(2)}, u32[]{:S(2)}) collective-permute-start(bf16[256,256]{1,0:T(8,128)(2,1)S(1)} %get-tuple-element.86), channel_id=1, source_target_pairs={{0,20},{4,16},{8,28},{12,24},{16,4},{20,0},{24,12},{28,8},{1,21},{... | collective-permute-start | bytes 393224 | tf_op jit(solution)/shard_map/ppermute | solution.py:605
  96.3 14.4 %copy-start.2 = (f32[1024]{0:T(1024)S(1)}, f32[1024]{0:T(1024)}, u32[]{:S(2)}) copy-start(f32[1024]{0:T(1024)} %param.15) | copy-start | bytes 12292
  96.3 5.1 %collective-permute-start.17 = (bf16[256,256]{1,0:T(8,128)(2,1)S(1)}, bf16[256,256]{1,0:T(8,128)(2,1)S(1)}, u32[]{:S(2)}, u32[]{:S(2)}) collective-permute-start(bf16[256,256]{1,0:T(8,128)(2,1)S(1)} %get-tuple-element.82), channel_id=1, source_target_pairs={{0,4},{4,0},{8,12},{12,8},{16,20},{20,16},{24,28},{28,24},{1,5},{5... | collective-permute-start | bytes 393224 | tf_op jit(solution)/shard_map/ppermute | solution.py:605
  96.4 5.9 %collective-permute-start.18 = (bf16[256,256]{1,0:T(8,128)(2,1)S(1)}, bf16[256,256]{1,0:T(8,128)(2,1)S(1)}, u32[]{:S(2)}, u32[]{:S(2)}) collective-permute-start(bf16[256,256]{1,0:T(8,128)(2,1)S(1)} %get-tuple-element.83), channel_id=1, source_target_pairs={{0,8},{4,12},{8,0},{12,4},{16,24},{20,28},{24,16},{28,20},{1,9},{5... | collective-permute-start | bytes 393224 | tf_op jit(solution)/shard_map/ppermute | solution.py:605
  97.9 11.1 %collective-permute-start.20 = (bf16[256,256]{1,0:T(8,128)(2,1)S(1)}, bf16[256,256]{1,0:T(8,128)(2,1)S(1)}, u32[]{:S(2)}, u32[]{:S(2)}) collective-permute-start(bf16[256,256]{1,0:T(8,128)(2,1)S(1)} %get-tuple-element.85), channel_id=1, source_target_pairs={{0,16},{4,20},{8,24},{12,28},{16,0},{20,4},{24,8},{28,12},{1,17},{... | collective-permute-start | bytes 393224 | tf_op jit(solution)/shard_map/ppermute | solution.py:605
  98.6 12.1 %collective-permute-start.22 = (bf16[256,256]{1,0:T(8,128)(2,1)S(1)}, bf16[256,256]{1,0:T(8,128)(2,1)S(1)}, u32[]{:S(2)}, u32[]{:S(2)}) collective-permute-start(bf16[256,256]{1,0:T(8,128)(2,1)S(1)} %get-tuple-element.87), channel_id=1, source_target_pairs={{0,24},{4,28},{8,16},{12,20},{16,8},{20,12},{24,0},{28,4},{1,25},{... | collective-permute-start | bytes 393224 | tf_op jit(solution)/shard_map/ppermute | solution.py:605
  100.2 10.5 %collective-permute-start.23 = (bf16[256,256]{1,0:T(8,128)(2,1)S(1)}, bf16[256,256]{1,0:T(8,128)(2,1)S(1)}, u32[]{:S(2)}, u32[]{:S(2)}) collective-permute-start(bf16[256,256]{1,0:T(8,128)(2,1)S(1)} %get-tuple-element.88), channel_id=1, source_target_pairs={{0,28},{4,24},{8,20},{12,16},{16,12},{20,8},{24,4},{28,0},{1,29},{... | collective-permute-start | bytes 393224 | tf_op jit(solution)/shard_map/ppermute | solution.py:605

commit v10 on v8

--- a/solution.py
+++ b/solution.py
@@ -176,7 +176,7 @@
 
 
 def attend(
-    meta, inter, queries, blocks, remote, plan, window, earlier=None, last=True, carry=None, slot=0
+    meta, inter, queries, blocks, remote, plan, window, earlier=None, last=True, carry=None
 ):
     local_views = len(blocks)
     sub, tokens = queries[0].shape
@@ -223,7 +223,7 @@
             for h in range(heads):
                 keys = keys_of(i)
                 weights = []
-                top = before[1][slot + i, h : h + 1, :] if held else None
+                top = before[1][i, h : h + 1, :] if held else None
                 for _, source, o in keys:
                     scores = upcoming
                     n += 1
@@ -239,7 +239,7 @@
                 values = jnp.concatenate([head_values(k[0], h) for k in keys], axis=1)
                 sums = dot(values, jnp.concatenate(weights, axis=0))
                 if held:
-                    sums = sums + before[0][slot + i, h * tall : (h + 1) * tall, :]
+                    sums = sums + before[0][i, h * tall : (h + 1) * tall, :]
                 if not last:
                     refs[0][i, h * tall : (h + 1) * tall, :] = sums
                     refs[1][i, h : h + 1, :] = top
@@ -634,22 +634,10 @@
         meta, inter, inner_queries, blocks, {}, [(v, []) for v, _ in inner_plan], window, last=False
     )
     attended = {}
-    inner = []
-    for n in range(2):
-        view, sources = inner_plan[n]
-        query = inner_queries[n] if n == 0 else after(inner_queries[n], inner[0])
-        inner += attend(
-            meta,
-            inter,
-            [query],
-            blocks,
-            {s[0]: far[s[0]] for s in sources},
-            [(view, sources)],
-            window,
-            earlier=tuple(local),
-            slot=n,
-        )
-    attended["a"], second = inner
+    attended["a"], second = attend(
+        meta, inter, inner_queries, blocks, dict(n1=far["n1"], p1=far["p1"]), inner_plan, window,
+        earlier=tuple(local),
+    )
 
     def attend_outer(view, sources, done, carry=None):
         (result,) = attend(
@@ -685,7 +673,7 @@
     pass_on("c")
     strips = rows // LANES
     wanted, code = prepare_requests(
-        after(match_block.reshape(strips, LANES), sent["c"]),
+        after(match_block.reshape(strips, LANES), sent["b"]),
         match_row.reshape(strips, LANES),
         peers,
         capacity,
@@ -710,7 +698,7 @@
     reply(first_masks, outgoing)
     *outgoing, own_rows = gather_rows(meta, wanted, layer, last_masks + [0], tokens)
     reply(last_masks, outgoing)
-    late = [m for m in last_masks if m > 1]
+    late = [m for m in first_masks if m < 3 * peers // 4]
     early = first_replies(
         meta, code, {0: own_rows, **{m: r for m, r in replies.items() if m not in late}}, tokens
     )

time: 117 us -> 115 us (0.983)
    ppermute x10, starting transfers between devices: 7.16 us -> 9.78 us  [partner(): return lax.ppermute(x, VIEWS, [(i, i ^ mask) for i in range(peers)])]
    ppermute x10, waiting for transfers between devices: 12.8 us -> 10.8 us  [partner(): return lax.ppermute(x, VIEWS, [(i, i ^ mask) for i in range(peers)])]
    ppermute x10, starting transfers between devices: 20.9 us -> 19 us  [across(): return lax.ppermute(x, HEADS, pairs)]
    ppermute x4, starting transfers between devices: 27.8 us -> 26.4 us  [along(): return lax.ppermute(x, VIEWS, [(i, (i + by) % peers) for i in range(peers)])]
    pallas_call x5 -> x4, Pallas kernels: 9.91 us -> 9.03 us  [attend(): pl.pallas_call(body, in_specs=[SMEM_SPEC, SMEM_SPEC] + many(VMEM_SPEC, he...]
  transfers between devices with their start and end apart: 24 -> 24, of which waited for: 10 -> 11; matrix products, arithmetic and copies ran while one was open for 0% -> 0% of each run, Pallas kernels for 17% -> 16%
where the time goes in v10:
time: 115 us; the launch traced here: 114 us
  starting transfers between devices  55.2 us (48%)
  waiting for transfers between devices  30 us (26%)
  Pallas kernels  27.7 us (24%)
    ppermute x4, starting transfers between devices, along(): return lax.ppermute(x, VIEWS, [(i, (i + by) % peers) for i in range(peers)])  26.4 us
    ppermute x10, waiting for transfers between devices, across(): return lax.ppermute(x, HEADS, pairs)  19.1 us
    ppermute x10, starting transfers between devices, across(): return lax.ppermute(x, HEADS, pairs)  19 us
    ppermute x10, waiting for transfers between devices, partner(): return lax.ppermute(x, VIEWS, [(i, i ^ mask) for i in range(peers)])  10.8 us
    ppermute x10, starting transfers between devices, partner(): return lax.ppermute(x, VIEWS, [(i, i ^ mask) for i in range(peers)])  9.78 us
    pallas_call x4, Pallas kernels, attend(): pl.pallas_call(body, in_specs=[SMEM_SPEC, SMEM_SPEC] + many(VMEM_SPEC, he...  9.03 us
    pallas_call x2, Pallas kernels, project_views(): pl.pallas_call(body, in_specs=[SMEM_SPEC, big, VMEM_SPEC, big], out_specs...  5.97 us
    pallas_call x3, Pallas kernels, partial_out(): pl.pallas_call(body, in_specs=[SMEM_SPEC] + many(VMEM_SPEC, 4 + len(base)...  3.26 us
  transfers between devices with their start and end apart: 24, of which 11 were waited for; matrix products, arithmetic and copies ran while one was open for 0% of the time, Pallas kernels for 16%

profile of v10, /device:TPU:0, one launch (start us, length us, event | category | flops | bytes accessed | tf_op | source)
XLA Modules:
  0.0 114.2 jit_solution(15527803046346648878)
XLA Ops:
  0.0 0.7 copy-done.1
  0.7 3.9 %proj.2 = (bf16[256,256]{1,0:T(8,128)(2,1)S(1)}, bf16[2,256,256]{2,1,0:T(8,128)(2,1)S(1)}, bf16[256,256]{1,0:T(8,128)(2,1)S(1)}, bf16[2,256,256]{2,1,0:T(8,128)(...) custom-call(s32[4]{0:T(128)S(1)} %compare_select_fusion.1.meta_ref, ...), custom_call_target="tpu_custom_call" | custom-call | flops 805306368 | bytes 3407872 | tf_op jit(solution)/shard_map/proj/pallas_call | solution.py:120
  4.6 3.4 %collective-permute-start = (bf16[2,256,256]{2,1,0:T(8,128)(2,1)S(1)}, bf16[2,256,256]{2,1,0:T(8,128)(2,1)S(1)}, u32[]{:S(2)}, u32[]{:S(2)}) collective-permute-start(bf16[2,256,256]{2,1,0:T(8,128)(2,1)S(1)} %get-tuple-element.52.refs_2_.refs_4_.refs_1_), channel_id=1, source_target_pairs={{0,28},{4,0},{8,4},{12,8},{16,12},{20,16},{24,20},{28,24},{1,29},{... | collective-permute-start | bytes 786440 | tf_op jit(solution)/shard_map/ppermute | solution.py:602
  8.1 2.1 %proj.3 = (bf16[256,256]{1,0:T(8,128)(2,1)S(1)}, bf16[2,256,256]{2,1,0:T(8,128)(2,1)S(1)}, bf16[256,256]{1,0:T(8,128)(2,1)S(1)}, bf16[2,256,256]{2,1,0:T(8,128)(2,1)S(1)}, bf16[2,256,512]{2,1,0:T(8,128)(2,1)S(1)}) custom-call(s32[4]{0:T(128)S(1)} %compare_select_fusion.1.meta_ref, bf16[2,256,1024]{2,1,0:T(8,128)(2,1)S(1)} %get-tuple-element.48.lat_ref, ...), custom_call_target="tpu_custom_call" | custom-call | flops 805306368 | bytes 3407872 | tf_op jit(solution)/shard_map/proj/pallas_call | solution.py:120
  10.2 3.5 %collective-permute-start.4 = (bf16[256,1024]{1,0:T(8,128)(2,1)S(1)}, bf16[256,1024]{1,0:T(8,128)(2,1)S(1)}, u32[]{:S(2)}, u32[]{:S(2)}) collective-permute-start(bf16[256,1024]{1,0:T(8,128)(2,1)S(1)} %copy-done), channel_id=1, source_target_pairs={{0,1},{3,2},{4,5},{7,6},{8,9},{11,10},{12,13},{15,14},{16,17},{19,... | collective-permute-start | bytes 1572872 | tf_op jit(solution)/shard_map/ppermute | solution.py:608
  13.7 2.9 %att.4 = (f32[2,320,256]{2,1,0:T(8,128)S(1)}, f32[2,4,256]{2,1,0:T(4,128)S(1)}) custom-call(s32[4]{0:T(128)S(1)} %compare_select_fusion.1.meta_ref, s32[2,32]{1,0:T(2,128)S(1)} %bitcast.9, bf16[256,256]{1,0:T(8,128)(2,1)S(1)} %get-tuple-element.50.refs_0_.refs_2_, bf16[256,256]{1,0:T(8,128)(2,1)S(1)} %get-tuple-element.51.refs_1_.refs_3_, ...), custom_call_target="tpu_custom_call" | custom-call | flops 1073741824 | bytes 4194304 | tf_op jit(solution)/shard_map/att/pallas_call | solution.py:288
  16.7 1.7 %att.5 = (bf16[256,256]{1,0:T(8,128)(2,1)S(1)}, bf16[256,256]{1,0:T(8,128)(2,1)S(1)}) custom-call(s32[4]{0:T(128)S(1)} %compare_select_fusion.1.meta_ref, s32[2,32]{1,0:T(2,128)S(1)} %bitcast.10, f32[2,320,256]{2,1,0:T(8,128)S(1)} %get-tuple-element.56.refs_0_, f32[2,4,256]{2,1,0:T(4,128)S(1)} %get-tuple-element.57.refs_1_, ...), custom_call_target="tpu_custom_call" | custom-call | flops 268435456 | bytes 1048576 | tf_op jit(solution)/shard_map/att/pallas_call | solution.py:288
  18.4 0.2 collective-permute-done.2.refs_6_
  18.6 2.2 %att.6 = bf16[2,256,256]{2,1,0:T(8,128)(2,1)S(1)} custom-call(s32[4]{0:T(128)S(1)} %compare_select_fusion.1.meta_ref, s32[2,32]{1,0:T(2,128)S(1)} %bitcast.11, bf16[256,256]{1,0:T(8,128)(2,1)S(1)} %get-tuple-element.59.refs_0_, bf16[2,256,256]{2,1,0:T(8,128)(2,1)S(1)} %get-tuple-element.52.refs_2_.refs_4_.refs_1_, ...), custom_call_target="tpu_custom_call" | custom-call | flops 671088640 | bytes 2621440 | tf_op jit(solution)/shard_map/att/pallas_call | solution.py:288
  20.8 3.5 %collective-permute-start.3 = (bf16[2,256,256]{2,1,0:T(8,128)(2,1)S(1)}, bf16[2,256,256]{2,1,0:T(8,128)(2,1)S(1)}, u32[]{:S(2)}, u32[]{:S(2)}) collective-permute-start(bf16[2,256,256]{2,1,0:T(8,128)(2,1)S(1)} %att.6), channel_id=1, source_target_pairs={{0,1},{3,2},{4,5},{7,6},{8,9},{11,10},{12,13},{15,14},{16,17},{19,... | collective-permute-start | bytes 786440 | tf_op jit(solution)/shard_map/ppermute | solution.py:608
  24.3 22.9 %collective-permute-start.13 = (bf16[2,256,256]{2,1,0:T(8,128)(2,1)S(1)}, bf16[2,256,256]{2,1,0:T(8,128)(2,1)S(1)}, u32[]{:S(2)}, u32[]{:S(2)}) collective-permute-start(bf16[2,256,256]{2,1,0:T(8,128)(2,1)S(1)} %get-tuple-element.53.refs_3_.refs_5_.refs_2_), channel_id=1, source_target_pairs={{0,28},{4,0},{8,4},{12,8},{16,12},{20,16},{24,20},{28,24},{1,29},{... | collective-permute-start | bytes 786440 | tf_op jit(solution)/shard_map/ppermute | solution.py:602
  47.2 1.6 %collective-permute-start.8 = (bf16[256,256]{1,0:T(8,128)(2,1)S(1)}, bf16[256,256]{1,0:T(8,128)(2,1)S(1)}, u32[]{:S(2)}, u32[]{:S(2)}) collective-permute-start(bf16[256,256]{1,0:T(8,128)(2,1)S(1)} %get-tuple-element.58.att), channel_id=1, source_target_pairs={{0,1},{3,2},{4,5},{7,6},{8,9},{11,10},{12,13},{15,14},{16,17},{19,... | collective-permute-start | bytes 393224 | tf_op jit(solution)/shard_map/ppermute | solution.py:608
  48.8 1.3 %part.3 = (f32[512,512]{1,0:T(8,128)S(1)}, bf16[512,512]{1,0:T(8,128)(2,1)S(1)}) custom-call(s32[4]{0:T(128)S(1)} %compare_select_fusion.1.meta_ref, bf16[2,256,256]{2,1,0:T(8,128)(2,1)S(1)} %att.6, bf16[2,256,256]{2,1,0:T(8,128)(2,1)S(1)} %collective-permute-done.3.near_ref, bf16[256,1024]{1,0:T(8,128)(2,1)S(1)} %copy-done, ...), custom_call_target="tpu_custom_call" | custom-call | flops 536870912 | bytes 4194304 | tf_op jit(solution)/shard_map/part/pallas_call | solution.py:360
  50.1 0.9 collective-permute-start.11
  51.0 0.3 collective-permute-done.8.near_ref
  51.3 1.0 part.4
  52.3 2.2 %att.7 = bf16[256,256]{1,0:T(8,128)(2,1)S(1)} custom-call(s32[4]{0:T(128)S(1)} %compare_select_fusion.1.meta_ref, s32[2,32]{1,0:T(2,128)S(1)} %bitcast.12, bf16[256,256]{1,0:T(8,128)(2,1)S(1)} %get-tuple-element.75.refs_0_, bf16[2,256,256]{2,1,0:T(8,128)(2,1)S(1)} %get-tuple-element.52.refs_2_.refs_4_.refs_1_, ...), custom_call_target="tpu_custom_call" | custom-call | flops 671088640 | bytes 2621440 | tf_op jit(solution)/shard_map/att/pallas_call | solution.py:288
  54.5 4.4 %collective-permute-start.14 = (bf16[256,256]{1,0:T(8,128)(2,1)S(1)}, bf16[256,256]{1,0:T(8,128)(2,1)S(1)}, u32[]{:S(2)}, u32[]{:S(2)}) collective-permute-start(bf16[256,256]{1,0:T(8,128)(2,1)S(1)} %att.7), channel_id=1, source_target_pairs={{0,1},{3,2},{4,5},{7,6},{8,9},{11,10},{12,13},{15,14},{16,17},{19,... | collective-permute-start | bytes 393224 | tf_op jit(solution)/shard_map/ppermute | solution.py:608
  58.9 0.7 collective-permute-start.9
  59.6 0.7 prep.1
  60.3 1.1 collective-permute-done.14.near_ref
  61.4 1.0 part.5
  62.4 0.7 collective-permute-start.15
  63.1 3.9 %collective-permute-start.6 = (s32[16,256]{1,0:T(8,128)S(1)}, s32[16,256]{1,0:T(8,128)S(1)}, u32[]{:S(2)}, u32[]{:S(2)}) collective-permute-start(s32[16,256]{1,0:T(8,128)S(1)} %pad_add_fusion.1), channel_id=1, source_target_pairs={{0,8},{4,12},{8,0},{12,4},{16,24},{20,28},{24,16},{28,20},{1,9},{5... | collective-permute-start | bytes 49160 | tf_op jit(solution)/shard_map/ppermute | solution.py:605
  67.0 0.7 merge.4
  67.7 1.3 %collective-permute-start.12 = (bf16[512,256]{1,0:T(8,128)(2,1)S(1)}, bf16[512,256]{1,0:T(8,128)(2,1)S(1)}, u32[]{:S(2)}, u32[]{:S(2)}) collective-permute-start(bf16[512,256]{1,0:T(8,128)(2,1)S(1)} %get-tuple-element.73), channel_id=1, source_target_pairs={{1,0},{2,3},{5,4},{6,7},{9,8},{10,11},{13,12},{14,15},{17,16},{18,... | collective-permute-start | bytes 786440 | tf_op jit(solution)/shard_map/ppermute | solution.py:608
  69.1 0.6 merge.3
  69.7 1.3 %collective-permute-start.10 = (bf16[256,256]{1,0:T(8,128)(2,1)S(1)}, bf16[256,256]{1,0:T(8,128)(2,1)S(1)}, u32[]{:S(2)}, u32[]{:S(2)}) collective-permute-start(bf16[256,256]{1,0:T(8,128)(2,1)S(1)} %get-tuple-element.70), channel_id=1, source_target_pairs={{1,0},{2,3},{5,4},{6,7},{9,8},{10,11},{13,12},{14,15},{17,16},{18,... | collective-permute-start | bytes 393224 | tf_op jit(solution)/shard_map/ppermute | solution.py:608
  71.0 0.6 merge.5
  71.6 1.3 %collective-permute-start.16 = (bf16[256,256]{1,0:T(8,128)(2,1)S(1)}, bf16[256,256]{1,0:T(8,128)(2,1)S(1)}, u32[]{:S(2)}, u32[]{:S(2)}) collective-permute-start(bf16[256,256]{1,0:T(8,128)(2,1)S(1)} %get-tuple-element.79), channel_id=1, source_target_pairs={{1,0},{2,3},{5,4},{6,7},{9,8},{10,11},{13,12},{14,15},{17,16},{18,... | collective-permute-start | bytes 393224 | tf_op jit(solution)/shard_map/ppermute | solution.py:608
  73.0 16.2 %collective-permute-done.10.refs_1_ = bf16[256,256]{1,0:T(8,128)(2,1)S(1)} collective-permute-done((bf16[256,256]{1,0:T(8,128)(2,1)S(1)}, bf16[256,256]{1,0:T(8,128)(2,1)S(1)}, u32[]{:S(2)}, u32[]{:S(2)}) %collective-permute-start.10) | collective-permute-done | bytes 131104 | tf_op jit(solution)/shard_map/ppermute | solution.py:608
  89.2 1.4 %collective-permute-done.16.refs_5_ = bf16[256,256]{1,0:T(8,128)(2,1)S(1)} collective-permute-done((bf16[256,256]{1,0:T(8,128)(2,1)S(1)}, bf16[256,256]{1,0:T(8,128)(2,1)S(1)}, u32[]{:S(2)}, u32[]{:S(2)}) %collective-permute-start.16) | collective-permute-done | bytes 131104 | tf_op jit(solution)/shard_map/ppermute | solution.py:608
  90.6 1.5 %gath.2 = (bf16[1024,256]{1,0:T(8,128)(2,1)S(1)}, bf16[256,256]{1,0:T(8,128)(2,1)S(1)}, bf16[256,256]{1,0:T(8,128)(2,1)S(1)}, bf16[256,256]{1,0:T(8,128)(2,1)S(1)}, bf16[256,256]{1,0:T(8,128)(2,1)S(1)}) custom-call(s32[4]{0:T(128)S(1)} %compare_select_fusion.1.meta_ref, s32[64,256]{1,0:T(8,128)S(1)} %constant_dynamic-update-slice_fusion.wanted_ref, ...), custom_call_target="tpu_custom_call" | custom-call | flops 536870912 | bytes 2097152 | tf_op jit(solution)/shard_map/gath/pallas_call | solution.py:482
  92.2 1.5 %gath.3 = (bf16[256,256]{1,0:T(8,128)(2,1)S(1)}, bf16[256,256]{1,0:T(8,128)(2,1)S(1)}, bf16[256,256]{1,0:T(8,128)(2,1)S(1)}, bf16[256,256]{1,0:T(8,128)(2,1)S(1)}) custom-call(s32[4]{0:T(128)S(1)} %compare_select_fusion.1.meta_ref, s32[64,256]{1,0:T(8,128)S(1)} %constant_dynamic-update-slice_fusion.wanted_ref, ...), custom_call_target="tpu_custom_call" | custom-call | flops 536870912 | bytes 2097152 | tf_op jit(solution)/shard_map/gath/pallas_call | solution.py:482
  93.7 0.1 collective-permute-start.17
  93.8 0.1 collective-permute-start.18
  93.9 1.8 %collective-permute-start.19 = (bf16[256,256]{1,0:T(8,128)(2,1)S(1)}, bf16[256,256]{1,0:T(8,128)(2,1)S(1)}, u32[]{:S(2)}, u32[]{:S(2)}) collective-permute-start(bf16[256,256]{1,0:T(8,128)(2,1)S(1)} %get-tuple-element.84), channel_id=1, source_target_pairs={{0,12},{4,8},{8,4},{12,0},{16,28},{20,24},{24,20},{28,16},{1,13},{... | collective-permute-start | bytes 393224 | tf_op jit(solution)/shard_map/ppermute | solution.py:605
  95.6 1.3 %collective-permute-start.20 = (bf16[256,256]{1,0:T(8,128)(2,1)S(1)}, bf16[256,256]{1,0:T(8,128)(2,1)S(1)}, u32[]{:S(2)}, u32[]{:S(2)}) collective-permute-start(bf16[256,256]{1,0:T(8,128)(2,1)S(1)} %get-tuple-element.85), channel_id=1, source_target_pairs={{0,24},{4,28},{8,16},{12,20},{16,8},{20,12},{24,0},{28,4},{1,25},{... | collective-permute-start | bytes 393224 | tf_op jit(solution)/shard_map/ppermute | solution.py:605
  96.9 1.3 %collective-permute-start.21 = (bf16[256,256]{1,0:T(8,128)(2,1)S(1)}, bf16[256,256]{1,0:T(8,128)(2,1)S(1)}, u32[]{:S(2)}, u32[]{:S(2)}) collective-permute-start(bf16[256,256]{1,0:T(8,128)(2,1)S(1)} %get-tuple-element.86), channel_id=1, source_target_pairs={{0,28},{4,24},{8,20},{12,16},{16,12},{20,8},{24,4},{28,0},{1,29},{... | collective-permute-start | bytes 393224 | tf_op jit(solution)/shard_map/ppermute | solution.py:605
  98.2 1.3 %collective-permute-start.22 = (bf16[256,256]{1,0:T(8,128)(2,1)S(1)}, bf16[256,256]{1,0:T(8,128)(2,1)S(1)}, u32[]{:S(2)}, u32[]{:S(2)}) collective-permute-start(bf16[256,256]{1,0:T(8,128)(2,1)S(1)} %get-tuple-element.87), channel_id=1, source_target_pairs={{0,16},{4,20},{8,24},{12,28},{16,0},{20,4},{24,8},{28,12},{1,17},{... | collective-permute-start | bytes 393224 | tf_op jit(solution)/shard_map/ppermute | solution.py:605
  99.5 0.7 collective-permute-done.18.refs_2_
  100.2 1.7 %collective-permute-done.19.refs_3_ = bf16[256,256]{1,0:T(8,128)(2,1)S(1)} collective-permute-done((bf16[256,256]{1,0:T(8,128)(2,1)S(1)}, bf16[256,256]{1,0:T(8,128)(2,1)S(1)}, u32[]{:S(2)}, u32[]{:S(2)}) %collective-permute-start.19) | collective-permute-done | bytes 131104 | tf_op jit(solution)/shard_map/ppermute | solution.py:605
  101.9 4.7 %collective-permute-done.20.refs_4_ = bf16[256,256]{1,0:T(8,128)(2,1)S(1)} collective-permute-done((bf16[256,256]{1,0:T(8,128)(2,1)S(1)}, bf16[256,256]{1,0:T(8,128)(2,1)S(1)}, u32[]{:S(2)}, u32[]{:S(2)}) %collective-permute-start.20) | collective-permute-done | bytes 131104 | tf_op jit(solution)/shard_map/ppermute | solution.py:605
  106.6 1.7 %collective-permute-done.21.refs_5_ = bf16[256,256]{1,0:T(8,128)(2,1)S(1)} collective-permute-done((bf16[256,256]{1,0:T(8,128)(2,1)S(1)}, bf16[256,256]{1,0:T(8,128)(2,1)S(1)}, u32[]{:S(2)}, u32[]{:S(2)}) %collective-permute-start.21) | collective-permute-done | bytes 131104 | tf_op jit(solution)/shard_map/ppermute | solution.py:605
  108.3 1.7 %first.1.early_ref = bf16[1024,256]{1,0:T(8,128)(2,1)S(1)} custom-call(s32[4]{0:T(128)S(1)} %compare_select_fusion.1.meta_ref, s32[8,128]{1,0:T(8,128)S(1)} %get-tuple-element.65.code_ref, bf16[256,256]{1,0:T(8,128)(2,1)S(1)} %get-tuple-element.81.refs_0_, bf16[256,256]{1,0:T(8,128)(2,1)S(1)} %collective-permute-done.17.refs_1_, ...), custom_call_target="tpu_custom_call" | custom-call | flops 805306368 | bytes 1048576 | tf_op jit(solution)/shard_map/first/pallas_call | solution.py:532
  110.0 0.3 collective-permute-done.22.refs_0_
  110.2 1.7 %collective-permute-done.23.refs_1_ = bf16[256,256]{1,0:T(8,128)(2,1)S(1)} collective-permute-done((bf16[256,256]{1,0:T(8,128)(2,1)S(1)}, bf16[256,256]{1,0:T(8,128)(2,1)S(1)}, u32[]{:S(2)}, u32[]{:S(2)}) %collective-permute-start.23) | collective-permute-done | bytes 131104 | tf_op jit(solution)/shard_map/ppermute | solution.py:605
  111.9 2.1 %fin.1 = f32[1024,256]{1,0:T(8,128)} custom-call(s32[4]{0:T(128)S(1)} %compare_select_fusion.1.meta_ref, s32[8,128]{1,0:T(8,128)S(1)} %get-tuple-element.65.code_ref, f32[8,128]{1,0:T(8,128)S(1)} %bitcast.8, bf16[1024,256]{1,0:T(8,128)(2,1)S(1)} %get-tuple-element.80.refs_0_.layer_ref, bf16[1024,256]{1,0:T(8,128)(2,1)S(1)} %first.1.early_ref, ...), custom_call_target="tpu_custom_call" | custom-call | flops 268435456 | bytes 2097152 | tf_op jit(solution)/shard_map/fin/pallas_call | solution.py:573
  (36 shorter events, 0.3 us)
Async XLA Ops:
  0.0 0.7 copy-start.1
  4.6 5.6 %copy-start = (bf16[256,1024]{1,0:T(8,128)(2,1)S(1)}, bf16[256,1024]{1,0:T(8,128)(2,1)}, u32[]{:S(2)}) copy-start(bf16[256,1024]{1,0:T(8,128)(2,1)} %own_ref.5) | copy-start | bytes 1572868
  4.6 9.1 %copy-start.3 = (s32[32,2]{0,1:T(2,128)S(1)}, s32[32,2]{0,1:T(2,128)}, u32[]{:S(2)}) copy-start(s32[32,2]{0,1:T(2,128)} %param.12) | copy-start | bytes 772
  4.6 12.0 %collective-permute-start = (bf16[2,256,256]{2,1,0:T(8,128)(2,1)S(1)}, bf16[2,256,256]{2,1,0:T(8,128)(2,1)S(1)}, u32[]{:S(2)}, u32[]{:S(2)}) collective-permute-start(bf16[2,256,256]{2,1,0:T(8,128)(2,1)S(1)} %get-tuple-element.52.refs_2_.refs_4_.refs_1_), channel_id=1, source_target_pairs={{0,28},{4,0},{8,4},{12,8},{16,12},{20,16},{24,20},{28,24},{1,29},{... | collective-permute-start | bytes 786440 | tf_op jit(solution)/shard_map/ppermute | solution.py:602
  8.0 8.6 %collective-permute-start.1 = (bf16[2,256,256]{2,1,0:T(8,128)(2,1)S(1)}, bf16[2,256,256]{2,1,0:T(8,128)(2,1)S(1)}, u32[]{:S(2)}, u32[]{:S(2)}) collective-permute-start(bf16[2,256,256]{2,1,0:T(8,128)(2,1)S(1)} %get-tuple-element.55.refs_5_.refs_7_.refs_4_), channel_id=1, source_target_pairs={{0,4},{4,8},{8,12},{12,16},{16,20},{20,24},{24,28},{28,0},{1,5},{5... | collective-permute-start | bytes 786440 | tf_op jit(solution)/shard_map/ppermute | solution.py:602
  10.1 8.5 %collective-permute-start.2 = (bf16[2,256,256]{2,1,0:T(8,128)(2,1)S(1)}, bf16[2,256,256]{2,1,0:T(8,128)(2,1)S(1)}, u32[]{:S(2)}, u32[]{:S(2)}) collective-permute-start(bf16[2,256,256]{2,1,0:T(8,128)(2,1)S(1)} %get-tuple-element.54.refs_4_.refs_6_.refs_3_), channel_id=1, source_target_pairs={{0,4},{4,8},{8,12},{12,16},{16,20},{20,24},{24,28},{28,0},{1,5},{5... | collective-permute-start | bytes 786440 | tf_op jit(solution)/shard_map/ppermute | solution.py:602
  10.2 38.6 %collective-permute-start.4 = (bf16[256,1024]{1,0:T(8,128)(2,1)S(1)}, bf16[256,1024]{1,0:T(8,128)(2,1)S(1)}, u32[]{:S(2)}, u32[]{:S(2)}) collective-permute-start(bf16[256,1024]{1,0:T(8,128)(2,1)S(1)} %copy-done), channel_id=1, source_target_pairs={{0,1},{3,2},{4,5},{7,6},{8,9},{11,10},{12,13},{15,14},{16,17},{19,... | collective-permute-start | bytes 1572872 | tf_op jit(solution)/shard_map/ppermute | solution.py:608
  20.8 28.0 %collective-permute-start.3 = (bf16[2,256,256]{2,1,0:T(8,128)(2,1)S(1)}, bf16[2,256,256]{2,1,0:T(8,128)(2,1)S(1)}, u32[]{:S(2)}, u32[]{:S(2)}) collective-permute-start(bf16[2,256,256]{2,1,0:T(8,128)(2,1)S(1)} %att.6), channel_id=1, source_target_pairs={{0,1},{3,2},{4,5},{7,6},{8,9},{11,10},{12,13},{15,14},{16,17},{19,... | collective-permute-start | bytes 786440 | tf_op jit(solution)/shard_map/ppermute | solution.py:608
  24.3 28.0 %collective-permute-start.13 = (bf16[2,256,256]{2,1,0:T(8,128)(2,1)S(1)}, bf16[2,256,256]{2,1,0:T(8,128)(2,1)S(1)}, u32[]{:S(2)}, u32[]{:S(2)}) collective-permute-start(bf16[2,256,256]{2,1,0:T(8,128)(2,1)S(1)} %get-tuple-element.53.refs_3_.refs_5_.refs_2_), channel_id=1, source_target_pairs={{0,28},{4,0},{8,4},{12,8},{16,12},{20,16},{24,20},{28,24},{1,29},{... | collective-permute-start | bytes 786440 | tf_op jit(solution)/shard_map/ppermute | solution.py:602
  47.2 4.1 %collective-permute-start.8 = (bf16[256,256]{1,0:T(8,128)(2,1)S(1)}, bf16[256,256]{1,0:T(8,128)(2,1)S(1)}, u32[]{:S(2)}, u32[]{:S(2)}) collective-permute-start(bf16[256,256]{1,0:T(8,128)(2,1)S(1)} %get-tuple-element.58.att), channel_id=1, source_target_pairs={{0,1},{3,2},{4,5},{7,6},{8,9},{11,10},{12,13},{15,14},{16,17},{19,... | collective-permute-start | bytes 393224 | tf_op jit(solution)/shard_map/ppermute | solution.py:608
  50.1 16.9 %collective-permute-start.11 = (bf16[512,512]{1,0:T(8,128)(2,1)S(1)}, bf16[512,512]{1,0:T(8,128)(2,1)S(1)}, u32[]{:S(2)}, u32[]{:S(2)}) collective-permute-start(bf16[512,512]{1,0:T(8,128)(2,1)S(1)} %get-tuple-element.63), channel_id=1, source_target_pairs={{1,2},{2,1},{5,6},{6,5},{9,10},{10,9},{13,14},{14,13},{17,18},{18,... | collective-permute-start | bytes 1572872 | tf_op jit(solution)/shard_map/ppermute | solution.py:608
  52.3 7.3 %copy-start.4 = (s32[1024,1]{0,1:T(1,128)S(1)}, s32[1024,1]{0,1:T(1,128)}, u32[]{:S(2)}) copy-start(s32[1024,1]{0,1:T(1,128)} %param.13) | copy-start | bytes 12292
  52.3 7.3 %copy-start.5 = (s32[1024]{0:T(1024)S(1)}, s32[1024]{0:T(1024)}, u32[]{:S(2)}) copy-start(s32[1024]{0:T(1024)} %param.14) | copy-start | bytes 12292
  54.5 6.9 %collective-permute-start.14 = (bf16[256,256]{1,0:T(8,128)(2,1)S(1)}, bf16[256,256]{1,0:T(8,128)(2,1)S(1)}, u32[]{:S(2)}, u32[]{:S(2)}) collective-permute-start(bf16[256,256]{1,0:T(8,128)(2,1)S(1)} %att.7), channel_id=1, source_target_pairs={{0,1},{3,2},{4,5},{7,6},{8,9},{11,10},{12,13},{15,14},{16,17},{19,... | collective-permute-start | bytes 393224 | tf_op jit(solution)/shard_map/ppermute | solution.py:608
  58.9 10.2 %collective-permute-start.9 = (bf16[256,512]{1,0:T(8,128)(2,1)S(1)}, bf16[256,512]{1,0:T(8,128)(2,1)S(1)}, u32[]{:S(2)}, u32[]{:S(2)}) collective-permute-start(bf16[256,512]{1,0:T(8,128)(2,1)S(1)} %get-tuple-element.68), channel_id=1, source_target_pairs={{1,2},{2,1},{5,6},{6,5},{9,10},{10,9},{13,14},{14,13},{17,18},{18,... | collective-permute-start | bytes 786440 | tf_op jit(solution)/shard_map/ppermute | solution.py:608
  60.3 2.8 %collective-permute-start.5 = (s32[8,256]{1,0:T(8,128)S(1)}, s32[8,256]{1,0:T(8,128)S(1)}, u32[]{:S(2)}, u32[]{:S(2)}) collective-permute-start(s32[8,256]{1,0:T(8,128)S(1)} %get-tuple-element.66), channel_id=1, source_target_pairs={{0,4},{4,0},{8,12},{12,8},{16,20},{20,16},{24,28},{28,24},{1,5},{5... | collective-permute-start | bytes 24584 | tf_op jit(solution)/shard_map/ppermute | solution.py:605
  62.4 8.7 %collective-permute-start.15 = (bf16[256,512]{1,0:T(8,128)(2,1)S(1)}, bf16[256,512]{1,0:T(8,128)(2,1)S(1)}, u32[]{:S(2)}, u32[]{:S(2)}) collective-permute-start(bf16[256,512]{1,0:T(8,128)(2,1)S(1)} %get-tuple-element.77), channel_id=1, source_target_pairs={{1,2},{2,1},{5,6},{6,5},{9,10},{10,9},{13,14},{14,13},{17,18},{18,... | collective-permute-start | bytes 786440 | tf_op jit(solution)/shard_map/ppermute | solution.py:608
  63.1 5.9 %collective-permute-start.6 = (s32[16,256]{1,0:T(8,128)S(1)}, s32[16,256]{1,0:T(8,128)S(1)}, u32[]{:S(2)}, u32[]{:S(2)}) collective-permute-start(s32[16,256]{1,0:T(8,128)S(1)} %pad_add_fusion.1), channel_id=1, source_target_pairs={{0,8},{4,12},{8,0},{12,4},{16,24},{20,28},{24,16},{28,20},{1,9},{5... | collective-permute-start | bytes 49160 | tf_op jit(solution)/shard_map/ppermute | solution.py:605
  67.7 22.9 %collective-permute-start.12 = (bf16[512,256]{1,0:T(8,128)(2,1)S(1)}, bf16[512,256]{1,0:T(8,128)(2,1)S(1)}, u32[]{:S(2)}, u32[]{:S(2)}) collective-permute-start(bf16[512,256]{1,0:T(8,128)(2,1)S(1)} %get-tuple-element.73), channel_id=1, source_target_pairs={{1,0},{2,3},{5,4},{6,7},{9,8},{10,11},{13,12},{14,15},{17,16},{18,... | collective-permute-start | bytes 786440 | tf_op jit(solution)/shard_map/ppermute | solution.py:608
  69.0 4.0 %collective-permute-start.7 = (s32[32,256]{1,0:T(8,128)S(1)}, s32[32,256]{1,0:T(8,128)S(1)}, u32[]{:S(2)}, u32[]{:S(2)}) collective-permute-start(s32[32,256]{1,0:T(8,128)S(1)} %pad_add_fusion), channel_id=1, source_target_pairs={{0,16},{4,20},{8,24},{12,28},{16,0},{20,4},{24,8},{28,12},{1,17},{... | collective-permute-start | bytes 98312 | tf_op jit(solution)/shard_map/ppermute | solution.py:605
  69.7 19.5 %collective-permute-start.10 = (bf16[256,256]{1,0:T(8,128)(2,1)S(1)}, bf16[256,256]{1,0:T(8,128)(2,1)S(1)}, u32[]{:S(2)}, u32[]{:S(2)}) collective-permute-start(bf16[256,256]{1,0:T(8,128)(2,1)S(1)} %get-tuple-element.70), channel_id=1, source_target_pairs={{1,0},{2,3},{5,4},{6,7},{9,8},{10,11},{13,12},{14,15},{17,16},{18,... | collective-permute-start | bytes 393224 | tf_op jit(solution)/shard_map/ppermute | solution.py:608
  71.6 19.0 %collective-permute-start.16 = (bf16[256,256]{1,0:T(8,128)(2,1)S(1)}, bf16[256,256]{1,0:T(8,128)(2,1)S(1)}, u32[]{:S(2)}, u32[]{:S(2)}) collective-permute-start(bf16[256,256]{1,0:T(8,128)(2,1)S(1)} %get-tuple-element.79), channel_id=1, source_target_pairs={{1,0},{2,3},{5,4},{6,7},{9,8},{10,11},{13,12},{14,15},{17,16},{18,... | collective-permute-start | bytes 393224 | tf_op jit(solution)/shard_map/ppermute | solution.py:608
  93.7 18.3 %copy-start.2 = (f32[1024]{0:T(1024)S(1)}, f32[1024]{0:T(1024)}, u32[]{:S(2)}) copy-start(f32[1024]{0:T(1024)} %param.15) | copy-start | bytes 12292
  93.7 4.5 %collective-permute-start.17 = (bf16[256,256]{1,0:T(8,128)(2,1)S(1)}, bf16[256,256]{1,0:T(8,128)(2,1)S(1)}, u32[]{:S(2)}, u32[]{:S(2)}) collective-permute-start(bf16[256,256]{1,0:T(8,128)(2,1)S(1)} %get-tuple-element.82), channel_id=1, source_target_pairs={{0,4},{4,0},{8,12},{12,8},{16,20},{20,16},{24,28},{28,24},{1,5},{5... | collective-permute-start | bytes 393224 | tf_op jit(solution)/shard_map/ppermute | solution.py:605
  93.8 6.4 %collective-permute-start.18 = (bf16[256,256]{1,0:T(8,128)(2,1)S(1)}, bf16[256,256]{1,0:T(8,128)(2,1)S(1)}, u32[]{:S(2)}, u32[]{:S(2)}) collective-permute-start(bf16[256,256]{1,0:T(8,128)(2,1)S(1)} %get-tuple-element.83), channel_id=1, source_target_pairs={{0,8},{4,12},{8,0},{12,4},{16,24},{20,28},{24,16},{28,20},{1,9},{5... | collective-permute-start | bytes 393224 | tf_op jit(solution)/shard_map/ppermute | solution.py:605
  93.9 8.1 %collective-permute-start.19 = (bf16[256,256]{1,0:T(8,128)(2,1)S(1)}, bf16[256,256]{1,0:T(8,128)(2,1)S(1)}, u32[]{:S(2)}, u32[]{:S(2)}) collective-permute-start(bf16[256,256]{1,0:T(8,128)(2,1)S(1)} %get-tuple-element.84), channel_id=1, source_target_pairs={{0,12},{4,8},{8,4},{12,0},{16,28},{20,24},{24,20},{28,16},{1,13},{... | collective-permute-start | bytes 393224 | tf_op jit(solution)/shard_map/ppermute | solution.py:605
  95.6 11.0 %collective-permute-start.20 = (bf16[256,256]{1,0:T(8,128)(2,1)S(1)}, bf16[256,256]{1,0:T(8,128)(2,1)S(1)}, u32[]{:S(2)}, u32[]{:S(2)}) collective-permute-start(bf16[256,256]{1,0:T(8,128)(2,1)S(1)} %get-tuple-element.85), channel_id=1, source_target_pairs={{0,24},{4,28},{8,16},{12,20},{16,8},{20,12},{24,0},{28,4},{1,25},{... | collective-permute-start | bytes 393224 | tf_op jit(solution)/shard_map/ppermute | solution.py:605
  96.9 11.3 %collective-permute-start.21 = (bf16[256,256]{1,0:T(8,128)(2,1)S(1)}, bf16[256,256]{1,0:T(8,128)(2,1)S(1)}, u32[]{:S(2)}, u32[]{:S(2)}) collective-permute-start(bf16[256,256]{1,0:T(8,128)(2,1)S(1)} %get-tuple-element.86), channel_id=1, source_target_pairs={{0,28},{4,24},{8,20},{12,16},{16,12},{20,8},{24,4},{28,0},{1,29},{... | collective-permute-start | bytes 393224 | tf_op jit(solution)/shard_map/ppermute | solution.py:605
  98.2 12.0 %collective-permute-start.22 = (bf16[256,256]{1,0:T(8,128)(2,1)S(1)}, bf16[256,256]{1,0:T(8,128)(2,1)S(1)}, u32[]{:S(2)}, u32[]{:S(2)}) collective-permute-start(bf16[256,256]{1,0:T(8,128)(2,1)S(1)} %get-tuple-element.87), channel_id=1, source_target_pairs={{0,16},{4,20},{8,24},{12,28},{16,0},{20,4},{24,8},{28,12},{1,17},{... | collective-permute-start | bytes 393224 | tf_op jit(solution)/shard_map/ppermute | solution.py:605
  100.2 11.7 %collective-permute-start.23 = (bf16[256,256]{1,0:T(8,128)(2,1)S(1)}, bf16[256,256]{1,0:T(8,128)(2,1)S(1)}, u32[]{:S(2)}, u32[]{:S(2)}) collective-permute-start(bf16[256,256]{1,0:T(8,128)(2,1)S(1)} %get-tuple-element.88), channel_id=1, source_target_pairs={{0,20},{4,16},{8,28},{12,24},{16,4},{20,0},{24,12},{28,8},{1,21},{... | collective-permute-start | bytes 393224 | tf_op jit(solution)/shard_map/ppermute | solution.py:605

commit v11 on v10

--- a/solution.py
+++ b/solution.py
@@ -698,7 +698,7 @@
     reply(first_masks, outgoing)
     *outgoing, own_rows = gather_rows(meta, wanted, layer, last_masks + [0], tokens)
     reply(last_masks, outgoing)
-    late = [m for m in first_masks if m < 3 * peers // 4]
+    late = late_masks(peers)
     early = first_replies(
         meta, code, {0: own_rows, **{m: r for m, r in replies.items() if m not in late}}, tokens
     )
@@ -719,6 +719,13 @@
     far_half = far_half[len(far_half) // 2 :] + far_half[: len(far_half) // 2]
     pairs = zip(far_half[: len(far_half) // 2], far_half[len(far_half) // 2 :])
     return [m for pair in pairs for m in pair], list(range(2, peers // 2)) + [1]
+
+
+def late_masks(peers):
+    first_masks, last_masks = reply_order(peers)
+    straight = [m for m in first_masks if m < 3 * peers // 4]
+    beside = [m for m in last_masks if m > 1]
+    return straight[len(straight) // 2 :] + beside[len(beside) // 2 :]
 
 
 def solution(mesh):

time: 115 us -> 111 us (0.965)
  waiting for transfers between devices: 30 us -> 26.6 us
    ppermute x10, waiting for transfers between devices: 10.8 us -> 7.35 us  [partner(): return lax.ppermute(x, VIEWS, [(i, i ^ mask) for i in range(peers)])]
  transfers between devices with their start and end apart: 24 -> 24, of which waited for: 11 -> 10; matrix products, arithmetic and copies ran while one was open for 0% -> 0% of each run, Pallas kernels for 16% -> 17%
where the time goes in v11:
time: 111 us
  starting transfers between devices  55.5 us (50%)
  Pallas kernels  27.7 us (25%)
  waiting for transfers between devices  26.6 us (24%)
    ppermute x4, starting transfers between devices, along(): return lax.ppermute(x, VIEWS, [(i, (i + by) % peers) for i in range(peers)])  26.4 us
    ppermute x10, waiting for transfers between devices, across(): return lax.ppermute(x, HEADS, pairs)  19.1 us
    ppermute x10, starting transfers between devices, across(): return lax.ppermute(x, HEADS, pairs)  19 us
    ppermute x10, starting transfers between devices, partner(): return lax.ppermute(x, VIEWS, [(i, i ^ mask) for i in range(peers)])  10.1 us
    pallas_call x4, Pallas kernels, attend(): pl.pallas_call(body, in_specs=[SMEM_SPEC, SMEM_SPEC] + many(VMEM_SPEC, he...  9.03 us
    ppermute x10, waiting for transfers between devices, partner(): return lax.ppermute(x, VIEWS, [(i, i ^ mask) for i in range(peers)])  7.35 us
    pallas_call x2, Pallas kernels, project_views(): pl.pallas_call(body, in_specs=[SMEM_SPEC, big, VMEM_SPEC, big], out_specs...  5.97 us
    pallas_call x3, Pallas kernels, partial_out(): pl.pallas_call(body, in_specs=[SMEM_SPEC] + many(VMEM_SPEC, 4 + len(base)...  3.26 us
  transfers between devices with their start and end apart: 24, of which 10 were waited for; matrix products, arithmetic and copies ran while one was open for 0% of the time, Pallas kernels for 17%

profile of v11, /device:TPU:0, one launch (start us, length us, event | category | flops | bytes accessed | tf_op | source)
XLA Modules:
  0.0 111.0 jit_solution(10671432970418561392)
XLA Ops:
  0.0 0.7 copy-done.1
  0.7 3.9 %proj.2 = (bf16[256,256]{1,0:T(8,128)(2,1)S(1)}, bf16[2,256,256]{2,1,0:T(8,128)(2,1)S(1)}, bf16[256,256]{1,0:T(8,128)(2,1)S(1)}, bf16[2,256,256]{2,1,0:T(8,128)(...) custom-call(s32[4]{0:T(128)S(1)} %compare_select_fusion.1.meta_ref, ...), custom_call_target="tpu_custom_call" | custom-call | flops 805306368 | bytes 3407872 | tf_op jit(solution)/shard_map/proj/pallas_call | solution.py:120
  4.6 3.4 %collective-permute-start = (bf16[2,256,256]{2,1,0:T(8,128)(2,1)S(1)}, bf16[2,256,256]{2,1,0:T(8,128)(2,1)S(1)}, u32[]{:S(2)}, u32[]{:S(2)}) collective-permute-start(bf16[2,256,256]{2,1,0:T(8,128)(2,1)S(1)} %get-tuple-element.52.refs_2_.refs_4_.refs_1_), channel_id=1, source_target_pairs={{0,28},{4,0},{8,4},{12,8},{16,12},{20,16},{24,20},{28,24},{1,29},{... | collective-permute-start | bytes 786440 | tf_op jit(solution)/shard_map/ppermute | solution.py:602
  8.1 2.1 %proj.3 = (bf16[256,256]{1,0:T(8,128)(2,1)S(1)}, bf16[2,256,256]{2,1,0:T(8,128)(2,1)S(1)}, bf16[256,256]{1,0:T(8,128)(2,1)S(1)}, bf16[2,256,256]{2,1,0:T(8,128)(2,1)S(1)}, bf16[2,256,512]{2,1,0:T(8,128)(2,1)S(1)}) custom-call(s32[4]{0:T(128)S(1)} %compare_select_fusion.1.meta_ref, bf16[2,256,1024]{2,1,0:T(8,128)(2,1)S(1)} %get-tuple-element.48.lat_ref, ...), custom_call_target="tpu_custom_call" | custom-call | flops 805306368 | bytes 3407872 | tf_op jit(solution)/shard_map/proj/pallas_call | solution.py:120
  10.2 3.5 %collective-permute-start.4 = (bf16[256,1024]{1,0:T(8,128)(2,1)S(1)}, bf16[256,1024]{1,0:T(8,128)(2,1)S(1)}, u32[]{:S(2)}, u32[]{:S(2)}) collective-permute-start(bf16[256,1024]{1,0:T(8,128)(2,1)S(1)} %copy-done), channel_id=1, source_target_pairs={{0,1},{3,2},{4,5},{7,6},{8,9},{11,10},{12,13},{15,14},{16,17},{19,... | collective-permute-start | bytes 1572872 | tf_op jit(solution)/shard_map/ppermute | solution.py:608
  13.7 2.9 %att.4 = (f32[2,320,256]{2,1,0:T(8,128)S(1)}, f32[2,4,256]{2,1,0:T(4,128)S(1)}) custom-call(s32[4]{0:T(128)S(1)} %compare_select_fusion.1.meta_ref, s32[2,32]{1,0:T(2,128)S(1)} %bitcast.9, bf16[256,256]{1,0:T(8,128)(2,1)S(1)} %get-tuple-element.50.refs_0_.refs_2_, bf16[256,256]{1,0:T(8,128)(2,1)S(1)} %get-tuple-element.51.refs_1_.refs_3_, ...), custom_call_target="tpu_custom_call" | custom-call | flops 1073741824 | bytes 4194304 | tf_op jit(solution)/shard_map/att/pallas_call | solution.py:288
  16.7 1.7 %att.5 = (bf16[256,256]{1,0:T(8,128)(2,1)S(1)}, bf16[256,256]{1,0:T(8,128)(2,1)S(1)}) custom-call(s32[4]{0:T(128)S(1)} %compare_select_fusion.1.meta_ref, s32[2,32]{1,0:T(2,128)S(1)} %bitcast.10, f32[2,320,256]{2,1,0:T(8,128)S(1)} %get-tuple-element.56.refs_0_, f32[2,4,256]{2,1,0:T(4,128)S(1)} %get-tuple-element.57.refs_1_, ...), custom_call_target="tpu_custom_call" | custom-call | flops 268435456 | bytes 1048576 | tf_op jit(solution)/shard_map/att/pallas_call | solution.py:288
  18.4 0.2 collective-permute-done.2.refs_6_
  18.6 2.2 %att.6 = bf16[2,256,256]{2,1,0:T(8,128)(2,1)S(1)} custom-call(s32[4]{0:T(128)S(1)} %compare_select_fusion.1.meta_ref, s32[2,32]{1,0:T(2,128)S(1)} %bitcast.11, bf16[256,256]{1,0:T(8,128)(2,1)S(1)} %get-tuple-element.59.refs_0_, bf16[2,256,256]{2,1,0:T(8,128)(2,1)S(1)} %get-tuple-element.52.refs_2_.refs_4_.refs_1_, ...), custom_call_target="tpu_custom_call" | custom-call | flops 671088640 | bytes 2621440 | tf_op jit(solution)/shard_map/att/pallas_call | solution.py:288
  20.8 3.5 %collective-permute-start.3 = (bf16[2,256,256]{2,1,0:T(8,128)(2,1)S(1)}, bf16[2,256,256]{2,1,0:T(8,128)(2,1)S(1)}, u32[]{:S(2)}, u32[]{:S(2)}) collective-permute-start(bf16[2,256,256]{2,1,0:T(8,128)(2,1)S(1)} %att.6), channel_id=1, source_target_pairs={{0,1},{3,2},{4,5},{7,6},{8,9},{11,10},{12,13},{15,14},{16,17},{19,... | collective-permute-start | bytes 786440 | tf_op jit(solution)/shard_map/ppermute | solution.py:608
  24.3 22.9 %collective-permute-start.13 = (bf16[2,256,256]{2,1,0:T(8,128)(2,1)S(1)}, bf16[2,256,256]{2,1,0:T(8,128)(2,1)S(1)}, u32[]{:S(2)}, u32[]{:S(2)}) collective-permute-start(bf16[2,256,256]{2,1,0:T(8,128)(2,1)S(1)} %get-tuple-element.53.refs_3_.refs_5_.refs_2_), channel_id=1, source_target_pairs={{0,28},{4,0},{8,4},{12,8},{16,12},{20,16},{24,20},{28,24},{1,29},{... | collective-permute-start | bytes 786440 | tf_op jit(solution)/shard_map/ppermute | solution.py:602
  47.2 1.6 %collective-permute-start.8 = (bf16[256,256]{1,0:T(8,128)(2,1)S(1)}, bf16[256,256]{1,0:T(8,128)(2,1)S(1)}, u32[]{:S(2)}, u32[]{:S(2)}) collective-permute-start(bf16[256,256]{1,0:T(8,128)(2,1)S(1)} %get-tuple-element.58.att), channel_id=1, source_target_pairs={{0,1},{3,2},{4,5},{7,6},{8,9},{11,10},{12,13},{15,14},{16,17},{19,... | collective-permute-start | bytes 393224 | tf_op jit(solution)/shard_map/ppermute | solution.py:608
  48.8 1.3 %part.3 = (f32[512,512]{1,0:T(8,128)S(1)}, bf16[512,512]{1,0:T(8,128)(2,1)S(1)}) custom-call(s32[4]{0:T(128)S(1)} %compare_select_fusion.1.meta_ref, bf16[2,256,256]{2,1,0:T(8,128)(2,1)S(1)} %att.6, bf16[2,256,256]{2,1,0:T(8,128)(2,1)S(1)} %collective-permute-done.3.near_ref, bf16[256,1024]{1,0:T(8,128)(2,1)S(1)} %copy-done, ...), custom_call_target="tpu_custom_call" | custom-call | flops 536870912 | bytes 4194304 | tf_op jit(solution)/shard_map/part/pallas_call | solution.py:360
  50.1 0.9 collective-permute-start.11
  51.0 0.3 collective-permute-done.8.near_ref
  51.3 1.0 part.4
  52.3 2.2 %att.7 = bf16[256,256]{1,0:T(8,128)(2,1)S(1)} custom-call(s32[4]{0:T(128)S(1)} %compare_select_fusion.1.meta_ref, s32[2,32]{1,0:T(2,128)S(1)} %bitcast.12, bf16[256,256]{1,0:T(8,128)(2,1)S(1)} %get-tuple-element.75.refs_0_, bf16[2,256,256]{2,1,0:T(8,128)(2,1)S(1)} %get-tuple-element.52.refs_2_.refs_4_.refs_1_, ...), custom_call_target="tpu_custom_call" | custom-call | flops 671088640 | bytes 2621440 | tf_op jit(solution)/shard_map/att/pallas_call | solution.py:288
  54.5 4.4 %collective-permute-start.14 = (bf16[256,256]{1,0:T(8,128)(2,1)S(1)}, bf16[256,256]{1,0:T(8,128)(2,1)S(1)}, u32[]{:S(2)}, u32[]{:S(2)}) collective-permute-start(bf16[256,256]{1,0:T(8,128)(2,1)S(1)} %att.7), channel_id=1, source_target_pairs={{0,1},{3,2},{4,5},{7,6},{8,9},{11,10},{12,13},{15,14},{16,17},{19,... | collective-permute-start | bytes 393224 | tf_op jit(solution)/shard_map/ppermute | solution.py:608
  58.9 0.7 collective-permute-start.9
  59.6 0.7 prep.1
  60.3 1.1 collective-permute-done.14.near_ref
  61.4 1.0 part.5
  62.4 0.7 collective-permute-start.15
  63.1 3.9 %collective-permute-start.6 = (s32[16,256]{1,0:T(8,128)S(1)}, s32[16,256]{1,0:T(8,128)S(1)}, u32[]{:S(2)}, u32[]{:S(2)}) collective-permute-start(s32[16,256]{1,0:T(8,128)S(1)} %pad_add_fusion.1), channel_id=1, source_target_pairs={{0,8},{4,12},{8,0},{12,4},{16,24},{20,28},{24,16},{28,20},{1,9},{5... | collective-permute-start | bytes 49160 | tf_op jit(solution)/shard_map/ppermute | solution.py:605
  67.0 0.7 merge.4
  67.7 1.3 %collective-permute-start.12 = (bf16[512,256]{1,0:T(8,128)(2,1)S(1)}, bf16[512,256]{1,0:T(8,128)(2,1)S(1)}, u32[]{:S(2)}, u32[]{:S(2)}) collective-permute-start(bf16[512,256]{1,0:T(8,128)(2,1)S(1)} %get-tuple-element.73), channel_id=1, source_target_pairs={{1,0},{2,3},{5,4},{6,7},{9,8},{10,11},{13,12},{14,15},{17,16},{18,... | collective-permute-start | bytes 786440 | tf_op jit(solution)/shard_map/ppermute | solution.py:608
  69.0 0.1 collective-permute-start.7
  69.1 0.6 merge.3
  69.7 1.3 %collective-permute-start.10 = (bf16[256,256]{1,0:T(8,128)(2,1)S(1)}, bf16[256,256]{1,0:T(8,128)(2,1)S(1)}, u32[]{:S(2)}, u32[]{:S(2)}) collective-permute-start(bf16[256,256]{1,0:T(8,128)(2,1)S(1)} %get-tuple-element.70), channel_id=1, source_target_pairs={{1,0},{2,3},{5,4},{6,7},{9,8},{10,11},{13,12},{14,15},{17,16},{18,... | collective-permute-start | bytes 393224 | tf_op jit(solution)/shard_map/ppermute | solution.py:608
  71.0 0.6 merge.5
  71.6 1.3 %collective-permute-start.16 = (bf16[256,256]{1,0:T(8,128)(2,1)S(1)}, bf16[256,256]{1,0:T(8,128)(2,1)S(1)}, u32[]{:S(2)}, u32[]{:S(2)}) collective-permute-start(bf16[256,256]{1,0:T(8,128)(2,1)S(1)} %get-tuple-element.79), channel_id=1, source_target_pairs={{1,0},{2,3},{5,4},{6,7},{9,8},{10,11},{13,12},{14,15},{17,16},{18,... | collective-permute-start | bytes 393224 | tf_op jit(solution)/shard_map/ppermute | solution.py:608
  73.0 16.2 %collective-permute-done.10.refs_1_ = bf16[256,256]{1,0:T(8,128)(2,1)S(1)} collective-permute-done((bf16[256,256]{1,0:T(8,128)(2,1)S(1)}, bf16[256,256]{1,0:T(8,128)(2,1)S(1)}, u32[]{:S(2)}, u32[]{:S(2)}) %collective-permute-start.10) | collective-permute-done | bytes 131104 | tf_op jit(solution)/shard_map/ppermute | solution.py:608
  89.2 1.4 %collective-permute-done.16.refs_5_ = bf16[256,256]{1,0:T(8,128)(2,1)S(1)} collective-permute-done((bf16[256,256]{1,0:T(8,128)(2,1)S(1)}, bf16[256,256]{1,0:T(8,128)(2,1)S(1)}, u32[]{:S(2)}, u32[]{:S(2)}) %collective-permute-start.16) | collective-permute-done | bytes 131104 | tf_op jit(solution)/shard_map/ppermute | solution.py:608
  90.6 1.5 %gath.2 = (bf16[1024,256]{1,0:T(8,128)(2,1)S(1)}, bf16[256,256]{1,0:T(8,128)(2,1)S(1)}, bf16[256,256]{1,0:T(8,128)(2,1)S(1)}, bf16[256,256]{1,0:T(8,128)(2,1)S(1)}, bf16[256,256]{1,0:T(8,128)(2,1)S(1)}) custom-call(s32[4]{0:T(128)S(1)} %compare_select_fusion.1.meta_ref, s32[64,256]{1,0:T(8,128)S(1)} %constant_dynamic-update-slice_fusion.wanted_ref, ...), custom_call_target="tpu_custom_call" | custom-call | flops 536870912 | bytes 2097152 | tf_op jit(solution)/shard_map/gath/pallas_call | solution.py:482
  92.2 1.5 %gath.3 = (bf16[256,256]{1,0:T(8,128)(2,1)S(1)}, bf16[256,256]{1,0:T(8,128)(2,1)S(1)}, bf16[256,256]{1,0:T(8,128)(2,1)S(1)}, bf16[256,256]{1,0:T(8,128)(2,1)S(1)}) custom-call(s32[4]{0:T(128)S(1)} %compare_select_fusion.1.meta_ref, s32[64,256]{1,0:T(8,128)S(1)} %constant_dynamic-update-slice_fusion.wanted_ref, ...), custom_call_target="tpu_custom_call" | custom-call | flops 536870912 | bytes 2097152 | tf_op jit(solution)/shard_map/gath/pallas_call | solution.py:482
  93.7 0.1 collective-permute-start.17
  93.8 0.1 collective-permute-start.18
  93.9 1.9 %collective-permute-start.19 = (bf16[256,256]{1,0:T(8,128)(2,1)S(1)}, bf16[256,256]{1,0:T(8,128)(2,1)S(1)}, u32[]{:S(2)}, u32[]{:S(2)}) collective-permute-start(bf16[256,256]{1,0:T(8,128)(2,1)S(1)} %get-tuple-element.84), channel_id=1, source_target_pairs={{0,16},{4,20},{8,24},{12,28},{16,0},{20,4},{24,8},{28,12},{1,17},{... | collective-permute-start | bytes 393224 | tf_op jit(solution)/shard_map/ppermute | solution.py:605
  95.7 1.6 %collective-permute-start.20 = (bf16[256,256]{1,0:T(8,128)(2,1)S(1)}, bf16[256,256]{1,0:T(8,128)(2,1)S(1)}, u32[]{:S(2)}, u32[]{:S(2)}) collective-permute-start(bf16[256,256]{1,0:T(8,128)(2,1)S(1)} %get-tuple-element.85), channel_id=1, source_target_pairs={{0,24},{4,28},{8,16},{12,20},{16,8},{20,12},{24,0},{28,4},{1,25},{... | collective-permute-start | bytes 393224 | tf_op jit(solution)/shard_map/ppermute | solution.py:605
  97.3 0.5 collective-permute-start.21
  97.8 1.9 %collective-permute-start.22 = (bf16[256,256]{1,0:T(8,128)(2,1)S(1)}, bf16[256,256]{1,0:T(8,128)(2,1)S(1)}, u32[]{:S(2)}, u32[]{:S(2)}) collective-permute-start(bf16[256,256]{1,0:T(8,128)(2,1)S(1)} %get-tuple-element.87), channel_id=1, source_target_pairs={{0,12},{4,8},{8,4},{12,0},{16,28},{20,24},{24,20},{28,16},{1,13},{... | collective-permute-start | bytes 393224 | tf_op jit(solution)/shard_map/ppermute | solution.py:605
  99.8 0.4 collective-permute-done.18.refs_2_
  100.2 3.6 %collective-permute-done.20.refs_4_ = bf16[256,256]{1,0:T(8,128)(2,1)S(1)} collective-permute-done((bf16[256,256]{1,0:T(8,128)(2,1)S(1)}, bf16[256,256]{1,0:T(8,128)(2,1)S(1)}, u32[]{:S(2)}, u32[]{:S(2)}) %collective-permute-start.20) | collective-permute-done | bytes 131104 | tf_op jit(solution)/shard_map/ppermute | solution.py:605
  103.8 1.7 %collective-permute-done.21.refs_5_ = bf16[256,256]{1,0:T(8,128)(2,1)S(1)} collective-permute-done((bf16[256,256]{1,0:T(8,128)(2,1)S(1)}, bf16[256,256]{1,0:T(8,128)(2,1)S(1)}, u32[]{:S(2)}, u32[]{:S(2)}) %collective-permute-start.21) | collective-permute-done | bytes 131104 | tf_op jit(solution)/shard_map/ppermute | solution.py:605
  105.5 1.7 %first.1.early_ref = bf16[1024,256]{1,0:T(8,128)(2,1)S(1)} custom-call(s32[4]{0:T(128)S(1)} %compare_select_fusion.1.meta_ref, s32[8,128]{1,0:T(8,128)S(1)} %get-tuple-element.65.code_ref, bf16[256,256]{1,0:T(8,128)(2,1)S(1)} %get-tuple-element.81.refs_0_, bf16[256,256]{1,0:T(8,128)(2,1)S(1)} %collective-permute-done.17.refs_1_, ...), custom_call_target="tpu_custom_call" | custom-call | flops 805306368 | bytes 1048576 | tf_op jit(solution)/shard_map/first/pallas_call | solution.py:532
  107.1 0.5 collective-permute-done.22.refs_0_
  107.6 1.2 %collective-permute-done.23.refs_1_ = bf16[256,256]{1,0:T(8,128)(2,1)S(1)} collective-permute-done((bf16[256,256]{1,0:T(8,128)(2,1)S(1)}, bf16[256,256]{1,0:T(8,128)(2,1)S(1)}, u32[]{:S(2)}, u32[]{:S(2)}) %collective-permute-start.23) | collective-permute-done | bytes 131104 | tf_op jit(solution)/shard_map/ppermute | solution.py:605
  108.8 2.1 %fin.1 = f32[1024,256]{1,0:T(8,128)} custom-call(s32[4]{0:T(128)S(1)} %compare_select_fusion.1.meta_ref, s32[8,128]{1,0:T(8,128)S(1)} %get-tuple-element.65.code_ref, f32[8,128]{1,0:T(8,128)S(1)} %bitcast.8, bf16[1024,256]{1,0:T(8,128)(2,1)S(1)} %get-tuple-element.80.refs_0_.layer_ref, bf16[1024,256]{1,0:T(8,128)(2,1)S(1)} %first.1.early_ref, ...), custom_call_target="tpu_custom_call" | custom-call | flops 268435456 | bytes 2097152 | tf_op jit(solution)/shard_map/fin/pallas_call | solution.py:573
  (36 shorter events, 0.2 us)
Async XLA Ops:
  0.0 0.7 copy-start.1
  4.6 5.6 %copy-start = (bf16[256,1024]{1,0:T(8,128)(2,1)S(1)}, bf16[256,1024]{1,0:T(8,128)(2,1)}, u32[]{:S(2)}) copy-start(bf16[256,1024]{1,0:T(8,128)(2,1)} %own_ref.5) | copy-start | bytes 1572868
  4.6 9.1 %copy-start.3 = (s32[32,2]{0,1:T(2,128)S(1)}, s32[32,2]{0,1:T(2,128)}, u32[]{:S(2)}) copy-start(s32[32,2]{0,1:T(2,128)} %param.12) | copy-start | bytes 772
  4.6 12.0 %collective-permute-start = (bf16[2,256,256]{2,1,0:T(8,128)(2,1)S(1)}, bf16[2,256,256]{2,1,0:T(8,128)(2,1)S(1)}, u32[]{:S(2)}, u32[]{:S(2)}) collective-permute-start(bf16[2,256,256]{2,1,0:T(8,128)(2,1)S(1)} %get-tuple-element.52.refs_2_.refs_4_.refs_1_), channel_id=1, source_target_pairs={{0,28},{4,0},{8,4},{12,8},{16,12},{20,16},{24,20},{28,24},{1,29},{... | collective-permute-start | bytes 786440 | tf_op jit(solution)/shard_map/ppermute | solution.py:602
  8.0 8.6 %collective-permute-start.1 = (bf16[2,256,256]{2,1,0:T(8,128)(2,1)S(1)}, bf16[2,256,256]{2,1,0:T(8,128)(2,1)S(1)}, u32[]{:S(2)}, u32[]{:S(2)}) collective-permute-start(bf16[2,256,256]{2,1,0:T(8,128)(2,1)S(1)} %get-tuple-element.55.refs_5_.refs_7_.refs_4_), channel_id=1, source_target_pairs={{0,4},{4,8},{8,12},{12,16},{16,20},{20,24},{24,28},{28,0},{1,5},{5... | collective-permute-start | bytes 786440 | tf_op jit(solution)/shard_map/ppermute | solution.py:602
  10.1 8.5 %collective-permute-start.2 = (bf16[2,256,256]{2,1,0:T(8,128)(2,1)S(1)}, bf16[2,256,256]{2,1,0:T(8,128)(2,1)S(1)}, u32[]{:S(2)}, u32[]{:S(2)}) collective-permute-start(bf16[2,256,256]{2,1,0:T(8,128)(2,1)S(1)} %get-tuple-element.54.refs_4_.refs_6_.refs_3_), channel_id=1, source_target_pairs={{0,4},{4,8},{8,12},{12,16},{16,20},{20,24},{24,28},{28,0},{1,5},{5... | collective-permute-start | bytes 786440 | tf_op jit(solution)/shard_map/ppermute | solution.py:602
  10.2 38.6 %collective-permute-start.4 = (bf16[256,1024]{1,0:T(8,128)(2,1)S(1)}, bf16[256,1024]{1,0:T(8,128)(2,1)S(1)}, u32[]{:S(2)}, u32[]{:S(2)}) collective-permute-start(bf16[256,1024]{1,0:T(8,128)(2,1)S(1)} %copy-done), channel_id=1, source_target_pairs={{0,1},{3,2},{4,5},{7,6},{8,9},{11,10},{12,13},{15,14},{16,17},{19,... | collective-permute-start | bytes 1572872 | tf_op jit(solution)/shard_map/ppermute | solution.py:608
  20.8 28.0 %collective-permute-start.3 = (bf16[2,256,256]{2,1,0:T(8,128)(2,1)S(1)}, bf16[2,256,256]{2,1,0:T(8,128)(2,1)S(1)}, u32[]{:S(2)}, u32[]{:S(2)}) collective-permute-start(bf16[2,256,256]{2,1,0:T(8,128)(2,1)S(1)} %att.6), channel_id=1, source_target_pairs={{0,1},{3,2},{4,5},{7,6},{8,9},{11,10},{12,13},{15,14},{16,17},{19,... | collective-permute-start | bytes 786440 | tf_op jit(solution)/shard_map/ppermute | solution.py:608
  24.3 28.0 %collective-permute-start.13 = (bf16[2,256,256]{2,1,0:T(8,128)(2,1)S(1)}, bf16[2,256,256]{2,1,0:T(8,128)(2,1)S(1)}, u32[]{:S(2)}, u32[]{:S(2)}) collective-permute-start(bf16[2,256,256]{2,1,0:T(8,128)(2,1)S(1)} %get-tuple-element.53.refs_3_.refs_5_.refs_2_), channel_id=1, source_target_pairs={{0,28},{4,0},{8,4},{12,8},{16,12},{20,16},{24,20},{28,24},{1,29},{... | collective-permute-start | bytes 786440 | tf_op jit(solution)/shard_map/ppermute | solution.py:602
  47.2 4.1 %collective-permute-start.8 = (bf16[256,256]{1,0:T(8,128)(2,1)S(1)}, bf16[256,256]{1,0:T(8,128)(2,1)S(1)}, u32[]{:S(2)}, u32[]{:S(2)}) collective-permute-start(bf16[256,256]{1,0:T(8,128)(2,1)S(1)} %get-tuple-element.58.att), channel_id=1, source_target_pairs={{0,1},{3,2},{4,5},{7,6},{8,9},{11,10},{12,13},{15,14},{16,17},{19,... | collective-permute-start | bytes 393224 | tf_op jit(solution)/shard_map/ppermute | solution.py:608
  50.1 16.9 %collective-permute-start.11 = (bf16[512,512]{1,0:T(8,128)(2,1)S(1)}, bf16[512,512]{1,0:T(8,128)(2,1)S(1)}, u32[]{:S(2)}, u32[]{:S(2)}) collective-permute-start(bf16[512,512]{1,0:T(8,128)(2,1)S(1)} %get-tuple-element.63), channel_id=1, source_target_pairs={{1,2},{2,1},{5,6},{6,5},{9,10},{10,9},{13,14},{14,13},{17,18},{18,... | collective-permute-start | bytes 1572872 | tf_op jit(solution)/shard_map/ppermute | solution.py:608
  52.3 7.3 %copy-start.4 = (s32[1024,1]{0,1:T(1,128)S(1)}, s32[1024,1]{0,1:T(1,128)}, u32[]{:S(2)}) copy-start(s32[1024,1]{0,1:T(1,128)} %param.13) | copy-start | bytes 12292
  52.3 7.3 %copy-start.5 = (s32[1024]{0:T(1024)S(1)}, s32[1024]{0:T(1024)}, u32[]{:S(2)}) copy-start(s32[1024]{0:T(1024)} %param.14) | copy-start | bytes 12292
  54.5 6.9 %collective-permute-start.14 = (bf16[256,256]{1,0:T(8,128)(2,1)S(1)}, bf16[256,256]{1,0:T(8,128)(2,1)S(1)}, u32[]{:S(2)}, u32[]{:S(2)}) collective-permute-start(bf16[256,256]{1,0:T(8,128)(2,1)S(1)} %att.7), channel_id=1, source_target_pairs={{0,1},{3,2},{4,5},{7,6},{8,9},{11,10},{12,13},{15,14},{16,17},{19,... | collective-permute-start | bytes 393224 | tf_op jit(solution)/shard_map/ppermute | solution.py:608
  58.9 10.2 %collective-permute-start.9 = (bf16[256,512]{1,0:T(8,128)(2,1)S(1)}, bf16[256,512]{1,0:T(8,128)(2,1)S(1)}, u32[]{:S(2)}, u32[]{:S(2)}) collective-permute-start(bf16[256,512]{1,0:T(8,128)(2,1)S(1)} %get-tuple-element.68), channel_id=1, source_target_pairs={{1,2},{2,1},{5,6},{6,5},{9,10},{10,9},{13,14},{14,13},{17,18},{18,... | collective-permute-start | bytes 786440 | tf_op jit(solution)/shard_map/ppermute | solution.py:608
  60.3 2.8 %collective-permute-start.5 = (s32[8,256]{1,0:T(8,128)S(1)}, s32[8,256]{1,0:T(8,128)S(1)}, u32[]{:S(2)}, u32[]{:S(2)}) collective-permute-start(s32[8,256]{1,0:T(8,128)S(1)} %get-tuple-element.66), channel_id=1, source_target_pairs={{0,4},{4,0},{8,12},{12,8},{16,20},{20,16},{24,28},{28,24},{1,5},{5... | collective-permute-start | bytes 24584 | tf_op jit(solution)/shard_map/ppermute | solution.py:605
  62.4 8.7 %collective-permute-start.15 = (bf16[256,512]{1,0:T(8,128)(2,1)S(1)}, bf16[256,512]{1,0:T(8,128)(2,1)S(1)}, u32[]{:S(2)}, u32[]{:S(2)}) collective-permute-start(bf16[256,512]{1,0:T(8,128)(2,1)S(1)} %get-tuple-element.77), channel_id=1, source_target_pairs={{1,2},{2,1},{5,6},{6,5},{9,10},{10,9},{13,14},{14,13},{17,18},{18,... | collective-permute-start | bytes 786440 | tf_op jit(solution)/shard_map/ppermute | solution.py:608
  63.1 5.9 %collective-permute-start.6 = (s32[16,256]{1,0:T(8,128)S(1)}, s32[16,256]{1,0:T(8,128)S(1)}, u32[]{:S(2)}, u32[]{:S(2)}) collective-permute-start(s32[16,256]{1,0:T(8,128)S(1)} %pad_add_fusion.1), channel_id=1, source_target_pairs={{0,8},{4,12},{8,0},{12,4},{16,24},{20,28},{24,16},{28,20},{1,9},{5... | collective-permute-start | bytes 49160 | tf_op jit(solution)/shard_map/ppermute | solution.py:605
  67.7 22.9 %collective-permute-start.12 = (bf16[512,256]{1,0:T(8,128)(2,1)S(1)}, bf16[512,256]{1,0:T(8,128)(2,1)S(1)}, u32[]{:S(2)}, u32[]{:S(2)}) collective-permute-start(bf16[512,256]{1,0:T(8,128)(2,1)S(1)} %get-tuple-element.73), channel_id=1, source_target_pairs={{1,0},{2,3},{5,4},{6,7},{9,8},{10,11},{13,12},{14,15},{17,16},{18,... | collective-permute-start | bytes 786440 | tf_op jit(solution)/shard_map/ppermute | solution.py:608
  69.0 4.0 %collective-permute-start.7 = (s32[32,256]{1,0:T(8,128)S(1)}, s32[32,256]{1,0:T(8,128)S(1)}, u32[]{:S(2)}, u32[]{:S(2)}) collective-permute-start(s32[32,256]{1,0:T(8,128)S(1)} %pad_add_fusion), channel_id=1, source_target_pairs={{0,16},{4,20},{8,24},{12,28},{16,0},{20,4},{24,8},{28,12},{1,17},{... | collective-permute-start | bytes 98312 | tf_op jit(solution)/shard_map/ppermute | solution.py:605
  69.7 19.5 %collective-permute-start.10 = (bf16[256,256]{1,0:T(8,128)(2,1)S(1)}, bf16[256,256]{1,0:T(8,128)(2,1)S(1)}, u32[]{:S(2)}, u32[]{:S(2)}) collective-permute-start(bf16[256,256]{1,0:T(8,128)(2,1)S(1)} %get-tuple-element.70), channel_id=1, source_target_pairs={{1,0},{2,3},{5,4},{6,7},{9,8},{10,11},{13,12},{14,15},{17,16},{18,... | collective-permute-start | bytes 393224 | tf_op jit(solution)/shard_map/ppermute | solution.py:608
  71.6 19.0 %collective-permute-start.16 = (bf16[256,256]{1,0:T(8,128)(2,1)S(1)}, bf16[256,256]{1,0:T(8,128)(2,1)S(1)}, u32[]{:S(2)}, u32[]{:S(2)}) collective-permute-start(bf16[256,256]{1,0:T(8,128)(2,1)S(1)} %get-tuple-element.79), channel_id=1, source_target_pairs={{1,0},{2,3},{5,4},{6,7},{9,8},{10,11},{13,12},{14,15},{17,16},{18,... | collective-permute-start | bytes 393224 | tf_op jit(solution)/shard_map/ppermute | solution.py:608
  93.7 15.1 %copy-start.2 = (f32[1024]{0:T(1024)S(1)}, f32[1024]{0:T(1024)}, u32[]{:S(2)}) copy-start(f32[1024]{0:T(1024)} %param.15) | copy-start | bytes 12292
  93.7 4.2 %collective-permute-start.17 = (bf16[256,256]{1,0:T(8,128)(2,1)S(1)}, bf16[256,256]{1,0:T(8,128)(2,1)S(1)}, u32[]{:S(2)}, u32[]{:S(2)}) collective-permute-start(bf16[256,256]{1,0:T(8,128)(2,1)S(1)} %get-tuple-element.82), channel_id=1, source_target_pairs={{0,4},{4,0},{8,12},{12,8},{16,20},{20,16},{24,28},{28,24},{1,5},{5... | collective-permute-start | bytes 393224 | tf_op jit(solution)/shard_map/ppermute | solution.py:605
  93.8 6.4 %collective-permute-start.18 = (bf16[256,256]{1,0:T(8,128)(2,1)S(1)}, bf16[256,256]{1,0:T(8,128)(2,1)S(1)}, u32[]{:S(2)}, u32[]{:S(2)}) collective-permute-start(bf16[256,256]{1,0:T(8,128)(2,1)S(1)} %get-tuple-element.83), channel_id=1, source_target_pairs={{0,8},{4,12},{8,0},{12,4},{16,24},{20,28},{24,16},{28,20},{1,9},{5... | collective-permute-start | bytes 393224 | tf_op jit(solution)/shard_map/ppermute | solution.py:605
  93.9 6.3 %collective-permute-start.19 = (bf16[256,256]{1,0:T(8,128)(2,1)S(1)}, bf16[256,256]{1,0:T(8,128)(2,1)S(1)}, u32[]{:S(2)}, u32[]{:S(2)}) collective-permute-start(bf16[256,256]{1,0:T(8,128)(2,1)S(1)} %get-tuple-element.84), channel_id=1, source_target_pairs={{0,16},{4,20},{8,24},{12,28},{16,0},{20,4},{24,8},{28,12},{1,17},{... | collective-permute-start | bytes 393224 | tf_op jit(solution)/shard_map/ppermute | solution.py:605
  95.7 8.1 %collective-permute-start.20 = (bf16[256,256]{1,0:T(8,128)(2,1)S(1)}, bf16[256,256]{1,0:T(8,128)(2,1)S(1)}, u32[]{:S(2)}, u32[]{:S(2)}) collective-permute-start(bf16[256,256]{1,0:T(8,128)(2,1)S(1)} %get-tuple-element.85), channel_id=1, source_target_pairs={{0,24},{4,28},{8,16},{12,20},{16,8},{20,12},{24,0},{28,4},{1,25},{... | collective-permute-start | bytes 393224 | tf_op jit(solution)/shard_map/ppermute | solution.py:605
  97.3 8.1 %collective-permute-start.21 = (bf16[256,256]{1,0:T(8,128)(2,1)S(1)}, bf16[256,256]{1,0:T(8,128)(2,1)S(1)}, u32[]{:S(2)}, u32[]{:S(2)}) collective-permute-start(bf16[256,256]{1,0:T(8,128)(2,1)S(1)} %get-tuple-element.86), channel_id=1, source_target_pairs={{0,28},{4,24},{8,20},{12,16},{16,12},{20,8},{24,4},{28,0},{1,29},{... | collective-permute-start | bytes 393224 | tf_op jit(solution)/shard_map/ppermute | solution.py:605
  97.8 9.8 %collective-permute-start.22 = (bf16[256,256]{1,0:T(8,128)(2,1)S(1)}, bf16[256,256]{1,0:T(8,128)(2,1)S(1)}, u32[]{:S(2)}, u32[]{:S(2)}) collective-permute-start(bf16[256,256]{1,0:T(8,128)(2,1)S(1)} %get-tuple-element.87), channel_id=1, source_target_pairs={{0,12},{4,8},{8,4},{12,0},{16,28},{20,24},{24,20},{28,16},{1,13},{... | collective-permute-start | bytes 393224 | tf_op jit(solution)/shard_map/ppermute | solution.py:605
  100.2 8.6 %collective-permute-start.23 = (bf16[256,256]{1,0:T(8,128)(2,1)S(1)}, bf16[256,256]{1,0:T(8,128)(2,1)S(1)}, u32[]{:S(2)}, u32[]{:S(2)}) collective-permute-start(bf16[256,256]{1,0:T(8,128)(2,1)S(1)} %get-tuple-element.88), channel_id=1, source_target_pairs={{0,20},{4,16},{8,28},{12,24},{16,4},{20,0},{24,12},{28,8},{1,21},{... | collective-permute-start | bytes 393224 | tf_op jit(solution)/shard_map/ppermute | solution.py:605
